TPU v7x, 32 devices: a whole 2x2x4 slice. The times are simulated.
32 devices in a mesh: head: 2 (over x), blk: 16 (over z, y, core).
Axes of the slice: x: 2, y: 2, z: 4, core: 2. Of those that a mesh axis runs over, the one named last changes fastest.
Arguments:
- tokens: bfloat16 [8192, 1024], P(('head', 'blk')), may hold values from -6 to 6
- cotangent: bfloat16 [8192, 1024], P(('head', 'blk')), may hold values from -6 to 6
- norm1_gain: float32 [1024], P(('head', 'blk')), may hold values from 0.1 to 1.9
- w_query: float32 [1024, 1024], P(('head', 'blk')), may hold values from -0.1875 to 0.1875
- w_key: float32 [1024, 1024], P(('head', 'blk')), may hold values from -0.1875 to 0.1875
- w_value: float32 [1024, 1024], P(('head', 'blk')), may hold values from -0.1875 to 0.1875
- w_out: float32 [1024, 1024], P(('head', 'blk')), may hold values from -0.75 to 0.75
- norm2_gain: float32 [1024], P(('head', 'blk')), may hold values from 0.1 to 1.9
- w_gate: float32 [1024, 4096], P(('head', 'blk')), may hold values from -0.1875 to 0.1875
- w_up: float32 [1024, 4096], P(('head', 'blk')), may hold values from -0.1875 to 0.1875
- w_down: float32 [4096, 1024], P(('head', 'blk')), may hold values from -0.09375 to 0.09375
- block_anchor: int32 [64], replicated, may hold values from 0 to 63, each once
- seq_lengths: int32 [8], replicated, may hold values from 1 to 4096, 8192 in all
Outputs:
- output: bfloat16 [8192, 1024], P(('head', 'blk'))
- tokens_grad: bfloat16 [8192, 1024], P(('head', 'blk'))
- norm1_gain_grad: float32 [1024], P(('head', 'blk'))
- w_query_grad: float32 [1024, 1024], P(('head', 'blk'))
- w_key_grad: float32 [1024, 1024], P(('head', 'blk'))
- w_value_grad: float32 [1024, 1024], P(('head', 'blk'))
- w_out_grad: float32 [1024, 1024], P(('head', 'blk'))
- norm2_gain_grad: float32 [1024], P(('head', 'blk'))
- w_gate_grad: float32 [1024, 4096], P(('head', 'blk'))
- w_up_grad: float32 [1024, 4096], P(('head', 'blk'))
- w_down_grad: float32 [4096, 1024], P(('head', 'blk'))
Inputs may be any that keep to these rules, and one draw needn't show every extreme that they name: `block_anchor`: a permutation of the 64 blocks. `seq_lengths`: they sum to 8192; the longest is exactly 4096.
All inputs are finite; a program needn't handle non-finite values.
Results may differ from a plain program's by a relative error of at most 0.04.
Values may be sent and summed in bfloat16 or wider, within the bound.
A program may use at most 384 MiB of HBM per device.

v0:
```python
import math

import jax
import jax.numpy as jnp
from jax import lax
from jax.sharding import PartitionSpec as P

HEAD_DIM = 64
BLOCK = 128


epsilon = 1e-06
masked_value = -1e30


def rms_parts(values):
    scaling = lax.rsqrt(jnp.mean(values * values, axis=-1, keepdims=True) + epsilon)
    return (values * scaling, scaling)


def norm_back(grad_out, normed, scaling, gain_vec):
    weighted = grad_out * gain_vec
    grad_in = scaling * (weighted - normed * jnp.mean(weighted * normed, axis=-1, keepdims=True))
    return (grad_in, jnp.sum(grad_out * normed, axis=0))


def row_outer(former, latter):
    return lax.dot_general(
        former, latter, (((0,), (0,)), ((), ())), preferred_element_type=jnp.float32
    )


def back_dot(gradient, weight):
    return lax.dot_general(
        gradient, weight, (((1,), (1,)), ((), ())), preferred_element_type=jnp.float32
    )


def allowed(query_pos, query_seg, key_pos, key_seg):
    return (query_seg[:, None] == key_seg[None, :]) & (key_pos[None, :] <= query_pos[:, None])


def masked_scores(query_block, key_block, visible, scale_factor):
    scores = (
        jnp.einsum("qhd,khd->hqk", query_block, key_block, preferred_element_type=jnp.float32)
        * scale_factor
    )
    return jnp.where(visible[None], scores, masked_value)


def online_step(carried, query_block, key_block, value_block, visible, scale_factor):

    def update(current):
        running_max, running_sum, running_acc = current
        scores = masked_scores(query_block, key_block, visible, scale_factor)
        new_max = jnp.maximum(running_max, jnp.max(scores, axis=-1))
        factor = jnp.exp(running_max - new_max)
        weights = jnp.where(visible[None], jnp.exp(scores - new_max[:, :, None]), 0.0)
        new_sum = running_sum * factor + jnp.sum(weights, axis=-1)
        contrib = jnp.einsum(
            "hqk,khd->qhd",
            weights.astype(jnp.bfloat16),
            value_block,
            preferred_element_type=jnp.float32,
        )
        new_acc = running_acc * jnp.transpose(factor)[:, :, None] + contrib
        return (new_max, new_sum, new_acc)

    return lax.cond(jnp.any(visible), update, lambda current: current, carried)


def pair_terms(query_side, key_block, value_block, visible, scale_factor):
    query_block, grad_block, norm_block, delta_block = query_side
    scores = masked_scores(query_block, key_block, visible, scale_factor)
    probabilities = jnp.where(visible[None], jnp.exp(scores - norm_block[:, :, None]), 0.0)
    prob_grad = jnp.einsum(
        "qhd,khd->hqk", grad_block, value_block, preferred_element_type=jnp.float32
    )
    score_grad = (probabilities * (prob_grad - delta_block[:, :, None])).astype(jnp.bfloat16)
    return (probabilities, score_grad)


def query_update(grad_acc, query_side, key_block, value_block, visible, scale_factor):

    def update(current):
        probabilities, score_grad = pair_terms(
            query_side, key_block, value_block, visible, scale_factor
        )
        return (
            current
            + jnp.einsum("hqk,khd->qhd", score_grad, key_block, preferred_element_type=jnp.float32)
            * scale_factor
        )

    return lax.cond(jnp.any(visible), update, lambda current: current, grad_acc)


def key_update(grad_pair, query_side, key_block, value_block, visible, scale_factor):

    def update(current):
        probabilities, score_grad = pair_terms(
            query_side, key_block, value_block, visible, scale_factor
        )
        key_grad = (
            current[0]
            + jnp.einsum(
                "hqk,qhd->khd", score_grad, query_side[0], preferred_element_type=jnp.float32
            )
            * scale_factor
        )
        value_grad = current[1] + jnp.einsum(
            "hqk,qhd->khd",
            probabilities.astype(jnp.bfloat16),
            query_side[1],
            preferred_element_type=jnp.float32,
        )
        return (key_grad, value_grad)

    return lax.cond(jnp.any(visible), update, lambda current: current, grad_pair)


def fold_labels(block_anchor, seq_lengths, head_count, fold_count):
    per_device = block_anchor.shape[0] // (head_count * fold_count)
    block_order = jnp.transpose(
        block_anchor.reshape(head_count, fold_count, per_device), (1, 0, 2)
    ).reshape(-1)
    positions = (
        block_order[:, None] * BLOCK + jnp.arange(BLOCK, dtype=jnp.int32)[None, :]
    ).reshape(-1)
    seq_ends = jnp.cumsum(seq_lengths)
    segments = jnp.sum((positions[:, None] >= seq_ends[None, :]).astype(jnp.int32), axis=1)
    return (positions, segments)


def cut_piece(members, label_sets, size_cap):
    length = members[0].shape[0]
    sub_rows = math.gcd(length, size_cap)
    blocks = length // sub_rows
    shaped = tuple((member.reshape(blocks, sub_rows, -1, HEAD_DIM) for member in members))
    cut_labels = tuple((label_set.reshape(blocks, sub_rows) for label_set in label_sets))
    return (shaped, cut_labels, sub_rows)


def cut_stats(statistics, length, sub_rows):
    blocks = length // sub_rows
    return tuple(
        (
            jnp.transpose(member.reshape(member.shape[0], blocks, sub_rows), (1, 0, 2))
            for member in statistics
        )
    )


def body(
    tokens,
    cotangent,
    norm1_gain,
    w_query,
    w_key,
    w_value,
    w_out,
    norm2_gain,
    w_gate,
    w_up,
    w_down,
    block_anchor,
    seq_lengths,
):
    head_count = lax.axis_size("head")
    fold_count = lax.axis_size("blk")
    scale_factor = 1.0 / math.sqrt(HEAD_DIM)
    gain_one, query_mat, key_mat, value_mat, out_mat, gain_two = (
        lax.all_gather(norm1_gain.astype(jnp.bfloat16), ("head", "blk"), axis=0, tiled=True),
        lax.all_gather(w_query.astype(jnp.bfloat16), ("head", "blk"), axis=0, tiled=True),
        lax.all_gather(w_key.astype(jnp.bfloat16), ("head", "blk"), axis=0, tiled=True),
        lax.all_gather(w_value.astype(jnp.bfloat16), ("head", "blk"), axis=0, tiled=True),
        lax.all_gather(w_out.astype(jnp.bfloat16), ("head", "blk"), axis=0, tiled=True),
        lax.all_gather(norm2_gain.astype(jnp.bfloat16), ("head", "blk"), axis=0, tiled=True),
    )
    inputs = tokens.astype(jnp.float32)
    normed_one, scaling_one = rms_parts(inputs)
    hidden_one = (normed_one * gain_one.astype(jnp.float32)).astype(jnp.bfloat16)
    query_rows = jnp.dot(hidden_one, query_mat, preferred_element_type=jnp.float32).astype(
        jnp.bfloat16
    )
    key_rows = jnp.dot(hidden_one, key_mat, preferred_element_type=jnp.float32).astype(jnp.bfloat16)
    value_rows = jnp.dot(hidden_one, value_mat, preferred_element_type=jnp.float32).astype(
        jnp.bfloat16
    )
    queries, key_heads, value_heads = (
        lax.all_to_all(query_rows, "head", split_axis=1, concat_axis=0, tiled=True),
        lax.all_to_all(key_rows, "head", split_axis=1, concat_axis=0, tiled=True),
        lax.all_to_all(value_rows, "head", split_axis=1, concat_axis=0, tiled=True),
    )
    group_rows = queries.shape[0]
    local_heads = queries.shape[1] // HEAD_DIM
    positions, segments = fold_labels(block_anchor, seq_lengths, head_count, fold_count)
    own_first = lax.axis_index("blk") * group_rows
    own_pos = lax.dynamic_slice_in_dim(positions, own_first, group_rows)
    own_seg = lax.dynamic_slice_in_dim(segments, own_first, group_rows)
    query_size = min(group_rows, 512)
    key_size = min(group_rows, 256)
    query_starts = list(range(0, group_rows, query_size))
    key_starts = list(range(0, group_rows, key_size))
    query_cube = queries.reshape(group_rows, local_heads, HEAD_DIM)
    key_cube = key_heads.reshape(group_rows, local_heads, HEAD_DIM)
    value_cube = value_heads.reshape(group_rows, local_heads, HEAD_DIM)
    start_state = tuple(
        (
            (
                jnp.full((local_heads, query_size), masked_value, jnp.float32),
                jnp.zeros((local_heads, query_size), jnp.float32),
                jnp.zeros((query_size, local_heads, HEAD_DIM), jnp.float32),
            )
            for offset in query_starts
        )
    )
    shaped, cut_labels, sub_rows = cut_piece(
        (
            lax.all_gather(key_heads, "blk", axis=0, tiled=True),
            lax.all_gather(value_heads, "blk", axis=0, tiled=True),
        ),
        (positions, segments),
        256,
    )

    def forward_one_block(inner_state, member):
        key_block, value_block, key_pos, key_seg = member
        return (
            tuple(
                (
                    online_step(
                        inner_state[slot_index],
                        query_cube,
                        key_block,
                        value_block,
                        allowed(own_pos, own_seg, key_pos, key_seg),
                        scale_factor,
                    )
                    for slot_index, offset in enumerate(query_starts)
                )
            ),
            None,
        )

    final_state = lax.scan(forward_one_block, start_state, shaped + cut_labels)[0]
    attn_heads = jnp.concatenate(
        [block_state[2] / jnp.transpose(block_state[1])[:, :, None] for block_state in final_state],
        axis=0,
    )
    log_norm = jnp.concatenate(
        [block_state[0] + jnp.log(block_state[1]) for block_state in final_state], axis=1
    )
    attn_rows = lax.all_to_all(
        attn_heads.reshape(group_rows, -1).astype(jnp.bfloat16),
        "head",
        split_axis=0,
        concat_axis=1,
        tiled=True,
    )
    residual = inputs + jnp.dot(attn_rows, out_mat, preferred_element_type=jnp.float32)
    normed_two, scaling_two = rms_parts(residual)
    hidden_two = (normed_two * gain_two.astype(jnp.float32)).astype(jnp.bfloat16)
    gate_mat, up_mat, down_mat = (
        lax.all_gather(w_gate.astype(jnp.bfloat16), ("head", "blk"), axis=0, tiled=True),
        lax.all_gather(w_up.astype(jnp.bfloat16), ("head", "blk"), axis=0, tiled=True),
        lax.all_gather(w_down.astype(jnp.bfloat16), ("head", "blk"), axis=0, tiled=True),
    )
    gate_lin = jnp.dot(hidden_two, gate_mat, preferred_element_type=jnp.float32)
    up_lin = jnp.dot(hidden_two, up_mat, preferred_element_type=jnp.float32)
    sigmoid_gate = jax.nn.sigmoid(gate_lin)
    hidden_mlp = (gate_lin * sigmoid_gate * up_lin).astype(jnp.bfloat16)
    branch_term = jnp.dot(hidden_mlp, down_mat, preferred_element_type=jnp.float32)
    output = (residual + branch_term).astype(jnp.bfloat16)
    gain_one, query_mat, key_mat, value_mat, out_mat, gain_two = (
        lax.all_gather(norm1_gain.astype(jnp.bfloat16), ("head", "blk"), axis=0, tiled=True),
        lax.all_gather(w_query.astype(jnp.bfloat16), ("head", "blk"), axis=0, tiled=True),
        lax.all_gather(w_key.astype(jnp.bfloat16), ("head", "blk"), axis=0, tiled=True),
        lax.all_gather(w_value.astype(jnp.bfloat16), ("head", "blk"), axis=0, tiled=True),
        lax.all_gather(w_out.astype(jnp.bfloat16), ("head", "blk"), axis=0, tiled=True),
        lax.all_gather(norm2_gain.astype(jnp.bfloat16), ("head", "blk"), axis=0, tiled=True),
    )
    down_grad = row_outer(hidden_mlp, cotangent)
    hidden_grad = back_dot(cotangent, down_mat)
    gate_back = (
        hidden_grad * up_lin * sigmoid_gate * (1.0 + gate_lin * (1.0 - sigmoid_gate))
    ).astype(jnp.bfloat16)
    up_back = (hidden_grad * gate_lin * sigmoid_gate).astype(jnp.bfloat16)
    gate_grad = row_outer(hidden_two, gate_back)
    up_grad = row_outer(hidden_two, up_back)
    normed_grad_two = back_dot(gate_back, gate_mat) + back_dot(up_back, up_mat)
    mlp_shares = (
        lax.psum_scatter(gate_grad, ("head", "blk"), scatter_dimension=0, tiled=True),
        lax.psum_scatter(up_grad, ("head", "blk"), scatter_dimension=0, tiled=True),
        lax.psum_scatter(down_grad, ("head", "blk"), scatter_dimension=0, tiled=True),
    )
    residual_part, gain_two_grad = norm_back(
        normed_grad_two, normed_two, scaling_two, gain_two.astype(jnp.float32)
    )
    residual_grad = cotangent.astype(jnp.float32) + residual_part
    branch_back = residual_grad.astype(jnp.bfloat16)
    out_grad = row_outer(attn_rows, branch_back)
    attn_back_rows = back_dot(branch_back, out_mat).astype(jnp.bfloat16)
    grad_heads = lax.all_to_all(attn_back_rows, "head", split_axis=1, concat_axis=0, tiled=True)
    grad_cube = grad_heads.reshape(group_rows, local_heads, HEAD_DIM)
    delta_rows = jnp.transpose(jnp.sum(grad_cube.astype(jnp.float32) * attn_heads, axis=-1))
    all_norm, all_delta = (
        lax.all_gather(log_norm.astype(jnp.bfloat16), "blk", axis=1, tiled=True).astype(
            log_norm.dtype
        ),
        lax.all_gather(delta_rows.astype(jnp.bfloat16), "blk", axis=1, tiled=True).astype(
            delta_rows.dtype
        ),
    )
    own_sides = [(query_cube, grad_cube, log_norm, delta_rows) for offset in query_starts]
    query_zero = tuple(
        (jnp.zeros((query_size, local_heads, HEAD_DIM), jnp.float32) for offset in query_starts)
    )
    key_zero = tuple(
        (
            (
                jnp.zeros((key_size, local_heads, HEAD_DIM), jnp.float32),
                jnp.zeros((key_size, local_heads, HEAD_DIM), jnp.float32),
            )
            for offset in key_starts
        )
    )
    shaped, cut_labels, sub_rows = cut_piece(
        (
            lax.all_gather(key_heads, "blk", axis=0, tiled=True),
            lax.all_gather(value_heads, "blk", axis=0, tiled=True),
        ),
        (positions, segments),
        256,
    )

    def keys_one_block(inner_state, member):
        key_block, value_block, key_pos, key_seg = member
        return (
            tuple(
                (
                    query_update(
                        inner_state[slot_index],
                        own_sides[slot_index],
                        key_block,
                        value_block,
                        allowed(own_pos, own_seg, key_pos, key_seg),
                        scale_factor,
                    )
                    for slot_index, offset in enumerate(query_starts)
                )
            ),
            None,
        )

    query_acc = lax.scan(keys_one_block, query_zero, shaped + cut_labels)[0]
    pieces = (
        lax.all_gather(queries, "blk", axis=0, tiled=True),
        lax.all_gather(grad_heads, "blk", axis=0, tiled=True),
    )
    shaped, cut_labels, sub_rows = cut_piece(pieces, (positions, segments), 512)
    norm_cut, delta_cut = cut_stats((all_norm, all_delta), pieces[0].shape[0], sub_rows)

    def queries_one_block(inner_state, member):
        query_block, grad_block, query_pos, query_seg, norm_block, delta_block = member
        return (
            tuple(
                (
                    key_update(
                        inner_state[slot_index],
                        (query_block, grad_block, norm_block, delta_block),
                        key_cube[offset : offset + key_size],
                        value_cube[offset : offset + key_size],
                        allowed(
                            query_pos,
                            query_seg,
                            own_pos[offset : offset + key_size],
                            own_seg[offset : offset + key_size],
                        ),
                        scale_factor,
                    )
                    for slot_index, offset in enumerate(key_starts)
                )
            ),
            None,
        )

    key_acc = lax.scan(queries_one_block, key_zero, shaped + cut_labels + (norm_cut, delta_cut))[0]
    query_grad_heads = query_acc[0].reshape(group_rows, -1).astype(jnp.bfloat16)
    key_grad_heads = (
        jnp.concatenate([grad_pair[0] for grad_pair in key_acc], axis=0)
        .reshape(group_rows, -1)
        .astype(jnp.bfloat16)
    )
    value_grad_heads = (
        jnp.concatenate([grad_pair[1] for grad_pair in key_acc], axis=0)
        .reshape(group_rows, -1)
        .astype(jnp.bfloat16)
    )
    query_back, key_back, value_back = (
        lax.all_to_all(query_grad_heads, "head", split_axis=0, concat_axis=1, tiled=True),
        lax.all_to_all(key_grad_heads, "head", split_axis=0, concat_axis=1, tiled=True),
        lax.all_to_all(value_grad_heads, "head", split_axis=0, concat_axis=1, tiled=True),
    )
    query_grad = row_outer(hidden_one, query_back)
    key_grad = row_outer(hidden_one, key_back)
    value_grad = row_outer(hidden_one, value_back)
    normed_grad_one = (
        back_dot(query_back, query_mat)
        + back_dot(key_back, key_mat)
        + back_dot(value_back, value_mat)
    )
    input_part, gain_one_grad = norm_back(
        normed_grad_one, normed_one, scaling_one, gain_one.astype(jnp.float32)
    )
    tokens_grad = (residual_grad + input_part).astype(jnp.bfloat16)
    attn_shares = (
        lax.psum_scatter(gain_one_grad, ("head", "blk"), scatter_dimension=0, tiled=True),
        lax.psum_scatter(query_grad, ("head", "blk"), scatter_dimension=0, tiled=True),
        lax.psum_scatter(key_grad, ("head", "blk"), scatter_dimension=0, tiled=True),
        lax.psum_scatter(value_grad, ("head", "blk"), scatter_dimension=0, tiled=True),
        lax.psum_scatter(out_grad, ("head", "blk"), scatter_dimension=0, tiled=True),
        lax.psum_scatter(gain_two_grad, ("head", "blk"), scatter_dimension=0, tiled=True),
    )
    return (
        output,
        tokens_grad,
        attn_shares[0],
        attn_shares[1],
        attn_shares[2],
        attn_shares[3],
        attn_shares[4],
        attn_shares[5],
        mlp_shares[0],
        mlp_shares[1],
        mlp_shares[2],
    )


def solution(mesh):
    return jax.shard_map(
        body,
        mesh=mesh,
        in_specs=(
            P(("head", "blk"), None),
            P(("head", "blk"), None),
            P(("head", "blk")),
            P(("head", "blk"), None),
            P(("head", "blk"), None),
            P(("head", "blk"), None),
            P(("head", "blk"), None),
            P(("head", "blk")),
            P(("head", "blk"), None),
            P(("head", "blk"), None),
            P(("head", "blk"), None),
            P(),
            P(),
        ),
        out_specs=(
            P(("head", "blk"), None),
            P(("head", "blk"), None),
            P(("head", "blk")),
            P(("head", "blk"), None),
            P(("head", "blk"), None),
            P(("head", "blk"), None),
            P(("head", "blk"), None),
            P(("head", "blk")),
            P(("head", "blk"), None),
            P(("head", "blk"), None),
            P(("head", "blk"), None),
        ),
        check_vma=False,
    )
```

profile of v0, /device:TPU:0, one launch (start us, length us, event | category | flops | bytes accessed | tf_op | source)
XLA Modules:
  0.0 2446.0 jit_solution(13409926971716504991)
XLA Ops:
  13.8 42.1 %all-reduce.5 = (bf16[1024]{0:T(1024)(128)(2,1)S(1)}, bf16[1024]{0:T(1024)(128)(2,1)S(1)}) all-reduce(bf16[1024]{0:T(1024)(128)(2,1)S(1)} %dynamic-update-slice, bf16[1024]{0:T(1024)(128)(2,1)S(1)} %dynamic-update-slice.1), channel_id=1, replica_groups=mesh['head'=2,'blk'=16] {'head','blk'}, use_global_device_ids=true, to_apply=%add | all-reduce | flops 2048 | bytes 8192
  57.1 13.6 all-gather.12.cloned.1.call-done
  73.3 12.4 all_to_all.140
  85.9 43.6 %all-gather.18.cloned.1.call-done = bf16[1024,1024]{1,0:T(8,128)(2,1)} async-done(((bf16[32,1024]{1,0:T(8,128)(2,1)}), bf16[1024,1024]{1,0:T(8,128)(2,1)}) %all-gather.18.cloned.1.call-update) | async-done | bytes 2097168 | tf_op jit(solution)/shard_map/all_gather | solution.py:176
  131.8 12.2 all_to_all.141
  148.0 40.2 %all-gather.16.cloned.1.call-done = bf16[1024,1024]{1,0:T(8,128)(2,1)} async-done(((bf16[32,1024]{1,0:T(8,128)(2,1)}), bf16[1024,1024]{1,0:T(8,128)(2,1)}) %all-gather.16.cloned.1.call-update) | async-done | bytes 2097168 | tf_op jit(solution)/shard_map/all_gather | solution.py:174
  204.4 59.6 %all-gather.14.cloned.1.call-done = bf16[8192,512]{1,0:T(8,128)(2,1)} async-done(((bf16[512,512]{1,0:T(8,128)(2,1)}), bf16[8192,512]{1,0:T(8,128)(2,1)}) %all-gather.14.cloned.1.call-update) | async-done | bytes 8388624 | tf_op jit(solution)/shard_map/all_gather | solution.py:220
  264.0 21.3 reshape.247
  285.3 17.4 copy.135
  302.7 36.5 %all-gather.20.cloned.1.call-done = bf16[8192,512]{1,0:T(8,128)(2,1)} async-done(((bf16[512,512]{1,0:T(8,128)(2,1)}), bf16[8192,512]{1,0:T(8,128)(2,1)}) %all-gather.20.cloned.1.call-update) | async-done | bytes 8388624 | tf_op jit(solution)/shard_map/all_gather | solution.py:221
  339.2 21.2 reshape.248
  360.4 17.1 copy.136
  377.6 207.9 %while.43 = (s32[]{:T(128)}, f32[8,512]{1,0:T(8,128)S(1)}, f32[8,512]{1,0:T(8,128)S(1)}, f32[512,8,64]{0,2,1:T(8,128)S(1)}, s32[512]{0:T(512)S(1)}, /*index=5*/s...) while((s32[]{:T(128)}, f32[8,512]{1,0:T(8,128)S(1)}, ...), condition=%wide.region_9.10_spmd, body=%wide.region_3.9_spmd.sunk | while | flops 283127808 | bytes 16526591 | solution.py:246
  617.5 20.3 all-gather.28.cloned.1.call-done
  637.9 12.3 multiply_convert_fusion.2
  663.2 11.8 all_to_all.142
  681.1 32.8 %all-gather.30.cloned.1.call-done = bf16[8192,512]{1,0:T(8,128)(2,1)} async-done(((bf16[512,512]{1,0:T(8,128)(2,1)}), bf16[8192,512]{1,0:T(8,128)(2,1)}) %all-gather.30.cloned.1.call-update) | async-done | bytes 8388624 | tf_op jit(solution)/shard_map/all_gather | solution.py:358
  714.0 21.3 reshape.245
  735.3 18.4 copy.149
  753.7 31.5 %all_gather.65 = bf16[8,8192]{1,0:T(8,128)(2,1)S(1)} all-gather(bf16[8,512]{1,0:T(8,128)(2,1)S(1)} %get-tuple-element.701), channel_id=1, replica_groups=mesh['head'=2,'blk'=16] {'blk'}, dimensions={1}, use_global_device_ids=true | all-gather | bytes 139264 | tf_op jit(solution)/shard_map/all_gather | solution.py:308
  792.5 310.9 %while.44 = (s32[]{:T(128)}, f32[512,8,64]{0,2,1:T(8,128)S(1)}, s32[512]{0:T(512)S(1)}, s32[32,256]{1,0:T(8,128)S(1)}, s32[32,256]{1,0:T(8,128)}, /*index=5*/s32...) while((s32[]{:T(128)}, f32[512,8,64]{0,2,1:T(8,128)S(1)}, ...), condition=%wide.region_17.18_spmd, body=%wide.region_13.17_spmd.sunk | while | flops 411041792 | bytes 12627679 | solution.py:356
  1108.0 17.5 all_gather.67
  1129.2 21.2 reshape.246
  1150.4 18.3 copy.150
  1171.3 332.6 %while.45 = (s32[]{:T(128)}, f32[256,8,64]{0,2,1:T(8,128)S(1)}, f32[256,8,64]{0,2,1:T(8,128)}, f32[256,8,64]{0,2,1:T(8,128)}, f32[256,8,64]{0,2,1:T(8,128)}, /*i...) while((s32[]{:T(128)}, f32[256,8,64]{0,2,1:T(8,128)S(1)}, ...), condition=%wide.region_25.26_spmd, body=%wide.region_18.25_spmd.sunk | while | flops 1100742656 | bytes 37675412 | solution.py:388
  1174.9 10.9 conditional.10
  1186.5 11.8 conditional.11
  1202.6 11.8 conditional.11
  1218.7 11.8 conditional.11
  1234.8 11.8 conditional.11
  1250.2 10.9 conditional.10
  1261.8 11.7 conditional.11
  1288.8 11.7 conditional.11
  1304.8 11.7 conditional.11
  1331.8 11.7 conditional.11
  1347.8 11.7 conditional.11
  1379.2 11.7 conditional.11
  1395.2 11.7 conditional.11
  1422.2 11.7 conditional.11
  1449.2 11.7 conditional.11
  1465.2 11.7 conditional.11
  1492.2 11.7 conditional.11
  1572.7 122.2 %all-reduce.4 = (f32[1024]{0:T(1024)S(1)}, f32[1024]{0:T(1024)S(1)}) all-reduce(f32[1024]{0:T(1024)S(1)} %get-tuple-element.609, f32[1024]{0:T(1024)S(1)} %copy-done.31), channel_id=2, replica_groups=mesh['head'=2,'blk'=16] {'head','blk'}, use_global_device_ids=true, to_apply=%region_28.29.clone | all-reduce | flops 2048 | bytes 16384
  1697.1 44.6 %reduce-scatter.10.cloned.1.call-done = f32[32,1024]{1,0:T(8,128)} async-done(((f32[1024,1024]{1,0:T(8,128)}), f32[32,1024]{1,0:T(8,128)}) %reduce-scatter.10.cloned.1.call-update) | async-done | bytes 131088 | tf_op jit(solution)/shard_map/reduce_scatter | solution.py:420
  1741.7 140.3 %reduce-scatter.12.cloned.1.call-done = f32[32,1024]{1,0:T(8,128)} async-done(((f32[1024,1024]{1,0:T(8,128)}), f32[32,1024]{1,0:T(8,128)}) %reduce-scatter.12.cloned.1.call-update) | async-done | bytes 131088 | tf_op jit(solution)/shard_map/reduce_scatter | solution.py:421
  1882.0 182.8 %reduce-scatter.16.cloned.1.call-done = f32[32,4096]{1,0:T(8,128)} async-done(((f32[1024,4096]{1,0:T(8,128)}), f32[32,4096]{1,0:T(8,128)}) %reduce-scatter.16.cloned.1.call-update) | async-done | bytes 524304 | tf_op jit(solution)/shard_map/reduce_scatter | solution.py:293
  2064.8 186.6 %reduce-scatter.18.cloned.1.call-done = f32[32,4096]{1,0:T(8,128)} async-done(((f32[1024,4096]{1,0:T(8,128)}), f32[32,4096]{1,0:T(8,128)}) %reduce-scatter.18.cloned.1.call-update) | async-done | bytes 524304 | tf_op jit(solution)/shard_map/reduce_scatter | solution.py:294
  2251.4 187.3 %reduce-scatter.20.cloned.1.call-done = f32[128,1024]{1,0:T(8,128)} async-done(((f32[4096,1024]{1,0:T(8,128)}), f32[128,1024]{1,0:T(8,128)}) %reduce-scatter.20.cloned.1.call-update) | async-done | bytes 524304 | tf_op jit(solution)/shard_map/reduce_scatter | solution.py:295
  (821 shorter events, 1421.9 us)
Async XLA Ops:
  7.2 122.3 %copy-start = (bf16[256,1024]{1,0:T(8,128)(2,1)S(1)}, bf16[256,1024]{1,0:T(8,128)(2,1)}, u32[]{:S(2)}) copy-start(bf16[256,1024]{1,0:T(8,128)(2,1)} %param.27) | copy-start | bytes 1572868
  7.2 63.5 %all-gather.12.cloned.1.call-start = ((), (), s32[]{:S(2)}) async-start(), calls=%async_computation.15 | async-start | bytes 2162688 | tf_op jit(solution)/shard_map/all_gather | solution.py:175
  8.8 120.6 %all-gather.18.cloned.1.call-start = ((), (), s32[]{:S(2)}) async-start(), calls=%async_computation.18 | async-start | bytes 2162688 | tf_op jit(solution)/shard_map/all_gather | solution.py:176
  10.5 177.7 %all-gather.16.cloned.1.call-start = ((), (), s32[]{:S(2)}) async-start(), calls=%async_computation.17 | async-start | bytes 2162688 | tf_op jit(solution)/shard_map/all_gather | solution.py:174
  12.1 251.9 %all-gather.14.cloned.1.call-start = ((), (), s32[]{:S(2)}) async-start(), calls=%async_computation.16 | async-start | bytes 8912896 | tf_op jit(solution)/shard_map/all_gather | solution.py:220
  73.3 70.9 %copy-start.29 = (f32[32,1024]{1,0:T(8,128)S(1)}, f32[32,1024]{1,0:T(8,128)}, u32[]{:S(2)}) copy-start(f32[32,1024]{1,0:T(8,128)} %param.33) | copy-start | bytes 393220
  73.3 71.6 %copy-start.26 = (f32[32,4096]{1,0:T(8,128)S(1)}, f32[32,4096]{1,0:T(8,128)}, u32[]{:S(2)}) copy-start(f32[32,4096]{1,0:T(8,128)} %param.35) | copy-start | bytes 1572868
  85.7 60.0 %copy-start.27 = (f32[32,4096]{1,0:T(8,128)S(1)}, f32[32,4096]{1,0:T(8,128)}, u32[]{:S(2)}) copy-start(f32[32,4096]{1,0:T(8,128)} %param.36) | copy-start | bytes 1572868
  85.8 60.7 %copy-start.28 = (f32[128,1024]{1,0:T(8,128)S(1)}, f32[128,1024]{1,0:T(8,128)}, u32[]{:S(2)}) copy-start(f32[128,1024]{1,0:T(8,128)} %param.37) | copy-start | bytes 1572868
  85.8 61.5 %copy-start.33 = (s32[64]{0:T(128)S(1)}, s32[64]{0:T(128)}, u32[]{:S(2)}) copy-start(s32[64]{0:T(128)} %param.38) | copy-start | bytes 772
  85.8 61.7 %copy-start.34 = (s32[8]{0:T(128)S(1)}, s32[8]{0:T(128)}, u32[]{:S(2)}) copy-start(s32[8]{0:T(128)} %param.39) | copy-start | bytes 100
  85.8 253.4 %all-gather.20.cloned.1.call-start = ((), (), s32[]{:S(2)}) async-start(), calls=%async_computation.19 | async-start | bytes 8912896 | tf_op jit(solution)/shard_map/all_gather | solution.py:221
  144.1 446.4 %all-gather.22.cloned.1.call-start = ((), (), s32[]{:S(2)}) async-start(), calls=%async_computation.20 | async-start | bytes 2162688 | tf_op jit(solution)/shard_map/all_gather | solution.py:177
  144.8 456.6 %all-gather.24.cloned.1.call-start = ((), (), s32[]{:S(2)}) async-start(), calls=%async_computation.21 | async-start | bytes 8650752 | tf_op jit(solution)/shard_map/all_gather | solution.py:265
  145.7 464.1 %all-gather.26.cloned.1.call-start = ((), (), s32[]{:S(2)}) async-start(), calls=%async_computation.22 | async-start | bytes 8650752 | tf_op jit(solution)/shard_map/all_gather | solution.py:266
  146.5 491.4 %all-gather.28.cloned.1.call-start = ((), (), s32[]{:S(2)}) async-start(), calls=%async_computation.23 | async-start | bytes 8650752 | tf_op jit(solution)/shard_map/all_gather | solution.py:267
  191.4 12.2 all-to-all-start.1
  194.9 519.1 %all-gather.30.cloned.1.call-start = ((), (), s32[]{:S(2)}) async-start(), calls=%async_computation.24 | async-start | bytes 8912896 | tf_op jit(solution)/shard_map/all_gather | solution.py:358
  585.6 13.1 copy-start.5
  585.6 15.7 copy-start.30
  586.7 11.9 all-to-all-start.3
  590.2 539.0 %all-gather.32.cloned.1.call-start = ((), (), s32[]{:S(2)}) async-start(), calls=%async_computation.25 | async-start | bytes 8912896 | tf_op jit(solution)/shard_map/all_gather | solution.py:359
  598.6 2.6 copy-start.16
  601.3 56.3 %copy-start.3 = (f32[256,1024]{1,0:T(8,128)}, f32[256,1024]{1,0:T(8,128)S(1)}, u32[]{:S(2)}) copy-start(f32[256,1024]{1,0:T(8,128)S(1)} %get-tuple-element.727) | copy-start | bytes 3145732
  601.5 8.3 copy-start.8
  609.7 28.1 %copy-start.22 = (bf16[256,1024]{1,0:T(8,128)(2,1)S(1)}, bf16[256,1024]{1,0:T(8,128)(2,1)}, u32[]{:S(2)}) copy-start(bf16[256,1024]{1,0:T(8,128)(2,1)} %param.28) | copy-start | bytes 1572868
  650.2 7.3 copy-start.25
  650.2 7.4 copy-start.24
  650.2 7.4 copy-start.32
  657.6 4.8 copy-start.7
  660.8 14.6 copy-start.12
  662.4 123.5 %copy-start.1 = (f32[256,1024]{1,0:T(8,128)}, f32[256,1024]{1,0:T(8,128)S(1)}, u32[]{:S(2)}) copy-start(f32[256,1024]{1,0:T(8,128)S(1)} %multiply_add_fusion.1) | copy-start | bytes 3145732
  662.4 15.5 copy-start.13
  675.0 1022.1 %reduce-scatter.14.cloned.1.call-start = ((), (), s32[]{:S(2)}) async-start(), calls=%async_computation.29 | async-start | bytes 4325376 | tf_op jit(solution)/shard_map/reduce_scatter | solution.py:422
  785.8 3.9 copy-start.15
  1104.5 21.8 all-to-all-start.5
  1108.0 589.2 %reduce-scatter.8.cloned.1.call-start = ((), (), s32[]{:S(2)}) async-start(), calls=%async_computation.26 | async-start | bytes 4325376 | tf_op jit(solution)/shard_map/reduce_scatter | solution.py:419
  1129.1 612.6 %reduce-scatter.10.cloned.1.call-start = ((), (), s32[]{:S(2)}) async-start(), calls=%async_computation.27 | async-start | bytes 4325376 | tf_op jit(solution)/shard_map/reduce_scatter | solution.py:420
  1514.9 2.9 copy-start.19
  1514.9 3.0 copy-start.18
  1517.8 364.3 %reduce-scatter.12.cloned.1.call-start = ((), (), s32[]{:S(2)}) async-start(), calls=%async_computation.28 | async-start | bytes 4325376 | tf_op jit(solution)/shard_map/reduce_scatter | solution.py:421
  1527.2 2.9 copy-start.10
  1527.2 3.1 copy-start.9
  1530.0 534.7 %reduce-scatter.16.cloned.1.call-start = ((), (), s32[]{:S(2)}) async-start(), calls=%async_computation.30 | async-start | bytes 17301504 | tf_op jit(solution)/shard_map/reduce_scatter | solution.py:293
  1540.1 711.3 %reduce-scatter.18.cloned.1.call-start = ((), (), s32[]{:S(2)}) async-start(), calls=%async_computation.31 | async-start | bytes 17301504 | tf_op jit(solution)/shard_map/reduce_scatter | solution.py:294
  1549.9 888.8 %reduce-scatter.20.cloned.1.call-start = ((), (), s32[]{:S(2)}) async-start(), calls=%async_computation.32 | async-start | bytes 17301504 | tf_op jit(solution)/shard_map/reduce_scatter | solution.py:295
  1561.9 7.3 copy-start.17
  1570.8 125.2 %copy-start.2 = (f32[256,1024]{1,0:T(8,128)S(1)}, f32[256,1024]{1,0:T(8,128)}, u32[]{:S(2)}) copy-start(f32[256,1024]{1,0:T(8,128)} %copy-done.1) | copy-start | bytes 3145732
  (8 other events, 13.9 us)
Sparse Core Ops, SparseCore 0:
  11.5 59.1 all-gather.11
  74.1 55.2 all-gather.17
  132.9 55.2 all-gather.15
  190.2 73.7 all-gather.13
  266.0 73.1 all-gather.19
  342.5 54.6 all-gather.21
  400.7 76.3 all-gather.23
  480.0 76.6 all-gather.25
  559.6 78.2 all-gather.27
  640.5 73.4 all-gather.29
  716.1 73.8 all-gather.31
  792.7 140.3 reduce-scatter.13
  1129.2 140.1 reduce-scatter.7
  1517.9 223.7 reduce-scatter.9
  1744.4 137.5 reduce-scatter.11
  1884.8 179.9 reduce-scatter.15
  2067.5 183.8 reduce-scatter.17
  2254.1 184.5 reduce-scatter.19
where the time goes:
time: 2440 us; the launch traced here: 2450 us
  waiting for transfers between devices  1010 us (41%)
  matrix products  730 us (30%)
  blocking collectives  268 us (11%)
  local copies, waits for them, and re-layouts  233 us (10%)
  other arithmetic  115 us (5%)
  loops' own time  67.4 us (3%)
    dot_general x83, matrix products, masked_scores(): jnp.einsum('qhd,khd->hqk', query_block, key_block, preferred_element_type...  228 us
    reduce_scatter x1, waiting for transfers between devices, body(): lax.psum_scatter(down_grad, ('head', 'blk'), scatter_dimension=0, tiled=T...  187 us
    reduce_scatter x1, waiting for transfers between devices, body(): lax.psum_scatter(up_grad, ('head', 'blk'), scatter_dimension=0, tiled=True)  187 us
    reduce_scatter x1, waiting for transfers between devices, body(): lax.psum_scatter(gate_grad, ('head', 'blk'), scatter_dimension=0, tiled=T...  183 us
    unnamed x2, blocking collectives  164 us
    reduce_scatter x1, waiting for transfers between devices, body(): lax.psum_scatter(value_grad, ('head', 'blk'), scatter_dimension=0, tiled=...  140 us
    dot_general x30, matrix products, update(): jnp.einsum('hqk,khd->qhd', score_grad, key_block, preferred_element_type=...  129 us
    dot_general x23, matrix products, update(): jnp.einsum('hqk,qhd->khd', score_grad, query_side[0], preferred_element_t...  111 us
  transfers between devices with their start and end apart: 21, of which 14 were waited for; matrix products, arithmetic and copies ran while one was open for 44% of the time, Pallas kernels for 0%

commit v1 on v0

v1 whole, which is shorter than its diff:
```python
import functools

import jax
import jax.numpy as jnp
from jax import lax
from jax.experimental import pallas as pl
from jax.experimental.pallas import tpu as pltpu
from jax.sharding import Mesh
from jax.sharding import PartitionSpec as P

HEAD_DIM = 64
BLOCK = 128
PAIR = 128
EPS = 1e-06
MASKED = -1e30
QTILE = 256
KTILE = 512
AXES = ("head", "z", "y", "core")
IDS = pl.DeviceIdType.MESH
F32 = jnp.float32
BF16 = jnp.bfloat16
ANY = pl.BlockSpec(memory_space=pl.ANY)
VM = pl.BlockSpec(memory_space=pltpu.VMEM)
SM = pl.BlockSpec(memory_space=pltpu.SMEM)


def struct(shape, dtype=BF16):
    return jax.ShapeDtypeStruct(tuple(shape), dtype)


def nt_dot(a, b):
    return lax.dot_general(a, b, (((1,), (1,)), ((), ())), preferred_element_type=F32)


def tn_dot(a, b):
    return lax.dot_general(a, b, (((0,), (0,)), ((), ())), preferred_element_type=F32)


def dot(a, b):
    return jnp.dot(a, b, preferred_element_type=F32)


def selection(rows, columns, shift, first=0, last=None):
    last = columns if last is None else last
    row = lax.broadcasted_iota(jnp.int32, (rows, columns), 0)
    column = lax.broadcasted_iota(jnp.int32, (rows, columns), 1)
    hit = (row == column + shift) & (column >= first) & (column < last)
    return hit.astype(F32).astype(BF16)


class Place:
    def __init__(self, z_count):
        self.z_count = z_count
        self.x, self.z, self.y, self.c = (lax.axis_index(a) for a in AXES)
        self.g = self.x * 2 + self.y
        self.chip = (self.x * z_count + self.z) * 2 + self.y

    def sibling(self):
        return (self.x, self.z, self.y, 1 - self.c)

    def plane(self, k):
        return (self.x ^ (k >> 1), self.z, self.y ^ (k & 1), self.c)

    def line(self, k):
        return (self.x, self.z ^ k, self.y, self.c)

    def any_chip(self, k):
        return (self.x ^ ((k >> 1) & 1), self.z ^ (k >> 2), self.y ^ (k & 1), self.c)


def meet(peers):
    barrier = pltpu.get_barrier_semaphore()
    for peer in peers:
        pl.semaphore_signal(barrier, inc=1, device_id=peer, device_id_type=IDS)
    pl.semaphore_wait(barrier, len(peers))


def send(source, target, sems, recvs, index, device):
    copy = pltpu.make_async_remote_copy(
        src_ref=source,
        dst_ref=target,
        send_sem=sems.at[index],
        recv_sem=recvs.at[index],
        device_id=device,
        device_id_type=IDS,
    )
    copy.start()
    return copy


def move(source, target, sems, index):
    copy = pltpu.make_async_copy(source, target, sems.at[index])
    copy.start()
    return copy


def exchange(kernel, ident, out_shape, scratch, args, sent):
    return pl.pallas_call(
        kernel,
        out_shape=out_shape,
        in_specs=[ANY] * len(args),
        out_specs=jax.tree.map(lambda _: ANY, out_shape),
        scratch_shapes=scratch,
        compiler_params=pltpu.CompilerParams(
            collective_id=ident, has_side_effects=True, vmem_limit_bytes=48 << 20
        ),
        cost_estimate=pl.CostEstimate(flops=0, bytes_accessed=sent, transcendentals=0),
    )(*args)


DMA = pltpu.SemaphoreType.DMA


def first_kernel(zc, n_ref, w_ref, f_ref, ng_ref, wg_ref, fg_ref, ls, ps, pr, fs, fr, ws, wr, bs, br):
    me = Place(zc)
    chips = 4 * zc
    meet([me.any_chip(k) for k in range(1, chips)] + [me.sibling()])
    own = [
        move(w_ref.at[me.g], wg_ref.at[me.chip, me.c], ls, 0),
        move(n_ref, ng_ref.at[me.g], ls, 1),
        move(f_ref.at[me.g], fg_ref.at[me.g], ls, 2),
    ]
    pieces = []
    for k in range(1, chips):
        there = me.any_chip(k)
        their_g = there[0] * 2 + there[2]
        pieces.append(send(w_ref.at[their_g], wg_ref.at[me.chip, me.c], ws, wr, k, there))
    rows = [send(n_ref, ng_ref.at[me.g], ps, pr, k, me.plane(k)) for k in range(1, 4)]
    wide = []
    for k in range(1, 4):
        there = me.plane(k)
        their_g = there[0] * 2 + there[2]
        wide.append(send(f_ref.at[their_g], fg_ref.at[me.g], fs, fr, k, there))
    own[0].wait()
    for copy in pieces:
        copy.wait()
    relay = send(wg_ref.at[:, me.c], wg_ref.at[:, me.c], bs, br, 0, me.sibling())
    for copy in own[1:] + rows + wide:
        copy.wait()
    relay.wait()


def first_exchange(zc, normed, w_send, f_send):
    chips = 4 * zc
    rows, cols = w_send.shape[1:]
    return exchange(
        functools.partial(first_kernel, zc),
        1,
        (
            struct((4,) + normed.shape),
            struct((chips, 2, rows, cols)),
            struct(f_send.shape),
        ),
        [DMA((3,))] + [DMA((4,))] * 4 + [DMA((chips,))] * 2 + [DMA((1,))] * 2,
        (normed, w_send, f_send),
        4 << 20,
    )


def heads_kernel(zc, q_ref, c_ref, a_ref, cg_ref, ls, zs, zr, bs, br, ps, pr):
    me = Place(zc)
    per = zc // q_ref.shape[0]
    meet([me.line(k) for k in range(1, zc)] + [me.plane(k) for k in range(1, 4)] + [me.sibling()])
    own = [
        move(q_ref.at[me.z // per], a_ref.at[me.z, me.c], ls, 0),
        move(c_ref, cg_ref.at[me.g], ls, 1),
    ]
    over = []
    for k in range(1, zc):
        over.append(
            send(q_ref.at[(me.z ^ k) // per], a_ref.at[me.z, me.c], zs, zr, k, me.line(k))
        )
    rows = [send(c_ref, cg_ref.at[me.g], ps, pr, k, me.plane(k)) for k in range(1, 4)]
    own[0].wait()
    relays = [send(a_ref.at[me.z, me.c], a_ref.at[me.z, me.c], bs, br, 0, me.sibling())]
    for k in range(1, zc):
        over[k - 1].wait()
        there = me.z ^ k
        relays.append(
            send(a_ref.at[there, me.c], a_ref.at[there, me.c], bs, br, k, me.sibling())
        )
    for copy in relays + rows + own[1:]:
        copy.wait()


def heads_exchange(zc, packed, cotangent):
    return exchange(
        functools.partial(heads_kernel, zc),
        2,
        (struct((zc, 2) + packed.shape[1:]), struct((4,) + cotangent.shape)),
        [DMA((2,))] + [DMA((zc,))] * 4 + [DMA((4,))] * 2,
        (packed, cotangent),
        4 << 20,
    )


def back_kernel(zc, o_ref, r_ref, mine, theirs, ls, bs, br, ss, rs):
    me = Place(zc)
    chips = 4 * zc
    per = r_ref.shape[1]
    meet([me.any_chip(k) for k in range(1, chips)] + [me.sibling()])
    other = send(o_ref.at[:, 1 - me.c], theirs, bs, br, 0, me.sibling())
    own = move(o_ref.at[:, me.c], mine, ls, 0)
    own.wait()
    other.wait()
    mine[...] = mine[...] + theirs[...]
    head = me.g * (r_ref.shape[0] // 4) + me.z // per
    part = me.z % per
    keep = move(mine.at[me.z, me.g], r_ref.at[head, part], ls, 1)
    sends = []
    for k in range(1, chips):
        there = me.any_chip(k)
        their_g = there[0] * 2 + there[2]
        sends.append(send(mine.at[there[1], their_g], r_ref.at[head, part], ss, rs, k, there))
    keep.wait()
    for copy in sends:
        copy.wait()


def back_exchange(zc, heads, slabs):
    chips = 4 * zc
    per = 4 * zc // heads
    half = (zc,) + slabs.shape[2:]
    return exchange(
        functools.partial(back_kernel, zc),
        3,
        struct((heads, per) + slabs.shape[3:]),
        [pltpu.VMEM(half, BF16)] * 2 + [DMA((2,))] + [DMA((1,))] * 2 + [DMA((chips,))] * 2,
        (slabs,),
        2 << 20,
    )


def plane_kernel(zc, n_ref, ng_ref, ls, ps, pr):
    me = Place(zc)
    meet([me.plane(k) for k in range(1, 4)])
    own = move(n_ref, ng_ref.at[me.g], ls, 0)
    rows = [send(n_ref, ng_ref.at[me.g], ps, pr, k, me.plane(k)) for k in range(1, 4)]
    for copy in [own] + rows:
        copy.wait()


def plane_gather(zc, rows):
    return exchange(
        functools.partial(plane_kernel, zc),
        4,
        struct((4,) + rows.shape),
        [DMA((1,))] + [DMA((4,))] * 2,
        (rows,),
        2 << 20,
    )


def scatter_kernel(zc, p_ref, r_ref, ls, ps, pr):
    me = Place(zc)
    meet([me.plane(k) for k in range(1, 4)])
    own = move(p_ref.at[me.g], r_ref.at[me.g], ls, 0)
    rows = []
    for k in range(1, 4):
        there = me.plane(k)
        rows.append(
            send(p_ref.at[there[0] * 2 + there[2]], r_ref.at[me.g], ps, pr, k, there)
        )
    for copy in [own] + rows:
        copy.wait()


def plane_scatter(zc, parts):
    return exchange(
        functools.partial(scatter_kernel, zc),
        5,
        struct(parts.shape),
        [DMA((1,))] + [DMA((4,))] * 2,
        (parts,),
        4 << 20,
    )


def grads_kernel(zc, d_ref, a_ref, ls, ss, rs, bs, br):
    me = Place(zc)
    chips = 4 * zc
    group = d_ref.shape[0] // 4
    per = zc // group
    meet([me.any_chip(k) for k in range(1, chips)] + [me.sibling()])
    own = move(d_ref.at[me.g * group + me.z // per], a_ref.at[me.z, me.c, me.g], ls, 0)
    sends = []
    for k in range(1, chips):
        there = me.any_chip(k)
        head = (there[0] * 2 + there[2]) * group + there[1] // per
        sends.append(send(d_ref.at[head], a_ref.at[me.z, me.c, me.g], ss, rs, k, there))
    own.wait()
    for copy in sends:
        copy.wait()
    relay = send(a_ref.at[:, me.c], a_ref.at[:, me.c], bs, br, 0, me.sibling())
    relay.wait()


def grads_exchange(zc, slabs):
    chips = 4 * zc
    return exchange(
        functools.partial(grads_kernel, zc),
        6,
        struct((zc, 2, 4) + slabs.shape[1:]),
        [DMA((1,))] + [DMA((chips,))] * 2 + [DMA((1,))] * 2,
        (slabs,),
        2 << 20,
    )


def rows_kernel(zc, d_ref, p_ref, r_ref, o_ref, mine, theirs, ls, bs, br, ss, rs, ps, pr):
    me = Place(zc)
    per = r_ref.shape[1]
    meet([me.line(k) for k in range(1, zc)] + [me.plane(k) for k in range(1, 4)] + [me.sibling()])
    other = send(d_ref.at[:, 1 - me.c], theirs, bs, br, 0, me.sibling())
    own = move(d_ref.at[:, me.c], mine, ls, 0)
    keep = move(p_ref.at[me.g], o_ref.at[me.g], ls, 2)
    outs = []
    for k in range(1, 4):
        there = me.plane(k)
        outs.append(
            send(p_ref.at[there[0] * 2 + there[2]], o_ref.at[me.g], ps, pr, k, there)
        )
    own.wait()
    other.wait()
    mine[...] = mine[...] + theirs[...]
    head = me.z // per
    part = me.z % per
    stay = move(mine.at[me.z], r_ref.at[head, part], ls, 1)
    sends = []
    for k in range(1, zc):
        sends.append(send(mine.at[me.z ^ k], r_ref.at[head, part], ss, rs, k, me.line(k)))
    for copy in [keep, stay] + sends + outs:
        copy.wait()


def rows_exchange(zc, heads, grads, parts):
    group = heads // 4
    per = zc // group
    half = (zc,) + grads.shape[2:]
    return exchange(
        functools.partial(rows_kernel, zc),
        7,
        (struct((group, per) + grads.shape[2:]), struct(parts.shape)),
        [pltpu.VMEM(half, BF16)] * 2
        + [DMA((3,))]
        + [DMA((1,))] * 2
        + [DMA((zc,))] * 2
        + [DMA((4,))] * 2,
        (grads, parts),
        6 << 20,
    )


def last_kernel(zc, p_ref, w_ref, f_ref, r_ref, gw_ref, gf_ref, mine, theirs, ls, bs, br, ss, rs, ps, pr, fs, fr):
    me = Place(zc)
    chips = 4 * zc
    meet([me.any_chip(k) for k in range(1, chips)] + [me.sibling()])
    other = send(w_ref.at[:, 1 - me.c], theirs, bs, br, 0, me.sibling())
    own = move(w_ref.at[:, me.c], mine, ls, 0)
    keep = [move(p_ref.at[me.g], r_ref.at[me.g], ls, 1), move(f_ref.at[me.g], gf_ref.at[me.g], ls, 2)]
    outs = []
    for k in range(1, 4):
        there = me.plane(k)
        their_g = there[0] * 2 + there[2]
        outs.append(send(p_ref.at[their_g], r_ref.at[me.g], ps, pr, k, there))
        outs.append(send(f_ref.at[their_g], gf_ref.at[me.g], fs, fr, k, there))
    own.wait()
    other.wait()
    mine[...] = mine[...] + theirs[...]
    stay = move(mine.at[me.chip], gw_ref.at[me.z, me.g], ls, 3)
    sends = []
    for k in range(1, chips):
        there = me.any_chip(k)
        chip = (there[0] * zc + there[1]) * 2 + there[2]
        sends.append(send(mine.at[chip], gw_ref.at[me.z, me.g], ss, rs, k, there))
    for copy in keep + [stay] + sends + outs:
        copy.wait()


def last_exchange(zc, parts, w_parts, f_parts):
    chips = 4 * zc
    piece = w_parts.shape[2:]
    return exchange(
        functools.partial(last_kernel, zc),
        8,
        (struct(parts.shape), struct((zc, 4) + piece), struct(f_parts.shape)),
        [pltpu.VMEM((chips,) + piece, BF16)] * 2
        + [DMA((4,))]
        + [DMA((1,))] * 2
        + [DMA((chips,))] * 2
        + [DMA((4,))] * 4,
        (parts, w_parts, f_parts),
        6 << 20,
    )


def project_kernel(group, n_ref, w_ref, o_ref):
    qw = group * HEAD_DIM
    out = dot(n_ref[0], w_ref[...]).astype(BF16)
    for head in range(group):
        left = selection(qw, PAIR, head * HEAD_DIM, 0, HEAD_DIM)
        right = selection(qw, PAIR, head * HEAD_DIM - HEAD_DIM, HEAD_DIM, PAIR)
        slab = dot(out[:BLOCK, :qw], left) + dot(out[BLOCK:, :qw], right)
        o_ref[head, 0, :BLOCK] = slab.astype(BF16)
        start = qw + head * PAIR
        o_ref[head, 0, BLOCK:] = out[:, start : start + PAIR]


def project(group, rows, weights):
    count, per, width = rows.shape
    return pl.pallas_call(
        functools.partial(project_kernel, group),
        out_shape=struct((group, count, BLOCK + per, PAIR)),
        grid=(count,),
        in_specs=[
            pl.BlockSpec((1, per, width), lambda i: (i, 0, 0)),
            pl.BlockSpec(weights.shape, lambda i: (0, 0)),
        ],
        out_specs=pl.BlockSpec((group, 1, BLOCK + per, PAIR), lambda i: (0, i, 0, 0)),
        compiler_params=pltpu.CompilerParams(vmem_limit_bytes=32 << 20),
    )(rows, weights)


def unproject_kernel(group, d_ref, w_ref, m_ref, c_ref):
    qw = group * HEAD_DIM
    upper = jnp.zeros((BLOCK, qw), F32)
    lower = jnp.zeros((BLOCK, qw), F32)
    for head in range(group):
        slab = d_ref[head, 0, 0]
        for extra in range(1, d_ref.shape[1]):
            slab = slab + d_ref[head, extra, 0]
        left = selection(PAIR, qw, -head * HEAD_DIM, head * HEAD_DIM, (head + 1) * HEAD_DIM)
        right = selection(
            PAIR, qw, HEAD_DIM - head * HEAD_DIM, head * HEAD_DIM, (head + 1) * HEAD_DIM
        )
        upper = upper + dot(slab[:BLOCK], left)
        lower = lower + dot(slab[:BLOCK], right)
        start = qw + head * PAIR
        m_ref[0, :, start : start + PAIR] = slab[BLOCK:]
    m_ref[0, :BLOCK, :qw] = upper.astype(BF16)
    m_ref[0, BLOCK:, :qw] = lower.astype(BF16)
    c_ref[0] = nt_dot(m_ref[0], w_ref[...]).astype(BF16)


def unproject(grads, weights):
    group, parts, count, rows, _ = grads.shape
    per = rows - BLOCK
    width, cols = weights.shape
    return pl.pallas_call(
        functools.partial(unproject_kernel, group),
        out_shape=(struct((count, per, cols)), struct((count, per, width))),
        grid=(count,),
        in_specs=[
            pl.BlockSpec((group, parts, 1, rows, PAIR), lambda i: (0, 0, i, 0, 0)),
            pl.BlockSpec((width, cols), lambda i: (0, 0)),
        ],
        out_specs=(
            pl.BlockSpec((1, per, cols), lambda i: (i, 0, 0)),
            pl.BlockSpec((1, per, width), lambda i: (i, 0, 0)),
        ),
        compiler_params=pltpu.CompilerParams(vmem_limit_bytes=32 << 20),
    )(grads, weights)


def join_kernel(o_ref, x_ref, w_ref, ob_ref, r_ref, n_ref):
    heads = o_ref.shape[0]
    for block in range(2):
        for pair in range(heads // 2):
            total = jnp.zeros((BLOCK, PAIR), F32)
            for side in range(2):
                slab = o_ref[2 * pair + side, 0]
                for extra in range(1, o_ref.shape[1]):
                    slab = slab + o_ref[2 * pair + side, extra]
                pick = selection(
                    PAIR, PAIR, (block - side) * HEAD_DIM, side * HEAD_DIM, (side + 1) * HEAD_DIM
                )
                total = total + dot(slab, pick)
            ob_ref[block * BLOCK : (block + 1) * BLOCK, pair * PAIR : (pair + 1) * PAIR] = (
                total.astype(BF16)
            )
    residual = x_ref[...].astype(F32) + dot(ob_ref[...], w_ref[...])
    r_ref[...] = residual
    mean = jnp.mean(residual * residual, axis=-1, keepdims=True)
    n_ref[...] = (residual * lax.rsqrt(mean + EPS)).astype(BF16)


def join(slabs, tokens, w_out):
    shape = tokens.shape
    return pl.pallas_call(
        join_kernel,
        out_shape=(struct(shape), struct(shape, F32), struct(shape)),
        in_specs=[VM] * 3,
        out_specs=(VM,) * 3,
        compiler_params=pltpu.CompilerParams(vmem_limit_bytes=32 << 20),
    )(slabs, tokens, w_out)


def part_kernel(c_ref, t_ref, r_ref, w_ref, d_ref, a_ref, s_ref):
    total = c_ref[0].astype(F32)
    for i in range(1, c_ref.shape[0]):
        total = total + c_ref[i].astype(F32)
    residual = r_ref[...]
    scaling = lax.rsqrt(jnp.mean(residual * residual, axis=-1, keepdims=True) + EPS)
    normed = residual * scaling
    middle = jnp.mean(total * normed, axis=-1, keepdims=True)
    grad = t_ref[...].astype(F32) + scaling * (total - normed * middle)
    d_ref[...] = grad
    low = grad.astype(BF16)
    a_ref[...] = low
    heads = s_ref.shape[0]
    back = nt_dot(low, w_ref[...]).astype(BF16)
    for pair in range(heads // 2):
        both = back[:, pair * PAIR : (pair + 1) * PAIR]
        for side in range(2):
            left = selection(PAIR, PAIR, side * HEAD_DIM, 0, HEAD_DIM)
            right = selection(PAIR, PAIR, (side - 1) * HEAD_DIM, HEAD_DIM, PAIR)
            slab = dot(both[:BLOCK], left) + dot(both[BLOCK:], right)
            s_ref[2 * pair + side] = slab.astype(BF16)


def part(c_parts, cotangent, residual, w_out):
    shape = cotangent.shape
    heads = w_out.shape[0] // HEAD_DIM
    return pl.pallas_call(
        part_kernel,
        out_shape=(struct(shape, F32), struct(shape), struct((heads, BLOCK, PAIR))),
        in_specs=[VM] * 4,
        out_specs=(VM,) * 3,
        compiler_params=pltpu.CompilerParams(vmem_limit_bytes=32 << 20),
    )(c_parts, cotangent, residual, w_out)


def segment_start(position, lens_ref):
    start = jnp.zeros_like(position)
    end = 0
    for j in range(lens_ref.shape[0]):
        end = end + lens_ref[j]
        start = jnp.where(position >= end, end, start)
    return start


def tile_of(turn, workers, worker):
    forward = turn * workers + worker
    backward = turn * workers + workers - 1 - worker
    return jnp.where((turn & 1) == 0, forward, backward)


def key_bounds(first, lens_ref):
    low_start = segment_start(first, lens_ref)
    high_start = segment_start(first + QTILE - 1, lens_ref)
    low = low_start // KTILE
    high = (first + QTILE + KTILE - 1) // KTILE
    plain = jnp.clip((high_start + KTILE - 1) // KTILE, low, high)
    stop = jnp.clip((first + 1) // KTILE, plain, high)
    return low, plain, stop, high


def visible(first, tile, starts):
    key = tile * KTILE + lax.broadcasted_iota(jnp.int32, (KTILE, QTILE), 0)
    query = first + lax.broadcasted_iota(jnp.int32, (KTILE, QTILE), 1)
    return (key <= query) & (key >= starts)


def forward_kernel(
    workers, anchor_ref, lens_ref, who_ref, a_ref, o_ref, kv_ref, kvt_ref, q_ref, qt_ref, ot_ref, l_ref, inv, pick
):
    blocks = anchor_ref.shape[0]
    turns = q_ref.shape[0]
    per = QTILE // BLOCK
    worker = who_ref[0]

    def note(i, carry):
        inv[anchor_ref[i]] = i
        return carry

    lax.fori_loop(0, blocks, note, 0)
    for half in range(2):
        pick[half] = selection(PAIR, PAIR, half * HEAD_DIM, 0, HEAD_DIM)
        row = lax.broadcasted_iota(jnp.int32, (PAIR, PAIR), 0)
        column = lax.broadcasted_iota(jnp.int32, (PAIR, PAIR), 1)
        hit = (column == row + half * HEAD_DIM) & (row < HEAD_DIM)
        pick[2 + half] = hit.astype(F32).astype(BF16)
    same = lax.broadcasted_iota(jnp.int32, (PAIR, PAIR), 0)
    pick[4] = (same == lax.broadcasted_iota(jnp.int32, (PAIR, PAIR), 1)).astype(F32).astype(BF16)
    o_ref[...] = jnp.zeros_like(o_ref)

    def order(i, carry):
        where = inv[i]
        slab, half = where >> 1, where & 1
        block = a_ref[slab, pl.ds(pl.multiple_of(BLOCK + half * BLOCK, BLOCK), BLOCK), :]
        at = pl.ds(pl.multiple_of(i * BLOCK, BLOCK), BLOCK)
        kv_ref[at, :] = block
        kvt_ref[:, at] = nt_dot(pick[4], block).astype(BF16)
        return carry

    lax.fori_loop(0, blocks, order, 0)

    def one_tile(turn, carry):
        tile = tile_of(turn, workers, worker)
        first = tile * QTILE
        for b in range(per):
            where = inv[tile * per + b]
            slab, half = where >> 1, where & 1
            rows = a_ref[slab, :BLOCK, :]
            q_ref[turn, b * BLOCK : (b + 1) * BLOCK, :] = (dot(rows, pick[half]) * 0.125).astype(BF16)
            qt_ref[turn, :, b * BLOCK : (b + 1) * BLOCK] = (
                nt_dot(pick[2 + half], rows) * 0.125
            ).astype(BF16)
        query = qt_ref[turn]
        starts = segment_start(first + lax.broadcasted_iota(jnp.int32, (1, QTILE), 1), lens_ref)
        low, plain, stop, high = key_bounds(first, lens_ref)

        def step(masked, kt, state):
            top, total, acc = state
            at = pl.ds(pl.multiple_of(kt * KTILE, KTILE), KTILE)
            scores = dot(kv_ref[at, :], query)
            if masked:
                seen = visible(first, kt, starts)
                scores = jnp.where(seen, scores, MASKED)
            new_top = jnp.maximum(top, jnp.max(scores, axis=0, keepdims=True))
            factor = jnp.exp(top - new_top)
            weights = jnp.exp(scores - new_top)
            if masked:
                weights = jnp.where(seen, weights, 0.0)
            total = total * factor + jnp.sum(weights, axis=0, keepdims=True)
            acc = acc * factor + dot(kvt_ref[HEAD_DIM:, at], weights.astype(BF16))
            return (new_top, total, acc)

        state = (
            jnp.full((1, QTILE), MASKED, F32),
            jnp.zeros((1, QTILE), F32),
            jnp.zeros((HEAD_DIM, QTILE), F32),
        )
        state = lax.fori_loop(low, plain, functools.partial(step, True), state)
        state = lax.fori_loop(plain, stop, functools.partial(step, False), state)
        top, total, acc = lax.fori_loop(stop, high, functools.partial(step, True), state)
        out = acc / total
        ot_ref[turn] = out
        l_ref[turn] = top + jnp.log(total)
        narrow = out.astype(BF16)
        for b in range(per):
            where = inv[tile * per + b]
            slab, half = where >> 1, where & 1
            piece = tn_dot(narrow[:, b * BLOCK : (b + 1) * BLOCK], pick[2 + half, :HEAD_DIM, :])
            o_ref[slab] = o_ref[slab] + piece.astype(BF16)
        return carry

    lax.fori_loop(0, turns, one_tile, 0)


def attention_forward(workers, anchors, lengths, who, packed):
    slabs = packed.shape[0]
    rows = slabs * 2 * BLOCK
    turns = rows // QTILE // workers
    return pl.pallas_call(
        functools.partial(forward_kernel, workers),
        out_shape=(
            struct((slabs, BLOCK, PAIR)),
            struct((rows, PAIR)),
            struct((PAIR, rows)),
            struct((turns, QTILE, PAIR)),
            struct((turns, PAIR, QTILE)),
            struct((turns, HEAD_DIM, QTILE), F32),
            struct((turns, 1, QTILE), F32),
        ),
        in_specs=[SM, SM, SM, VM],
        out_specs=(VM,) * 7,
        scratch_shapes=[pltpu.SMEM((2 * slabs,), jnp.int32), pltpu.VMEM((5, PAIR, PAIR), BF16)],
        compiler_params=pltpu.CompilerParams(vmem_limit_bytes=60 << 20),
        cost_estimate=pl.CostEstimate(
            flops=rows * rows * 64, bytes_accessed=rows * 1024, transcendentals=rows * rows // 8
        ),
    )(anchors, lengths, who, packed)


def backward_kernel(
    workers,
    anchor_ref,
    lens_ref,
    who_ref,
    d_ref,
    kv_ref,
    kvt_ref,
    q_ref,
    qt_ref,
    ot_ref,
    l_ref,
    g_ref,
    inv,
    pick,
    dn,
    dt,
    acc,
):
    blocks = anchor_ref.shape[0]
    turns = q_ref.shape[0]
    per = QTILE // BLOCK
    worker = who_ref[0]

    def note(i, carry):
        inv[anchor_ref[i]] = i
        return carry

    lax.fori_loop(0, blocks, note, 0)
    row = lax.broadcasted_iota(jnp.int32, (PAIR, PAIR), 0)
    column = lax.broadcasted_iota(jnp.int32, (PAIR, PAIR), 1)
    for half in range(2):
        hit = (row - half * HEAD_DIM == column - HEAD_DIM) & (column >= HEAD_DIM)
        pick[half] = hit.astype(F32).astype(BF16)
        hit = (column - half * HEAD_DIM == row - HEAD_DIM) & (row >= HEAD_DIM)
        pick[2 + half] = hit.astype(F32).astype(BF16)
        hit = (column == row + half * HEAD_DIM) & (row < HEAD_DIM)
        pick[4 + half] = hit.astype(F32).astype(BF16)
    acc[...] = jnp.zeros_like(acc)
    g_ref[:, :BLOCK, :] = jnp.zeros((g_ref.shape[0], BLOCK, PAIR), BF16)

    def one_tile(turn, carry):
        tile = tile_of(turn, workers, worker)
        first = tile * QTILE
        for b in range(per):
            where = inv[tile * per + b]
            slab, half = where >> 1, where & 1
            rows = d_ref[slab]
            dn[b * BLOCK : (b + 1) * BLOCK, :] = dot(rows, pick[half]).astype(BF16)
            dt[:, b * BLOCK : (b + 1) * BLOCK] = nt_dot(pick[2 + half], rows).astype(BF16)
        query, query_rows = qt_ref[turn], q_ref[turn]
        grad, grad_rows = dt[...], dn[...]
        norm = l_ref[turn]
        delta = jnp.sum(grad[HEAD_DIM:].astype(F32) * ot_ref[turn], axis=0, keepdims=True)
        starts = segment_start(first + lax.broadcasted_iota(jnp.int32, (1, QTILE), 1), lens_ref)
        low, plain, stop, high = key_bounds(first, lens_ref)

        def step(masked, kt, total):
            at = pl.ds(pl.multiple_of(kt * KTILE, KTILE), KTILE)
            keys = kv_ref[at, :]
            weights = jnp.exp(dot(keys, query) - norm)
            if masked:
                weights = jnp.where(visible(first, kt, starts), weights, 0.0)
            score_grad = (weights * (dot(keys, grad) - delta)).astype(BF16)
            acc[at, :] += dot(score_grad, query_rows) + dot(weights.astype(BF16), grad_rows)
            return total + dot(kvt_ref[:HEAD_DIM, at], score_grad)

        total = jnp.zeros((HEAD_DIM, QTILE), F32)
        total = lax.fori_loop(low, plain, functools.partial(step, True), total)
        total = lax.fori_loop(plain, stop, functools.partial(step, False), total)
        total = lax.fori_loop(stop, high, functools.partial(step, True), total)
        narrow = (total * 0.125).astype(BF16)
        for b in range(per):
            where = inv[tile * per + b]
            slab, half = where >> 1, where & 1
            piece = tn_dot(narrow[:, b * BLOCK : (b + 1) * BLOCK], pick[4 + half, :HEAD_DIM, :])
            g_ref[slab, :BLOCK] = g_ref[slab, :BLOCK] + piece.astype(BF16)
        return carry

    lax.fori_loop(0, turns, one_tile, 0)

    def place(i, carry):
        where = inv[i]
        slab, half = where >> 1, where & 1
        at = pl.ds(pl.multiple_of(i * BLOCK, BLOCK), BLOCK)
        to = pl.ds(pl.multiple_of(BLOCK + half * BLOCK, BLOCK), BLOCK)
        g_ref[slab, to, :] = acc[at, :].astype(BF16)
        return carry

    lax.fori_loop(0, blocks, place, 0)


def attention_backward(workers, anchors, lengths, who, grads, kept):
    slabs = grads.shape[0]
    rows = slabs * 2 * BLOCK
    return pl.pallas_call(
        functools.partial(backward_kernel, workers),
        out_shape=struct((slabs, 3 * BLOCK, PAIR)),
        in_specs=[SM, SM, SM] + [VM] * 7,
        out_specs=VM,
        scratch_shapes=[
            pltpu.SMEM((2 * slabs,), jnp.int32),
            pltpu.VMEM((6, PAIR, PAIR), BF16),
            pltpu.VMEM((QTILE, PAIR), BF16),
            pltpu.VMEM((PAIR, QTILE), BF16),
            pltpu.VMEM((rows, PAIR), F32),
        ],
        compiler_params=pltpu.CompilerParams(vmem_limit_bytes=60 << 20),
        cost_estimate=pl.CostEstimate(
            flops=rows * rows * 160, bytes_accessed=rows * 1024, transcendentals=rows * rows // 8
        ),
    )(anchors, lengths, who, grads, *kept)


def norm_parts(values):
    scaling = lax.rsqrt(jnp.mean(values * values, axis=-1, keepdims=True) + EPS)
    return values * scaling, scaling


def body(
    zc,
    tokens,
    cotangent,
    norm1_gain,
    w_query,
    w_key,
    w_value,
    w_out,
    norm2_gain,
    w_gate,
    w_up,
    w_down,
    block_anchor,
    seq_lengths,
):
    own_rows, width = tokens.shape
    heads = width // HEAD_DIM
    group = heads // 4
    per_head = zc // group
    workers = 2 * per_head
    feature_rows = w_query.shape[0]
    hidden = w_gate.shape[1]
    units = w_down.shape[0]
    slice_units = hidden // 4

    low = lambda v: v.astype(BF16).astype(F32)
    gain1, gain2 = low(norm1_gain)[:, None], low(norm2_gain)[:, None]
    query_w, key_w, value_w = low(w_query), low(w_key), low(w_value)
    gate_w, up_w = low(w_gate), low(w_up)
    q_part = (gain1 * query_w).reshape(feature_rows, 4, group * HEAD_DIM)
    kv_part = jnp.stack(
        [
            (gain1 * key_w).reshape(feature_rows, 4, group, HEAD_DIM),
            (gain1 * value_w).reshape(feature_rows, 4, group, HEAD_DIM),
        ],
        axis=3,
    ).reshape(feature_rows, 4, group * PAIR)
    w_send = jnp.transpose(jnp.concatenate([q_part, kv_part], axis=2).astype(BF16), (1, 0, 2))

    def slices(weight):
        return jnp.transpose(
            weight.reshape(feature_rows, 2, zc, 2, 2 * units), (1, 3, 0, 2, 4)
        ).reshape(4, feature_rows, slice_units)

    f_send = jnp.stack([slices((gain2 * gate_w).astype(BF16)), slices((gain2 * up_w).astype(BF16))], axis=1)
    out_mat = lax.all_gather(w_out.astype(BF16), AXES, axis=0, tiled=True)

    inputs = tokens.astype(F32)
    normed_one, scaling_one = norm_parts(inputs)
    n1_all, qkv_w, f_all = first_exchange(zc, normed_one.astype(BF16), w_send, f_send)
    qkv_w = qkv_w.reshape(width, 3 * group * HEAD_DIM)

    ffn_in = jnp.concatenate([f_all.reshape(-1, slice_units), w_down.astype(BF16)], axis=0)
    ffn_all = lax.all_gather(ffn_in, ("z", "core"), axis=0, tiled=False)
    wide = 8 * feature_rows
    gate_up = jnp.transpose(
        ffn_all[:, :wide].reshape(zc, 2, 2, 2, 2, feature_rows, slice_units), (4, 2, 0, 3, 1, 5, 6)
    ).reshape(2, width, slice_units)
    gate_mat, up_mat = gate_up[0], gate_up[1]
    down_mat = ffn_all[:, wide:].reshape(slice_units, width)

    packed = project(group, n1_all, qkv_w)
    by_head, cot_all = heads_exchange(zc, packed, cotangent)

    anchors = jnp.transpose(block_anchor.reshape(2, zc, 2, 2, 2), (1, 3, 0, 2, 4)).reshape(-1)
    who = ((lax.axis_index("z") % per_head) * 2 + lax.axis_index("core")).astype(jnp.int32).reshape(1)
    slab_count = zc * 8
    o_slabs, *kept = attention_forward(
        workers, anchors, seq_lengths, who, by_head.reshape((slab_count,) + by_head.shape[3:])
    )
    o_rows = back_exchange(zc, heads, o_slabs.reshape(zc, 2, 4, BLOCK, PAIR))
    attn_rows, residual, normed_two = join(o_rows, tokens, out_mat)

    n2_all = plane_gather(zc, normed_two).reshape(-1, width)
    cot_rows = cot_all.reshape(-1, width)
    gate = dot(n2_all, gate_mat)
    up = dot(n2_all, up_mat)
    sig = jax.nn.sigmoid(gate)
    hid = (gate * sig * up).astype(BF16)
    out_parts = dot(hid, down_mat).astype(BF16)
    hid_grad = nt_dot(cot_rows, down_mat)
    gate_back = (hid_grad * up * sig * (1.0 + gate * (1.0 - sig))).astype(BF16)
    up_back = (hid_grad * gate * sig).astype(BF16)
    c2_parts = (nt_dot(gate_back, gate_mat) + nt_dot(up_back, up_mat)).astype(BF16)
    gate_grad = tn_dot(n2_all, gate_back).astype(BF16)
    up_grad = tn_dot(n2_all, up_back).astype(BF16)
    down_grad = tn_dot(hid, cot_rows).astype(BF16)

    c2_all = plane_scatter(zc, c2_parts.reshape(4, own_rows, width))
    residual_grad, branch_back, do_slabs = part(c2_all, cotangent, residual, out_mat)
    do_heads = grads_exchange(zc, do_slabs)

    out_w_grad = tn_dot(attn_rows, branch_back).astype(BF16)

    def by_owner(grad):
        cols = grad.shape[-1]
        return jnp.transpose(
            grad.reshape(2, zc, 2, 2, feature_rows, cols), (1, 3, 0, 2, 4, 5)
        ).reshape(zc * 2, 4, 1, feature_rows, cols)

    shares = jnp.concatenate(
        [
            jnp.concatenate(
                [by_owner(gate_grad), by_owner(up_grad), by_owner(out_w_grad)], axis=2
            ).reshape(zc * 2, -1, width),
            down_grad.reshape(zc * 2, units, width),
        ],
        axis=1,
    )
    rows_each = shares.shape[1]
    shares = lax.psum_scatter(
        shares.reshape(zc * 2 * rows_each, width), ("z", "core"), scatter_dimension=0, tiled=True
    )
    down_share = shares[rows_each - units :]
    ffn_share = shares[: rows_each - units].reshape(4, 3, feature_rows, width)

    grad_heads = attention_backward(
        workers, anchors, seq_lengths, who, do_heads.reshape(slab_count, BLOCK, PAIR), kept
    )
    grad_rows, out_all = rows_exchange(
        zc,
        heads,
        grad_heads.reshape(zc, 2, 4, 3 * BLOCK, PAIR),
        out_parts.reshape(4, own_rows, width),
    )
    qkv_grad, c1_parts = unproject(grad_rows, qkv_w)
    w_grad = tn_dot(n1_all.reshape(-1, width), qkv_grad.reshape(-1, qkv_grad.shape[-1])).astype(BF16)
    c1_all, w_all, f_grad = last_exchange(
        zc, c1_parts, w_grad.reshape(4 * zc, 2, feature_rows, -1), ffn_share
    )

    output = (residual + jnp.sum(out_all.astype(F32), axis=0)).astype(BF16)
    c1 = jnp.sum(c1_all.astype(F32), axis=0)
    middle = jnp.mean(c1 * normed_one, axis=-1, keepdims=True)
    tokens_grad = (residual_grad + scaling_one * (c1 - normed_one * middle)).astype(BF16)

    w_sum = jnp.sum(w_all.astype(F32), axis=0)
    q_cols = group * HEAD_DIM
    query_raw = jnp.transpose(w_sum[:, :, :q_cols], (1, 0, 2)).reshape(feature_rows, width)
    kv_raw = w_sum[:, :, q_cols:].reshape(4, feature_rows, group, 2, HEAD_DIM)
    key_raw = jnp.transpose(kv_raw[:, :, :, 0], (1, 0, 2, 3)).reshape(feature_rows, width)
    value_raw = jnp.transpose(kv_raw[:, :, :, 1], (1, 0, 2, 3)).reshape(feature_rows, width)
    gain1_grad = jnp.sum(query_raw * query_w + key_raw * key_w + value_raw * value_w, axis=1)

    def unslice(grad):
        return jnp.transpose(
            grad.astype(F32).reshape(2, 2, feature_rows, zc, 2 * units), (2, 0, 3, 1, 4)
        ).reshape(feature_rows, hidden)

    gate_raw, up_raw = unslice(f_grad[:, 0]), unslice(f_grad[:, 1])
    gain2_grad = jnp.sum(gate_raw * gate_w + up_raw * up_w, axis=1)
    out_share = jnp.sum(f_grad[:, 2].astype(F32), axis=0)
    return (
        output,
        tokens_grad,
        gain1_grad,
        gain1 * query_raw,
        gain1 * key_raw,
        gain1 * value_raw,
        out_share,
        gain2_grad,
        gain2 * gate_raw,
        gain2 * up_raw,
        down_share.astype(F32),
    )


def solution(mesh):
    blk = mesh.shape["blk"]
    grid = Mesh(mesh.devices.reshape(mesh.shape["head"], blk // 4, 2, 2), AXES)
    rows, vector, whole = P(AXES, None), P(AXES), P()
    return jax.shard_map(
        functools.partial(body, blk // 4),
        mesh=grid,
        in_specs=(rows, rows, vector, rows, rows, rows, rows, vector, rows, rows, rows, whole, whole),
        out_specs=(rows, rows, vector, rows, rows, rows, rows, vector, rows, rows, rows),
        check_vma=False,
    )
```

time: 2440 us -> 532 us (0.22)
  waiting for transfers between devices: 1010 us -> 0.07 us
  matrix products: 730 us -> 31.6 us
  Pallas kernels: 0 us -> 413 us
  blocking collectives: 268 us -> 0 us
  local copies, waits for them, and re-layouts: 233 us -> 44.8 us
  other arithmetic: 115 us -> 23 us
  loops' own time: 67.4 us -> 0 us
    reduce_scatter x7 -> x1, waiting for transfers between devices: 742 us -> 0.02 us  [body(): lax.psum_scatter(shares.reshape(zc * 2 * rows_each, width), ('z', 'core')...]
    dot_general x210 -> x11, matrix products: 730 us -> 31.6 us  [the longest x3 13.1 us: dot(): return jnp.dot(a, b, preferred_element_type=F32)]
    pallas_call x0 -> x14, Pallas kernels: none -> 413 us  [the longest x8 305 us: exchange(): pl.pallas_call(kernel, out_shape=out_shape, in_specs=[ANY] * len(args), o...]
    all_gather x11 -> x2, waiting for transfers between devices: 247 us -> 0.01 us  [the longest x1 0.01 us: body(): out_mat = lax.all_gather(w_out.astype(BF16), AXES, axis=0, tiled=True)]
    unnamed x2 -> x0, blocking collectives: 164 us -> none
    reshape x10 -> x21, local copies, waits for them, and re-layouts: 90.3 us -> 10.8 us  [the longest x6 5.56 us: unslice(): return jnp.transpose(grad.astype(F32).reshape(2, 2, feature_rows, zc, 2 *...]
    while x4 -> x0, local copies, waits for them, and re-layouts: 71.1 us -> none  [the longest x2 36.7 us: body(): lax.scan(queries_one_block, key_zero, shaped + cut_labels + (norm_cut, de...]
    reduce_or x80 -> x0, other arithmetic: 67.6 us -> none  [the longest x32 26.3 us: query_update(): return lax.cond(jnp.any(visible), update, lambda current: current, grad_acc)]
  transfers between devices with their start and end apart: 21 -> 3, of which waited for: 14 -> 0; matrix products, arithmetic and copies ran while one was open for 44% -> 3% of each run, Pallas kernels for 0% -> 63%
where the time goes in v1:
time: 532 us; the launch traced here: 528 us
  Pallas kernels  413 us (78%)
  local copies, waits for them, and re-layouts  44.8 us (8%)
  matrix products  31.6 us (6%)
  other arithmetic  23 us (4%)
  between operations  14.8 us (3%)
    pallas_call x8, Pallas kernels, exchange(): pl.pallas_call(kernel, out_shape=out_shape, in_specs=[ANY] * len(args), o...  305 us
    pallas_call x1, Pallas kernels, attention_forward(): pl.pallas_call(functools.partial(forward_kernel, workers), out_shape=(str...  55.5 us
    pallas_call x1, Pallas kernels, attention_backward(): pl.pallas_call(functools.partial(backward_kernel, workers), out_shape=str...  42.9 us
    unnamed x83, local copies, waits for them, and re-layouts  19.4 us
    dot_general x3, matrix products, dot(): return jnp.dot(a, b, preferred_element_type=F32)  13.1 us
    dot_general x5, matrix products, tn_dot(): lax.dot_general(a, b, (((0,), (0,)), ((), ())), preferred_element_type=F32)  11.3 us
  transfers between devices with their start and end apart: 3, of which 0 were waited for; matrix products, arithmetic and copies ran while one was open for 3% of the time, Pallas kernels for 63%

profile of v1, /device:TPU:0, one launch (start us, length us, event | category | flops | bytes accessed | tf_op | source)
XLA Modules:
  0.0 527.5 jit_solution(10708104473358124439)
XLA Ops:
  7.3 1.6 convert_element_type.141
  9.6 1.1 fusion.13
  14.2 47.6 %shard_map.212 = (bf16[4,256,1024]{2,1,0:T(8,128)(2,1)S(1)}, bf16[16,2,32,768]{3,2,1,0:T(8,128)(2,1)S(1)}, bf16[4,2,32,1024]{3,2,1,0:T(8,128)(2,1)S(1)}) custom-call(bf16[256,1024]{1,0:T(8,128)(2,1)S(1)} %fusion.2.n_ref, bf16[4,32,768]{2,1,0:T(8,128)(2,1)S(1)} %maximum_bitcast_fusion.w_ref, bf16[4,2,32,1024]{3,2,1,0:T(8,128)(2,1)S(1)} %pad_maximum_fusion.3.f_ref), custom_call_target="tpu_custom_call" | custom-call | bytes 4194304 | tf_op jit(solution)/shard_map/pallas_call | solution.py:98
  61.9 1.3 copy-done.5
  65.6 1.6 copy-done.6
  67.2 3.3 shard_map.213.q_ref
  70.5 35.4 %shard_map.214 = (bf16[4,2,4,384,128]{4,3,2,1,0:T(8,128)(2,1)}, bf16[4,256,1024]{2,1,0:T(8,128)(2,1)S(1)}) custom-call(bf16[4,4,384,128]{3,2,1,0:T(8,128)(2,1)S(1)} %shard_map.213.q_ref, bf16[256,1024]{1,0:T(8,128)(2,1)S(1)} %copy-done.12), custom_call_target="tpu_custom_call" | custom-call | bytes 4194304 | tf_op jit(solution)/shard_map/pallas_call | solution.py:98
  105.9 1.4 copy-done.22
  107.3 55.5 %shard_map.215 = (bf16[32,128,128]{2,1,0:T(8,128)(2,1)}, bf16[8192,128]{1,0:T(8,128)(2,1)}, bf16[128,8192]{1,0:T(8,128)(2,1)}, bf16[16,256,128]{2,1,0:T(8,128)(2...) custom-call(s32[64]{0:T(128)} %reshape.169.anchor_ref, s32[8]{0:T(128)} %lens_ref.3, ...), custom_call_target="tpu_custom_call" | custom-call | flops 4294967296 | bytes 8388608 | tf_op jit(solution)/shard_map/pallas_call | solution.py:655
  162.8 1.2 copy-done.15
  164.0 48.7 %shard_map.216.o_ref = bf16[16,1,128,128]{3,2,1,0:T(8,128)(2,1)S(1)} custom-call(bf16[4,2,4,128,128]{4,3,2,1,0:T(8,128)(2,1)S(1)} %bitcast.101), custom_call_target="tpu_custom_call" | custom-call | bytes 2097152 | tf_op jit(solution)/shard_map/pallas_call | solution.py:98
  213.5 1.6 copy-done.1
  216.2 1.1 shard_map.217
  218.1 25.8 %shard_map.218 = bf16[4,256,1024]{2,1,0:T(8,128)(2,1)S(1)} custom-call(bf16[256,1024]{1,0:T(8,128)(2,1)S(1)} %get-tuple-element.43.n_ref), custom_call_target="tpu_custom_call" | custom-call | bytes 2097152 | tf_op jit(solution)/shard_map/pallas_call | solution.py:98
  243.9 1.4 copy-done.3
  245.3 1.8 slice.54
  247.1 3.4 slice.55
  251.5 1.3 copy-done.23
  252.8 2.4 fusion.21
  255.2 2.3 fusion.22
  257.5 4.4 multiply_convert_fusion
  262.0 2.4 convolution_convert_fusion.3
  264.4 2.4 fusion.23
  266.8 3.8 convolution_convert_fusion
  270.6 2.4 convolution_convert_fusion.2
  273.0 2.4 add_convert_fusion
  275.6 25.2 %shard_map.219.c_ref = bf16[4,256,1024]{2,1,0:T(8,128)(2,1)S(1)} custom-call(bf16[4,256,1024]{2,1,0:T(8,128)(2,1)S(1)} %bitcast.98), custom_call_target="tpu_custom_call" | custom-call | bytes 4194304 | tf_op jit(solution)/shard_map/pallas_call | solution.py:98
  301.0 1.4 copy-done.2
  302.5 1.5 shard_map.220
  305.9 4.0 copy.57
  309.9 7.7 %pad_maximum_fusion = bf16[8,512,1024]{2,1,0:T(8,128)(2,1)} fusion(bf16[8,128,1024]{2,1,0:T(8,128)(2,1)} %bitcast.125, bf16[8,384,1024]{2,1,0:T(8,128)(2,1)} %bitcast.106), kind=kLoop, calls=%fused_computation | loop fusion | flops 16777216 | bytes 16777216 | tf_op jit(solution)/shard_map/concatenate | solution.py:896
  318.7 21.9 %shard_map.221 = bf16[4,2,4,128,128]{4,3,2,1,0:T(8,128)(2,1)S(1)} custom-call(bf16[16,128,128]{2,1,0:T(8,128)(2,1)S(1)} %copy-done.19), custom_call_target="tpu_custom_call" | custom-call | bytes 2097152 | tf_op jit(solution)/shard_map/pallas_call | solution.py:98
  340.6 6.4 %convolution_convert_fusion.4 = bf16[1024,1024]{1,0:T(8,128)(2,1)} fusion(bf16[1024,1024]{1,0:T(8,128)(2,1)} %copy-done.40, bf16[1024,1024]{1,0:T(8,128)(2,1)} %bitcast.116), kind=kOutput, calls=%fused_computation.14 | convolution fusion | flops 2148532224 | bytes 6291456 | tf_op jit(solution)/shard_map/dot_general | solution.py:40
  347.0 42.9 %shard_map.222 = bf16[32,384,128]{2,1,0:T(8,128)(2,1)} custom-call(s32[64]{0:T(128)} %reshape.169.anchor_ref, s32[8]{0:T(128)} %lens_ref.3, s32[1]{0:T(128)} %bitcast.1.who_ref, bf16[32,128,128]{2,1,0:T(8,128)(2,1)} %bitcast.100, bf16[8192,128]{1,0:T(8,128)(2,1)} %get-tuple-element.45.kv_ref, bf16[128,8192]{1,0:T(8,128)(2,1)} %get-tuple-element.46.kvt_ref, ...), custom_call_target="tpu_custom_call" | custom-call | flops 10737418240 | bytes 8388608 | tf_op jit(solution)/shard_map/pallas_call | solution.py:771
  389.9 1.6 copy-done.9
  391.5 45.7 %shard_map.223 = (bf16[4,1,4,384,128]{4,3,2,1,0:T(8,128)(2,1)S(1)}, bf16[4,256,1024]{2,1,0:T(8,128)(2,1)S(1)}) custom-call(bf16[4,2,4,384,128]{4,3,2,1,0:T(8,128)(2,1)} %bitcast.114, bf16[4,256,1024]{2,1,0:T(8,128)(2,1)S(1)} %bitcast.97), custom_call_target="tpu_custom_call" | custom-call | bytes 6291456 | tf_op jit(solution)/shard_map/pallas_call | solution.py:98
  437.2 3.5 shard_map.224
  443.3 1.9 bitcast_convert_fusion
  445.2 1.2 slice.58
  446.4 54.3 %shard_map.225 = (bf16[4,256,1024]{2,1,0:T(8,128)(2,1)S(1)}, bf16[4,4,32,768]{3,2,1,0:T(8,128)(2,1)S(1)}, bf16[4,3,32,1024]{3,2,1,0:T(8,128)(2,1)S(1)}) custom-call(bf16[4,256,1024]{2,1,0:T(8,128)(2,1)} %copy-done.8, bf16[16,2,32,768]{3,2,1,0:T(8,128)(2,1)S(1)} %bitcast.99, bf16[4,3,32,1024]{3,2,1,0:T(8,128)(2,1)S(1)} %bitcast.92), custom_call_target="tpu_custom_call" | custom-call | bytes 6291456 | tf_op jit(solution)/shard_map/pallas_call | solution.py:98
  503.7 1.2 reshape.209
  504.9 1.6 copy.65
  506.9 1.1 fusion.20
  511.3 1.4 copy.61
  512.8 1.2 reshape.207
  515.7 1.8 broadcast_multiply_fusion
  517.5 1.4 broadcast_multiply_fusion.2
  518.9 1.8 slice_convert_fusion
  (136 shorter events, 24.1 us)
Async XLA Ops:
  7.2 5.2 copy-start.32
  7.2 5.3 %copy-start.39 = (f32[32]{0:T(128)S(1)}, f32[32]{0:T(128)}, u32[]{:S(2)}) copy-start(f32[32]{0:T(128)} %param.20) | copy-start | bytes 388
  7.2 5.3 %copy-start.27 = (f32[32,4096]{1,0:T(8,128)S(1)}, f32[32,4096]{1,0:T(8,128)}, u32[]{:S(2)}) copy-start(f32[32,4096]{1,0:T(8,128)} %param.22) | copy-start | bytes 1572868
  7.2 5.3 %copy-start.25 = (f32[32,4096]{1,0:T(8,128)S(1)}, f32[32,4096]{1,0:T(8,128)}, u32[]{:S(2)}) copy-start(f32[32,4096]{1,0:T(8,128)} %param.21) | copy-start | bytes 1572868
  7.2 206.3 %all-gather.4.cloned.1.call-start = ((), (), s32[]{:S(2)}) async-start(), calls=%async_computation.1 | async-start | bytes 2162688 | tf_op jit(solution)/shard_map/all_gather | solution.py:841
  8.9 236.4 %all-gather.6.cloned.1.call-start = ((), (), s32[]{:S(2)}) async-start(), calls=%async_computation.3 | async-start | bytes 7077888 | tf_op jit(solution)/shard_map/all_gather | solution.py:849
  12.8 1.0 copy-start
  14.1 50.7 %copy-start.38 = (s32[64]{0:T(128)S(1)}, s32[64]{0:T(128)}, u32[]{:S(2)}) copy-start(s32[64]{0:T(128)} %param.24) | copy-start | bytes 772
  61.9 1.3 copy-start.5
  64.2 381.0 %reduce-scatter.2.cloned.1.call-start = ((), (), s32[]{:S(2)}) async-start(), calls=%async_computation.2 | async-start | bytes 9437184 | tf_op jit(solution)/shard_map/reduce_scatter | solution.py:906
  65.6 1.6 copy-start.6
  67.2 3.3 copy-start.12
  105.9 1.4 copy-start.22
  162.8 1.2 copy-start.15
  212.7 0.8 copy-start.10
  213.5 1.6 copy-start.1
  215.1 1.0 copy-start.11
  217.3 0.8 copy-start.20
  243.9 1.4 copy-start.3
  247.1 4.4 copy-start.24
  251.2 1.6 copy-start.23
  252.8 2.4 copy-start.4
  261.9 4.8 copy-start.40
  300.8 1.6 copy-start.2
  300.9 1.7 copy-start.13
  302.5 1.6 copy-start.21
  304.1 1.1 copy-start.16
  304.1 1.1 copy-start.18
  317.6 1.0 copy-start.19
  340.6 6.4 %copy-start.14 = (bf16[4,2,4,128,128]{4,3,2,1,0:T(8,128)(2,1)}, bf16[4,2,4,128,128]{4,3,2,1,0:T(8,128)(2,1)S(1)}, u32[]{:S(2)}) copy-start(bf16[4,2,4,128,128]{4,3,2,1,0:T(8,128)(2,1)S(1)} %shard_map.221) | copy-start | bytes 3145732
  389.9 1.6 copy-start.9
  440.8 1.5 copy-start.8
  441.2 2.1 copy-start.7
  501.6 1.4 copy-start.31
  503.0 3.5 slice-start
  508.3 5.7 %copy-start.17 = (f32[256,1024]{1,0:T(8,128)S(1)}, f32[256,1024]{1,0:T(8,128)}, u32[]{:S(2)}) copy-start(f32[256,1024]{1,0:T(8,128)} %copy-done.16) | copy-start | bytes 3145732
  514.0 1.1 copy-start.26
  514.0 1.2 copy-start.28
  514.0 1.5 copy-start.29
  514.0 1.7 copy-start.30
  515.7 1.8 copy-start.33
  515.7 1.8 copy-start.34
  515.7 1.8 copy-start.35
  515.7 1.8 copy-start.36
  515.7 1.8 copy-start.37
Sparse Core Ops, SparseCore 0:
  11.5 76.8 all-gather.3
  90.0 72.6 all-gather.5
  317.8 100.0 reduce-scatter.1

commit v2 on v1

v2 whole, which is shorter than its diff:
```python
import functools

import jax
import jax.numpy as jnp
from jax import lax
from jax.experimental import pallas as pl
from jax.experimental.pallas import tpu as pltpu
from jax.sharding import Mesh
from jax.sharding import PartitionSpec as P

HEAD_DIM = 64
BLOCK = 128
PAIR = 128
EPS = 1e-06
MASKED = -1e30
QTILE = 256
KTILE = 512
AXES = ("head", "z", "y", "core")
IDS = pl.DeviceIdType.MESH
F32 = jnp.float32
BF16 = jnp.bfloat16
ANY = pl.BlockSpec(memory_space=pl.ANY)
VM = pl.BlockSpec(memory_space=pltpu.VMEM)
SM = pl.BlockSpec(memory_space=pltpu.SMEM)


def struct(shape, dtype=BF16):
    return jax.ShapeDtypeStruct(tuple(shape), dtype)


def nt_dot(a, b):
    return lax.dot_general(a, b, (((1,), (1,)), ((), ())), preferred_element_type=F32)


def tn_dot(a, b):
    return lax.dot_general(a, b, (((0,), (0,)), ((), ())), preferred_element_type=F32)


def dot(a, b):
    return jnp.dot(a, b, preferred_element_type=F32)


def selection(rows, columns, shift, first=0, last=None):
    last = columns if last is None else last
    row = lax.broadcasted_iota(jnp.int32, (rows, columns), 0)
    column = lax.broadcasted_iota(jnp.int32, (rows, columns), 1)
    hit = (row == column + shift) & (column >= first) & (column < last)
    return hit.astype(F32).astype(BF16)


class Place:
    def __init__(self, z_count):
        self.x, self.z, self.y, self.c = (lax.axis_index(a) for a in AXES)
        self.g = self.x * 2 + self.y
        self.chip = (self.x * z_count + self.z) * 2 + self.y

    def sibling(self):
        return (self.x, self.z, self.y, 1 - self.c)

    def plane(self, k):
        return (self.x ^ (k // 2), self.z, self.y ^ (k % 2), self.c)

    def line(self, k):
        return (self.x, self.z ^ k, self.y, self.c)

    def any_chip(self, k):
        return (self.x ^ (k // 2 % 2), self.z ^ (k // 4), self.y ^ (k % 2), self.c)


def meet(peers):
    barrier = pltpu.get_barrier_semaphore()
    for peer in peers:
        pl.semaphore_signal(barrier, inc=1, device_id=peer, device_id_type=IDS)
    pl.semaphore_wait(barrier, len(peers))


def trip(source, target, sems, index, device):
    return pltpu.make_async_remote_copy(
        src_ref=source,
        dst_ref=target,
        send_sem=sems[0].at[index],
        recv_sem=sems[1].at[index],
        device_id=device,
        device_id_type=IDS,
    )


def send(*given):
    copy = trip(*given)
    copy.start()
    return copy


def move(source, target, sems, index):
    copy = pltpu.make_async_copy(source, target, sems.at[index])
    copy.start()
    return copy


DMA = pltpu.SemaphoreType.DMA


def both(count):
    return [DMA((count,)), DMA((count,))]


def exchange(kernel, ident, out_shape, in_specs, out_specs, scratch, args, flops, sent):
    return pl.pallas_call(
        kernel,
        out_shape=out_shape,
        in_specs=in_specs,
        out_specs=out_specs,
        scratch_shapes=scratch,
        compiler_params=pltpu.CompilerParams(
            collective_id=ident, has_side_effects=True, vmem_limit_bytes=56 << 20
        ),
        cost_estimate=pl.CostEstimate(flops=flops, bytes_accessed=sent, transcendentals=0),
    )(*args)


def head_kernel(
    zc,
    group,
    t_ref,
    w_ref,
    f_ref,
    o_ref,
    ng_ref,
    wg_ref,
    fg_ref,
    og_ref,
    a_ref,
    rows,
    weights,
    packed,
    ls,
    w0,
    w1,
    n0,
    n1,
    f0,
    f1,
    o0,
    o1,
    p0,
    p1,
    z0,
    z1,
    b0,
    b1,
    s0,
    s1,
):
    me = Place(zc)
    chips = 4 * zc
    per = zc // group
    qw = group * HEAD_DIM
    width = t_ref.shape[1]
    x = t_ref[...].astype(F32)
    rows[0] = (x * lax.rsqrt(jnp.mean(x * x, axis=-1, keepdims=True) + EPS)).astype(BF16)
    meet([me.any_chip(k) for k in range(1, chips)] + [me.sibling()])
    local = [
        move(w_ref.at[me.g], weights.at[me.chip, me.c], ls, 0),
        move(o_ref, og_ref.at[me.x, me.z, me.y, me.c], ls, 1),
        move(f_ref.at[me.g], fg_ref.at[me.g], ls, 2),
    ]
    pieces = []
    for k in reversed(range(1, chips)):
        there = me.any_chip(k)
        their_g = there[0] * 2 + there[2]
        pieces.append(
            send(w_ref.at[their_g], weights.at[me.chip, me.c], (w0, w1), k, there)
        )
    outs = [
        send(o_ref, og_ref.at[me.x, me.z, me.y, me.c], (o0, o1), k, me.line(k))
        for k in range(1, zc)
    ]
    blocks = [send(rows.at[0], rows.at[k], (n0, n1), k, me.plane(k)) for k in range(1, 4)]
    wide = []
    for k in range(1, 4):
        there = me.plane(k)
        their_g = there[0] * 2 + there[2]
        wide.append(send(f_ref.at[their_g], fg_ref.at[me.g], (f0, f1), k, there))
    local[0].wait()
    for copy in pieces:
        copy.wait()
    relay = send(
        weights.at[:, me.c], weights.at[:, me.c], (s0, s1), 0, me.sibling()
    )
    relay.wait()
    kept = [move(weights, wg_ref, ls, 3)]

    def project(k, carry):
        @pl.when(k > 0)
        def _():
            trip(rows.at[0], rows.at[k], (n0, n1), k, me.plane(k)).wait_recv()

        at = (me.x ^ (k // 2)) * 2 + (me.y ^ (k % 2))
        out = dot(rows[k], weights[...].reshape(width, 3 * qw)).astype(BF16)
        for head in range(group):
            left = selection(qw, PAIR, head * HEAD_DIM, 0, HEAD_DIM)
            right = selection(qw, PAIR, head * HEAD_DIM - HEAD_DIM, HEAD_DIM, PAIR)
            slab = dot(out[:BLOCK, :qw], left) + dot(out[BLOCK:, :qw], right)
            packed[head, k, :BLOCK] = slab.astype(BF16)
            start = qw + head * PAIR
            packed[head, k, BLOCK:] = out[:, start : start + PAIR]
        for over in range(1, zc):
            trip(
                packed.at[(me.z ^ over) // per, k],
                a_ref.at[me.z, me.c, at],
                (z0, z1),
                k * zc + over,
                me.line(over),
            ).start()
        trip(
            packed.at[me.z // per, k], a_ref.at[me.z, me.c, at], (b0, b1), k * zc, me.sibling()
        ).start()
        pltpu.make_async_copy(
            packed.at[me.z // per, k], a_ref.at[me.z, me.c, at], ls.at[4 + k]
        ).start()
        return carry

    lax.fori_loop(0, 4, project, 0)
    kept.append(move(rows, ng_ref, ls, 8))
    for copy in outs + local[1:2]:
        copy.wait()
    mine = og_ref.at[me.x, :, me.y, me.c]
    out_rows = [send(mine, mine, (p0, p1), k, me.plane(k)) for k in range(1, 4)]

    def pass_on(step, carry):
        k, over = step // (zc - 1), step % (zc - 1) + 1
        at = (me.x ^ (k // 2)) * 2 + (me.y ^ (k % 2))
        there = me.z ^ over
        trip(
            packed.at[there // per, k],
            a_ref.at[me.z, me.c, at],
            (z0, z1),
            k * zc + over,
            me.line(over),
        ).wait()
        landed = a_ref.at[there, me.c, at]
        trip(landed, landed, (b0, b1), k * zc + over, me.sibling()).start()
        return carry

    lax.fori_loop(0, 4 * (zc - 1), pass_on, 0)
    for copy in out_rows:
        copy.wait()
    every = og_ref.at[:, :, :, me.c]
    last = send(every, every, (s0, s1), 1, me.sibling())

    def finish(step, carry):
        k, over = step // zc, step % zc
        at = (me.x ^ (k // 2)) * 2 + (me.y ^ (k % 2))
        landed = a_ref.at[me.z ^ over, me.c, at]
        trip(landed, landed, (b0, b1), k * zc + over, me.sibling()).wait()
        return carry

    lax.fori_loop(0, 4 * zc, finish, 0)
    for k in range(4):
        pltpu.make_async_copy(
            packed.at[me.z // per, k], a_ref.at[me.z, me.c, me.g], ls.at[4 + k]
        ).wait()
    for copy in [last] + local[2:] + kept + wide:
        copy.wait()
    for copy in blocks:
        copy.wait_send()


def head_exchange(zc, group, tokens, w_send, f_send, w_out):
    chips = 4 * zc
    own, width = tokens.shape
    piece = w_send.shape[1:]
    return exchange(
        functools.partial(head_kernel, zc, group),
        1,
        (
            struct((4, own, width)),
            struct((chips, 2) + piece),
            struct(f_send.shape),
            struct((2, zc, 2, 2) + w_out.shape),
            struct((zc, 2, 4, BLOCK + own, PAIR)),
        ),
        [VM, ANY, ANY, ANY],
        (ANY,) * 5,
        [
            pltpu.VMEM((4, own, width), BF16),
            pltpu.VMEM((chips, 2) + piece, BF16),
            pltpu.VMEM((group, 4, BLOCK + own, PAIR), BF16),
            DMA((9,)),
        ]
        + both(chips)
        + both(4)
        + both(4)
        + both(zc)
        + both(4)
        + both(4 * zc)
        + both(4 * zc)
        + both(2),
        (tokens, w_send, f_send, w_out),
        2 * 4 * own * width * width,
        16 << 20,
    )


def join_kernel(zc, s_ref, x_ref, w_ref, ob_ref, r_ref, n_ref, mine, theirs, slabs, ls, b0, b1, c0, c1):
    me = Place(zc)
    chips = 4 * zc
    heads, per = slabs.shape[:2]
    meet([me.any_chip(k) for k in range(1, chips)] + [me.sibling()])
    other = send(s_ref.at[:, 1 - me.c], theirs, (b0, b1), 0, me.sibling())
    own = move(s_ref.at[:, me.c], mine, ls, 0)
    own.wait()
    other.wait()
    mine[...] = mine[...] + theirs[...]
    head = me.g * (heads // 4) + me.z // per
    place = me.z % per
    keep = move(mine.at[me.z, me.g], slabs.at[head, place], ls, 1)
    sends = []
    for k in reversed(range(1, chips)):
        there = me.any_chip(k)
        their_g = there[0] * 2 + there[2]
        sends.append(
            send(mine.at[there[1], their_g], slabs.at[head, place], (c0, c1), k, there)
        )
    keep.wait()
    for copy in sends:
        copy.wait()
    for block in range(2):
        for pair in range(heads // 2):
            total = jnp.zeros((BLOCK, PAIR), F32)
            for side in range(2):
                slab = slabs[2 * pair + side, 0]
                for extra in range(1, per):
                    slab = slab + slabs[2 * pair + side, extra]
                pick = selection(
                    PAIR, PAIR, (block - side) * HEAD_DIM, side * HEAD_DIM, (side + 1) * HEAD_DIM
                )
                total = total + dot(slab, pick)
            ob_ref[block * BLOCK : (block + 1) * BLOCK, pair * PAIR : (pair + 1) * PAIR] = (
                total.astype(BF16)
            )
    residual = x_ref[...].astype(F32) + dot(ob_ref[...], w_ref[...])
    r_ref[...] = residual
    mean = jnp.mean(residual * residual, axis=-1, keepdims=True)
    n_ref[...] = (residual * lax.rsqrt(mean + EPS)).astype(BF16)


def join_exchange(zc, heads, slabs, tokens, w_out):
    chips = 4 * zc
    per = 4 * zc // heads
    half = (zc,) + slabs.shape[2:]
    shape = tokens.shape
    return exchange(
        functools.partial(join_kernel, zc),
        2,
        (struct(shape), struct(shape, F32), struct(shape)),
        [ANY, VM, VM],
        (VM,) * 3,
        [
            pltpu.VMEM(half, BF16),
            pltpu.VMEM(half, BF16),
            pltpu.VMEM((heads, per) + slabs.shape[3:], BF16),
            DMA((2,)),
        ]
        + both(1)
        + both(chips),
        (slabs, tokens, w_out),
        2 * shape[0] * shape[1] * shape[1],
        4 << 20,
    )


def middle_kernel(
    zc,
    n_ref,
    ca_ref,
    cb_ref,
    cc_ref,
    cd_ref,
    f_ref,
    wo_ref,
    r_ref,
    ob_ref,
    out_ref,
    dr_ref,
    sh_ref,
    do_ref,
    rows,
    cots,
    gate_w,
    up_w,
    down_w,
    hid,
    dgate,
    dup,
    c_out,
    c_in,
    stage,
    slabs,
    ls,
    n0,
    n1,
    c0,
    c1,
    d0,
    d1,
    b0,
    b1,
):
    me = Place(zc)
    chips = 4 * zc
    width = n_ref.shape[1]
    heads = slabs.shape[0]
    group = heads // 4
    per = zc // group
    loads = []
    for g in range(4):
        x, y = g // 2, g % 2
        loads.append(move(f_ref.at[:, :, 2 * g], gate_w.at[x, :, y], ls, 3 * g))
        loads.append(move(f_ref.at[:, :, 2 * g + 1], up_w.at[x, :, y], ls, 3 * g + 1))
    loads.append(move(f_ref.at[:, :, 8:], down_w, ls, 2))
    rows[0] = n_ref[...]
    for k, ref in enumerate((ca_ref, cb_ref, cc_ref, cd_ref)):
        cots[k] = ref[...]
    meet([me.any_chip(k) for k in range(1, chips)] + [me.sibling()])
    gathers = [send(rows.at[0], rows.at[k], (n0, n1), k, me.plane(k)) for k in range(1, 4)]
    for copy in loads:
        copy.wait()
    square = (width, width)

    def block(k, carry):
        @pl.when(k > 0)
        def _():
            trip(rows.at[0], rows.at[k], (n0, n1), k, me.plane(k)).wait_recv()

        gate_mat, up_mat = gate_w[...].reshape(square), up_w[...].reshape(square)
        gate = dot(rows[k], gate_mat)
        up = dot(rows[k], up_mat)
        back = nt_dot(cots[k], down_w[...].reshape(square))
        sig = jax.nn.sigmoid(gate)
        soft = gate * sig
        hid[k] = (soft * up).astype(BF16)
        dgate[k] = (back * up * sig * (1.0 + gate * (1.0 - sig))).astype(BF16)
        dup[k] = (back * soft).astype(BF16)
        c_out[k] = (nt_dot(dgate[k], gate_mat) + nt_dot(dup[k], up_mat)).astype(BF16)

        @pl.when(k > 0)
        def _():
            trip(c_out.at[k], c_in.at[k], (c0, c1), k, me.plane(k)).start()

        return carry

    lax.fori_loop(0, 4, block, 0)

    def finish_out(k, carry):
        out_ref[k] = dot(hid[k], down_w[...].reshape(square)).astype(BF16)
        return carry

    lax.fori_loop(0, 4, finish_out, 0)
    all_rows = (4 * n_ref.shape[0], width)
    left_t = stage.shape[0]
    stage_sq = [stage.at[i] for i in range(left_t)]

    def weight_grad(left, right, slot):
        chunk = 256
        for first in range(0, width, chunk):
            value = tn_dot(left[:, first : first + chunk], right).astype(BF16)
            stage[slot, first : first + chunk] = value

    shares = []

    def share(slot, which, by_rows):
        parts = stage_sq[slot].reshape(2, zc, 2, 2, width // (8 * zc), width)
        for g in range(4):
            x, y = g // 2, g % 2
            shares.append(
                move(parts.at[x, :, y], sh_ref.at[:, :, 3 * g + which], ls, 12 + 3 * g + which)
            )

    flat = lambda ref: ref[...].reshape(all_rows)
    weight_grad(flat(rows), flat(dgate), 0)
    share(0, 0, True)
    weight_grad(flat(rows), flat(dup), 1)
    share(1, 1, True)
    weight_grad(flat(hid), flat(cots), 2)
    shares.append(
        move(stage_sq[2].reshape(zc, 2, 4, width // (8 * zc), width), sh_ref.at[:, :, 12:], ls, 24)
    )
    total = c_out[0].astype(F32)
    for k in range(1, 4):
        trip(c_out.at[k], c_in.at[k], (c0, c1), k, me.plane(k)).wait_recv()
        total = total + c_in[k].astype(F32)
    residual = r_ref[...]
    scaling = lax.rsqrt(jnp.mean(residual * residual, axis=-1, keepdims=True) + EPS)
    normed = residual * scaling
    middle = jnp.mean(total * normed, axis=-1, keepdims=True)
    grad = cots[0].astype(F32) + scaling * (total - normed * middle)
    dr_ref[...] = grad
    low = grad.astype(BF16)
    back = nt_dot(low, wo_ref[...]).astype(BF16)
    for pair in range(heads // 2):
        two = back[:, pair * PAIR : (pair + 1) * PAIR]
        for side in range(2):
            left = selection(PAIR, PAIR, side * HEAD_DIM, 0, HEAD_DIM)
            right = selection(PAIR, PAIR, (side - 1) * HEAD_DIM, HEAD_DIM, PAIR)
            slab = dot(two[:BLOCK], left) + dot(two[BLOCK:], right)
            slabs[2 * pair + side] = slab.astype(BF16)
    to = do_ref.at[me.z, me.c, me.g]
    own = move(slabs.at[me.g * group + me.z // per], to, ls, 25)
    sends = []
    for k in reversed(range(1, chips)):
        there = me.any_chip(k)
        head = (there[0] * 2 + there[2]) * group + there[1] // per
        sends.append(send(slabs.at[head], to, (d0, d1), k, there))
    weight_grad(ob_ref[...], low, 3)
    share(3, 2, True)
    own.wait()
    for copy in sends:
        copy.wait()
    half = do_ref.at[:, me.c]
    relay = send(half, half, (b0, b1), 0, me.sibling())
    for copy in shares:
        copy.wait()
    for copy in gathers:
        copy.wait_send()
    for k in range(1, 4):
        trip(c_out.at[k], c_in.at[k], (c0, c1), k, me.plane(k)).wait_send()
    relay.wait()


def middle_exchange(zc, normed, cots, weights, w_out, residual, attn_rows):
    chips = 4 * zc
    own, width = normed.shape
    heads = width // HEAD_DIM
    piece = width // (8 * zc)
    blocks = pltpu.VMEM((4, own, width), BF16)
    wide = pltpu.VMEM((2, zc, 2, 2, piece, width), BF16)
    return exchange(
        functools.partial(middle_kernel, zc),
        3,
        (
            struct((4, own, width)),
            struct((own, width), F32),
            struct((zc, 2, 16, piece, width)),
            struct((zc, 2, 4, BLOCK, PAIR)),
        ),
        [VM] * 5 + [ANY] + [VM] * 3,
        (VM, VM, ANY, ANY),
        [blocks, blocks, wide, wide, pltpu.VMEM((zc, 2, 4, piece, width), BF16)]
        + [blocks] * 5
        + [pltpu.VMEM((4, width, width), BF16), pltpu.VMEM((heads, BLOCK, PAIR), BF16), DMA((26,))]
        + both(4)
        + both(4)
        + both(chips)
        + both(1),
        (normed, *cots, weights, w_out, residual, attn_rows),
        2 * 4 * own * width * width * 9,
        64 << 20,
    )


def tail_kernel(
    zc,
    d_ref,
    n_ref,
    w_ref,
    x_ref,
    g_ref,
    tg_ref,
    gw_ref,
    mine,
    theirs,
    landed,
    grads,
    c_out,
    c_in,
    stage,
    other_w,
    ls,
    b0,
    b1,
    z0,
    z1,
    c0,
    c1,
    s0,
    s1,
    w0,
    w1,
):
    me = Place(zc)
    chips = 4 * zc
    group, per = landed.shape[:2]
    qw = group * HEAD_DIM
    meet([me.any_chip(k) for k in range(1, chips)] + [me.sibling()])
    head, place = me.z // per, me.z % per

    def slot(k):
        return (me.x ^ (k // 2)) * 2 + (me.y ^ (k % 2))

    order = (3, 2, 1, 0)
    halves = []
    for k in order:
        halves.append(
            (
                send(d_ref.at[:, 1 - me.c, slot(k)], theirs.at[k], (b0, b1), k, me.sibling()),
                move(d_ref.at[:, me.c, slot(k)], mine.at[k], ls, k),
            )
        )
    for k, (far, near) in zip(order, halves):
        near.wait()
        far.wait()
        mine[k] = mine[k] + theirs[k]
        for over in range(1, zc):
            send(
                mine.at[k, me.z ^ over],
                landed.at[head, place, k],
                (z0, z1),
                k * zc + over,
                me.line(over),
            )
        move(mine.at[k, me.z], landed.at[head, place, k], ls, 4 + k)

    def block(step, carry):
        k = 3 - step
        pltpu.make_async_copy(
            mine.at[k, me.z], landed.at[head, place, k], ls.at[4 + k]
        ).wait()
        for over in range(1, zc):
            trip(
                mine.at[k, me.z ^ over],
                landed.at[head, place, k],
                (z0, z1),
                k * zc + over,
                me.line(over),
            ).wait()
        upper = jnp.zeros((BLOCK, qw), F32)
        lower = jnp.zeros((BLOCK, qw), F32)
        for h in range(group):
            slab = landed[h, 0, k]
            for extra in range(1, per):
                slab = slab + landed[h, extra, k]
            first, last = h * HEAD_DIM, (h + 1) * HEAD_DIM
            upper = upper + dot(slab[:BLOCK], selection(PAIR, qw, -first, first, last))
            lower = lower + dot(slab[:BLOCK], selection(PAIR, qw, HEAD_DIM - first, first, last))
            start = qw + h * PAIR
            grads[k, :, start : start + PAIR] = slab[BLOCK:]
        grads[k, :BLOCK, :qw] = upper.astype(BF16)
        grads[k, BLOCK:, :qw] = lower.astype(BF16)
        c_out[k] = nt_dot(grads[k], w_ref[...]).astype(BF16)

        @pl.when(k > 0)
        def _():
            trip(c_out.at[k], c_in.at[k], (c0, c1), k, me.plane(k)).start()

        return carry

    lax.fori_loop(0, 4, block, 0)
    width, cols = w_ref.shape
    all_rows = 4 * n_ref.shape[1]
    normed_all = n_ref[...].reshape(all_rows, width)
    grads_all = grads[...].reshape(all_rows, cols)
    piece = stage.shape[2]
    chunk = 256
    each = chunk // (2 * piece)
    for first in range(0, width, chunk):
        value = tn_dot(normed_all[:, first : first + chunk], grads_all).astype(BF16)
        at = first // (2 * piece)
        stage[at : at + each] = value.reshape(each, 2, piece, cols)
    swap = send(stage.at[:, 1 - me.c], other_w, (s0, s1), 0, me.sibling())
    swap.wait()

    def add(i, carry):
        other_w[i] = stage[i, me.c] + other_w[i]
        return carry

    lax.fori_loop(0, chips, add, 0)
    stay = move(other_w.at[me.chip], gw_ref.at[me.z, me.g], ls, 8)
    sends = []
    for k in reversed(range(1, chips)):
        there = me.any_chip(k)
        chip = (there[0] * zc + there[1]) * 2 + there[2]
        sends.append(send(other_w.at[chip], gw_ref.at[me.z, me.g], (w0, w1), k, there))
    total = c_out[0].astype(F32)
    for k in range(1, 4):
        trip(c_out.at[k], c_in.at[k], (c0, c1), k, me.plane(k)).wait()
        total = total + c_in[k].astype(F32)
    x = x_ref[...].astype(F32)
    scaling = lax.rsqrt(jnp.mean(x * x, axis=-1, keepdims=True) + EPS)
    normed = x * scaling
    middle = jnp.mean(total * normed, axis=-1, keepdims=True)
    tg_ref[...] = (g_ref[...] + scaling * (total - normed * middle)).astype(BF16)
    stay.wait()
    for copy in sends:
        copy.wait()


def tail_exchange(zc, group, slab_grads, n_all, weights, tokens, residual_grad):
    chips = 4 * zc
    per = zc // group
    own, width = tokens.shape
    cols = weights.shape[1]
    slab = slab_grads.shape[3:]
    piece = width // (2 * chips)
    blocks = pltpu.VMEM((4, own, width), BF16)
    return exchange(
        functools.partial(tail_kernel, zc),
        4,
        (struct((own, width)), struct((zc, 4, piece, cols))),
        [ANY] + [VM] * 4,
        (VM, ANY),
        [
            pltpu.VMEM((4, zc) + slab, BF16),
            pltpu.VMEM((4, zc) + slab, BF16),
            pltpu.VMEM((group, per, 4) + slab, BF16),
            pltpu.VMEM((4, own, cols), BF16),
            blocks,
            blocks,
            pltpu.VMEM((chips, 2, piece, cols), BF16),
            pltpu.VMEM((chips, piece, cols), BF16),
            DMA((9,)),
        ]
        + both(4)
        + both(4 * zc)
        + both(4)
        + both(1)
        + both(chips),
        (slab_grads, n_all, weights, tokens, residual_grad),
        2 * 4 * own * width * cols * 2,
        24 << 20,
    )


def share_kernel(zc, f_ref, gf_ref, ls, f0, f1):
    me = Place(zc)
    meet([me.plane(k) for k in range(1, 4)])
    copies = [move(f_ref.at[me.g], gf_ref.at[me.g], ls, 0)]
    for k in range(1, 4):
        there = me.plane(k)
        copies.append(
            send(f_ref.at[there[0] * 2 + there[2]], gf_ref.at[me.g], (f0, f1), k, there)
        )
    for copy in copies:
        copy.wait()


def share_exchange(zc, shares):
    return exchange(
        functools.partial(share_kernel, zc),
        5,
        struct(shares.shape),
        [ANY],
        ANY,
        [DMA((1,))] + both(4),
        (shares,),
        0,
        2 << 20,
    )


def segment_start(position, lens_ref):
    start = jnp.zeros_like(position)
    end = 0
    for j in range(lens_ref.shape[0]):
        end = end + lens_ref[j]
        start = jnp.where(position >= end, end, start)
    return start


def tile_of(turn, workers, worker):
    forward = turn * workers + worker
    backward = turn * workers + workers - 1 - worker
    return jnp.where((turn & 1) == 0, forward, backward)


def key_bounds(first, lens_ref):
    low_start = segment_start(first, lens_ref)
    high_start = segment_start(first + QTILE - 1, lens_ref)
    low = low_start // KTILE
    high = (first + QTILE + KTILE - 1) // KTILE
    plain = jnp.clip((high_start + KTILE - 1) // KTILE, low, high)
    stop = jnp.clip((first + 1) // KTILE, plain, high)
    return low, plain, stop, high


def visible(first, tile, starts):
    key = tile * KTILE + lax.broadcasted_iota(jnp.int32, (KTILE, QTILE), 0)
    query = first + lax.broadcasted_iota(jnp.int32, (KTILE, QTILE), 1)
    return (key <= query) & (key >= starts)


def forward_kernel(
    workers, anchor_ref, lens_ref, who_ref, a_ref, o_ref, kv_ref, kvt_ref, q_ref, qt_ref, ot_ref, l_ref, inv, pick
):
    blocks = anchor_ref.shape[0]
    turns = q_ref.shape[0]
    per = QTILE // BLOCK
    worker = who_ref[0]

    def note(i, carry):
        inv[anchor_ref[i]] = i
        return carry

    lax.fori_loop(0, blocks, note, 0)
    for half in range(2):
        pick[half] = selection(PAIR, PAIR, half * HEAD_DIM, 0, HEAD_DIM)
        row = lax.broadcasted_iota(jnp.int32, (PAIR, PAIR), 0)
        column = lax.broadcasted_iota(jnp.int32, (PAIR, PAIR), 1)
        hit = (column == row + half * HEAD_DIM) & (row < HEAD_DIM)
        pick[2 + half] = hit.astype(F32).astype(BF16)
    same = lax.broadcasted_iota(jnp.int32, (PAIR, PAIR), 0)
    pick[4] = (same == lax.broadcasted_iota(jnp.int32, (PAIR, PAIR), 1)).astype(F32).astype(BF16)
    o_ref[...] = jnp.zeros_like(o_ref)

    def order(i, carry):
        where = inv[i]
        slab, half = where >> 1, where & 1
        block = a_ref[slab, pl.ds(pl.multiple_of(BLOCK + half * BLOCK, BLOCK), BLOCK), :]
        at = pl.ds(pl.multiple_of(i * BLOCK, BLOCK), BLOCK)
        kv_ref[at, :] = block
        kvt_ref[:, at] = nt_dot(pick[4], block).astype(BF16)
        return carry

    lax.fori_loop(0, blocks, order, 0)

    def one_tile(turn, carry):
        tile = tile_of(turn, workers, worker)
        first = tile * QTILE
        for b in range(per):
            where = inv[tile * per + b]
            slab, half = where >> 1, where & 1
            rows = a_ref[slab, :BLOCK, :]
            q_ref[turn, b * BLOCK : (b + 1) * BLOCK, :] = (dot(rows, pick[half]) * 0.125).astype(BF16)
            qt_ref[turn, :, b * BLOCK : (b + 1) * BLOCK] = (
                nt_dot(pick[2 + half], rows) * 0.125
            ).astype(BF16)
        query = qt_ref[turn]
        starts = segment_start(first + lax.broadcasted_iota(jnp.int32, (1, QTILE), 1), lens_ref)
        low, plain, stop, high = key_bounds(first, lens_ref)

        def step(masked, kt, state):
            top, total, acc = state
            at = pl.ds(pl.multiple_of(kt * KTILE, KTILE), KTILE)
            scores = dot(kv_ref[at, :], query)
            if masked:
                seen = visible(first, kt, starts)
                scores = jnp.where(seen, scores, MASKED)
            new_top = jnp.maximum(top, jnp.max(scores, axis=0, keepdims=True))
            factor = jnp.exp(top - new_top)
            weights = jnp.exp(scores - new_top)
            if masked:
                weights = jnp.where(seen, weights, 0.0)
            total = total * factor + jnp.sum(weights, axis=0, keepdims=True)
            acc = acc * factor + dot(kvt_ref[HEAD_DIM:, at], weights.astype(BF16))
            return (new_top, total, acc)

        state = (
            jnp.full((1, QTILE), MASKED, F32),
            jnp.zeros((1, QTILE), F32),
            jnp.zeros((HEAD_DIM, QTILE), F32),
        )
        state = lax.fori_loop(low, plain, functools.partial(step, True), state)
        state = lax.fori_loop(plain, stop, functools.partial(step, False), state)
        top, total, acc = lax.fori_loop(stop, high, functools.partial(step, True), state)
        out = acc / total
        ot_ref[turn] = out
        l_ref[turn] = top + jnp.log(total)
        narrow = out.astype(BF16)
        for b in range(per):
            where = inv[tile * per + b]
            slab, half = where >> 1, where & 1
            piece = tn_dot(narrow[:, b * BLOCK : (b + 1) * BLOCK], pick[2 + half, :HEAD_DIM, :])
            o_ref[slab] = o_ref[slab] + piece.astype(BF16)
        return carry

    lax.fori_loop(0, turns, one_tile, 0)


def attention_forward(workers, anchors, lengths, who, packed):
    slabs = packed.shape[0]
    rows = slabs * 2 * BLOCK
    turns = rows // QTILE // workers
    return pl.pallas_call(
        functools.partial(forward_kernel, workers),
        out_shape=(
            struct((slabs, BLOCK, PAIR)),
            struct((rows, PAIR)),
            struct((PAIR, rows)),
            struct((turns, QTILE, PAIR)),
            struct((turns, PAIR, QTILE)),
            struct((turns, HEAD_DIM, QTILE), F32),
            struct((turns, 1, QTILE), F32),
        ),
        in_specs=[SM, SM, SM, VM],
        out_specs=(VM,) * 7,
        scratch_shapes=[pltpu.SMEM((2 * slabs,), jnp.int32), pltpu.VMEM((5, PAIR, PAIR), BF16)],
        compiler_params=pltpu.CompilerParams(vmem_limit_bytes=60 << 20),
        cost_estimate=pl.CostEstimate(
            flops=rows * rows * 64, bytes_accessed=rows * 1024, transcendentals=rows * rows // 8
        ),
    )(anchors, lengths, who, packed)


def backward_kernel(
    workers,
    anchor_ref,
    lens_ref,
    who_ref,
    d_ref,
    kv_ref,
    kvt_ref,
    q_ref,
    qt_ref,
    ot_ref,
    l_ref,
    g_ref,
    inv,
    pick,
    dn,
    dt,
    acc,
):
    blocks = anchor_ref.shape[0]
    turns = q_ref.shape[0]
    per = QTILE // BLOCK
    worker = who_ref[0]

    def note(i, carry):
        inv[anchor_ref[i]] = i
        return carry

    lax.fori_loop(0, blocks, note, 0)
    row = lax.broadcasted_iota(jnp.int32, (PAIR, PAIR), 0)
    column = lax.broadcasted_iota(jnp.int32, (PAIR, PAIR), 1)
    for half in range(2):
        hit = (row - half * HEAD_DIM == column - HEAD_DIM) & (column >= HEAD_DIM)
        pick[half] = hit.astype(F32).astype(BF16)
        hit = (column - half * HEAD_DIM == row - HEAD_DIM) & (row >= HEAD_DIM)
        pick[2 + half] = hit.astype(F32).astype(BF16)
        hit = (column == row + half * HEAD_DIM) & (row < HEAD_DIM)
        pick[4 + half] = hit.astype(F32).astype(BF16)
    acc[...] = jnp.zeros_like(acc)
    g_ref[:, :BLOCK, :] = jnp.zeros((g_ref.shape[0], BLOCK, PAIR), BF16)

    def one_tile(turn, carry):
        tile = tile_of(turn, workers, worker)
        first = tile * QTILE
        for b in range(per):
            where = inv[tile * per + b]
            slab, half = where >> 1, where & 1
            rows = d_ref[slab]
            dn[b * BLOCK : (b + 1) * BLOCK, :] = dot(rows, pick[half]).astype(BF16)
            dt[:, b * BLOCK : (b + 1) * BLOCK] = nt_dot(pick[2 + half], rows).astype(BF16)
        query, query_rows = qt_ref[turn], q_ref[turn]
        grad, grad_rows = dt[...], dn[...]
        norm = l_ref[turn]
        delta = jnp.sum(grad[HEAD_DIM:].astype(F32) * ot_ref[turn], axis=0, keepdims=True)
        starts = segment_start(first + lax.broadcasted_iota(jnp.int32, (1, QTILE), 1), lens_ref)
        low, plain, stop, high = key_bounds(first, lens_ref)

        def step(masked, kt, total):
            at = pl.ds(pl.multiple_of(kt * KTILE, KTILE), KTILE)
            keys = kv_ref[at, :]
            weights = jnp.exp(dot(keys, query) - norm)
            if masked:
                weights = jnp.where(visible(first, kt, starts), weights, 0.0)
            score_grad = (weights * (dot(keys, grad) - delta)).astype(BF16)
            acc[at, :] += dot(score_grad, query_rows) + dot(weights.astype(BF16), grad_rows)
            return total + dot(kvt_ref[:HEAD_DIM, at], score_grad)

        total = jnp.zeros((HEAD_DIM, QTILE), F32)
        total = lax.fori_loop(low, plain, functools.partial(step, True), total)
        total = lax.fori_loop(plain, stop, functools.partial(step, False), total)
        total = lax.fori_loop(stop, high, functools.partial(step, True), total)
        narrow = (total * 0.125).astype(BF16)
        for b in range(per):
            where = inv[tile * per + b]
            slab, half = where >> 1, where & 1
            piece = tn_dot(narrow[:, b * BLOCK : (b + 1) * BLOCK], pick[4 + half, :HEAD_DIM, :])
            g_ref[slab, :BLOCK] = g_ref[slab, :BLOCK] + piece.astype(BF16)
        return carry

    lax.fori_loop(0, turns, one_tile, 0)

    def place(i, carry):
        where = inv[i]
        slab, half = where >> 1, where & 1
        at = pl.ds(pl.multiple_of(i * BLOCK, BLOCK), BLOCK)
        to = pl.ds(pl.multiple_of(BLOCK + half * BLOCK, BLOCK), BLOCK)
        g_ref[slab, to, :] = acc[at, :].astype(BF16)
        return carry

    lax.fori_loop(0, blocks, place, 0)


def attention_backward(workers, anchors, lengths, who, grads, kept):
    slabs = grads.shape[0]
    rows = slabs * 2 * BLOCK
    return pl.pallas_call(
        functools.partial(backward_kernel, workers),
        out_shape=struct((slabs, 3 * BLOCK, PAIR)),
        in_specs=[SM, SM, SM] + [VM] * 7,
        out_specs=VM,
        scratch_shapes=[
            pltpu.SMEM((2 * slabs,), jnp.int32),
            pltpu.VMEM((6, PAIR, PAIR), BF16),
            pltpu.VMEM((QTILE, PAIR), BF16),
            pltpu.VMEM((PAIR, QTILE), BF16),
            pltpu.VMEM((rows, PAIR), F32),
        ],
        compiler_params=pltpu.CompilerParams(vmem_limit_bytes=60 << 20),
        cost_estimate=pl.CostEstimate(
            flops=rows * rows * 160, bytes_accessed=rows * 1024, transcendentals=rows * rows // 8
        ),
    )(anchors, lengths, who, grads, *kept)


def around(value, k):
    return lax.ppermute(value, ("head", "y"), [(i, i ^ k) for i in range(4)])


def body(
    zc,
    tokens,
    cotangent,
    norm1_gain,
    w_query,
    w_key,
    w_value,
    w_out,
    norm2_gain,
    w_gate,
    w_up,
    w_down,
    block_anchor,
    seq_lengths,
):
    width = tokens.shape[1]
    heads = width // HEAD_DIM
    group = heads // 4
    per_head = zc // group
    workers = 2 * per_head
    feature_rows = w_query.shape[0]
    hidden = w_gate.shape[1]
    units = w_down.shape[0]
    slice_units = hidden // 4

    low = lambda v: v.astype(BF16).astype(F32)
    gain1, gain2 = low(norm1_gain)[:, None], low(norm2_gain)[:, None]
    query_w, key_w, value_w = low(w_query), low(w_key), low(w_value)
    gate_w, up_w = low(w_gate), low(w_up)
    q_part = (gain1 * query_w).reshape(feature_rows, 4, group * HEAD_DIM)
    kv_part = jnp.stack(
        [
            (gain1 * key_w).reshape(feature_rows, 4, group, HEAD_DIM),
            (gain1 * value_w).reshape(feature_rows, 4, group, HEAD_DIM),
        ],
        axis=3,
    ).reshape(feature_rows, 4, group * PAIR)
    w_send = jnp.transpose(jnp.concatenate([q_part, kv_part], axis=2).astype(BF16), (1, 0, 2))

    def slices(weight):
        return jnp.transpose(
            weight.reshape(feature_rows, 2, zc, 2, 2 * units), (1, 3, 0, 2, 4)
        ).reshape(4, feature_rows, slice_units)

    f_send = jnp.stack([slices((gain2 * gate_w).astype(BF16)), slices((gain2 * up_w).astype(BF16))], axis=1)

    n1_all, qkv_w, f_all, out_all, by_head = head_exchange(
        zc, group, tokens, w_send, f_send, w_out.astype(BF16)
    )
    qkv_w = qkv_w.reshape(width, 3 * group * HEAD_DIM)
    out_mat = out_all.reshape(width, width)

    ffn_in = jnp.concatenate(
        [f_all.reshape(8, feature_rows, width), w_down.astype(BF16).reshape(4, feature_rows, width)], axis=0
    )
    ffn_all = lax.all_gather(ffn_in, ("z", "core"), axis=0, tiled=False).reshape(
        zc, 2, 12, feature_rows, width
    )
    by_head, near = lax.optimization_barrier((by_head, cotangent))
    cots = [cotangent] + [around(near, k) for k in range(1, 4)]

    anchors = jnp.transpose(block_anchor.reshape(2, zc, 2, 2, 2), (1, 3, 0, 2, 4)).reshape(-1)
    who = ((lax.axis_index("z") % per_head) * 2 + lax.axis_index("core")).astype(jnp.int32).reshape(1)
    slab_count = zc * 8
    o_slabs, *kept = attention_forward(
        workers, anchors, seq_lengths, who, by_head.reshape((slab_count,) + by_head.shape[3:])
    )
    attn_rows, residual, normed_two = join_exchange(
        zc, heads, o_slabs.reshape(zc, 2, 4, BLOCK, PAIR), tokens, out_mat
    )
    out_parts, residual_grad, shares, do_heads = middle_exchange(
        zc, normed_two, cots, ffn_all, out_mat, residual, attn_rows
    )
    outs = [out_parts[0]] + [around(out_parts[k], k) for k in range(1, 4)]
    shares = lax.psum_scatter(
        shares.reshape(zc * 2 * 16, feature_rows, width), ("z", "core"), scatter_dimension=0, tiled=True
    )
    grad_heads = attention_backward(
        workers, anchors, seq_lengths, who, do_heads.reshape(slab_count, BLOCK, PAIR), kept
    )
    tokens_grad, w_all = tail_exchange(
        zc,
        group,
        grad_heads.reshape(zc, 2, 4, 3 * BLOCK, PAIR),
        n1_all,
        qkv_w,
        tokens,
        residual_grad,
    )
    shares, tokens_grad = lax.optimization_barrier((shares, tokens_grad))
    f_grad = share_exchange(zc, shares[:12].reshape(4, 3, feature_rows, width))
    down_share = shares[12:].reshape(units, width)

    output = (residual + sum(v.astype(F32) for v in outs)).astype(BF16)
    w_sum = jnp.sum(w_all.astype(F32), axis=0)
    q_cols = group * HEAD_DIM
    query_raw = jnp.transpose(w_sum[:, :, :q_cols], (1, 0, 2)).reshape(feature_rows, width)
    kv_raw = w_sum[:, :, q_cols:].reshape(4, feature_rows, group, 2, HEAD_DIM)
    key_raw = jnp.transpose(kv_raw[:, :, :, 0], (1, 0, 2, 3)).reshape(feature_rows, width)
    value_raw = jnp.transpose(kv_raw[:, :, :, 1], (1, 0, 2, 3)).reshape(feature_rows, width)
    gain1_grad = jnp.sum(query_raw * query_w + key_raw * key_w + value_raw * value_w, axis=1)

    def unslice(grad):
        return jnp.transpose(
            grad.astype(F32).reshape(2, 2, feature_rows, zc, 2 * units), (2, 0, 3, 1, 4)
        ).reshape(feature_rows, hidden)

    gate_raw, up_raw = unslice(f_grad[:, 0]), unslice(f_grad[:, 1])
    gain2_grad = jnp.sum(gate_raw * gate_w + up_raw * up_w, axis=1)
    out_share = jnp.sum(f_grad[:, 2].astype(F32), axis=0)
    return (
        output,
        tokens_grad,
        gain1_grad,
        gain1 * query_raw,
        gain1 * key_raw,
        gain1 * value_raw,
        out_share,
        gain2_grad,
        gain2 * gate_raw,
        gain2 * up_raw,
        down_share.astype(F32),
    )


def solution(mesh):
    blk = mesh.shape["blk"]
    grid = Mesh(mesh.devices.reshape(mesh.shape["head"], blk // 4, 2, 2), AXES)
    rows, vector, whole = P(AXES, None), P(AXES), P()
    return jax.shard_map(
        functools.partial(body, blk // 4),
        mesh=grid,
        in_specs=(rows, rows, vector, rows, rows, rows, rows, vector, rows, rows, rows, whole, whole),
        out_specs=(rows, rows, vector, rows, rows, rows, rows, vector, rows, rows, rows),
        check_vma=False,
    )
```

time: 532 us -> 420 us (0.79); the launches traced: 528 us -> 422 us
  Pallas kernels: 413 us -> 367 us
  local copies, waits for them, and re-layouts: 44.8 us -> 12.8 us
  matrix products: 31.6 us -> 0 us
  starting transfers between devices: 0.65 us -> 7.15 us
    pallas_call x12 -> x5, Pallas kernels: 314 us -> 277 us  [exchange(): pl.pallas_call(kernel, out_shape=out_shape, in_specs=in_specs, out_specs=...]
    dot_general x11 -> x0, matrix products: 31.6 us -> none  [the longest x3 13.1 us: dot(): return jnp.dot(a, b, preferred_element_type=F32)]
    unnamed x83 -> x24, local copies, waits for them, and re-layouts: 19.4 us -> 3.47 us
    concatenate x3 -> x1, other arithmetic: 9.34 us -> 2.09 us  [body(): jnp.concatenate([f_all.reshape(8, feature_rows, width), w_down.astype(BF1...]
    ppermute x0 -> x6, starting transfers between devices: none -> 7.07 us  [around(): return lax.ppermute(value, ('head', 'y'), [(i, i ^ k) for i in range(4)])]
  transfers between devices with their start and end apart: 3 -> 8, of which waited for: 0 -> 0; matrix products, arithmetic and copies ran while one was open for 3% -> 2% of each run, Pallas kernels for 63% -> 51%
where the time goes in v2:
time: 420 us; the launch traced here: 422 us
  Pallas kernels  367 us (87%)
  other arithmetic  20.6 us (5%)
  between operations  14.5 us (3%)
  local copies, waits for them, and re-layouts  12.8 us (3%)
  starting transfers between devices  7.15 us (2%)
    pallas_call x5, Pallas kernels, exchange(): pl.pallas_call(kernel, out_shape=out_shape, in_specs=in_specs, out_specs=...  277 us
    pallas_call x1, Pallas kernels, attention_forward(): pl.pallas_call(functools.partial(forward_kernel, workers), out_shape=(str...  51.1 us
    pallas_call x1, Pallas kernels, attention_backward(): pl.pallas_call(functools.partial(backward_kernel, workers), out_shape=str...  38.8 us
  transfers between devices with their start and end apart: 8, of which 0 were waited for; matrix products, arithmetic and copies ran while one was open for 2% of the time, Pallas kernels for 51%

profile of v2, /device:TPU:0, one launch (start us, length us, event | category | flops | bytes accessed | tf_op | source)
XLA Modules:
  0.0 422.4 jit_solution(1981333594930219431)
XLA Ops:
  7.3 0.8 convert_convert_fusion.1
  8.0 0.7 convert_convert_fusion
  8.7 1.5 convert_element_type.112.o_ref
  10.2 1.1 fusion.8
  11.5 0.2 copy.52
  11.9 0.2 copy.53
  12.1 0.7 pad_maximum_fusion.2
  12.8 0.2 reshape.122
  13.7 0.2 reshape.124
  14.1 0.7 maximum_bitcast_fusion.w_ref
  14.8 0.8 pad_maximum_fusion.1.f_ref
  15.7 69.7 %shard_map.212 = (bf16[4,256,1024]{2,1,0:T(8,128)(2,1)}, bf16[16,2,32,768]{3,2,1,0:T(8,128)(2,1)}, bf16[4,2,32,1024]{3,2,1,0:T(8,128)(2,1)}, bf16[2,4,2,2,32,102...) custom-call(bf16[256,1024]{1,0:T(8,128)(2,1)} %x_ref.3, bf16[4,32,768]{2,1,0:T(8,128)(2,1)} %maximum_bitcast_fusion.w_ref, ...), custom_call_target="tpu_custom_call" | custom-call | flops 2147483648 | bytes 16777216 | tf_op jit(solution)/shard_map/pallas_call | solution.py:108
  85.4 2.1 pad_maximum_fusion
  87.6 1.2 collective-permute-start.2
  88.8 0.9 collective-permute-start.1
  89.7 1.5 collective-permute-start
  91.3 0.6 reshape.119.anchor_ref
  91.9 51.1 %shard_map.213 = (bf16[32,128,128]{2,1,0:T(8,128)(2,1)}, bf16[8192,128]{1,0:T(8,128)(2,1)}, bf16[128,8192]{1,0:T(8,128)(2,1)}, bf16[16,256,128]{2,1,0:T(8,128)(2...) custom-call(s32[64]{0:T(128)} %reshape.119.anchor_ref, s32[8]{0:T(128)} %lens_ref.3, ...), custom_call_target="tpu_custom_call" | custom-call | flops 4294967296 | bytes 8388608 | tf_op jit(solution)/shard_map/pallas_call | solution.py:883
  143.0 29.2 %shard_map.214 = (bf16[256,1024]{1,0:T(8,128)(2,1)}, f32[256,1024]{1,0:T(8,128)}, bf16[256,1024]{1,0:T(8,128)(2,1)}) custom-call(bf16[4,2,4,128,128]{4,3,2,1,0:T(8,128)(2,1)} %bitcast.61, bf16[256,1024]{1,0:T(8,128)(2,1)} %x_ref.3, bf16[1024,1024]{1,0:T(8,128)(2,1)} %bitcast.57), custom_call_target="tpu_custom_call" | custom-call | flops 536870912 | bytes 4194304 | tf_op jit(solution)/shard_map/pallas_call | solution.py:108
  172.3 0.7 copy-done.8
  173.4 70.4 %shard_map.215 = (bf16[4,256,1024]{2,1,0:T(8,128)(2,1)}, f32[256,1024]{1,0:T(8,128)}, bf16[4,2,16,32,1024]{4,3,2,1,0:T(8,128)(2,1)}, bf16[4,2,4,128,128]{4,3,2,1,0:T(8,128)(2,1)}) custom-call(bf16[256,1024]{1,0:T(8,128)(2,1)} %get-tuple-element.41.n_ref, bf16[256,1024]{1,0:T(8,128)(2,1)} %ca_ref.1, bf16[256,1024]{1,0:T(8,128)(2,1)} %copy-done.10, ...), custom_call_target="tpu_custom_call" | custom-call | flops 19327352832 | bytes 67108864 | tf_op jit(solution)/shard_map/pallas_call | solution.py:108
  243.8 1.6 copy-done
  245.4 1.2 slice_bitcast_fusion.2
  246.5 0.8 collective-permute-start.3
  247.4 1.8 collective-permute-start.5
  249.2 0.9 collective-permute-start.4
  250.0 38.8 %shard_map.216 = bf16[32,384,128]{2,1,0:T(8,128)(2,1)} custom-call(s32[64]{0:T(128)} %reshape.119.anchor_ref, s32[8]{0:T(128)} %lens_ref.3, s32[1]{0:T(128)} %bitcast.1.who_ref, bf16[32,128,128]{2,1,0:T(8,128)(2,1)} %bitcast.76, bf16[8192,128]{1,0:T(8,128)(2,1)} %get-tuple-element.48.kv_ref, bf16[128,8192]{1,0:T(8,128)(2,1)} %get-tuple-element.49.kvt_ref, ...), custom_call_target="tpu_custom_call" | custom-call | flops 10737418240 | bytes 8388608 | tf_op jit(solution)/shard_map/pallas_call | solution.py:999
  288.8 95.5 %shard_map.217 = (bf16[256,1024]{1,0:T(8,128)(2,1)}, bf16[4,4,32,768]{3,2,1,0:T(8,128)(2,1)}) custom-call(bf16[4,2,4,384,128]{4,3,2,1,0:T(8,128)(2,1)} %bitcast.74, bf16[4,256,1024]{2,1,0:T(8,128)(2,1)} %get-tuple-element.54.n_ref, bf16[1024,768]{1,0:T(8,128)(2,1)} %bitcast.75, bf16[256,1024]{1,0:T(8,128)(2,1)} %x_ref.3, f32[256,1024]{1,0:T(8,128)} %get-tuple-element.56.g_ref), custom_call_target="tpu_custom_call" | custom-call | flops 3221225472 | bytes 25165824 | tf_op jit(solution)/shard_map/pallas_call | solution.py:108
  384.4 1.3 convert_reduce_fusion
  385.7 0.4 reshape.136
  386.1 0.4 fusion.14
  386.6 0.2 reshape.138
  386.9 0.2 reshape.137
  387.1 2.5 broadcast_multiply_fusion.2
  389.6 2.9 fusion.3
  392.5 2.1 slice.47
  394.5 12.5 %shard_map.218 = bf16[4,3,32,1024]{3,2,1,0:T(8,128)(2,1)} custom-call(bf16[4,3,32,1024]{3,2,1,0:T(8,128)(2,1)} %bitcast.56), custom_call_target="tpu_custom_call" | custom-call | bytes 2097152 | tf_op jit(solution)/shard_map/pallas_call | solution.py:108
  407.1 1.7 convert_reduce_fusion.1
  408.7 1.1 slice_convert_fusion
  409.9 0.9 bitcast_convert_fusion
  410.8 0.2 reshape.155
  411.0 0.4 copy.61
  411.4 0.4 reshape.148
  411.9 0.2 reshape.153
  412.1 0.4 copy.60
  412.5 0.4 reshape.146
  413.0 1.7 broadcast_multiply_fusion
  414.7 0.8 copy.71
  (51 shorter events, 2.0 us)
Async XLA Ops:
  7.2 5.8 %copy-start.4 = (f32[128,1024]{1,0:T(8,128)S(1)}, f32[128,1024]{1,0:T(8,128)}, u32[]{:S(2)}) copy-start(f32[128,1024]{1,0:T(8,128)} %param.23) | copy-start | bytes 1572868
  7.2 5.9 %copy-start.2 = (f32[32,4096]{1,0:T(8,128)S(1)}, f32[32,4096]{1,0:T(8,128)}, u32[]{:S(2)}) copy-start(f32[32,4096]{1,0:T(8,128)} %param.22) | copy-start | bytes 1572868
  7.2 5.9 %copy-start.1 = (f32[32,4096]{1,0:T(8,128)S(1)}, f32[32,4096]{1,0:T(8,128)}, u32[]{:S(2)}) copy-start(f32[32,4096]{1,0:T(8,128)} %param.21) | copy-start | bytes 1572868
  7.2 165.1 %all-gather.3.cloned.1.call-start = ((), (), s32[]{:S(2)}) async-start(), calls=%async_computation.2 | async-start | bytes 7077888 | tf_op jit(solution)/shard_map/all_gather | solution.py:1078
  85.4 2.2 copy-start.7
  85.4 5.8 %copy-start.6 = (s32[64]{0:T(128)S(1)}, s32[64]{0:T(128)}, u32[]{:S(2)}) copy-start(s32[64]{0:T(128)} %param.24) | copy-start | bytes 772
  87.5 304.9 %reduce-scatter.2.cloned.1.call-start = ((), (), s32[]{:S(2)}) async-start(), calls=%async_computation.1 | async-start | bytes 9437184 | tf_op jit(solution)/shard_map/reduce_scatter | solution.py:1097
  87.6 84.7 %collective-permute-start.2 = (bf16[256,1024]{1,0:T(8,128)(2,1)S(1)}, bf16[256,1024]{1,0:T(8,128)(2,1)S(1)}, u32[]{:S(2)}, u32[]{:S(2)}) collective-permute-start(bf16[256,1024]{1,0:T(8,128)(2,1)S(1)} %copy-done.7), channel_id=1, source_target_pairs={{0,18},{2,16},{16,2},{18,0},{1,19},{3,17},{17,3},{19,1},{4,22},{6,... | collective-permute-start | bytes 1572872 | tf_op jit(solution)/shard_map/ppermute | solution.py:1019
  88.8 83.5 %collective-permute-start.1 = (bf16[256,1024]{1,0:T(8,128)(2,1)S(1)}, bf16[256,1024]{1,0:T(8,128)(2,1)S(1)}, u32[]{:S(2)}, u32[]{:S(2)}) collective-permute-start(bf16[256,1024]{1,0:T(8,128)(2,1)S(1)} %copy-done.7), channel_id=1, source_target_pairs={{0,16},{2,18},{16,0},{18,2},{1,17},{3,19},{17,1},{19,3},{4,20},{6,... | collective-permute-start | bytes 1572872 | tf_op jit(solution)/shard_map/ppermute | solution.py:1019
  89.7 82.6 %collective-permute-start = (bf16[256,1024]{1,0:T(8,128)(2,1)S(1)}, bf16[256,1024]{1,0:T(8,128)(2,1)S(1)}, u32[]{:S(2)}, u32[]{:S(2)}) collective-permute-start(bf16[256,1024]{1,0:T(8,128)(2,1)S(1)} %copy-done.7), channel_id=1, source_target_pairs={{0,2},{2,0},{16,18},{18,16},{1,3},{3,1},{17,19},{19,17},{4,6},{6,4... | collective-permute-start | bytes 1572872 | tf_op jit(solution)/shard_map/ppermute | solution.py:1019
  172.3 0.8 copy-start.8
  172.3 0.9 copy-start.9
  172.3 1.1 copy-start.10
  243.8 1.6 copy-start
  246.5 143.0 %collective-permute-start.3 = (bf16[256,1024]{1,0:T(8,128)(2,1)}, bf16[256,1024]{1,0:T(8,128)(2,1)}, u32[]{:S(2)}, u32[]{:S(2)}) collective-permute-start(bf16[256,1024]{1,0:T(8,128)(2,1)} %get-tuple-element.61), channel_id=1, source_target_pairs={{0,2},{2,0},{16,18},{18,16},{1,3},{3,1},{17,19},{19,17},{4,6},{6,4... | collective-permute-start | bytes 1572872 | tf_op jit(solution)/shard_map/ppermute | solution.py:1019
  247.4 142.2 %collective-permute-start.5 = (bf16[256,1024]{1,0:T(8,128)(2,1)}, bf16[256,1024]{1,0:T(8,128)(2,1)}, u32[]{:S(2)}, u32[]{:S(2)}) collective-permute-start(bf16[256,1024]{1,0:T(8,128)(2,1)} %get-tuple-element.62), channel_id=1, source_target_pairs={{0,18},{2,16},{16,2},{18,0},{1,19},{3,17},{17,3},{19,1},{4,22},{6,... | collective-permute-start | bytes 1572872 | tf_op jit(solution)/shard_map/ppermute | solution.py:1019
  249.2 140.4 %collective-permute-start.4 = (bf16[256,1024]{1,0:T(8,128)(2,1)}, bf16[256,1024]{1,0:T(8,128)(2,1)}, u32[]{:S(2)}, u32[]{:S(2)}) collective-permute-start(bf16[256,1024]{1,0:T(8,128)(2,1)} %get-tuple-element.63), channel_id=1, source_target_pairs={{0,16},{2,18},{16,0},{18,2},{1,17},{3,19},{17,1},{19,3},{4,20},{6,... | collective-permute-start | bytes 1572872 | tf_op jit(solution)/shard_map/ppermute | solution.py:1019
  394.5 15.3 %slice-start = ((bf16[16,32,1024]{2,1,0:T(8,128)(2,1)}), bf16[4,32,1024]{2,1,0:T(8,128)(2,1)S(1)}, s32[]{:S(2)}) async-start(bf16[16,32,1024]{2,1,0:T(8,128)(2,1)} %reduce-scatter.2.cloned.1.call-done), calls=%async_computation.3 | async-start | bytes 524288 | tf_op jit(solution)/shard_map/slice | solution.py:1114
  411.4 1.6 copy-start.3
  412.5 2.2 copy-start.5
Sparse Core Ops, SparseCore 0:
  87.6 63.9 all-gather.2
  243.9 113.9 reduce-scatter.1

commit v3 on v2

--- a/solution.py
+++ b/solution.py
@@ -13,7 +13,8 @@
 PAIR = 128
 EPS = 1e-06
 MASKED = -1e30
-QTILE = 256
+LOWEST = -1e20
+QTILE = 512
 KTILE = 512
 AXES = ("head", "z", "y", "core")
 IDS = pl.DeviceIdType.MESH
@@ -46,6 +47,35 @@
     column = lax.broadcasted_iota(jnp.int32, (rows, columns), 1)
     hit = (row == column + shift) & (column >= first) & (column < last)
     return hit.astype(F32).astype(BF16)
+
+
+def pair_up(first, first_half, second, second_half):
+    lane = lax.broadcasted_iota(jnp.int32, first.shape, 1)
+    left = first if first_half == 0 else pltpu.roll(first, HEAD_DIM, 1)
+    right = second if second_half == 1 else pltpu.roll(second, HEAD_DIM, 1)
+    return jnp.where(lane < HEAD_DIM, left, right)
+
+
+def column_of(row):
+    count = row.shape[1]
+    i = lax.broadcasted_iota(jnp.int32, (count, count), 0)
+    j = lax.broadcasted_iota(jnp.int32, (count, count), 1)
+    return jnp.sum(jnp.where(i == j, row, 0.0), axis=1, keepdims=True)
+
+
+def row_of(column):
+    count = column.shape[0]
+    i = lax.broadcasted_iota(jnp.int32, (count, count), 0)
+    j = lax.broadcasted_iota(jnp.int32, (count, count), 1)
+    return jnp.sum(jnp.where(i == j, column, 0.0), axis=0, keepdims=True)
+
+
+def low(value):
+    return value.astype(BF16).astype(F32)
+
+
+def lanes(index):
+    return slice(index * PAIR, (index + 1) * PAIR)
 
 
 class Place:
@@ -122,14 +152,24 @@
     zc,
     group,
     t_ref,
-    w_ref,
-    f_ref,
-    o_ref,
+    q_w,
+    k_w,
+    v_w,
+    o_w,
+    g_w,
+    u_w,
+    d_w,
+    gain1,
+    gain2,
     ng_ref,
     wg_ref,
     fg_ref,
     og_ref,
     a_ref,
+    w_ref,
+    f_ref,
+    o_ref,
+    e_ref,
     rows,
     weights,
     packed,
@@ -156,13 +196,24 @@
     per = zc // group
     qw = group * HEAD_DIM
     width = t_ref.shape[1]
+    first_gain, second_gain = column_of(low(gain1[...])), column_of(low(gain2[...]))
+    for g in range(4):
+        at = slice(g * qw, (g + 1) * qw)
+        w_ref[g, :, :qw] = (first_gain * low(q_w[:, at])).astype(BF16)
+        for pair in range(group // 2):
+            at = lanes(g * group // 2 + pair)
+            key, value = first_gain * low(k_w[:, at]), first_gain * low(v_w[:, at])
+            for half in range(2):
+                start = qw + (2 * pair + half) * PAIR
+                w_ref[g, :, start : start + PAIR] = pair_up(key, half, value, half).astype(BF16)
+    o_ref[...] = o_w[...].astype(BF16)
+    e_ref[...] = d_w[...].astype(BF16).reshape(e_ref.shape)
     x = t_ref[...].astype(F32)
     rows[0] = (x * lax.rsqrt(jnp.mean(x * x, axis=-1, keepdims=True) + EPS)).astype(BF16)
     meet([me.any_chip(k) for k in range(1, chips)] + [me.sibling()])
     local = [
         move(w_ref.at[me.g], weights.at[me.chip, me.c], ls, 0),
         move(o_ref, og_ref.at[me.x, me.z, me.y, me.c], ls, 1),
-        move(f_ref.at[me.g], fg_ref.at[me.g], ls, 2),
     ]
     pieces = []
     for k in reversed(range(1, chips)):
@@ -176,11 +227,28 @@
         for k in range(1, zc)
     ]
     blocks = [send(rows.at[0], rows.at[k], (n0, n1), k, me.plane(k)) for k in range(1, 4)]
-    wide = []
+    units = g_w.shape[1] // (4 * zc)
+    for which, ref in enumerate((g_w, u_w)):
+        for g in range(4):
+            px, py = g // 2, g % 2
+            if units % PAIR == 0:
+                for z in range(zc):
+                    at = ((px * zc + z) * 2 + py) * units
+                    f_ref[g, which, :, z * units : (z + 1) * units] = (
+                        second_gain * low(ref[:, at : at + units])
+                    ).astype(BF16)
+            else:
+                for z in range(0, zc, 2):
+                    near, far = (second_gain * low(ref[:, lanes(px * zc + i)]) for i in (z, z + 1))
+                    f_ref[g, which, :, lanes(z // 2)] = pair_up(near, py, far, py).astype(BF16)
+    wide = [
+        move(f_ref.at[me.g], fg_ref.at[pl.ds(2 * me.g, 2)], ls, 2),
+        move(e_ref, fg_ref.at[pl.ds(8, 4)], ls, 9),
+    ]
     for k in range(1, 4):
         there = me.plane(k)
         their_g = there[0] * 2 + there[2]
-        wide.append(send(f_ref.at[their_g], fg_ref.at[me.g], (f0, f1), k, there))
+        wide.append(send(f_ref.at[their_g], fg_ref.at[pl.ds(2 * me.g, 2)], (f0, f1), k, there))
     local[0].wait()
     for copy in pieces:
         copy.wait()
@@ -260,33 +328,38 @@
         pltpu.make_async_copy(
             packed.at[me.z // per, k], a_ref.at[me.z, me.c, me.g], ls.at[4 + k]
         ).wait()
-    for copy in [last] + local[2:] + kept + wide:
+    for copy in [last] + kept + wide:
         copy.wait()
     for copy in blocks:
         copy.wait_send()
 
 
-def head_exchange(zc, group, tokens, w_send, f_send, w_out):
+def head_exchange(zc, group, tokens, matrices, gains):
     chips = 4 * zc
     own, width = tokens.shape
-    piece = w_send.shape[1:]
+    count = matrices[0].shape[0]
+    piece = (count, 3 * group * HEAD_DIM)
     return exchange(
         functools.partial(head_kernel, zc, group),
         1,
         (
             struct((4, own, width)),
             struct((chips, 2) + piece),
-            struct(f_send.shape),
-            struct((2, zc, 2, 2) + w_out.shape),
+            struct((12, count, width)),
+            struct((2, zc, 2, 2, count, width)),
             struct((zc, 2, 4, BLOCK + own, PAIR)),
         ),
-        [VM, ANY, ANY, ANY],
+        [VM] * 10,
         (ANY,) * 5,
         [
+            pltpu.VMEM((4,) + piece, BF16),
+            pltpu.VMEM((4, 2, count, width), BF16),
+            pltpu.VMEM((count, width), BF16),
+            pltpu.VMEM((4, count, width), BF16),
             pltpu.VMEM((4, own, width), BF16),
             pltpu.VMEM((chips, 2) + piece, BF16),
             pltpu.VMEM((group, 4, BLOCK + own, PAIR), BF16),
-            DMA((9,)),
+            DMA((10,)),
         ]
         + both(chips)
         + both(4)
@@ -296,7 +369,7 @@
         + both(4 * zc)
         + both(4 * zc)
         + both(2),
-        (tokens, w_send, f_send, w_out),
+        (tokens, *matrices, *(g.reshape(1, -1) for g in gains)),
         2 * 4 * own * width * width,
         16 << 20,
     )
@@ -378,13 +451,9 @@
     cc_ref,
     cd_ref,
     f_ref,
-    wo_ref,
-    r_ref,
-    ob_ref,
     out_ref,
-    dr_ref,
+    cs_ref,
     sh_ref,
-    do_ref,
     rows,
     cots,
     gate_w,
@@ -396,40 +465,33 @@
     c_out,
     c_in,
     stage,
-    slabs,
     ls,
     n0,
     n1,
     c0,
     c1,
-    d0,
-    d1,
-    b0,
-    b1,
 ):
     me = Place(zc)
-    chips = 4 * zc
     width = n_ref.shape[1]
-    heads = slabs.shape[0]
-    group = heads // 4
-    per = zc // group
+    rows[0] = n_ref[...]
+    meet([me.plane(k) for k in range(1, 4)])
+    farthest = send(rows.at[0], rows.at[3], (n0, n1), 3, me.plane(3))
     loads = []
     for g in range(4):
         x, y = g // 2, g % 2
         loads.append(move(f_ref.at[:, :, 2 * g], gate_w.at[x, :, y], ls, 3 * g))
         loads.append(move(f_ref.at[:, :, 2 * g + 1], up_w.at[x, :, y], ls, 3 * g + 1))
     loads.append(move(f_ref.at[:, :, 8:], down_w, ls, 2))
-    rows[0] = n_ref[...]
     for k, ref in enumerate((ca_ref, cb_ref, cc_ref, cd_ref)):
         cots[k] = ref[...]
-    meet([me.any_chip(k) for k in range(1, chips)] + [me.sibling()])
-    gathers = [send(rows.at[0], rows.at[k], (n0, n1), k, me.plane(k)) for k in range(1, 4)]
     for copy in loads:
         copy.wait()
     square = (width, width)
 
-    def block(k, carry):
-        @pl.when(k > 0)
+    def block(step, carry):
+        k = jnp.where(step == 0, 0, jnp.where(step == 1, 3, step - 1))
+
+        @pl.when(step > 0)
         def _():
             trip(rows.at[0], rows.at[k], (n0, n1), k, me.plane(k)).wait_recv()
 
@@ -444,22 +506,20 @@
         dup[k] = (back * soft).astype(BF16)
         c_out[k] = (nt_dot(dgate[k], gate_mat) + nt_dot(dup[k], up_mat)).astype(BF16)
 
-        @pl.when(k > 0)
+        @pl.when(step > 0)
         def _():
             trip(c_out.at[k], c_in.at[k], (c0, c1), k, me.plane(k)).start()
 
+        @pl.when(step == 0)
+        def _():
+            trip(rows.at[0], rows.at[3], (n0, n1), 3, me.plane(3)).wait_send()
+            for near in (1, 2):
+                trip(rows.at[0], rows.at[near], (n0, n1), near, me.plane(near)).start()
+
         return carry
 
     lax.fori_loop(0, 4, block, 0)
-
-    def finish_out(k, carry):
-        out_ref[k] = dot(hid[k], down_w[...].reshape(square)).astype(BF16)
-        return carry
-
-    lax.fori_loop(0, 4, finish_out, 0)
     all_rows = (4 * n_ref.shape[0], width)
-    left_t = stage.shape[0]
-    stage_sq = [stage.at[i] for i in range(left_t)]
 
     def weight_grad(left, right, slot):
         chunk = 256
@@ -468,70 +528,44 @@
             stage[slot, first : first + chunk] = value
 
     shares = []
-
-    def share(slot, which, by_rows):
-        parts = stage_sq[slot].reshape(2, zc, 2, 2, width // (8 * zc), width)
+    piece = width // (8 * zc)
+
+    def share(slot, which):
+        parts = stage.at[slot].reshape(2, zc, 2, 2, piece, width)
         for g in range(4):
             x, y = g // 2, g % 2
             shares.append(
-                move(parts.at[x, :, y], sh_ref.at[:, :, 3 * g + which], ls, 12 + 3 * g + which)
+                move(parts.at[x, :, y], sh_ref.at[:, :, 2 * g + which], ls, 12 + 2 * g + which)
             )
 
     flat = lambda ref: ref[...].reshape(all_rows)
     weight_grad(flat(rows), flat(dgate), 0)
-    share(0, 0, True)
+    share(0, 0)
     weight_grad(flat(rows), flat(dup), 1)
-    share(1, 1, True)
+    share(1, 1)
     weight_grad(flat(hid), flat(cots), 2)
     shares.append(
-        move(stage_sq[2].reshape(zc, 2, 4, width // (8 * zc), width), sh_ref.at[:, :, 12:], ls, 24)
-    )
+        move(stage.at[2].reshape(zc, 2, 4, piece, width), sh_ref.at[:, :, 8:], ls, 20)
+    )
+
+    def finish_out(k, carry):
+        out_ref[k] = dot(hid[k], down_w[...].reshape(square)).astype(BF16)
+        return carry
+
+    lax.fori_loop(0, 4, finish_out, 0)
     total = c_out[0].astype(F32)
     for k in range(1, 4):
-        trip(c_out.at[k], c_in.at[k], (c0, c1), k, me.plane(k)).wait_recv()
+        trip(c_out.at[k], c_in.at[k], (c0, c1), k, me.plane(k)).wait()
         total = total + c_in[k].astype(F32)
-    residual = r_ref[...]
-    scaling = lax.rsqrt(jnp.mean(residual * residual, axis=-1, keepdims=True) + EPS)
-    normed = residual * scaling
-    middle = jnp.mean(total * normed, axis=-1, keepdims=True)
-    grad = cots[0].astype(F32) + scaling * (total - normed * middle)
-    dr_ref[...] = grad
-    low = grad.astype(BF16)
-    back = nt_dot(low, wo_ref[...]).astype(BF16)
-    for pair in range(heads // 2):
-        two = back[:, pair * PAIR : (pair + 1) * PAIR]
-        for side in range(2):
-            left = selection(PAIR, PAIR, side * HEAD_DIM, 0, HEAD_DIM)
-            right = selection(PAIR, PAIR, (side - 1) * HEAD_DIM, HEAD_DIM, PAIR)
-            slab = dot(two[:BLOCK], left) + dot(two[BLOCK:], right)
-            slabs[2 * pair + side] = slab.astype(BF16)
-    to = do_ref.at[me.z, me.c, me.g]
-    own = move(slabs.at[me.g * group + me.z // per], to, ls, 25)
-    sends = []
-    for k in reversed(range(1, chips)):
-        there = me.any_chip(k)
-        head = (there[0] * 2 + there[2]) * group + there[1] // per
-        sends.append(send(slabs.at[head], to, (d0, d1), k, there))
-    weight_grad(ob_ref[...], low, 3)
-    share(3, 2, True)
-    own.wait()
-    for copy in sends:
-        copy.wait()
-    half = do_ref.at[:, me.c]
-    relay = send(half, half, (b0, b1), 0, me.sibling())
+    cs_ref[...] = total
     for copy in shares:
         copy.wait()
-    for copy in gathers:
-        copy.wait_send()
-    for k in range(1, 4):
-        trip(c_out.at[k], c_in.at[k], (c0, c1), k, me.plane(k)).wait_send()
-    relay.wait()
-
-
-def middle_exchange(zc, normed, cots, weights, w_out, residual, attn_rows):
-    chips = 4 * zc
+    for near in (1, 2):
+        trip(rows.at[0], rows.at[near], (n0, n1), near, me.plane(near)).wait_send()
+
+
+def middle_exchange(zc, normed, cots, weights):
     own, width = normed.shape
-    heads = width // HEAD_DIM
     piece = width // (8 * zc)
     blocks = pltpu.VMEM((4, own, width), BF16)
     wide = pltpu.VMEM((2, zc, 2, 2, piece, width), BF16)
@@ -541,21 +575,127 @@
         (
             struct((4, own, width)),
             struct((own, width), F32),
-            struct((zc, 2, 16, piece, width)),
-            struct((zc, 2, 4, BLOCK, PAIR)),
+            struct((zc, 2, 12, piece, width)),
         ),
-        [VM] * 5 + [ANY] + [VM] * 3,
-        (VM, VM, ANY, ANY),
+        [VM] * 5 + [ANY],
+        (VM, VM, ANY),
         [blocks, blocks, wide, wide, pltpu.VMEM((zc, 2, 4, piece, width), BF16)]
         + [blocks] * 5
-        + [pltpu.VMEM((4, width, width), BF16), pltpu.VMEM((heads, BLOCK, PAIR), BF16), DMA((26,))]
+        + [pltpu.VMEM((3, width, width), BF16), DMA((21,))]
         + both(4)
-        + both(4)
-        + both(chips)
-        + both(1),
-        (normed, *cots, weights, w_out, residual, attn_rows),
+        + both(4),
+        (normed, *cots, weights),
         2 * 4 * own * width * width * 9,
         64 << 20,
+    )
+
+
+def turn_kernel(
+    zc,
+    c_ref,
+    t_ref,
+    r_ref,
+    wo_ref,
+    ob_ref,
+    op_ref,
+    dr_ref,
+    do_ref,
+    dw_ref,
+    out_ref,
+    slabs,
+    stage,
+    o_in,
+    ls,
+    d0,
+    d1,
+    b0,
+    b1,
+    o0,
+    o1,
+):
+    me = Place(zc)
+    chips = 4 * zc
+    heads = slabs.shape[0]
+    group = heads // 4
+    per = zc // group
+    width = t_ref.shape[1]
+    meet([me.any_chip(k) for k in range(1, chips)] + [me.sibling()])
+    outs = [send(op_ref.at[k], o_in.at[k], (o0, o1), k, me.plane(k)) for k in (3, 1, 2)]
+    outs.append(move(op_ref.at[0], o_in.at[0], ls, 5))
+    total, residual = c_ref[...], r_ref[...]
+    scaling = lax.rsqrt(jnp.mean(residual * residual, axis=-1, keepdims=True) + EPS)
+    normed = residual * scaling
+    middle = jnp.mean(total * normed, axis=-1, keepdims=True)
+    grad = t_ref[...].astype(F32) + scaling * (total - normed * middle)
+    dr_ref[...] = grad
+    narrow = grad.astype(BF16)
+    back = nt_dot(narrow, wo_ref[...]).astype(BF16)
+    for pair in range(heads // 2):
+        two = back[:, pair * PAIR : (pair + 1) * PAIR]
+        for side in range(2):
+            left = selection(PAIR, PAIR, side * HEAD_DIM, 0, HEAD_DIM)
+            right = selection(PAIR, PAIR, (side - 1) * HEAD_DIM, HEAD_DIM, PAIR)
+            slab = dot(two[:BLOCK], left) + dot(two[BLOCK:], right)
+            slabs[2 * pair + side] = slab.astype(BF16)
+    to = do_ref.at[me.z, me.c, me.g]
+    own = move(slabs.at[me.g * group + me.z // per], to, ls, 0)
+    sends = []
+    for k in reversed(range(1, chips)):
+        there = me.any_chip(k)
+        head = (there[0] * 2 + there[2]) * group + there[1] // per
+        sends.append(send(slabs.at[head], to, (d0, d1), k, there))
+    chunk = 256
+    attended = ob_ref[...]
+    for first in range(0, width, chunk):
+        stage[first : first + chunk] = tn_dot(attended[:, first : first + chunk], narrow).astype(BF16)
+    parts = stage.reshape(2, zc, 2, 2, width // (8 * zc), width)
+    keeps = []
+    for k in range(4):
+        there = me.plane(k)
+        keeps.append(move(parts.at[there[0], :, there[2]], dw_ref.at[k], ls, 1 + k))
+    own.wait()
+    for copy in sends:
+        copy.wait()
+    half = do_ref.at[:, me.c]
+    relay = send(half, half, (b0, b1), 0, me.sibling())
+    for copy in outs:
+        copy.wait()
+    final = residual
+    for k in range(4):
+        final = final + o_in[k].astype(F32)
+    out_ref[...] = final.astype(BF16)
+    for copy in keeps:
+        copy.wait()
+    relay.wait()
+
+
+def turn_exchange(zc, c_sum, cotangent, residual, w_out, attn_rows, out_parts):
+    chips = 4 * zc
+    own, width = cotangent.shape
+    heads = width // HEAD_DIM
+    return exchange(
+        functools.partial(turn_kernel, zc),
+        6,
+        (
+            struct((own, width), F32),
+            struct((zc, 2, 4, BLOCK, PAIR)),
+            struct((4, zc, 2, width // (8 * zc), width)),
+            struct((own, width)),
+        ),
+        [VM] * 5 + [ANY],
+        (VM, ANY, ANY, VM),
+        [
+            pltpu.VMEM((heads, BLOCK, PAIR), BF16),
+            pltpu.VMEM((width, width), BF16),
+            pltpu.VMEM((4, own, width), BF16),
+            DMA((6,)),
+        ]
+        + both(chips)
+        + both(1)
+        + both(4),
+        (c_sum, cotangent, residual, w_out, attn_rows, out_parts),
+        2 * 2 * own * width * width,
+        8 << 20,
     )
 
 
@@ -566,8 +706,14 @@
     w_ref,
     x_ref,
     g_ref,
+    v_ref,
     tg_ref,
     gw_ref,
+    go_ref,
+    o_in,
+    o_mine,
+    o_theirs,
+    o_land,
     mine,
     theirs,
     landed,
@@ -587,6 +733,10 @@
     s1,
     w0,
     w1,
+    q0,
+    q1,
+    v0,
+    v1,
 ):
     me = Place(zc)
     chips = 4 * zc
@@ -607,6 +757,9 @@
                 move(d_ref.at[:, me.c, slot(k)], mine.at[k], ls, k),
             )
         )
+    o_parts = [move(v_ref.at[0], o_in.at[0], ls, 9)]
+    for k in (3, 1, 2):
+        o_parts.append(send(v_ref.at[k], o_in.at[k], (v0, v1), k, me.plane(k)))
     for k, (far, near) in zip(order, halves):
         near.wait()
         far.wait()
@@ -656,6 +809,13 @@
         return carry
 
     lax.fori_loop(0, 4, block, 0)
+    for copy in o_parts:
+        copy.wait()
+    o_sum = o_in[0].astype(F32)
+    for k in range(1, 4):
+        o_sum = o_sum + o_in[k].astype(F32)
+    o_mine[...] = o_sum.astype(BF16)
+    o_swap = send(o_mine.at[:, 1 - me.c], o_theirs, (s0, s1), 1, me.sibling())
     width, cols = w_ref.shape
     all_rows = 4 * n_ref.shape[1]
     normed_all = n_ref[...].reshape(all_rows, width)
@@ -668,6 +828,11 @@
         at = first // (2 * piece)
         stage[at : at + each] = value.reshape(each, 2, piece, cols)
     swap = send(stage.at[:, 1 - me.c], other_w, (s0, s1), 0, me.sibling())
+    o_swap.wait()
+    o_theirs[...] = o_theirs[...] + o_mine[:, me.c]
+    sends = [
+        send(o_theirs.at[me.z ^ k], o_land.at[k], (q0, q1), k, me.line(k)) for k in range(1, zc)
+    ]
     swap.wait()
 
     def add(i, carry):
@@ -676,7 +841,6 @@
 
     lax.fori_loop(0, chips, add, 0)
     stay = move(other_w.at[me.chip], gw_ref.at[me.z, me.g], ls, 8)
-    sends = []
     for k in reversed(range(1, chips)):
         there = me.any_chip(k)
         chip = (there[0] * zc + there[1]) * 2 + there[2]
@@ -693,9 +857,13 @@
     stay.wait()
     for copy in sends:
         copy.wait()
-
-
-def tail_exchange(zc, group, slab_grads, n_all, weights, tokens, residual_grad):
+    o_sum = o_theirs[me.z].astype(F32)
+    for k in range(1, zc):
+        o_sum = o_sum + o_land[k].astype(F32)
+    go_ref[...] = o_sum
+
+
+def tail_exchange(zc, group, slab_grads, n_all, weights, tokens, residual_grad, out_grads):
     chips = 4 * zc
     per = zc // group
     own, width = tokens.shape
@@ -706,10 +874,14 @@
     return exchange(
         functools.partial(tail_kernel, zc),
         4,
-        (struct((own, width)), struct((zc, 4, piece, cols))),
-        [ANY] + [VM] * 4,
-        (VM, ANY),
+        (struct((own, width)), struct((zc, 4, piece, cols)), struct((piece, width), F32)),
+        [ANY] + [VM] * 4 + [ANY],
+        (VM, ANY, VM),
         [
+            pltpu.VMEM((4, zc, 2, piece, width), BF16),
+            pltpu.VMEM((zc, 2, piece, width), BF16),
+            pltpu.VMEM((zc, piece, width), BF16),
+            pltpu.VMEM((zc, piece, width), BF16),
             pltpu.VMEM((4, zc) + slab, BF16),
             pltpu.VMEM((4, zc) + slab, BF16),
             pltpu.VMEM((group, per, 4) + slab, BF16),
@@ -718,14 +890,16 @@
             blocks,
             pltpu.VMEM((chips, 2, piece, cols), BF16),
             pltpu.VMEM((chips, piece, cols), BF16),
-            DMA((9,)),
+            DMA((10,)),
         ]
         + both(4)
         + both(4 * zc)
         + both(4)
-        + both(1)
-        + both(chips),
-        (slab_grads, n_all, weights, tokens, residual_grad),
+        + both(2)
+        + both(chips)
+        + both(zc)
+        + both(4),
+        (slab_grads, n_all, weights, tokens, residual_grad, out_grads),
         2 * 4 * own * width * cols * 2,
         24 << 20,
     )
@@ -734,12 +908,12 @@
 def share_kernel(zc, f_ref, gf_ref, ls, f0, f1):
     me = Place(zc)
     meet([me.plane(k) for k in range(1, 4)])
-    copies = [move(f_ref.at[me.g], gf_ref.at[me.g], ls, 0)]
-    for k in range(1, 4):
+    copies = []
+    for k in (3, 1, 2):
         there = me.plane(k)
-        copies.append(
-            send(f_ref.at[there[0] * 2 + there[2]], gf_ref.at[me.g], (f0, f1), k, there)
-        )
+        part = f_ref.at[pl.ds(2 * (there[0] * 2 + there[2]), 2)]
+        copies.append(send(part, gf_ref.at[me.g], (f0, f1), k, there))
+    copies.append(move(f_ref.at[pl.ds(2 * me.g, 2)], gf_ref.at[me.g], ls, 0))
     for copy in copies:
         copy.wait()
 
@@ -748,13 +922,115 @@
     return exchange(
         functools.partial(share_kernel, zc),
         5,
-        struct(shares.shape),
+        struct((4, 2) + shares.shape[1:]),
         [ANY],
         ANY,
         [DMA((1,))] + both(4),
         (shares,),
         0,
         2 << 20,
+    )
+
+
+def last_kernel(
+    zc,
+    group,
+    t_ref,
+    o_ref,
+    wo_ref,
+    gw_ref,
+    gf_ref,
+    ds_ref,
+    q_w,
+    k_w,
+    v_w,
+    g_w,
+    u_w,
+    gain1,
+    gain2,
+    tg_ref,
+    out_ref,
+    go_ref,
+    g1_ref,
+    q_ref,
+    k_ref,
+    v_ref,
+    g2_ref,
+    g_ref,
+    u_ref,
+    d_ref,
+):
+    tg_ref[...] = t_ref[...]
+    out_ref[...] = o_ref[...]
+    go_ref[...] = wo_ref[...]
+    d_ref[...] = ds_ref[8:].astype(F32).reshape(d_ref.shape)
+    first_gain, second_gain = column_of(low(gain1[...])), column_of(low(gain2[...]))
+    count = q_w.shape[0]
+    qw = group * HEAD_DIM
+    score = jnp.zeros((count, PAIR), F32)
+    for g in range(4):
+        raw = gw_ref[0, g].astype(F32)
+        for z in range(1, zc):
+            raw = raw + gw_ref[z, g].astype(F32)
+        for pair in range(group // 2):
+            at = lanes(g * group // 2 + pair)
+            start = qw + 2 * pair * PAIR
+            even, odd = raw[:, start : start + PAIR], raw[:, start + PAIR : start + 2 * PAIR]
+            query = raw[:, lanes(pair)]
+            key, value = pair_up(even, 0, odd, 0), pair_up(even, 1, odd, 1)
+            score = score + query * low(q_w[:, at]) + key * low(k_w[:, at]) + value * low(v_w[:, at])
+            q_ref[:, at] = first_gain * query
+            k_ref[:, at] = first_gain * key
+            v_ref[:, at] = first_gain * value
+    g1_ref[...] = row_of(jnp.sum(score, axis=1, keepdims=True))
+    units = g_w.shape[1] // (4 * zc)
+    score = jnp.zeros((count, PAIR), F32)
+    for which, (weight, target) in enumerate(((g_w, g_ref), (u_w, u_ref))):
+        for chunk in range(weight.shape[1] // PAIR):
+            if units % PAIR == 0:
+                owner, piece = divmod(chunk, units // PAIR)
+                x, z, y = owner // (2 * zc), owner // 2 % zc, owner % 2
+                raw = gf_ref[2 * x + y, which, :, lanes(z * units // PAIR + piece)].astype(F32)
+            else:
+                x, z = chunk // zc, chunk % zc
+                near = gf_ref[2 * x, which, :, lanes(z // 2)].astype(F32)
+                far = gf_ref[2 * x + 1, which, :, lanes(z // 2)].astype(F32)
+                raw = pair_up(near, z % 2, far, z % 2)
+            score = score + raw * low(weight[:, lanes(chunk)])
+            target[:, lanes(chunk)] = second_gain * raw
+    g2_ref[...] = row_of(jnp.sum(score, axis=1, keepdims=True))
+
+
+def last_step(zc, group, tokens_grad, output, out_share, w_all, f_all, shares, matrices, gains):
+    own, width = output.shape
+    count, hidden = matrices[3].shape
+    return pl.pallas_call(
+        functools.partial(last_kernel, zc, group),
+        out_shape=(
+            struct((own, width)),
+            struct((own, width)),
+            struct((count, width), F32),
+            struct((1, count), F32),
+            struct((count, width), F32),
+            struct((count, width), F32),
+            struct((count, width), F32),
+            struct((1, count), F32),
+            struct((count, hidden), F32),
+            struct((count, hidden), F32),
+            struct((4 * count, width), F32),
+        ),
+        in_specs=[VM] * 13,
+        out_specs=(VM,) * 11,
+        compiler_params=pltpu.CompilerParams(vmem_limit_bytes=32 << 20),
+    )(
+        tokens_grad,
+        output,
+        out_share,
+        w_all,
+        f_all,
+        shares,
+        *matrices,
+        *(g.reshape(1, -1) for g in gains),
     )
 
 
@@ -767,10 +1043,30 @@
     return start
 
 
-def tile_of(turn, workers, worker):
-    forward = turn * workers + worker
-    backward = turn * workers + workers - 1 - worker
-    return jnp.where((turn & 1) == 0, forward, backward)
+def note_tiles(workers, worker, tiles, lens_ref, mine):
+    turns = tiles // workers
+
+    def snake(turn, carry):
+        forward = turn * workers + worker
+        backward = turn * workers + workers - 1 - worker
+        mine[turn] = jnp.where((turn & 1) == 0, forward, backward)
+        return carry
+
+    def weigh(step, ahead):
+        turn = turns - 1 - step
+        loads = []
+        for tile in (2 * turn, 2 * turn + 1):
+            first, _, _, last = key_bounds(tile * QTILE, lens_ref)
+            loads.append(last - first)
+        lighter_first = loads[0] <= loads[1]
+        first_to_zero = jnp.where(ahead > 0, lighter_first, loads[0] > loads[1])
+        mine[turn] = 2 * turn + jnp.where(first_to_zero, worker, 1 - worker)
+        return ahead + jnp.where(first_to_zero, loads[0] - loads[1], loads[1] - loads[0])
+
+    if workers == 2:
+        lax.fori_loop(0, turns, weigh, 0)
+    else:
+        lax.fori_loop(0, turns, snake, 0)
 
 
 def key_bounds(first, lens_ref):
@@ -789,51 +1085,64 @@
     return (key <= query) & (key >= starts)
 
 
+def note_places(anchor_ref, inv):
+    def note(i, carry):
+        inv[anchor_ref[i]] = i
+        return carry
+
+    lax.fori_loop(0, anchor_ref.shape[0], note, 0)
+
+
+def half_lanes(rows, half):
+    lane = lax.broadcasted_iota(jnp.int32, rows.shape, 1)
+    return jnp.where((lane // HEAD_DIM) == half, rows, jnp.zeros_like(rows))
+
+
+def fold(rows, columns, first):
+    row = lax.broadcasted_iota(jnp.int32, (rows, columns), 0)
+    column = lax.broadcasted_iota(jnp.int32, (rows, columns), 1)
+    return (row % HEAD_DIM == column - first).astype(F32).astype(BF16)
+
+
+def unfold(rows, columns, first):
+    row = lax.broadcasted_iota(jnp.int32, (rows, columns), 0)
+    column = lax.broadcasted_iota(jnp.int32, (rows, columns), 1)
+    return (column % HEAD_DIM == row - first).astype(F32).astype(BF16)
+
+
 def forward_kernel(
-    workers, anchor_ref, lens_ref, who_ref, a_ref, o_ref, kv_ref, kvt_ref, q_ref, qt_ref, ot_ref, l_ref, inv, pick
+    workers, anchor_ref, lens_ref, who_ref, a_ref, o_ref, kv_ref, kvt_ref, q_ref, qt_ref, ot_ref, l_ref, inv, mine, raw
 ):
     blocks = anchor_ref.shape[0]
     turns = q_ref.shape[0]
     per = QTILE // BLOCK
     worker = who_ref[0]
-
-    def note(i, carry):
-        inv[anchor_ref[i]] = i
+    note_places(anchor_ref, inv)
+    note_tiles(workers, worker, turns * workers, lens_ref, mine)
+    o_ref[...] = jnp.zeros_like(o_ref)
+    same = selection(PAIR, PAIR, 0)
+
+    def order(step, carry):
+        for b in range(per):
+            i = step * per + b
+            where = inv[i]
+            slab, half = where >> 1, where & 1
+            at = pl.ds(pl.multiple_of(i * BLOCK, BLOCK), BLOCK)
+            kv_ref[at, :] = a_ref[slab, pl.ds(pl.multiple_of(BLOCK + half * BLOCK, BLOCK), BLOCK), :]
+        at = pl.ds(pl.multiple_of(step * QTILE, QTILE), QTILE)
+        kvt_ref[:, at] = nt_dot(same, kv_ref[at, :]).astype(BF16)
         return carry
 
-    lax.fori_loop(0, blocks, note, 0)
-    for half in range(2):
-        pick[half] = selection(PAIR, PAIR, half * HEAD_DIM, 0, HEAD_DIM)
-        row = lax.broadcasted_iota(jnp.int32, (PAIR, PAIR), 0)
-        column = lax.broadcasted_iota(jnp.int32, (PAIR, PAIR), 1)
-        hit = (column == row + half * HEAD_DIM) & (row < HEAD_DIM)
-        pick[2 + half] = hit.astype(F32).astype(BF16)
-    same = lax.broadcasted_iota(jnp.int32, (PAIR, PAIR), 0)
-    pick[4] = (same == lax.broadcasted_iota(jnp.int32, (PAIR, PAIR), 1)).astype(F32).astype(BF16)
-    o_ref[...] = jnp.zeros_like(o_ref)
-
-    def order(i, carry):
-        where = inv[i]
-        slab, half = where >> 1, where & 1
-        block = a_ref[slab, pl.ds(pl.multiple_of(BLOCK + half * BLOCK, BLOCK), BLOCK), :]
-        at = pl.ds(pl.multiple_of(i * BLOCK, BLOCK), BLOCK)
-        kv_ref[at, :] = block
-        kvt_ref[:, at] = nt_dot(pick[4], block).astype(BF16)
-        return carry
-
-    lax.fori_loop(0, blocks, order, 0)
+    lax.fori_loop(0, blocks // per, order, 0)
 
     def one_tile(turn, carry):
-        tile = tile_of(turn, workers, worker)
+        tile = mine[turn]
         first = tile * QTILE
         for b in range(per):
             where = inv[tile * per + b]
-            slab, half = where >> 1, where & 1
-            rows = a_ref[slab, :BLOCK, :]
-            q_ref[turn, b * BLOCK : (b + 1) * BLOCK, :] = (dot(rows, pick[half]) * 0.125).astype(BF16)
-            qt_ref[turn, :, b * BLOCK : (b + 1) * BLOCK] = (
-                nt_dot(pick[2 + half], rows) * 0.125
-            ).astype(BF16)
+            raw[b * BLOCK : (b + 1) * BLOCK, :] = half_lanes(a_ref[where >> 1, :BLOCK, :], where & 1)
+        q_ref[turn] = (dot(raw[...], fold(PAIR, PAIR, 0)) * 0.125).astype(BF16)
+        qt_ref[turn] = (nt_dot(unfold(PAIR, PAIR, 0), raw[...]) * 0.125).astype(BF16)
         query = qt_ref[turn]
         starts = segment_start(first + lax.broadcasted_iota(jnp.int32, (1, QTILE), 1), lens_ref)
         low, plain, stop, high = key_bounds(first, lens_ref)
@@ -843,19 +1152,16 @@
             at = pl.ds(pl.multiple_of(kt * KTILE, KTILE), KTILE)
             scores = dot(kv_ref[at, :], query)
             if masked:
-                seen = visible(first, kt, starts)
-                scores = jnp.where(seen, scores, MASKED)
+                scores = jnp.where(visible(first, kt, starts), scores, MASKED)
             new_top = jnp.maximum(top, jnp.max(scores, axis=0, keepdims=True))
             factor = jnp.exp(top - new_top)
             weights = jnp.exp(scores - new_top)
-            if masked:
-                weights = jnp.where(seen, weights, 0.0)
             total = total * factor + jnp.sum(weights, axis=0, keepdims=True)
             acc = acc * factor + dot(kvt_ref[HEAD_DIM:, at], weights.astype(BF16))
             return (new_top, total, acc)
 
         state = (
-            jnp.full((1, QTILE), MASKED, F32),
+            jnp.full((1, QTILE), LOWEST, F32),
             jnp.zeros((1, QTILE), F32),
             jnp.zeros((HEAD_DIM, QTILE), F32),
         )
@@ -865,12 +1171,11 @@
         out = acc / total
         ot_ref[turn] = out
         l_ref[turn] = top + jnp.log(total)
-        narrow = out.astype(BF16)
+        wide = tn_dot(out.astype(BF16), unfold(HEAD_DIM, PAIR, 0)).astype(BF16)
         for b in range(per):
             where = inv[tile * per + b]
-            slab, half = where >> 1, where & 1
-            piece = tn_dot(narrow[:, b * BLOCK : (b + 1) * BLOCK], pick[2 + half, :HEAD_DIM, :])
-            o_ref[slab] = o_ref[slab] + piece.astype(BF16)
+            slab = where >> 1
+            o_ref[slab] = o_ref[slab] + half_lanes(wide[b * BLOCK : (b + 1) * BLOCK], where & 1)
         return carry
 
     lax.fori_loop(0, turns, one_tile, 0)
@@ -893,7 +1198,11 @@
         ),
         in_specs=[SM, SM, SM, VM],
         out_specs=(VM,) * 7,
-        scratch_shapes=[pltpu.SMEM((2 * slabs,), jnp.int32), pltpu.VMEM((5, PAIR, PAIR), BF16)],
+        scratch_shapes=[
+            pltpu.SMEM((2 * slabs,), jnp.int32),
+            pltpu.SMEM((turns,), jnp.int32),
+            pltpu.VMEM((QTILE, PAIR), BF16),
+        ],
         compiler_params=pltpu.CompilerParams(vmem_limit_bytes=60 << 20),
         cost_estimate=pl.CostEstimate(
             flops=rows * rows * 64, bytes_accessed=rows * 1024, transcendentals=rows * rows // 8
@@ -915,7 +1224,8 @@
     l_ref,
     g_ref,
     inv,
-    pick,
+    mine,
+    raw,
     dn,
     dt,
     acc,
@@ -924,33 +1234,19 @@
     turns = q_ref.shape[0]
     per = QTILE // BLOCK
     worker = who_ref[0]
-
-    def note(i, carry):
-        inv[anchor_ref[i]] = i
-        return carry
-
-    lax.fori_loop(0, blocks, note, 0)
-    row = lax.broadcasted_iota(jnp.int32, (PAIR, PAIR), 0)
-    column = lax.broadcasted_iota(jnp.int32, (PAIR, PAIR), 1)
-    for half in range(2):
-        hit = (row - half * HEAD_DIM == column - HEAD_DIM) & (column >= HEAD_DIM)
-        pick[half] = hit.astype(F32).astype(BF16)
-        hit = (column - half * HEAD_DIM == row - HEAD_DIM) & (row >= HEAD_DIM)
-        pick[2 + half] = hit.astype(F32).astype(BF16)
-        hit = (column == row + half * HEAD_DIM) & (row < HEAD_DIM)
-        pick[4 + half] = hit.astype(F32).astype(BF16)
+    note_places(anchor_ref, inv)
+    note_tiles(workers, worker, turns * workers, lens_ref, mine)
     acc[...] = jnp.zeros_like(acc)
     g_ref[:, :BLOCK, :] = jnp.zeros((g_ref.shape[0], BLOCK, PAIR), BF16)
 
     def one_tile(turn, carry):
-        tile = tile_of(turn, workers, worker)
+        tile = mine[turn]
         first = tile * QTILE
         for b in range(per):
             where = inv[tile * per + b]
-            slab, half = where >> 1, where & 1
-            rows = d_ref[slab]
-            dn[b * BLOCK : (b + 1) * BLOCK, :] = dot(rows, pick[half]).astype(BF16)
-            dt[:, b * BLOCK : (b + 1) * BLOCK] = nt_dot(pick[2 + half], rows).astype(BF16)
+            raw[b * BLOCK : (b + 1) * BLOCK, :] = half_lanes(d_ref[where >> 1], where & 1)
+        dn[...] = dot(raw[...], fold(PAIR, PAIR, HEAD_DIM)).astype(BF16)
+        dt[...] = nt_dot(unfold(PAIR, PAIR, HEAD_DIM), raw[...]).astype(BF16)
         query, query_rows = qt_ref[turn], q_ref[turn]
         grad, grad_rows = dt[...], dn[...]
         norm = l_ref[turn]
@@ -961,9 +1257,10 @@
         def step(masked, kt, total):
             at = pl.ds(pl.multiple_of(kt * KTILE, KTILE), KTILE)
             keys = kv_ref[at, :]
-            weights = jnp.exp(dot(keys, query) - norm)
+            scores = dot(keys, query)
             if masked:
-                weights = jnp.where(visible(first, kt, starts), weights, 0.0)
+                scores = jnp.where(visible(first, kt, starts), scores, MASKED)
+            weights = jnp.exp(scores - norm)
             score_grad = (weights * (dot(keys, grad) - delta)).astype(BF16)
             acc[at, :] += dot(score_grad, query_rows) + dot(weights.astype(BF16), grad_rows)
             return total + dot(kvt_ref[:HEAD_DIM, at], score_grad)
@@ -972,25 +1269,28 @@
         total = lax.fori_loop(low, plain, functools.partial(step, True), total)
         total = lax.fori_loop(plain, stop, functools.partial(step, False), total)
         total = lax.fori_loop(stop, high, functools.partial(step, True), total)
-        narrow = (total * 0.125).astype(BF16)
+        wide = tn_dot((total * 0.125).astype(BF16), unfold(HEAD_DIM, PAIR, 0)).astype(BF16)
         for b in range(per):
             where = inv[tile * per + b]
+            slab = where >> 1
+            g_ref[slab, :BLOCK] = g_ref[slab, :BLOCK] + half_lanes(
+                wide[b * BLOCK : (b + 1) * BLOCK], where & 1
+            )
+        return carry
+
+    lax.fori_loop(0, turns, one_tile, 0)
+
+    def place(step, carry):
+        for b in range(per):
+            i = step * per + b
+            where = inv[i]
             slab, half = where >> 1, where & 1
-            piece = tn_dot(narrow[:, b * BLOCK : (b + 1) * BLOCK], pick[4 + half, :HEAD_DIM, :])
-            g_ref[slab, :BLOCK] = g_ref[slab, :BLOCK] + piece.astype(BF16)
+            at = pl.ds(pl.multiple_of(i * BLOCK, BLOCK), BLOCK)
+            to = pl.ds(pl.multiple_of(BLOCK + half * BLOCK, BLOCK), BLOCK)
+            g_ref[slab, to, :] = acc[at, :].astype(BF16)
         return carry
 
-    lax.fori_loop(0, turns, one_tile, 0)
-
-    def place(i, carry):
-        where = inv[i]
-        slab, half = where >> 1, where & 1
-        at = pl.ds(pl.multiple_of(i * BLOCK, BLOCK), BLOCK)
-        to = pl.ds(pl.multiple_of(BLOCK + half * BLOCK, BLOCK), BLOCK)
-        g_ref[slab, to, :] = acc[at, :].astype(BF16)
-        return carry
-
-    lax.fori_loop(0, blocks, place, 0)
+    lax.fori_loop(0, blocks // per, place, 0)
 
 
 def attention_backward(workers, anchors, lengths, who, grads, kept):
@@ -1003,7 +1303,8 @@
         out_specs=VM,
         scratch_shapes=[
             pltpu.SMEM((2 * slabs,), jnp.int32),
-            pltpu.VMEM((6, PAIR, PAIR), BF16),
+            pltpu.SMEM((rows // QTILE // workers,), jnp.int32),
+            pltpu.VMEM((QTILE, PAIR), BF16),
             pltpu.VMEM((QTILE, PAIR), BF16),
             pltpu.VMEM((PAIR, QTILE), BF16),
             pltpu.VMEM((rows, PAIR), F32),
@@ -1041,40 +1342,17 @@
     per_head = zc // group
     workers = 2 * per_head
     feature_rows = w_query.shape[0]
-    hidden = w_gate.shape[1]
-    units = w_down.shape[0]
-    slice_units = hidden // 4
-
-    low = lambda v: v.astype(BF16).astype(F32)
-    gain1, gain2 = low(norm1_gain)[:, None], low(norm2_gain)[:, None]
-    query_w, key_w, value_w = low(w_query), low(w_key), low(w_value)
-    gate_w, up_w = low(w_gate), low(w_up)
-    q_part = (gain1 * query_w).reshape(feature_rows, 4, group * HEAD_DIM)
-    kv_part = jnp.stack(
-        [
-            (gain1 * key_w).reshape(feature_rows, 4, group, HEAD_DIM),
-            (gain1 * value_w).reshape(feature_rows, 4, group, HEAD_DIM),
-        ],
-        axis=3,
-    ).reshape(feature_rows, 4, group * PAIR)
-    w_send = jnp.transpose(jnp.concatenate([q_part, kv_part], axis=2).astype(BF16), (1, 0, 2))
-
-    def slices(weight):
-        return jnp.transpose(
-            weight.reshape(feature_rows, 2, zc, 2, 2 * units), (1, 3, 0, 2, 4)
-        ).reshape(4, feature_rows, slice_units)
-
-    f_send = jnp.stack([slices((gain2 * gate_w).astype(BF16)), slices((gain2 * up_w).astype(BF16))], axis=1)
-
-    n1_all, qkv_w, f_all, out_all, by_head = head_exchange(
-        zc, group, tokens, w_send, f_send, w_out.astype(BF16)
+
+    n1_all, qkv_w, ffn_in, out_all, by_head = head_exchange(
+        zc,
+        group,
+        tokens,
+        (w_query, w_key, w_value, w_out, w_gate, w_up, w_down),
+        (norm1_gain, norm2_gain),
     )
     qkv_w = qkv_w.reshape(width, 3 * group * HEAD_DIM)
     out_mat = out_all.reshape(width, width)
 
-    ffn_in = jnp.concatenate(
-        [f_all.reshape(8, feature_rows, width), w_down.astype(BF16).reshape(4, feature_rows, width)], axis=0
-    )
     ffn_all = lax.all_gather(ffn_in, ("z", "core"), axis=0, tiled=False).reshape(
         zc, 2, 12, feature_rows, width
     )
@@ -1090,17 +1368,17 @@
     attn_rows, residual, normed_two = join_exchange(
         zc, heads, o_slabs.reshape(zc, 2, 4, BLOCK, PAIR), tokens, out_mat
     )
-    out_parts, residual_grad, shares, do_heads = middle_exchange(
-        zc, normed_two, cots, ffn_all, out_mat, residual, attn_rows
-    )
-    outs = [out_parts[0]] + [around(out_parts[k], k) for k in range(1, 4)]
+    out_parts, c_sum, shares = middle_exchange(zc, normed_two, cots, ffn_all)
     shares = lax.psum_scatter(
-        shares.reshape(zc * 2 * 16, feature_rows, width), ("z", "core"), scatter_dimension=0, tiled=True
+        shares.reshape(zc * 2 * 12, feature_rows, width), ("z", "core"), scatter_dimension=0, tiled=True
+    )
+    residual_grad, do_heads, out_grads, output = turn_exchange(
+        zc, c_sum, cotangent, residual, out_mat, attn_rows, out_parts
     )
     grad_heads = attention_backward(
         workers, anchors, seq_lengths, who, do_heads.reshape(slab_count, BLOCK, PAIR), kept
     )
-    tokens_grad, w_all = tail_exchange(
+    tokens_grad, w_all, out_share = tail_exchange(
         zc,
         group,
         grad_heads.reshape(zc, 2, 4, 3 * BLOCK, PAIR),
@@ -1108,40 +1386,45 @@
         qkv_w,
         tokens,
         residual_grad,
-    )
-    shares, tokens_grad = lax.optimization_barrier((shares, tokens_grad))
-    f_grad = share_exchange(zc, shares[:12].reshape(4, 3, feature_rows, width))
-    down_share = shares[12:].reshape(units, width)
-
-    output = (residual + sum(v.astype(F32) for v in outs)).astype(BF16)
-    w_sum = jnp.sum(w_all.astype(F32), axis=0)
-    q_cols = group * HEAD_DIM
-    query_raw = jnp.transpose(w_sum[:, :, :q_cols], (1, 0, 2)).reshape(feature_rows, width)
-    kv_raw = w_sum[:, :, q_cols:].reshape(4, feature_rows, group, 2, HEAD_DIM)
-    key_raw = jnp.transpose(kv_raw[:, :, :, 0], (1, 0, 2, 3)).reshape(feature_rows, width)
-    value_raw = jnp.transpose(kv_raw[:, :, :, 1], (1, 0, 2, 3)).reshape(feature_rows, width)
-    gain1_grad = jnp.sum(query_raw * query_w + key_raw * key_w + value_raw * value_w, axis=1)
-
-    def unslice(grad):
-        return jnp.transpose(
-            grad.astype(F32).reshape(2, 2, feature_rows, zc, 2 * units), (2, 0, 3, 1, 4)
-        ).reshape(feature_rows, hidden)
-
-    gate_raw, up_raw = unslice(f_grad[:, 0]), unslice(f_grad[:, 1])
-    gain2_grad = jnp.sum(gate_raw * gate_w + up_raw * up_w, axis=1)
-    out_share = jnp.sum(f_grad[:, 2].astype(F32), axis=0)
+        out_grads,
+    )
+    shares, w_all = lax.optimization_barrier((shares, w_all))
+    (
+        tokens_grad,
+        output,
+        out_grad,
+        gain1_grad,
+        query_grad,
+        key_grad,
+        value_grad,
+        gain2_grad,
+        gate_grad,
+        up_grad,
+        down_grad,
+    ) = last_step(
+        zc,
+        group,
+        tokens_grad,
+        output,
+        out_share,
+        w_all,
+        share_exchange(zc, shares),
+        shares,
+        (w_query, w_key, w_value, w_gate, w_up),
+        (norm1_gain, norm2_gain),
+    )
     return (
         output,
         tokens_grad,
-        gain1_grad,
-        gain1 * query_raw,
-        gain1 * key_raw,
-        gain1 * value_raw,
-        out_share,
-        gain2_grad,
-        gain2 * gate_raw,
-        gain2 * up_raw,
-        down_share.astype(F32),
+        gain1_grad.reshape(-1),
+        query_grad,
+        key_grad,
+        value_grad,
+        out_grad,
+        gain2_grad.reshape(-1),
+        gate_grad,
+        up_grad,
+        down_grad,
     )
 
 

time: 420 us -> 380 us (0.905)
  other arithmetic: 20.6 us -> 0 us
  Pallas kernels: 367 us -> 354 us
  local copies, waits for them, and re-layouts: 12.8 us -> 6.06 us
    pallas_call x1, Pallas kernels: 51.1 us -> 34.4 us  [attention_forward(): pl.pallas_call(functools.partial(forward_kernel, workers), out_shape=(str...]
    convert_element_type x7 -> x0, other arithmetic: 6.86 us -> none  [the longest x1 2.88 us: body(): output = (residual + sum((v.astype(F32) for v in outs))).astype(BF16)]
    mul x2 -> x0, other arithmetic: 4.22 us -> none  [the longest x1 2.47 us: body(): gain1 * value_raw]
    pallas_call x5 -> x6, Pallas kernels: 277 us -> 279 us  [exchange(): pl.pallas_call(kernel, out_shape=out_shape, in_specs=in_specs, out_specs=...]
  transfers between devices with their start and end apart: 8 -> 5, of which waited for: 0 -> 1; matrix products, arithmetic and copies ran while one was open for 2% -> 0% of each run, Pallas kernels for 51% -> 58%
where the time goes in v3:
time: 380 us; the launch traced here: 379 us
  Pallas kernels  354 us (93%)
  between operations  14.3 us (4%)
  local copies, waits for them, and re-layouts  6.06 us (2%)
    pallas_call x6, Pallas kernels, exchange(): pl.pallas_call(kernel, out_shape=out_shape, in_specs=in_specs, out_specs=...  279 us
    pallas_call x1, Pallas kernels, attention_backward(): pl.pallas_call(functools.partial(backward_kernel, workers), out_shape=str...  37.8 us
    pallas_call x1, Pallas kernels, attention_forward(): pl.pallas_call(functools.partial(forward_kernel, workers), out_shape=(str...  34.4 us
  transfers between devices with their start and end apart: 5, of which 1 were waited for; matrix products, arithmetic and copies ran while one was open for 0% of the time, Pallas kernels for 58%

profile of v3, /device:TPU:0, one launch (start us, length us, event | category | flops | bytes accessed | tf_op | source)
XLA Modules:
  0.0 379.0 jit_solution(16703168114127642675)
XLA Ops:
  7.2 0.0 all-gather.3.cloned.1.call-start
  7.2 0.0 copy-start.13
  7.2 0.0 copy-start.14
  7.2 70.3 %shard_map.212 = (bf16[4,256,1024]{2,1,0:T(8,128)(2,1)}, bf16[16,2,32,768]{3,2,1,0:T(8,128)(2,1)}, bf16[12,32,1024]{2,1,0:T(8,128)(2,1)}, bf16[2,4,2,2,32,1024]{...) custom-call(bf16[256,1024]{1,0:T(8,128)(2,1)} %x_ref.3, f32[32,1024]{1,0:T(8,128)} %q_w.3, f32[32,1024]{1,0:T(8,128)} %k_w.3, ...), custom_call_target="tpu_custom_call" | custom-call | flops 2147483648 | bytes 16777216 | tf_op jit(solution)/shard_map/pallas_call | solution.py:138
  77.5 0.0 all-gather.3.cloned.1.call-update
  77.6 0.0 reduce-scatter.2.cloned.1.call-start
  77.6 1.2 collective-permute-start.2
  78.8 0.9 collective-permute-start.1
  79.7 1.5 collective-permute-start
  81.2 0.0 copy-done.14
  81.2 0.1 reshape.69
  81.3 0.6 reshape.70.anchor_ref
  82.0 34.4 %shard_map.213 = (bf16[32,128,128]{2,1,0:T(8,128)(2,1)}, bf16[8192,128]{1,0:T(8,128)(2,1)}, bf16[128,8192]{1,0:T(8,128)(2,1)}, bf16[8,512,128]{2,1,0:T(8,128)(2,...) custom-call(s32[64]{0:T(128)} %reshape.70.anchor_ref, s32[8]{0:T(128)} %lens_ref.3, ...), custom_call_target="tpu_custom_call" | custom-call | flops 4294967296 | bytes 8388608 | tf_op jit(solution)/shard_map/pallas_call | solution.py:1188
  116.4 35.1 %shard_map.214 = (bf16[256,1024]{1,0:T(8,128)(2,1)}, f32[256,1024]{1,0:T(8,128)}, bf16[256,1024]{1,0:T(8,128)(2,1)}) custom-call(bf16[4,2,4,128,128]{4,3,2,1,0:T(8,128)(2,1)} %bitcast.21, bf16[256,1024]{1,0:T(8,128)(2,1)} %x_ref.3, bf16[1024,1024]{1,0:T(8,128)(2,1)} %bitcast.18), custom_call_target="tpu_custom_call" | custom-call | flops 536870912 | bytes 4194304 | tf_op jit(solution)/shard_map/pallas_call | solution.py:138
  151.5 0.0 collective-permute-done.2.cd_ref
  151.5 0.0 copy-start.15
  151.5 0.0 collective-permute-done.1.cc_ref
  151.5 0.0 copy-start.16
  151.5 0.0 collective-permute-done.cb_ref
  151.5 0.0 copy-start.17
  151.5 1.3 all-gather.3.cloned.1.call-done
  152.8 0.0 copy-done.17
  152.8 52.9 %shard_map.215 = (bf16[4,256,1024]{2,1,0:T(8,128)(2,1)}, f32[256,1024]{1,0:T(8,128)}, bf16[4,2,12,32,1024]{4,3,2,1,0:T(8,128)(2,1)}) custom-call(bf16[256,1024]{1,0:T(8,128)(2,1)} %get-tuple-element.55.n_ref, bf16[256,1024]{1,0:T(8,128)(2,1)} %t_ref.3, bf16[256,1024]{1,0:T(8,128)(2,1)} %copy-done.17, bf16[256,1024]{1,0:T(8,128)(2,1)} %copy-done.16, ...), custom_call_target="tpu_custom_call" | custom-call | flops 19327352832 | bytes 67108864 | tf_op jit(solution)/shard_map/pallas_call | solution.py:138
  205.7 0.0 reduce-scatter.2.cloned.1.call-update
  205.7 39.9 %shard_map.216 = (f32[256,1024]{1,0:T(8,128)}, bf16[4,2,4,128,128]{4,3,2,1,0:T(8,128)(2,1)}, bf16[4,4,2,32,1024]{4,3,2,1,0:T(8,128)(2,1)}, bf16[256,1024]{1,0:T(8,128)(2,1)}) custom-call(f32[256,1024]{1,0:T(8,128)} %get-tuple-element.58.c_ref, bf16[256,1024]{1,0:T(8,128)(2,1)} %t_ref.3, f32[256,1024]{1,0:T(8,128)} %get-tuple-element.59.r_ref, ...), custom_call_target="tpu_custom_call" | custom-call | flops 1073741824 | bytes 8388608 | tf_op jit(solution)/shard_map/pallas_call | solution.py:138
  245.6 37.8 %shard_map.217 = bf16[32,384,128]{2,1,0:T(8,128)(2,1)} custom-call(s32[64]{0:T(128)} %reshape.70.anchor_ref, s32[8]{0:T(128)} %lens_ref.3, s32[1]{0:T(128)} %bitcast.1.who_ref, bf16[32,128,128]{2,1,0:T(8,128)(2,1)} %bitcast.24, bf16[8192,128]{1,0:T(8,128)(2,1)} %get-tuple-element.63.kv_ref, bf16[128,8192]{1,0:T(8,128)(2,1)} %get-tuple-element.64.kvt_ref, ...), custom_call_target="tpu_custom_call" | custom-call | flops 10737418240 | bytes 8388608 | tf_op jit(solution)/shard_map/pallas_call | solution.py:1299
  283.4 0.0 copy-start.7
  283.4 0.0 copy-start.8
  283.4 0.0 copy-start.9
  283.4 0.0 copy-start.11
  283.4 0.0 copy-start.12
  283.5 72.5 %shard_map.218 = (bf16[256,1024]{1,0:T(8,128)(2,1)}, bf16[4,4,32,768]{3,2,1,0:T(8,128)(2,1)}, f32[32,1024]{1,0:T(8,128)}) custom-call(bf16[4,2,4,384,128]{4,3,2,1,0:T(8,128)(2,1)} %bitcast.28, bf16[4,256,1024]{2,1,0:T(8,128)(2,1)} %get-tuple-element.69.n_ref, bf16[1024,768]{1,0:T(8,128)(2,1)} %bitcast.29, bf16[256,1024]{1,0:T(8,128)(2,1)} %x_ref.3, ...), custom_call_target="tpu_custom_call" | custom-call | flops 3221225472 | bytes 25165824 | tf_op jit(solution)/shard_map/pallas_call | solution.py:138
  356.0 0.0 reduce-scatter.2.cloned.1.call-done.f_ref.ds_ref
  356.0 8.7 %shard_map.219.gf_ref = bf16[4,2,32,1024]{3,2,1,0:T(8,128)(2,1)} custom-call(bf16[12,32,1024]{2,1,0:T(8,128)(2,1)} %reduce-scatter.2.cloned.1.call-done.f_ref.ds_ref), custom_call_target="tpu_custom_call" | custom-call | bytes 2097152 | tf_op jit(solution)/shard_map/pallas_call | solution.py:138
  364.8 0.0 copy-done.3
  364.8 0.0 copy-done.4
  364.8 0.0 copy-done.5
  364.8 0.0 copy-done.7
  364.8 0.0 copy-done.8
  364.8 0.0 copy-done.9
  364.8 0.0 copy-done.11
  364.8 0.0 copy-done.12
  364.8 1.1 copy-done
  366.0 1.0 copy-done.1
  367.0 1.1 copy-done.2
  368.1 1.0 copy-done.6
  369.2 0.9 copy-done.10
  370.1 2.1 shard_map.220
  (12 shorter events, 0.0 us)
Async XLA Ops:
  7.2 145.7 %all-gather.3.cloned.1.call-start = ((), (), s32[]{:S(2)}) async-start(), calls=%async_computation.2 | async-start | bytes 7077888 | tf_op jit(solution)/shard_map/all_gather | solution.py:1356
  7.2 70.4 %copy-start.13 = (bf16[256,1024]{1,0:T(8,128)(2,1)S(1)}, bf16[256,1024]{1,0:T(8,128)(2,1)}, u32[]{:S(2)}) copy-start(bf16[256,1024]{1,0:T(8,128)(2,1)} %t_ref.3) | copy-start | bytes 1572868
  7.2 74.0 %copy-start.14 = (s32[64]{0:T(128)S(1)}, s32[64]{0:T(128)}, u32[]{:S(2)}) copy-start(s32[64]{0:T(128)} %param.24) | copy-start | bytes 772
  77.6 278.5 %reduce-scatter.2.cloned.1.call-start = ((), (), s32[]{:S(2)}) async-start(), calls=%async_computation.1 | async-start | bytes 7077888 | tf_op jit(solution)/shard_map/reduce_scatter | solution.py:1372
  77.6 73.8 %collective-permute-start.2 = (bf16[256,1024]{1,0:T(8,128)(2,1)S(1)}, bf16[256,1024]{1,0:T(8,128)(2,1)S(1)}, u32[]{:S(2)}, u32[]{:S(2)}) collective-permute-start(bf16[256,1024]{1,0:T(8,128)(2,1)S(1)} %copy-done.13), channel_id=1, source_target_pairs={{0,18},{2,16},{16,2},{18,0},{1,19},{3,17},{17,3},{19,1},{4,22},{6,... | collective-permute-start | bytes 1572872 | tf_op jit(solution)/shard_map/ppermute | solution.py:1320
  78.8 72.7 %collective-permute-start.1 = (bf16[256,1024]{1,0:T(8,128)(2,1)S(1)}, bf16[256,1024]{1,0:T(8,128)(2,1)S(1)}, u32[]{:S(2)}, u32[]{:S(2)}) collective-permute-start(bf16[256,1024]{1,0:T(8,128)(2,1)S(1)} %copy-done.13), channel_id=1, source_target_pairs={{0,16},{2,18},{16,0},{18,2},{1,17},{3,19},{17,1},{19,3},{4,20},{6,... | collective-permute-start | bytes 1572872 | tf_op jit(solution)/shard_map/ppermute | solution.py:1320
  79.7 71.8 %collective-permute-start = (bf16[256,1024]{1,0:T(8,128)(2,1)S(1)}, bf16[256,1024]{1,0:T(8,128)(2,1)S(1)}, u32[]{:S(2)}, u32[]{:S(2)}) collective-permute-start(bf16[256,1024]{1,0:T(8,128)(2,1)S(1)} %copy-done.13), channel_id=1, source_target_pairs={{0,2},{2,0},{16,18},{18,16},{1,3},{3,1},{17,19},{19,17},{4,6},{6,4... | collective-permute-start | bytes 1572872 | tf_op jit(solution)/shard_map/ppermute | solution.py:1320
  151.5 1.4 copy-start.15
  151.5 1.3 copy-start.16
  151.5 1.3 copy-start.17
  283.4 81.4 %copy-start.3 = (f32[32,4096]{1,0:T(8,128)S(1)}, f32[32,4096]{1,0:T(8,128)}, u32[]{:S(2)}) copy-start(f32[32,4096]{1,0:T(8,128)} %g_w.3) | copy-start | bytes 1572868
  283.4 81.4 %copy-start.4 = (f32[32,4096]{1,0:T(8,128)S(1)}, f32[32,4096]{1,0:T(8,128)}, u32[]{:S(2)}) copy-start(f32[32,4096]{1,0:T(8,128)} %u_w.3) | copy-start | bytes 1572868
  283.4 81.4 %copy-start.5 = (bf16[256,1024]{1,0:T(8,128)(2,1)S(1)}, bf16[256,1024]{1,0:T(8,128)(2,1)}, u32[]{:S(2)}) copy-start(bf16[256,1024]{1,0:T(8,128)(2,1)} %get-tuple-element.74.o_ref) | copy-start | bytes 1572868
  283.4 81.4 %copy-start.7 = (f32[32,1024]{1,0:T(8,128)S(1)}, f32[32,1024]{1,0:T(8,128)}, u32[]{:S(2)}) copy-start(f32[32,1024]{1,0:T(8,128)} %q_w.3) | copy-start | bytes 393220
  283.4 81.4 %copy-start.8 = (f32[32,1024]{1,0:T(8,128)S(1)}, f32[32,1024]{1,0:T(8,128)}, u32[]{:S(2)}) copy-start(f32[32,1024]{1,0:T(8,128)} %k_w.3) | copy-start | bytes 393220
  283.4 81.4 %copy-start.9 = (f32[32,1024]{1,0:T(8,128)S(1)}, f32[32,1024]{1,0:T(8,128)}, u32[]{:S(2)}) copy-start(f32[32,1024]{1,0:T(8,128)} %v_w.3) | copy-start | bytes 393220
  283.4 81.4 %copy-start.11 = (f32[32]{0:T(128)S(1)}, f32[32]{0:T(128)}, u32[]{:S(2)}) copy-start(f32[32]{0:T(128)} %param.15) | copy-start | bytes 388
  283.4 81.4 %copy-start.12 = (f32[32]{0:T(128)S(1)}, f32[32]{0:T(128)}, u32[]{:S(2)}) copy-start(f32[32]{0:T(128)} %param.20) | copy-start | bytes 388
  364.8 1.1 copy-start
  366.0 1.0 copy-start.1
  367.0 1.1 copy-start.2
  368.1 1.0 copy-start.6
  369.2 0.9 copy-start.10
Sparse Core Ops, SparseCore 0:
  77.7 75.1 all-gather.2
  205.9 77.4 reduce-scatter.1

commit v4 on v3

--- a/solution.py
+++ b/solution.py
@@ -16,6 +16,7 @@
 LOWEST = -1e20
 QTILE = 512
 KTILE = 512
+TURNED = 2048
 AXES = ("head", "z", "y", "core")
 IDS = pl.DeviceIdType.MESH
 F32 = jnp.float32
@@ -142,7 +143,7 @@
         out_specs=out_specs,
         scratch_shapes=scratch,
         compiler_params=pltpu.CompilerParams(
-            collective_id=ident, has_side_effects=True, vmem_limit_bytes=56 << 20
+            collective_id=ident, has_side_effects=True, vmem_limit_bytes=60 << 20
         ),
         cost_estimate=pl.CostEstimate(flops=flops, bytes_accessed=sent, transcendentals=0),
     )(*args)
@@ -155,20 +156,23 @@
     q_w,
     k_w,
     v_w,
-    o_w,
     g_w,
     u_w,
     d_w,
+    o_w,
+    t2_ref,
     gain1,
     gain2,
     ng_ref,
     wg_ref,
     fg_ref,
-    og_ref,
     a_ref,
+    ca_ref,
+    cb_ref,
+    cc_ref,
+    wo_ref,
     w_ref,
     f_ref,
-    o_ref,
     e_ref,
     rows,
     weights,
@@ -180,16 +184,14 @@
     n1,
     f0,
     f1,
-    o0,
-    o1,
-    p0,
-    p1,
     z0,
     z1,
     b0,
     b1,
     s0,
     s1,
+    t0,
+    t1,
 ):
     me = Place(zc)
     chips = 4 * zc
@@ -206,15 +208,12 @@
             for half in range(2):
                 start = qw + (2 * pair + half) * PAIR
                 w_ref[g, :, start : start + PAIR] = pair_up(key, half, value, half).astype(BF16)
-    o_ref[...] = o_w[...].astype(BF16)
     e_ref[...] = d_w[...].astype(BF16).reshape(e_ref.shape)
+    wo_ref[...] = o_w[...].astype(BF16)
     x = t_ref[...].astype(F32)
     rows[0] = (x * lax.rsqrt(jnp.mean(x * x, axis=-1, keepdims=True) + EPS)).astype(BF16)
     meet([me.any_chip(k) for k in range(1, chips)] + [me.sibling()])
-    local = [
-        move(w_ref.at[me.g], weights.at[me.chip, me.c], ls, 0),
-        move(o_ref, og_ref.at[me.x, me.z, me.y, me.c], ls, 1),
-    ]
+    local = [move(w_ref.at[me.g], weights.at[me.chip, me.c], ls, 0)]
     pieces = []
     for k in reversed(range(1, chips)):
         there = me.any_chip(k)
@@ -222,10 +221,6 @@
         pieces.append(
             send(w_ref.at[their_g], weights.at[me.chip, me.c], (w0, w1), k, there)
         )
-    outs = [
-        send(o_ref, og_ref.at[me.x, me.z, me.y, me.c], (o0, o1), k, me.line(k))
-        for k in range(1, zc)
-    ]
     blocks = [send(rows.at[0], rows.at[k], (n0, n1), k, me.plane(k)) for k in range(1, 4)]
     units = g_w.shape[1] // (4 * zc)
     for which, ref in enumerate((g_w, u_w)):
@@ -249,6 +244,8 @@
         there = me.plane(k)
         their_g = there[0] * 2 + there[2]
         wide.append(send(f_ref.at[their_g], fg_ref.at[pl.ds(2 * me.g, 2)], (f0, f1), k, there))
+    for k, ref in ((3, cc_ref), (1, ca_ref), (2, cb_ref)):
+        wide.append(send(t2_ref, ref, (t0, t1), k, me.plane(k)))
     local[0].wait()
     for copy in pieces:
         copy.wait()
@@ -264,14 +261,12 @@
             trip(rows.at[0], rows.at[k], (n0, n1), k, me.plane(k)).wait_recv()
 
         at = (me.x ^ (k // 2)) * 2 + (me.y ^ (k % 2))
-        out = dot(rows[k], weights[...].reshape(width, 3 * qw)).astype(BF16)
+        out = dot(rows[k], weights[...].reshape(width, 3 * qw))
         for head in range(group):
-            left = selection(qw, PAIR, head * HEAD_DIM, 0, HEAD_DIM)
-            right = selection(qw, PAIR, head * HEAD_DIM - HEAD_DIM, HEAD_DIM, PAIR)
-            slab = dot(out[:BLOCK, :qw], left) + dot(out[BLOCK:, :qw], right)
-            packed[head, k, :BLOCK] = slab.astype(BF16)
+            two, half = out[:, lanes(head // 2)], head % 2
+            packed[head, k, :BLOCK] = pair_up(two[:BLOCK], half, two[BLOCK:], half).astype(BF16)
             start = qw + head * PAIR
-            packed[head, k, BLOCK:] = out[:, start : start + PAIR]
+            packed[head, k, BLOCK:] = out[:, start : start + PAIR].astype(BF16)
         for over in range(1, zc):
             trip(
                 packed.at[(me.z ^ over) // per, k],
@@ -290,10 +285,6 @@
 
     lax.fori_loop(0, 4, project, 0)
     kept.append(move(rows, ng_ref, ls, 8))
-    for copy in outs + local[1:2]:
-        copy.wait()
-    mine = og_ref.at[me.x, :, me.y, me.c]
-    out_rows = [send(mine, mine, (p0, p1), k, me.plane(k)) for k in range(1, 4)]
 
     def pass_on(step, carry):
         k, over = step // (zc - 1), step % (zc - 1) + 1
@@ -311,10 +302,6 @@
         return carry
 
     lax.fori_loop(0, 4 * (zc - 1), pass_on, 0)
-    for copy in out_rows:
-        copy.wait()
-    every = og_ref.at[:, :, :, me.c]
-    last = send(every, every, (s0, s1), 1, me.sibling())
 
     def finish(step, carry):
         k, over = step // zc, step % zc
@@ -328,13 +315,13 @@
         pltpu.make_async_copy(
             packed.at[me.z // per, k], a_ref.at[me.z, me.c, me.g], ls.at[4 + k]
         ).wait()
-    for copy in [last] + kept + wide:
+    for copy in kept + wide:
         copy.wait()
     for copy in blocks:
         copy.wait_send()
 
 
-def head_exchange(zc, group, tokens, matrices, gains):
+def head_exchange(zc, group, tokens, matrices, cotangent, gains):
     chips = 4 * zc
     own, width = tokens.shape
     count = matrices[0].shape[0]
@@ -346,15 +333,17 @@
             struct((4, own, width)),
             struct((chips, 2) + piece),
             struct((12, count, width)),
-            struct((2, zc, 2, 2, count, width)),
             struct((zc, 2, 4, BLOCK + own, PAIR)),
+            struct((own, width)),
+            struct((own, width)),
+            struct((own, width)),
+            struct((count, width)),
         ),
-        [VM] * 10,
-        (ANY,) * 5,
+        [VM] * 8 + [ANY] + [VM] * 2,
+        (ANY,) * 7 + (VM,),
         [
             pltpu.VMEM((4,) + piece, BF16),
             pltpu.VMEM((4, 2, count, width), BF16),
-            pltpu.VMEM((count, width), BF16),
             pltpu.VMEM((4, count, width), BF16),
             pltpu.VMEM((4, own, width), BF16),
             pltpu.VMEM((chips, 2) + piece, BF16),
@@ -364,22 +353,32 @@
         + both(chips)
         + both(4)
         + both(4)
-        + both(zc)
-        + both(4)
         + both(4 * zc)
         + both(4 * zc)
-        + both(2),
-        (tokens, *matrices, *(g.reshape(1, -1) for g in gains)),
+        + both(1)
+        + both(4),
+        (tokens, *matrices, cotangent, *(g.reshape(1, -1) for g in gains)),
         2 * 4 * own * width * width,
         16 << 20,
     )
 
 
-def join_kernel(zc, s_ref, x_ref, w_ref, ob_ref, r_ref, n_ref, mine, theirs, slabs, ls, b0, b1, c0, c1):
+def join_kernel(
+    zc,
+    s_ref,
+    x_ref,
+    *rest,
+):
+    w_refs, rest = rest[:zc], rest[zc:]
+    ob_ref, r_ref, n_ref, og_ref, mine, theirs, slabs, all_w, ls, b0, b1, c0, c1, p0, p1 = rest
     me = Place(zc)
     chips = 4 * zc
     heads, per = slabs.shape[:2]
+    for k, ref in enumerate(w_refs):
+        all_w[me.x, me.z ^ k, me.y, me.c] = ref[...]
     meet([me.any_chip(k) for k in range(1, chips)] + [me.sibling()])
+    column = all_w.at[me.x, :, me.y, me.c]
+    planes = [send(column, column, (p0, p1), k, me.plane(k)) for k in range(1, 4)]
     other = send(s_ref.at[:, 1 - me.c], theirs, (b0, b1), 0, me.sibling())
     own = move(s_ref.at[:, me.c], mine, ls, 0)
     own.wait()
@@ -395,49 +394,56 @@
         sends.append(
             send(mine.at[there[1], their_g], slabs.at[head, place], (c0, c1), k, there)
         )
+    for copy in planes:
+        copy.wait()
+    half = all_w.at[:, :, :, me.c]
+    relay = send(half, half, (p0, p1), 0, me.sibling())
     keep.wait()
     for copy in sends:
         copy.wait()
     for block in range(2):
         for pair in range(heads // 2):
-            total = jnp.zeros((BLOCK, PAIR), F32)
+            sides = []
             for side in range(2):
-                slab = slabs[2 * pair + side, 0]
+                slab = slabs[2 * pair + side, 0].astype(F32)
                 for extra in range(1, per):
-                    slab = slab + slabs[2 * pair + side, extra]
-                pick = selection(
-                    PAIR, PAIR, (block - side) * HEAD_DIM, side * HEAD_DIM, (side + 1) * HEAD_DIM
-                )
-                total = total + dot(slab, pick)
-            ob_ref[block * BLOCK : (block + 1) * BLOCK, pair * PAIR : (pair + 1) * PAIR] = (
-                total.astype(BF16)
-            )
-    residual = x_ref[...].astype(F32) + dot(ob_ref[...], w_ref[...])
+                    slab = slab + slabs[2 * pair + side, extra].astype(F32)
+                sides.append(slab)
+            ob_ref[block * BLOCK : (block + 1) * BLOCK, lanes(pair)] = pair_up(
+                sides[0], block, sides[1], block
+            ).astype(BF16)
+    relay.wait()
+    save = move(all_w, og_ref, ls, 2)
+    residual = x_ref[...].astype(F32) + dot(ob_ref[...], all_w[...].reshape(x_ref.shape[1], x_ref.shape[1]))
     r_ref[...] = residual
     mean = jnp.mean(residual * residual, axis=-1, keepdims=True)
     n_ref[...] = (residual * lax.rsqrt(mean + EPS)).astype(BF16)
-
-
-def join_exchange(zc, heads, slabs, tokens, w_out):
+    save.wait()
+
+
+def join_exchange(zc, heads, slabs, tokens, w_parts):
     chips = 4 * zc
     per = 4 * zc // heads
     half = (zc,) + slabs.shape[2:]
     shape = tokens.shape
+    whole = (2, zc, 2, 2) + w_parts[0].shape
     return exchange(
         functools.partial(join_kernel, zc),
         2,
-        (struct(shape), struct(shape, F32), struct(shape)),
-        [ANY, VM, VM],
-        (VM,) * 3,
+        (struct(shape), struct(shape, F32), struct(shape), struct(whole)),
+        [ANY, VM] + [VM] * zc,
+        (VM,) * 3 + (ANY,),
         [
             pltpu.VMEM(half, BF16),
             pltpu.VMEM(half, BF16),
             pltpu.VMEM((heads, per) + slabs.shape[3:], BF16),
-            DMA((2,)),
+            pltpu.VMEM(whole, BF16),
+            DMA((3,)),
         ]
         + both(1)
-        + both(chips),
-        (slabs, tokens, w_out),
+        + both(chips)
+        + both(4),
+        (slabs, tokens, *w_parts),
         2 * shape[0] * shape[1] * shape[1],
         4 << 20,
     )
@@ -451,7 +457,10 @@
     cc_ref,
     cd_ref,
     f_ref,
-    out_ref,
+    oa_ref,
+    ob_ref,
+    oc_ref,
+    od_ref,
     cs_ref,
     sh_ref,
     rows,
@@ -548,11 +557,8 @@
         move(stage.at[2].reshape(zc, 2, 4, piece, width), sh_ref.at[:, :, 8:], ls, 20)
     )
 
-    def finish_out(k, carry):
-        out_ref[k] = dot(hid[k], down_w[...].reshape(square)).astype(BF16)
-        return carry
-
-    lax.fori_loop(0, 4, finish_out, 0)
+    for k, ref in enumerate((oa_ref, ob_ref, oc_ref, od_ref)):
+        ref[...] = dot(hid[k], down_w[...].reshape(square)).astype(BF16)
     total = c_out[0].astype(F32)
     for k in range(1, 4):
         trip(c_out.at[k], c_in.at[k], (c0, c1), k, me.plane(k)).wait()
@@ -573,12 +579,12 @@
         functools.partial(middle_kernel, zc),
         3,
         (
-            struct((4, own, width)),
+            *[struct((own, width))] * 4,
             struct((own, width), F32),
             struct((zc, 2, 12, piece, width)),
         ),
         [VM] * 5 + [ANY],
-        (VM, VM, ANY),
+        (VM,) * 5 + (ANY,),
         [blocks, blocks, wide, wide, pltpu.VMEM((zc, 2, 4, piece, width), BF16)]
         + [blocks] * 5
         + [pltpu.VMEM((3, width, width), BF16), DMA((21,))]
@@ -597,21 +603,16 @@
     r_ref,
     wo_ref,
     ob_ref,
-    op_ref,
     dr_ref,
     do_ref,
     dw_ref,
-    out_ref,
     slabs,
     stage,
-    o_in,
     ls,
     d0,
     d1,
     b0,
     b1,
-    o0,
-    o1,
 ):
     me = Place(zc)
     chips = 4 * zc
@@ -620,8 +621,6 @@
     per = zc // group
     width = t_ref.shape[1]
     meet([me.any_chip(k) for k in range(1, chips)] + [me.sibling()])
-    outs = [send(op_ref.at[k], o_in.at[k], (o0, o1), k, me.plane(k)) for k in (3, 1, 2)]
-    outs.append(move(op_ref.at[0], o_in.at[0], ls, 5))
     total, residual = c_ref[...], r_ref[...]
     scaling = lax.rsqrt(jnp.mean(residual * residual, axis=-1, keepdims=True) + EPS)
     normed = residual * scaling
@@ -629,14 +628,11 @@
     grad = t_ref[...].astype(F32) + scaling * (total - normed * middle)
     dr_ref[...] = grad
     narrow = grad.astype(BF16)
-    back = nt_dot(narrow, wo_ref[...]).astype(BF16)
+    back = nt_dot(narrow, wo_ref[...])
     for pair in range(heads // 2):
-        two = back[:, pair * PAIR : (pair + 1) * PAIR]
+        two = back[:, lanes(pair)]
         for side in range(2):
-            left = selection(PAIR, PAIR, side * HEAD_DIM, 0, HEAD_DIM)
-            right = selection(PAIR, PAIR, (side - 1) * HEAD_DIM, HEAD_DIM, PAIR)
-            slab = dot(two[:BLOCK], left) + dot(two[BLOCK:], right)
-            slabs[2 * pair + side] = slab.astype(BF16)
+            slabs[2 * pair + side] = pair_up(two[:BLOCK], side, two[BLOCK:], side).astype(BF16)
     to = do_ref.at[me.z, me.c, me.g]
     own = move(slabs.at[me.g * group + me.z // per], to, ls, 0)
     sends = []
@@ -658,18 +654,12 @@
         copy.wait()
     half = do_ref.at[:, me.c]
     relay = send(half, half, (b0, b1), 0, me.sibling())
-    for copy in outs:
-        copy.wait()
-    final = residual
-    for k in range(4):
-        final = final + o_in[k].astype(F32)
-    out_ref[...] = final.astype(BF16)
     for copy in keeps:
         copy.wait()
     relay.wait()
 
 
-def turn_exchange(zc, c_sum, cotangent, residual, w_out, attn_rows, out_parts):
+def turn_exchange(zc, c_sum, cotangent, residual, w_out, attn_rows):
     chips = 4 * zc
     own, width = cotangent.shape
     heads = width // HEAD_DIM
@@ -680,20 +670,17 @@
             struct((own, width), F32),
             struct((zc, 2, 4, BLOCK, PAIR)),
             struct((4, zc, 2, width // (8 * zc), width)),
-            struct((own, width)),
         ),
-        [VM] * 5 + [ANY],
-        (VM, ANY, ANY, VM),
+        [VM] * 5,
+        (VM, ANY, ANY),
         [
             pltpu.VMEM((heads, BLOCK, PAIR), BF16),
             pltpu.VMEM((width, width), BF16),
-            pltpu.VMEM((4, own, width), BF16),
-            DMA((6,)),
+            DMA((5,)),
         ]
         + both(chips)
-        + both(1)
-        + both(4),
-        (c_sum, cotangent, residual, w_out, attn_rows, out_parts),
+        + both(1),
+        (c_sum, cotangent, residual, w_out, attn_rows),
         2 * 2 * own * width * width,
         8 << 20,
     )
@@ -707,9 +694,19 @@
     x_ref,
     g_ref,
     v_ref,
+    f_ref,
+    r_ref,
+    ya_ref,
+    yb_ref,
+    yc_ref,
+    yd_ref,
     tg_ref,
     gw_ref,
     go_ref,
+    gf_ref,
+    out_ref,
+    r_in,
+    y_in,
     o_in,
     o_mine,
     o_theirs,
@@ -737,6 +734,8 @@
     q1,
     v0,
     v1,
+    f0,
+    f1,
 ):
     me = Place(zc)
     chips = 4 * zc
@@ -760,6 +759,14 @@
     o_parts = [move(v_ref.at[0], o_in.at[0], ls, 9)]
     for k in (3, 1, 2):
         o_parts.append(send(v_ref.at[k], o_in.at[k], (v0, v1), k, me.plane(k)))
+    f_parts = [move(f_ref.at[pl.ds(2 * me.g, 2)], gf_ref.at[me.g], ls, 10)]
+    for k in (3, 1, 2):
+        there = me.plane(k)
+        part = f_ref.at[pl.ds(2 * (there[0] * 2 + there[2]), 2)]
+        f_parts.append(send(part, gf_ref.at[me.g], (f0, f1), k, there))
+    out_parts = [move(r_ref, r_in, ls, 11)]
+    for i, ref in enumerate((ya_ref, yb_ref, yc_ref, yd_ref)):
+        out_parts.append(move(ref, y_in.at[i], ls, 12 + i))
     for k, (far, near) in zip(order, halves):
         near.wait()
         far.wait()
@@ -774,6 +781,13 @@
             )
         move(mine.at[k, me.z], landed.at[head, place, k], ls, 4 + k)
 
+    for copy in out_parts:
+        copy.wait()
+    final = r_in[...]
+    for i in range(4):
+        final = final + y_in[i].astype(F32)
+    out_ref[...] = final.astype(BF16)
+
     def block(step, carry):
         k = 3 - step
         pltpu.make_async_copy(
@@ -787,23 +801,24 @@
                 k * zc + over,
                 me.line(over),
             ).wait()
-        upper = jnp.zeros((BLOCK, qw), F32)
-        lower = jnp.zeros((BLOCK, qw), F32)
-        for h in range(group):
-            slab = landed[h, 0, k]
-            for extra in range(1, per):
-                slab = slab + landed[h, extra, k]
-            first, last = h * HEAD_DIM, (h + 1) * HEAD_DIM
-            upper = upper + dot(slab[:BLOCK], selection(PAIR, qw, -first, first, last))
-            lower = lower + dot(slab[:BLOCK], selection(PAIR, qw, HEAD_DIM - first, first, last))
-            start = qw + h * PAIR
-            grads[k, :, start : start + PAIR] = slab[BLOCK:]
-        grads[k, :BLOCK, :qw] = upper.astype(BF16)
-        grads[k, BLOCK:, :qw] = lower.astype(BF16)
-        c_out[k] = nt_dot(grads[k], w_ref[...]).astype(BF16)
+        for pair in range(group // 2):
+            sides = []
+            for side in range(2):
+                h = 2 * pair + side
+                slab = landed[h, 0, k]
+                for extra in range(1, per):
+                    slab = slab + landed[h, extra, k]
+                start = qw + h * PAIR
+                grads[k, :, start : start + PAIR] = slab[BLOCK:]
+                sides.append(slab[:BLOCK].astype(F32))
+            for b in range(2):
+                grads[k, b * BLOCK : (b + 1) * BLOCK, lanes(pair)] = pair_up(
+                    sides[0], b, sides[1], b
+                ).astype(BF16)
 
         @pl.when(k > 0)
         def _():
+            c_out[k] = nt_dot(grads[k], w_ref[...]).astype(BF16)
             trip(c_out.at[k], c_in.at[k], (c0, c1), k, me.plane(k)).start()
 
         return carry
@@ -823,17 +838,28 @@
     piece = stage.shape[2]
     chunk = 256
     each = chunk // (2 * piece)
+    swaps = []
     for first in range(0, width, chunk):
         value = tn_dot(normed_all[:, first : first + chunk], grads_all).astype(BF16)
         at = first // (2 * piece)
         stage[at : at + each] = value.reshape(each, 2, piece, cols)
-    swap = send(stage.at[:, 1 - me.c], other_w, (s0, s1), 0, me.sibling())
+        swaps.append(
+            send(
+                stage.at[at : at + each, 1 - me.c],
+                other_w.at[at : at + each],
+                (s0, s1),
+                2 + first // chunk,
+                me.sibling(),
+            )
+        )
     o_swap.wait()
     o_theirs[...] = o_theirs[...] + o_mine[:, me.c]
     sends = [
         send(o_theirs.at[me.z ^ k], o_land.at[k], (q0, q1), k, me.line(k)) for k in range(1, zc)
     ]
-    swap.wait()
+    c_out[0] = nt_dot(grads[0], w_ref[...]).astype(BF16)
+    for swap in swaps:
+        swap.wait()
 
     def add(i, carry):
         other_w[i] = stage[i, me.c] + other_w[i]
@@ -855,7 +881,7 @@
     middle = jnp.mean(total * normed, axis=-1, keepdims=True)
     tg_ref[...] = (g_ref[...] + scaling * (total - normed * middle)).astype(BF16)
     stay.wait()
-    for copy in sends:
+    for copy in sends + f_parts:
         copy.wait()
     o_sum = o_theirs[me.z].astype(F32)
     for k in range(1, zc):
@@ -863,7 +889,7 @@
     go_ref[...] = o_sum
 
 
-def tail_exchange(zc, group, slab_grads, n_all, weights, tokens, residual_grad, out_grads):
+def tail_exchange(zc, group, slab_grads, n_all, weights, tokens, residual_grad, out_grads, shares, residual, outs):
     chips = 4 * zc
     per = zc // group
     own, width = tokens.shape
@@ -874,10 +900,18 @@
     return exchange(
         functools.partial(tail_kernel, zc),
         4,
-        (struct((own, width)), struct((zc, 4, piece, cols)), struct((piece, width), F32)),
-        [ANY] + [VM] * 4 + [ANY],
-        (VM, ANY, VM),
+        (
+            struct((own, width)),
+            struct((zc, 4, piece, cols)),
+            struct((piece, width), F32),
+            struct((4, 2, piece, width)),
+            struct((own, width)),
+        ),
+        [ANY] + [VM] * 4 + [ANY] * 7,
+        (VM, ANY, VM, ANY, VM),
         [
+            pltpu.VMEM((own, width), F32),
+            pltpu.VMEM((4, own, width), BF16),
             pltpu.VMEM((4, zc, 2, piece, width), BF16),
             pltpu.VMEM((zc, 2, piece, width), BF16),
             pltpu.VMEM((zc, piece, width), BF16),
@@ -890,62 +924,36 @@
             blocks,
             pltpu.VMEM((chips, 2, piece, cols), BF16),
             pltpu.VMEM((chips, piece, cols), BF16),
-            DMA((10,)),
+            DMA((16,)),
         ]
         + both(4)
         + both(4 * zc)
         + both(4)
-        + both(2)
+        + both(2 + width // 256)
         + both(chips)
         + both(zc)
+        + both(4)
         + both(4),
-        (slab_grads, n_all, weights, tokens, residual_grad, out_grads),
+        (slab_grads, n_all, weights, tokens, residual_grad, out_grads, shares, residual, *outs),
         2 * 4 * own * width * cols * 2,
         24 << 20,
-    )
-
-
-def share_kernel(zc, f_ref, gf_ref, ls, f0, f1):
-    me = Place(zc)
-    meet([me.plane(k) for k in range(1, 4)])
-    copies = []
-    for k in (3, 1, 2):
-        there = me.plane(k)
-        part = f_ref.at[pl.ds(2 * (there[0] * 2 + there[2]), 2)]
-        copies.append(send(part, gf_ref.at[me.g], (f0, f1), k, there))
-    copies.append(move(f_ref.at[pl.ds(2 * me.g, 2)], gf_ref.at[me.g], ls, 0))
-    for copy in copies:
-        copy.wait()
-
-
-def share_exchange(zc, shares):
-    return exchange(
-        functools.partial(share_kernel, zc),
-        5,
-        struct((4, 2) + shares.shape[1:]),
-        [ANY],
-        ANY,
-        [DMA((1,))] + both(4),
-        (shares,),
-        0,
-        2 << 20,
     )
 
 
 def last_kernel(
     zc,
     group,
-    t_ref,
-    o_ref,
-    wo_ref,
-    gw_ref,
-    gf_ref,
-    ds_ref,
-    q_w,
-    k_w,
-    v_w,
-    g_w,
-    u_w,
+    t_any,
+    o_any,
+    wo_any,
+    gw_any,
+    gf_any,
+    ds_any,
+    q_any,
+    k_any,
+    v_any,
+    g_any,
+    u_any,
     gain1,
     gain2,
     tg_ref,
@@ -959,10 +967,21 @@
     g_ref,
     u_ref,
     d_ref,
+    gw_ref,
+    gf_ref,
+    ds_ref,
+    q_w,
+    k_w,
+    v_w,
+    g_w,
+    u_w,
+    ls,
 ):
-    tg_ref[...] = t_ref[...]
-    out_ref[...] = o_ref[...]
-    go_ref[...] = wo_ref[...]
+    given = (gw_any, q_any, k_any, v_any, gf_any, g_any, u_any, ds_any, t_any, o_any, wo_any)
+    taken = (gw_ref, q_w, k_w, v_w, gf_ref, g_w, u_w, ds_ref, tg_ref, out_ref, go_ref)
+    copies = [move(a, b, ls, i) for i, (a, b) in enumerate(zip(given, taken))]
+    for copy in copies:
+        copy.wait()
     d_ref[...] = ds_ref[8:].astype(F32).reshape(d_ref.shape)
     first_gain, second_gain = column_of(low(gain1[...])), column_of(low(gain2[...]))
     count = q_w.shape[0]
@@ -1019,9 +1038,13 @@
             struct((count, hidden), F32),
             struct((4 * count, width), F32),
         ),
-        in_specs=[VM] * 13,
+        in_specs=[ANY] * 11 + [VM] * 2,
         out_specs=(VM,) * 11,
-        compiler_params=pltpu.CompilerParams(vmem_limit_bytes=32 << 20),
+        scratch_shapes=[
+            pltpu.VMEM(v.shape, v.dtype) for v in (w_all, f_all, shares, *matrices)
+        ]
+        + [DMA((11,))],
+        compiler_params=pltpu.CompilerParams(vmem_limit_bytes=60 << 20),
     )(
         tokens_grad,
         output,
@@ -1114,7 +1137,7 @@
     workers, anchor_ref, lens_ref, who_ref, a_ref, o_ref, kv_ref, kvt_ref, q_ref, qt_ref, ot_ref, l_ref, inv, mine, raw
 ):
     blocks = anchor_ref.shape[0]
-    turns = q_ref.shape[0]
+    turns = qt_ref.shape[0]
     per = QTILE // BLOCK
     worker = who_ref[0]
     note_places(anchor_ref, inv)
@@ -1129,11 +1152,16 @@
             slab, half = where >> 1, where & 1
             at = pl.ds(pl.multiple_of(i * BLOCK, BLOCK), BLOCK)
             kv_ref[at, :] = a_ref[slab, pl.ds(pl.multiple_of(BLOCK + half * BLOCK, BLOCK), BLOCK), :]
-        at = pl.ds(pl.multiple_of(step * QTILE, QTILE), QTILE)
+        return carry
+
+    lax.fori_loop(0, blocks // per, order, 0)
+
+    def flip(step, carry):
+        at = pl.ds(pl.multiple_of(step * TURNED, TURNED), TURNED)
         kvt_ref[:, at] = nt_dot(same, kv_ref[at, :]).astype(BF16)
         return carry
 
-    lax.fori_loop(0, blocks // per, order, 0)
+    lax.fori_loop(0, blocks * BLOCK // TURNED, flip, 0)
 
     def one_tile(turn, carry):
         tile = mine[turn]
@@ -1226,12 +1254,12 @@
     inv,
     mine,
     raw,
-    dn,
+    both_rows,
     dt,
     acc,
 ):
     blocks = anchor_ref.shape[0]
-    turns = q_ref.shape[0]
+    turns = qt_ref.shape[0]
     per = QTILE // BLOCK
     worker = who_ref[0]
     note_places(anchor_ref, inv)
@@ -1245,10 +1273,10 @@
         for b in range(per):
             where = inv[tile * per + b]
             raw[b * BLOCK : (b + 1) * BLOCK, :] = half_lanes(d_ref[where >> 1], where & 1)
-        dn[...] = dot(raw[...], fold(PAIR, PAIR, HEAD_DIM)).astype(BF16)
+        both_rows[:QTILE] = q_ref[turn]
+        both_rows[QTILE:] = dot(raw[...], fold(PAIR, PAIR, HEAD_DIM)).astype(BF16)
         dt[...] = nt_dot(unfold(PAIR, PAIR, HEAD_DIM), raw[...]).astype(BF16)
-        query, query_rows = qt_ref[turn], q_ref[turn]
-        grad, grad_rows = dt[...], dn[...]
+        query, grad = qt_ref[turn], dt[...]
         norm = l_ref[turn]
         delta = jnp.sum(grad[HEAD_DIM:].astype(F32) * ot_ref[turn], axis=0, keepdims=True)
         starts = segment_start(first + lax.broadcasted_iota(jnp.int32, (1, QTILE), 1), lens_ref)
@@ -1262,7 +1290,8 @@
                 scores = jnp.where(visible(first, kt, starts), scores, MASKED)
             weights = jnp.exp(scores - norm)
             score_grad = (weights * (dot(keys, grad) - delta)).astype(BF16)
-            acc[at, :] += dot(score_grad, query_rows) + dot(weights.astype(BF16), grad_rows)
+            both_grads = jnp.concatenate([score_grad, weights.astype(BF16)], axis=1)
+            acc[at, :] += dot(both_grads, both_rows[...])
             return total + dot(kvt_ref[:HEAD_DIM, at], score_grad)
 
         total = jnp.zeros((HEAD_DIM, QTILE), F32)
@@ -1305,7 +1334,7 @@
             pltpu.SMEM((2 * slabs,), jnp.int32),
             pltpu.SMEM((rows // QTILE // workers,), jnp.int32),
             pltpu.VMEM((QTILE, PAIR), BF16),
-            pltpu.VMEM((QTILE, PAIR), BF16),
+            pltpu.VMEM((2 * QTILE, PAIR), BF16),
             pltpu.VMEM((PAIR, QTILE), BF16),
             pltpu.VMEM((rows, PAIR), F32),
         ],
@@ -1318,6 +1347,10 @@
 
 def around(value, k):
     return lax.ppermute(value, ("head", "y"), [(i, i ^ k) for i in range(4)])
+
+
+def along(value, k):
+    return lax.ppermute(value, "z", [(i, i ^ k) for i in range(lax.axis_size("z"))])
 
 
 def body(
@@ -1343,21 +1376,21 @@
     workers = 2 * per_head
     feature_rows = w_query.shape[0]
 
-    n1_all, qkv_w, ffn_in, out_all, by_head = head_exchange(
+    n1_all, qkv_w, ffn_in, by_head, *near, w_o = head_exchange(
         zc,
         group,
         tokens,
-        (w_query, w_key, w_value, w_out, w_gate, w_up, w_down),
+        (w_query, w_key, w_value, w_gate, w_up, w_down, w_out),
+        cotangent,
         (norm1_gain, norm2_gain),
     )
+    cots = [cotangent] + near
+    w_parts = [w_o] + [along(w_o, k) for k in range(1, zc)]
     qkv_w = qkv_w.reshape(width, 3 * group * HEAD_DIM)
-    out_mat = out_all.reshape(width, width)
 
     ffn_all = lax.all_gather(ffn_in, ("z", "core"), axis=0, tiled=False).reshape(
         zc, 2, 12, feature_rows, width
     )
-    by_head, near = lax.optimization_barrier((by_head, cotangent))
-    cots = [cotangent] + [around(near, k) for k in range(1, 4)]
 
     anchors = jnp.transpose(block_anchor.reshape(2, zc, 2, 2, 2), (1, 3, 0, 2, 4)).reshape(-1)
     who = ((lax.axis_index("z") % per_head) * 2 + lax.axis_index("core")).astype(jnp.int32).reshape(1)
@@ -1365,20 +1398,23 @@
     o_slabs, *kept = attention_forward(
         workers, anchors, seq_lengths, who, by_head.reshape((slab_count,) + by_head.shape[3:])
     )
-    attn_rows, residual, normed_two = join_exchange(
-        zc, heads, o_slabs.reshape(zc, 2, 4, BLOCK, PAIR), tokens, out_mat
-    )
-    out_parts, c_sum, shares = middle_exchange(zc, normed_two, cots, ffn_all)
+    attn_rows, residual, normed_two, out_mat = join_exchange(
+        zc, heads, o_slabs.reshape(zc, 2, 4, BLOCK, PAIR), tokens, w_parts
+    )
+    out_mat = out_mat.reshape(width, width)
+    *out_parts, c_sum, shares = middle_exchange(zc, normed_two, cots, ffn_all)
     shares = lax.psum_scatter(
         shares.reshape(zc * 2 * 12, feature_rows, width), ("z", "core"), scatter_dimension=0, tiled=True
     )
-    residual_grad, do_heads, out_grads, output = turn_exchange(
-        zc, c_sum, cotangent, residual, out_mat, attn_rows, out_parts
-    )
+    residual_grad, do_heads, out_grads = turn_exchange(
+        zc, c_sum, cotangent, residual, out_mat, attn_rows
+    )
+    do_heads, *out_parts = lax.optimization_barrier((do_heads, *out_parts))
+    outs = [out_parts[0]] + [around(out_parts[k], k) for k in range(1, 4)]
     grad_heads = attention_backward(
         workers, anchors, seq_lengths, who, do_heads.reshape(slab_count, BLOCK, PAIR), kept
     )
-    tokens_grad, w_all, out_share = tail_exchange(
+    tokens_grad, w_all, out_share, f_all, output = tail_exchange(
         zc,
         group,
         grad_heads.reshape(zc, 2, 4, 3 * BLOCK, PAIR),
@@ -1387,8 +1423,10 @@
         tokens,
         residual_grad,
         out_grads,
-    )
-    shares, w_all = lax.optimization_barrier((shares, w_all))
+        shares,
+        residual,
+        outs,
+    )
     (
         tokens_grad,
         output,
@@ -1408,7 +1446,7 @@
         output,
         out_share,
         w_all,
-        share_exchange(zc, shares),
+        f_all,
         shares,
         (w_query, w_key, w_value, w_gate, w_up),
         (norm1_gain, norm2_gain),

time: 380 us -> 367 us (0.966)
  Pallas kernels: 354 us -> 335 us
  waiting for transfers between devices: 1.36 us -> 7.56 us
  local copies, waits for them, and re-layouts: 6.06 us -> 1.41 us
  starting transfers between devices: 3.65 us -> 8.1 us
    pallas_call x6 -> x5, Pallas kernels: 279 us -> 265 us  [exchange(): pl.pallas_call(kernel, out_shape=out_shape, in_specs=in_specs, out_specs=...]
    reduce_scatter x1, waiting for transfers between devices: 0.02 us -> 6.87 us  [body(): lax.psum_scatter(shares.reshape(zc * 2 * 12, feature_rows, width), ('z',...]
    unnamed x36 -> x20, local copies, waits for them, and re-layouts: 5.32 us -> 0.66 us
    ppermute x0 -> x3, starting transfers between devices: none -> 4.45 us  [along(): lax.ppermute(value, 'z', [(i, i ^ k) for i in range(lax.axis_size('z'))])]
  transfers between devices with their start and end apart: 5 -> 8, of which waited for: 1 -> 2; matrix products, arithmetic and copies ran while one was open for 0% -> 0% of each run, Pallas kernels for 58% -> 36%
where the time goes in v4:
time: 367 us; the launch traced here: 366 us
  Pallas kernels  335 us (91%)
  between operations  14.2 us (4%)
  starting transfers between devices  8.1 us (2%)
  waiting for transfers between devices  7.56 us (2%)
    pallas_call x5, Pallas kernels, exchange(): pl.pallas_call(kernel, out_shape=out_shape, in_specs=in_specs, out_specs=...  265 us
    pallas_call x1, Pallas kernels, attention_backward(): pl.pallas_call(functools.partial(backward_kernel, workers), out_shape=str...  34 us
    pallas_call x1, Pallas kernels, attention_forward(): pl.pallas_call(functools.partial(forward_kernel, workers), out_shape=(str...  30.9 us
  transfers between devices with their start and end apart: 8, of which 2 were waited for; matrix products, arithmetic and copies ran while one was open for 0% of the time, Pallas kernels for 36%

profile of v4, /device:TPU:0, one launch (start us, length us, event | category | flops | bytes accessed | tf_op | source)
XLA Modules:
  0.0 366.3 jit_solution(10102596005577727583)
XLA Ops:
  7.2 0.0 all-gather.3.cloned.1.call-start
  7.2 0.0 copy-start.3
  7.2 71.0 %shard_map.212 = (bf16[4,256,1024]{2,1,0:T(8,128)(2,1)}, bf16[16,2,32,768]{3,2,1,0:T(8,128)(2,1)}, bf16[12,32,1024]{2,1,0:T(8,128)(2,1)}, bf16[4,2,4,384,128]{4,...) custom-call(bf16[256,1024]{1,0:T(8,128)(2,1)} %x_ref.3, ...), custom_call_target="tpu_custom_call" | custom-call | flops 2147483648 | bytes 16777216 | tf_op jit(solution)/shard_map/pallas_call | solution.py:139
  78.3 0.0 all-gather.3.cloned.1.call-update
  78.3 0.0 reduce-scatter.2.cloned.1.call-start
  78.3 0.6 collective-permute-start.2
  79.0 1.6 collective-permute-start.1
  80.5 2.3 collective-permute-start
  82.8 0.0 copy-done.3
  82.8 0.1 reshape.69
  82.9 0.6 reshape.70.anchor_ref
  83.6 30.9 %shard_map.213 = (bf16[32,128,128]{2,1,0:T(8,128)(2,1)}, bf16[8192,128]{1,0:T(8,128)(2,1)}, bf16[128,8192]{1,0:T(8,128)(2,1)}, bf16[8,512,128]{2,1,0:T(8,128)(2,...) custom-call(s32[64]{0:T(128)} %reshape.70.anchor_ref, s32[8]{0:T(128)} %lens_ref.3, ...), custom_call_target="tpu_custom_call" | custom-call | flops 4294967296 | bytes 8388608 | tf_op jit(solution)/shard_map/pallas_call | solution.py:1216
  114.4 0.0 collective-permute-done.2.rest_3_
  114.4 0.0 copy-start.7
  114.4 0.0 collective-permute-done.1.rest_2_
  114.4 0.0 copy-start.8
  114.4 0.0 collective-permute-done.rest_1_
  114.5 0.0 copy-start.9
  114.5 0.6 copy-done.7
  115.0 0.0 copy-done.8
  115.1 0.0 copy-done.9
  115.1 35.9 %shard_map.214 = (bf16[256,1024]{1,0:T(8,128)(2,1)}, f32[256,1024]{1,0:T(8,128)}, bf16[256,1024]{1,0:T(8,128)(2,1)}, bf16[2,4,2,2,32,1024]{5,4,3,2,1,0:T(8,128)(2,1)}) custom-call(bf16[4,2,4,128,128]{4,3,2,1,0:T(8,128)(2,1)} %bitcast.28, bf16[256,1024]{1,0:T(8,128)(2,1)} %x_ref.3, bf16[32,1024]{1,0:T(8,128)(2,1)} %get-tuple-element.62.rest_0_, ...), custom_call_target="tpu_custom_call" | custom-call | flops 536870912 | bytes 4194304 | tf_op jit(solution)/shard_map/pallas_call | solution.py:139
  151.0 0.6 all-gather.3.cloned.1.call-done
  151.7 52.8 %shard_map.215 = (bf16[256,1024]{1,0:T(8,128)(2,1)}, bf16[256,1024]{1,0:T(8,128)(2,1)}, bf16[256,1024]{1,0:T(8,128)(2,1)}, bf16[256,1024]{1,0:T(8,128)(2,1)}, f3...) custom-call(bf16[256,1024]{1,0:T(8,128)(2,1)} %get-tuple-element.63.n_ref, bf16[256,1024]{1,0:T(8,128)(2,1)} %t_ref.3, ...), custom_call_target="tpu_custom_call" | custom-call | flops 19327352832 | bytes 67108864 | tf_op jit(solution)/shard_map/pallas_call | solution.py:139
  204.5 0.0 reduce-scatter.2.cloned.1.call-update
  204.5 0.0 copy-start.6
  204.5 0.0 copy-start.5
  204.5 0.0 copy-start.4
  204.5 32.4 %shard_map.216 = (f32[256,1024]{1,0:T(8,128)}, bf16[4,2,4,128,128]{4,3,2,1,0:T(8,128)(2,1)}, bf16[4,4,2,32,1024]{4,3,2,1,0:T(8,128)(2,1)}) custom-call(f32[256,1024]{1,0:T(8,128)} %get-tuple-element.68.c_ref, bf16[256,1024]{1,0:T(8,128)(2,1)} %t_ref.3, f32[256,1024]{1,0:T(8,128)} %get-tuple-element.69.r_ref, bf16[1024,1024]{1,0:T(8,128)(2,1)} %bitcast.16, ...), custom_call_target="tpu_custom_call" | custom-call | flops 1073741824 | bytes 8388608 | tf_op jit(solution)/shard_map/pallas_call | solution.py:139
  237.0 0.0 copy-done.6
  237.0 0.3 collective-permute-start.3
  237.3 0.0 copy-done.5
  237.3 0.1 collective-permute-start.4
  237.4 0.0 copy-done.4
  237.4 3.1 collective-permute-start.5
  240.6 34.0 %shard_map.217 = bf16[32,384,128]{2,1,0:T(8,128)(2,1)} custom-call(s32[64]{0:T(128)} %reshape.70.anchor_ref, s32[8]{0:T(128)} %lens_ref.3, s32[1]{0:T(128)} %bitcast.1.who_ref, bf16[32,128,128]{2,1,0:T(8,128)(2,1)} %bitcast.24, bf16[8192,128]{1,0:T(8,128)(2,1)} %get-tuple-element.78.kv_ref, bf16[128,8192]{1,0:T(8,128)(2,1)} %get-tuple-element.79.kvt_ref, ...), custom_call_target="tpu_custom_call" | custom-call | flops 10737418240 | bytes 8388608 | tf_op jit(solution)/shard_map/pallas_call | solution.py:1328
  274.5 0.0 collective-permute-done.3.yb_ref
  274.5 0.0 copy-start
  274.5 0.0 collective-permute-done.4.yc_ref
  274.5 0.0 copy-start.1
  274.6 0.0 collective-permute-done.5.yd_ref
  274.6 0.0 copy-start.2
  274.6 6.9 %reduce-scatter.2.cloned.1.call-done.f_ref.ds_any = bf16[12,32,1024]{2,1,0:T(8,128)(2,1)} async-done(((bf16[96,32,1024]{2,1,0:T(8,128)(2,1)}), bf16[12,32,1024]{2,1,0:T(8,128)(2,1)}) %reduce-scatter.2.cloned.1.call-update) | async-done | bytes 786448 | tf_op jit(solution)/shard_map/reduce_scatter | solution.py:1406
  281.4 0.0 copy-done
  281.4 0.0 copy-done.1
  281.4 0.0 copy-done.2
  281.5 73.2 %shard_map.218 = (bf16[256,1024]{1,0:T(8,128)(2,1)}, bf16[4,4,32,768]{3,2,1,0:T(8,128)(2,1)}, f32[32,1024]{1,0:T(8,128)}, bf16[4,2,32,1024]{3,2,1,0:T(8,128)(2,1)}, bf16[256,1024]{1,0:T(8,128)(2,1)}) custom-call(bf16[4,2,4,384,128]{4,3,2,1,0:T(8,128)(2,1)} %bitcast.15, bf16[4,256,1024]{2,1,0:T(8,128)(2,1)} %get-tuple-element.84.n_ref, ...), custom_call_target="tpu_custom_call" | custom-call | flops 3221225472 | bytes 25165824 | tf_op jit(solution)/shard_map/pallas_call | solution.py:139
  354.7 4.8 %shard_map.219 = (bf16[256,1024]{1,0:T(8,128)(2,1)}, bf16[256,1024]{1,0:T(8,128)(2,1)}, f32[32,1024]{1,0:T(8,128)}, f32[1,32]{1,0:T(1,128)}, f32[32,1024]{1,0:T(...) custom-call(bf16[256,1024]{1,0:T(8,128)(2,1)} %get-tuple-element.93., ...), custom_call_target="tpu_custom_call" | custom-call | tf_op jit(solution)/shard_map/pallas_call | solution.py:1026
  (1 shorter events, 0.0 us)
Async XLA Ops:
  7.2 144.5 %all-gather.3.cloned.1.call-start = ((), (), s32[]{:S(2)}) async-start(), calls=%async_computation.2 | async-start | bytes 7077888 | tf_op jit(solution)/shard_map/all_gather | solution.py:1391
  7.2 75.6 %copy-start.3 = (s32[64]{0:T(128)S(1)}, s32[64]{0:T(128)}, u32[]{:S(2)}) copy-start(s32[64]{0:T(128)} %param.24) | copy-start | bytes 772
  78.3 203.2 %reduce-scatter.2.cloned.1.call-start = ((), (), s32[]{:S(2)}) async-start(), calls=%async_computation.1 | async-start | bytes 7077888 | tf_op jit(solution)/shard_map/reduce_scatter | solution.py:1406
  78.3 36.1 %collective-permute-start.2 = (bf16[32,1024]{1,0:T(8,128)(2,1)}, bf16[32,1024]{1,0:T(8,128)(2,1)S(1)}, u32[]{:S(2)}, u32[]{:S(2)}) collective-permute-start(bf16[32,1024]{1,0:T(8,128)(2,1)} %get-tuple-element.62.rest_0_), channel_id=1, source_target_pairs={{0,12},{4,8},{8,4},{12,0},{1,13},{5,9},{9,5},{13,1},{2,14},{6,10},... | collective-permute-start | bytes 196616 | tf_op jit(solution)/shard_map/ppermute | solution.py:1353
  79.0 35.5 %collective-permute-start.1 = (bf16[32,1024]{1,0:T(8,128)(2,1)}, bf16[32,1024]{1,0:T(8,128)(2,1)S(1)}, u32[]{:S(2)}, u32[]{:S(2)}) collective-permute-start(bf16[32,1024]{1,0:T(8,128)(2,1)} %get-tuple-element.62.rest_0_), channel_id=1, source_target_pairs={{0,8},{4,12},{8,0},{12,4},{1,9},{5,13},{9,1},{13,5},{2,10},{6,14},... | collective-permute-start | bytes 196616 | tf_op jit(solution)/shard_map/ppermute | solution.py:1353
  80.5 33.9 %collective-permute-start = (bf16[32,1024]{1,0:T(8,128)(2,1)}, bf16[32,1024]{1,0:T(8,128)(2,1)S(1)}, u32[]{:S(2)}, u32[]{:S(2)}) collective-permute-start(bf16[32,1024]{1,0:T(8,128)(2,1)} %get-tuple-element.62.rest_0_), channel_id=1, source_target_pairs={{0,4},{4,0},{8,12},{12,8},{1,5},{5,1},{9,13},{13,9},{2,6},{6,2},{1... | collective-permute-start | bytes 196616 | tf_op jit(solution)/shard_map/ppermute | solution.py:1353
  114.4 0.6 copy-start.7
  114.4 0.6 copy-start.8
  114.5 0.6 copy-start.9
  204.5 32.5 %copy-start.6 = (bf16[256,1024]{1,0:T(8,128)(2,1)S(1)}, bf16[256,1024]{1,0:T(8,128)(2,1)}, u32[]{:S(2)}) copy-start(bf16[256,1024]{1,0:T(8,128)(2,1)} %get-tuple-element.90) | copy-start | bytes 1572868
  204.5 32.8 %copy-start.5 = (bf16[256,1024]{1,0:T(8,128)(2,1)S(1)}, bf16[256,1024]{1,0:T(8,128)(2,1)}, u32[]{:S(2)}) copy-start(bf16[256,1024]{1,0:T(8,128)(2,1)} %get-tuple-element.91) | copy-start | bytes 1572868
  204.5 32.9 %copy-start.4 = (bf16[256,1024]{1,0:T(8,128)(2,1)S(1)}, bf16[256,1024]{1,0:T(8,128)(2,1)}, u32[]{:S(2)}) copy-start(bf16[256,1024]{1,0:T(8,128)(2,1)} %get-tuple-element.92) | copy-start | bytes 1572868
  237.0 37.5 %collective-permute-start.3 = (bf16[256,1024]{1,0:T(8,128)(2,1)S(1)}, bf16[256,1024]{1,0:T(8,128)(2,1)S(1)}, u32[]{:S(2)}, u32[]{:S(2)}) collective-permute-start(bf16[256,1024]{1,0:T(8,128)(2,1)S(1)} %copy-done.6), channel_id=1, source_target_pairs={{0,2},{2,0},{16,18},{18,16},{1,3},{3,1},{17,19},{19,17},{4,6},{6,4... | collective-permute-start | bytes 1572872 | tf_op jit(solution)/shard_map/ppermute | solution.py:1349
  237.3 37.2 %collective-permute-start.4 = (bf16[256,1024]{1,0:T(8,128)(2,1)S(1)}, bf16[256,1024]{1,0:T(8,128)(2,1)S(1)}, u32[]{:S(2)}, u32[]{:S(2)}) collective-permute-start(bf16[256,1024]{1,0:T(8,128)(2,1)S(1)} %copy-done.5), channel_id=1, source_target_pairs={{0,16},{2,18},{16,0},{18,2},{1,17},{3,19},{17,1},{19,3},{4,20},{6,... | collective-permute-start | bytes 1572872 | tf_op jit(solution)/shard_map/ppermute | solution.py:1349
  237.4 37.1 %collective-permute-start.5 = (bf16[256,1024]{1,0:T(8,128)(2,1)S(1)}, bf16[256,1024]{1,0:T(8,128)(2,1)S(1)}, u32[]{:S(2)}, u32[]{:S(2)}) collective-permute-start(bf16[256,1024]{1,0:T(8,128)(2,1)S(1)} %copy-done.4), channel_id=1, source_target_pairs={{0,18},{2,16},{16,2},{18,0},{1,19},{3,17},{17,3},{19,1},{4,22},{6,... | collective-permute-start | bytes 1572872 | tf_op jit(solution)/shard_map/ppermute | solution.py:1349
  274.5 6.9 %copy-start = (bf16[256,1024]{1,0:T(8,128)(2,1)}, bf16[256,1024]{1,0:T(8,128)(2,1)S(1)}, u32[]{:S(2)}) copy-start(bf16[256,1024]{1,0:T(8,128)(2,1)S(1)} %collective-permute-done.3.yb_ref) | copy-start | bytes 1572868
  274.5 6.9 %copy-start.1 = (bf16[256,1024]{1,0:T(8,128)(2,1)}, bf16[256,1024]{1,0:T(8,128)(2,1)S(1)}, u32[]{:S(2)}) copy-start(bf16[256,1024]{1,0:T(8,128)(2,1)S(1)} %collective-permute-done.4.yc_ref) | copy-start | bytes 1572868
  274.6 6.9 %copy-start.2 = (bf16[256,1024]{1,0:T(8,128)(2,1)}, bf16[256,1024]{1,0:T(8,128)(2,1)S(1)}, u32[]{:S(2)}) copy-start(bf16[256,1024]{1,0:T(8,128)(2,1)S(1)} %collective-permute-done.5.yd_ref) | copy-start | bytes 1572868
Sparse Core Ops, SparseCore 0:
  78.4 73.2 all-gather.2
  204.6 76.7 reduce-scatter.1

commit v5 on v4

--- a/solution.py
+++ b/solution.py
@@ -169,11 +169,11 @@
     a_ref,
     ca_ref,
     cb_ref,
-    cc_ref,
-    wo_ref,
+    og_ref,
     w_ref,
     f_ref,
     e_ref,
+    wo_ref,
     rows,
     weights,
     packed,
@@ -192,6 +192,8 @@
     s1,
     t0,
     t1,
+    o0,
+    o1,
 ):
     me = Place(zc)
     chips = 4 * zc
@@ -213,7 +215,8 @@
     x = t_ref[...].astype(F32)
     rows[0] = (x * lax.rsqrt(jnp.mean(x * x, axis=-1, keepdims=True) + EPS)).astype(BF16)
     meet([me.any_chip(k) for k in range(1, chips)] + [me.sibling()])
-    local = [move(w_ref.at[me.g], weights.at[me.chip, me.c], ls, 0)]
+    here = og_ref.at[me.z]
+    local = [move(w_ref.at[me.g], weights.at[me.chip, me.c], ls, 0), move(wo_ref, here, ls, 1)]
     pieces = []
     for k in reversed(range(1, chips)):
         there = me.any_chip(k)
@@ -221,6 +224,7 @@
         pieces.append(
             send(w_ref.at[their_g], weights.at[me.chip, me.c], (w0, w1), k, there)
         )
+    outs = [send(wo_ref, here, (o0, o1), k, me.line(k)) for k in range(1, zc)]
     blocks = [send(rows.at[0], rows.at[k], (n0, n1), k, me.plane(k)) for k in range(1, 4)]
     units = g_w.shape[1] // (4 * zc)
     for which, ref in enumerate((g_w, u_w)):
@@ -237,14 +241,16 @@
                     near, far = (second_gain * low(ref[:, lanes(px * zc + i)]) for i in (z, z + 1))
                     f_ref[g, which, :, lanes(z // 2)] = pair_up(near, py, far, py).astype(BF16)
     wide = [
-        move(f_ref.at[me.g], fg_ref.at[pl.ds(2 * me.g, 2)], ls, 2),
-        move(e_ref, fg_ref.at[pl.ds(8, 4)], ls, 9),
+        move(f_ref.at[me.g], fg_ref.at[me.x, me.y, pl.ds(0, 2)], ls, 2),
+        move(e_ref, fg_ref.at[:, :, 2], ls, 9),
     ]
     for k in range(1, 4):
         there = me.plane(k)
         their_g = there[0] * 2 + there[2]
-        wide.append(send(f_ref.at[their_g], fg_ref.at[pl.ds(2 * me.g, 2)], (f0, f1), k, there))
-    for k, ref in ((3, cc_ref), (1, ca_ref), (2, cb_ref)):
+        wide.append(
+            send(f_ref.at[their_g], fg_ref.at[me.x, me.y, pl.ds(0, 2)], (f0, f1), k, there)
+        )
+    for k, ref in ((1, ca_ref), (2, cb_ref)):
         wide.append(send(t2_ref, ref, (t0, t1), k, me.plane(k)))
     local[0].wait()
     for copy in pieces:
@@ -315,7 +321,7 @@
         pltpu.make_async_copy(
             packed.at[me.z // per, k], a_ref.at[me.z, me.c, me.g], ls.at[4 + k]
         ).wait()
-    for copy in kept + wide:
+    for copy in kept + wide + outs + local[1:]:
         copy.wait()
     for copy in blocks:
         copy.wait_send()
@@ -332,19 +338,19 @@
         (
             struct((4, own, width)),
             struct((chips, 2) + piece),
-            struct((12, count, width)),
+            struct((2, 2, 3, count, width)),
             struct((zc, 2, 4, BLOCK + own, PAIR)),
             struct((own, width)),
             struct((own, width)),
-            struct((own, width)),
-            struct((count, width)),
+            struct((zc, count, width)),
         ),
         [VM] * 8 + [ANY] + [VM] * 2,
-        (ANY,) * 7 + (VM,),
+        (ANY,) * 7,
         [
             pltpu.VMEM((4,) + piece, BF16),
             pltpu.VMEM((4, 2, count, width), BF16),
-            pltpu.VMEM((4, count, width), BF16),
+            pltpu.VMEM((2, 2, count, width), BF16),
+            pltpu.VMEM((count, width), BF16),
             pltpu.VMEM((4, own, width), BF16),
             pltpu.VMEM((chips, 2) + piece, BF16),
             pltpu.VMEM((group, 4, BLOCK + own, PAIR), BF16),
@@ -356,7 +362,8 @@
         + both(4 * zc)
         + both(4 * zc)
         + both(1)
-        + both(4),
+        + both(4)
+        + both(zc),
         (tokens, *matrices, cotangent, *(g.reshape(1, -1) for g in gains)),
         2 * 4 * own * width * width,
         16 << 20,
@@ -367,20 +374,35 @@
     zc,
     s_ref,
     x_ref,
-    *rest,
+    w_ref,
+    ob_ref,
+    r_ref,
+    n_ref,
+    og_ref,
+    mine,
+    theirs,
+    slabs,
+    all_w,
+    ls,
+    b0,
+    b1,
+    c0,
+    c1,
+    p0,
+    p1,
 ):
-    w_refs, rest = rest[:zc], rest[zc:]
-    ob_ref, r_ref, n_ref, og_ref, mine, theirs, slabs, all_w, ls, b0, b1, c0, c1, p0, p1 = rest
     me = Place(zc)
     chips = 4 * zc
     heads, per = slabs.shape[:2]
-    for k, ref in enumerate(w_refs):
-        all_w[me.x, me.z ^ k, me.y, me.c] = ref[...]
     meet([me.any_chip(k) for k in range(1, chips)] + [me.sibling()])
-    column = all_w.at[me.x, :, me.y, me.c]
-    planes = [send(column, column, (p0, p1), k, me.plane(k)) for k in range(1, 4)]
     other = send(s_ref.at[:, 1 - me.c], theirs, (b0, b1), 0, me.sibling())
     own = move(s_ref.at[:, me.c], mine, ls, 0)
+    column = all_w.at[me.x, :, me.y, me.c]
+    planes = []
+    for k in range(1, 4):
+        there = me.plane(k)
+        planes.append(send(w_ref, column, (p0, p1), k, there))
+    planes.append(move(w_ref, column, ls, 2))
     own.wait()
     other.wait()
     mine[...] = mine[...] + theirs[...]
@@ -413,86 +435,77 @@
                 sides[0], block, sides[1], block
             ).astype(BF16)
     relay.wait()
-    save = move(all_w, og_ref, ls, 2)
-    residual = x_ref[...].astype(F32) + dot(ob_ref[...], all_w[...].reshape(x_ref.shape[1], x_ref.shape[1]))
+    save = move(all_w, og_ref, ls, 3)
+    square = (x_ref.shape[1], x_ref.shape[1])
+    residual = x_ref[...].astype(F32) + dot(ob_ref[...], all_w[...].reshape(square))
     r_ref[...] = residual
     mean = jnp.mean(residual * residual, axis=-1, keepdims=True)
     n_ref[...] = (residual * lax.rsqrt(mean + EPS)).astype(BF16)
     save.wait()
 
 
-def join_exchange(zc, heads, slabs, tokens, w_parts):
+def join_exchange(zc, heads, slabs, tokens, w_column):
     chips = 4 * zc
     per = 4 * zc // heads
     half = (zc,) + slabs.shape[2:]
     shape = tokens.shape
-    whole = (2, zc, 2, 2) + w_parts[0].shape
+    whole = (2, zc, 2, 2) + w_column.shape[1:]
     return exchange(
         functools.partial(join_kernel, zc),
         2,
         (struct(shape), struct(shape, F32), struct(shape), struct(whole)),
-        [ANY, VM] + [VM] * zc,
+        [ANY, VM, ANY],
         (VM,) * 3 + (ANY,),
         [
             pltpu.VMEM(half, BF16),
             pltpu.VMEM(half, BF16),
             pltpu.VMEM((heads, per) + slabs.shape[3:], BF16),
             pltpu.VMEM(whole, BF16),
-            DMA((3,)),
+            DMA((4,)),
         ]
         + both(1)
         + both(chips)
         + both(4),
-        (slabs, tokens, *w_parts),
-        2 * shape[0] * shape[1] * shape[1],
-        4 << 20,
-    )
-
-
-def middle_kernel(
-    zc,
-    n_ref,
-    ca_ref,
-    cb_ref,
-    cc_ref,
-    cd_ref,
-    f_ref,
-    oa_ref,
-    ob_ref,
-    oc_ref,
-    od_ref,
-    cs_ref,
-    sh_ref,
-    rows,
-    cots,
-    gate_w,
-    up_w,
-    down_w,
-    hid,
-    dgate,
-    dup,
-    c_out,
-    c_in,
-    stage,
-    ls,
-    n0,
-    n1,
-    c0,
-    c1,
-):
+        (slabs, tokens, w_column),
+        0,
+        0,
+    )
+
+
+def middle_kernel(zc, n_ref, ca_ref, cb_ref, cc_ref, cd_ref, *rest):
+    f_refs, rest = rest[: zc // 2 + 1], rest[zc // 2 + 1 :]
+    oa_ref, ob_ref, oc_ref, od_ref, cs_ref, sh_ref, rows, cots, gate_w, up_w, down_w, *rest = rest
+    hid, dgate, dup, c_out, c_in, stage, ls, n0, n1, c0, c1, f0, f1, h0, h1 = rest
     me = Place(zc)
     width = n_ref.shape[1]
     rows[0] = n_ref[...]
-    meet([me.plane(k) for k in range(1, 4)])
+    meet([me.plane(k) for k in range(1, 4)] + [me.line(1), me.sibling()])
     farthest = send(rows.at[0], rows.at[3], (n0, n1), 3, me.plane(3))
-    loads = []
-    for g in range(4):
-        x, y = g // 2, g % 2
-        loads.append(move(f_ref.at[:, :, 2 * g], gate_w.at[x, :, y], ls, 3 * g))
-        loads.append(move(f_ref.at[:, :, 2 * g + 1], up_w.at[x, :, y], ls, 3 * g + 1))
-    loads.append(move(f_ref.at[:, :, 8:], down_w, ls, 2))
+    def places(there):
+        return (
+            gate_w.at[:, there, :, me.c],
+            up_w.at[:, there, :, me.c],
+            down_w.at[there, me.c],
+        )
+
+    given = dict(zip([1, *range(0, zc, 2)], f_refs))
+    hops, loads = [], []
+    for k in range(2, zc, 2):
+        for i, place in enumerate(places(me.z ^ k)):
+            hops.append(send(given[k].at[:, :, i], place, (h0, h1), 3 * k + i, me.line(1)))
+    for k, ref in given.items():
+        for i, place in enumerate(places(me.z ^ k)):
+            loads.append(send(ref.at[:, :, i], place, (f0, f1), 3 * k + i, me.sibling()))
+            loads.append(move(ref.at[:, :, i], place, ls, 21 + 3 * k + i))
     for k, ref in enumerate((ca_ref, cb_ref, cc_ref, cd_ref)):
         cots[k] = ref[...]
+    farthest.wait_send()
+    near_rows = [send(rows.at[0], rows.at[k], (n0, n1), k, me.plane(k)) for k in (1, 2)]
+    for copy in hops:
+        copy.wait()
+    for k in range(3, zc, 2):
+        for i, place in enumerate(places(me.z ^ k)):
+            loads.append(send(place, place, (f0, f1), 3 * k + i, me.sibling()))
     for copy in loads:
         copy.wait()
     square = (width, width)
@@ -519,12 +532,6 @@
         def _():
             trip(c_out.at[k], c_in.at[k], (c0, c1), k, me.plane(k)).start()
 
-        @pl.when(step == 0)
-        def _():
-            trip(rows.at[0], rows.at[3], (n0, n1), 3, me.plane(3)).wait_send()
-            for near in (1, 2):
-                trip(rows.at[0], rows.at[near], (n0, n1), near, me.plane(near)).start()
-
         return carry
 
     lax.fori_loop(0, 4, block, 0)
@@ -566,8 +573,8 @@
     cs_ref[...] = total
     for copy in shares:
         copy.wait()
-    for near in (1, 2):
-        trip(rows.at[0], rows.at[near], (n0, n1), near, me.plane(near)).wait_send()
+    for copy in near_rows:
+        copy.wait_send()
 
 
 def middle_exchange(zc, normed, cots, weights):
@@ -583,14 +590,16 @@
             struct((own, width), F32),
             struct((zc, 2, 12, piece, width)),
         ),
-        [VM] * 5 + [ANY],
+        [VM] * 5 + [ANY] * len(weights),
         (VM,) * 5 + (ANY,),
-        [blocks, blocks, wide, wide, pltpu.VMEM((zc, 2, 4, piece, width), BF16)]
+        [blocks, blocks, wide, wide, pltpu.VMEM((zc, 2, 2, 2, piece, width), BF16)]
         + [blocks] * 5
-        + [pltpu.VMEM((3, width, width), BF16), DMA((21,))]
+        + [pltpu.VMEM((3, width, width), BF16), DMA((21 + 3 * zc,))]
         + both(4)
-        + both(4),
-        (normed, *cots, weights),
+        + both(4)
+        + both(3 * zc)
+        + both(3 * zc),
+        (normed, *cots, *weights),
         2 * 4 * own * width * width * 9,
         64 << 20,
     )
@@ -823,7 +832,7 @@
 
         return carry
 
-    lax.fori_loop(0, 4, block, 0)
+    lax.fori_loop(0, 3, block, 0)
     for copy in o_parts:
         copy.wait()
     o_sum = o_in[0].astype(F32)
@@ -831,6 +840,12 @@
         o_sum = o_sum + o_in[k].astype(F32)
     o_mine[...] = o_sum.astype(BF16)
     o_swap = send(o_mine.at[:, 1 - me.c], o_theirs, (s0, s1), 1, me.sibling())
+    o_swap.wait()
+    o_theirs[...] = o_theirs[...] + o_mine[:, me.c]
+    sends = [
+        send(o_theirs.at[me.z ^ k], o_land.at[k], (q0, q1), k, me.line(k)) for k in range(1, zc)
+    ]
+    lax.fori_loop(3, 4, block, 0)
     width, cols = w_ref.shape
     all_rows = 4 * n_ref.shape[1]
     normed_all = n_ref[...].reshape(all_rows, width)
@@ -852,11 +867,6 @@
                 me.sibling(),
             )
         )
-    o_swap.wait()
-    o_theirs[...] = o_theirs[...] + o_mine[:, me.c]
-    sends = [
-        send(o_theirs.at[me.z ^ k], o_land.at[k], (q0, q1), k, me.line(k)) for k in range(1, zc)
-    ]
     c_out[0] = nt_dot(grads[0], w_ref[...]).astype(BF16)
     for swap in swaps:
         swap.wait()
@@ -1353,6 +1363,13 @@
     return lax.ppermute(value, "z", [(i, i ^ k) for i in range(lax.axis_size("z"))])
 
 
+def doubling(pieces, first, last):
+    while first >= last:
+        pieces = {**pieces, **{k + first: along(pieces[k], first) for k in pieces}}
+        first //= 2
+    return pieces
+
+
 def body(
     zc,
     tokens,
@@ -1376,7 +1393,7 @@
     workers = 2 * per_head
     feature_rows = w_query.shape[0]
 
-    n1_all, qkv_w, ffn_in, by_head, *near, w_o = head_exchange(
+    n1_all, qkv_w, ffn_own, by_head, *near, w_column = head_exchange(
         zc,
         group,
         tokens,
@@ -1384,13 +1401,12 @@
         cotangent,
         (norm1_gain, norm2_gain),
     )
-    cots = [cotangent] + near
-    w_parts = [w_o] + [along(w_o, k) for k in range(1, zc)]
     qkv_w = qkv_w.reshape(width, 3 * group * HEAD_DIM)
 
-    ffn_all = lax.all_gather(ffn_in, ("z", "core"), axis=0, tiled=False).reshape(
-        zc, 2, 12, feature_rows, width
-    )
+    ffn_own, far = lax.optimization_barrier((ffn_own, cotangent))
+    cots = [cotangent] + near + [around(far, 3)]
+    ffn_parts = doubling({0: ffn_own}, zc // 2, 2)
+    close = along(ffn_own, 1)
 
     anchors = jnp.transpose(block_anchor.reshape(2, zc, 2, 2, 2), (1, 3, 0, 2, 4)).reshape(-1)
     who = ((lax.axis_index("z") % per_head) * 2 + lax.axis_index("core")).astype(jnp.int32).reshape(1)
@@ -1399,10 +1415,12 @@
         workers, anchors, seq_lengths, who, by_head.reshape((slab_count,) + by_head.shape[3:])
     )
     attn_rows, residual, normed_two, out_mat = join_exchange(
-        zc, heads, o_slabs.reshape(zc, 2, 4, BLOCK, PAIR), tokens, w_parts
+        zc, heads, o_slabs.reshape(zc, 2, 4, BLOCK, PAIR), tokens, w_column
     )
     out_mat = out_mat.reshape(width, width)
-    *out_parts, c_sum, shares = middle_exchange(zc, normed_two, cots, ffn_all)
+    *out_parts, c_sum, shares = middle_exchange(
+        zc, normed_two, cots, [close] + [ffn_parts[k] for k in range(0, zc, 2)]
+    )
     shares = lax.psum_scatter(
         shares.reshape(zc * 2 * 12, feature_rows, width), ("z", "core"), scatter_dimension=0, tiled=True
     )

time: 367 us -> 359 us (0.978)
  Pallas kernels: 335 us -> 325 us
    pallas_call x5, Pallas kernels: 265 us -> 256 us  [exchange(): pl.pallas_call(kernel, out_shape=out_shape, in_specs=in_specs, out_specs=...]
  transfers between devices with their start and end apart: 8 -> 7, of which waited for: 2 -> 1; matrix products, arithmetic and copies ran while one was open for 0% -> 0% of each run, Pallas kernels for 36% -> 34%
where the time goes in v5:
time: 359 us; the launch traced here: 358 us
  Pallas kernels  325 us (91%)
  between operations  14.3 us (4%)
  waiting for transfers between devices  8.23 us (2%)
  starting transfers between devices  8.17 us (2%)
    pallas_call x5, Pallas kernels, exchange(): pl.pallas_call(kernel, out_shape=out_shape, in_specs=in_specs, out_specs=...  256 us
    pallas_call x1, Pallas kernels, attention_backward(): pl.pallas_call(functools.partial(backward_kernel, workers), out_shape=str...  34.2 us
    pallas_call x1, Pallas kernels, attention_forward(): pl.pallas_call(functools.partial(forward_kernel, workers), out_shape=(str...  30.3 us
    reduce_scatter x1, waiting for transfers between devices, body(): lax.psum_scatter(shares.reshape(zc * 2 * 12, feature_rows, width), ('z',...  8.2 us
  transfers between devices with their start and end apart: 7, of which 1 were waited for; matrix products, arithmetic and copies ran while one was open for 0% of the time, Pallas kernels for 34%

profile of v5, /device:TPU:0, one launch (start us, length us, event | category | flops | bytes accessed | tf_op | source)
XLA Modules:
  0.0 357.6 jit_solution(10448660240251417881)
XLA Ops:
  7.2 0.0 reduce-scatter.2.cloned.1.call-start
  7.2 0.0 copy-start.3
  7.2 0.0 copy-start.4
  7.2 68.6 %shard_map.212 = (bf16[4,256,1024]{2,1,0:T(8,128)(2,1)}, bf16[16,2,32,768]{3,2,1,0:T(8,128)(2,1)}, bf16[2,2,3,32,1024]{4,3,2,1,0:T(8,128)(2,1)}, bf16[4,2,4,384,...) custom-call(bf16[256,1024]{1,0:T(8,128)(2,1)} %x_ref.3, ...), custom_call_target="tpu_custom_call" | custom-call | flops 2147483648 | bytes 16777216 | tf_op jit(solution)/shard_map/pallas_call | solution.py:139
  75.8 3.5 collective-permute-start.2
  79.4 0.2 collective-permute-start.1
  79.6 0.0 copy-done.3
  79.6 0.8 collective-permute-start
  80.4 0.0 copy-done.4
  80.4 0.1 reshape.66
  80.5 0.6 reshape.67.anchor_ref
  81.2 30.3 %shard_map.213 = (bf16[32,128,128]{2,1,0:T(8,128)(2,1)}, bf16[8192,128]{1,0:T(8,128)(2,1)}, bf16[128,8192]{1,0:T(8,128)(2,1)}, bf16[8,512,128]{2,1,0:T(8,128)(2,...) custom-call(s32[64]{0:T(128)} %reshape.67.anchor_ref, s32[8]{0:T(128)} %lens_ref.3, ...), custom_call_target="tpu_custom_call" | custom-call | flops 4294967296 | bytes 8388608 | tf_op jit(solution)/shard_map/pallas_call | solution.py:1226
  111.5 26.5 %shard_map.214 = (bf16[256,1024]{1,0:T(8,128)(2,1)}, f32[256,1024]{1,0:T(8,128)}, bf16[256,1024]{1,0:T(8,128)(2,1)}, bf16[2,4,2,2,32,1024]{5,4,3,2,1,0:T(8,128)(2,1)}) custom-call(bf16[4,2,4,128,128]{4,3,2,1,0:T(8,128)(2,1)} %bitcast.17, bf16[256,1024]{1,0:T(8,128)(2,1)} %x_ref.3, bf16[4,32,1024]{2,1,0:T(8,128)(2,1)} %get-tuple-element.63.w_ref), custom_call_target="tpu_custom_call" | custom-call | tf_op jit(solution)/shard_map/pallas_call | solution.py:139
  138.0 0.0 collective-permute-done.cd_ref
  138.0 0.0 copy-start.10
  138.0 0.0 collective-permute-done.2.rest_2_
  138.0 0.0 copy-start.5
  138.0 0.0 collective-permute-done.1.rest_0_
  138.0 0.0 copy-start.6
  138.1 0.7 copy-done.10
  138.8 0.3 copy-done.5
  139.1 0.3 copy-done.6
  139.3 59.7 %shard_map.215 = (bf16[256,1024]{1,0:T(8,128)(2,1)}, bf16[256,1024]{1,0:T(8,128)(2,1)}, bf16[256,1024]{1,0:T(8,128)(2,1)}, bf16[256,1024]{1,0:T(8,128)(2,1)}, f3...) custom-call(bf16[256,1024]{1,0:T(8,128)(2,1)} %get-tuple-element.64.n_ref, bf16[256,1024]{1,0:T(8,128)(2,1)} %t_ref.3, ...), custom_call_target="tpu_custom_call" | custom-call | flops 19327352832 | bytes 67108864 | tf_op jit(solution)/shard_map/pallas_call | solution.py:139
  199.0 0.0 reduce-scatter.2.cloned.1.call-update
  199.0 0.0 copy-start.9
  199.0 0.0 copy-start.8
  199.1 0.0 copy-start.7
  199.1 30.4 %shard_map.216 = (f32[256,1024]{1,0:T(8,128)}, bf16[4,2,4,128,128]{4,3,2,1,0:T(8,128)(2,1)}, bf16[4,4,2,32,1024]{4,3,2,1,0:T(8,128)(2,1)}) custom-call(f32[256,1024]{1,0:T(8,128)} %get-tuple-element.70.c_ref, bf16[256,1024]{1,0:T(8,128)(2,1)} %t_ref.3, f32[256,1024]{1,0:T(8,128)} %get-tuple-element.71.r_ref, bf16[1024,1024]{1,0:T(8,128)(2,1)} %bitcast.15, ...), custom_call_target="tpu_custom_call" | custom-call | flops 1073741824 | bytes 8388608 | tf_op jit(solution)/shard_map/pallas_call | solution.py:139
  229.5 0.0 copy-done.9
  229.5 1.4 collective-permute-start.3
  230.8 0.0 copy-done.8
  230.8 1.5 collective-permute-start.4
  232.3 0.0 copy-done.7
  232.3 0.8 collective-permute-start.5
  233.1 34.2 %shard_map.217 = bf16[32,384,128]{2,1,0:T(8,128)(2,1)} custom-call(s32[64]{0:T(128)} %reshape.67.anchor_ref, s32[8]{0:T(128)} %lens_ref.3, s32[1]{0:T(128)} %bitcast.1.who_ref, bf16[32,128,128]{2,1,0:T(8,128)(2,1)} %bitcast.23, bf16[8192,128]{1,0:T(8,128)(2,1)} %get-tuple-element.80.kv_ref, bf16[128,8192]{1,0:T(8,128)(2,1)} %get-tuple-element.81.kvt_ref, ...), custom_call_target="tpu_custom_call" | custom-call | flops 10737418240 | bytes 8388608 | tf_op jit(solution)/shard_map/pallas_call | solution.py:1338
  267.3 0.0 collective-permute-done.3.yb_ref
  267.3 0.0 copy-start
  267.3 0.0 collective-permute-done.4.yc_ref
  267.3 0.0 copy-start.1
  267.3 0.0 collective-permute-done.5.yd_ref
  267.3 0.0 copy-start.2
  267.3 8.2 %reduce-scatter.2.cloned.1.call-done.f_ref.ds_any = bf16[12,32,1024]{2,1,0:T(8,128)(2,1)} async-done(((bf16[96,32,1024]{2,1,0:T(8,128)(2,1)}), bf16[12,32,1024]{2,1,0:T(8,128)(2,1)}) %reduce-scatter.2.cloned.1.call-update) | async-done | bytes 786448 | tf_op jit(solution)/shard_map/reduce_scatter | solution.py:1424
  275.5 0.0 copy-done
  275.5 0.0 copy-done.1
  275.5 0.0 copy-done.2
  275.5 70.4 %shard_map.218 = (bf16[256,1024]{1,0:T(8,128)(2,1)}, bf16[4,4,32,768]{3,2,1,0:T(8,128)(2,1)}, f32[32,1024]{1,0:T(8,128)}, bf16[4,2,32,1024]{3,2,1,0:T(8,128)(2,1)}, bf16[256,1024]{1,0:T(8,128)(2,1)}) custom-call(bf16[4,2,4,384,128]{4,3,2,1,0:T(8,128)(2,1)} %bitcast.14, bf16[4,256,1024]{2,1,0:T(8,128)(2,1)} %get-tuple-element.86.n_ref, ...), custom_call_target="tpu_custom_call" | custom-call | flops 3221225472 | bytes 25165824 | tf_op jit(solution)/shard_map/pallas_call | solution.py:139
  345.9 4.8 %shard_map.219 = (bf16[256,1024]{1,0:T(8,128)(2,1)}, bf16[256,1024]{1,0:T(8,128)(2,1)}, f32[32,1024]{1,0:T(8,128)}, f32[1,32]{1,0:T(1,128)}, f32[32,1024]{1,0:T(...) custom-call(bf16[256,1024]{1,0:T(8,128)(2,1)} %get-tuple-element.95., ...), custom_call_target="tpu_custom_call" | custom-call | tf_op jit(solution)/shard_map/pallas_call | solution.py:1036
  (1 shorter events, 0.0 us)
Async XLA Ops:
  7.2 268.3 %reduce-scatter.2.cloned.1.call-start = ((), (), s32[]{:S(2)}) async-start(), calls=%async_computation.1 | async-start | bytes 7077888 | tf_op jit(solution)/shard_map/reduce_scatter | solution.py:1424
  7.2 72.4 %copy-start.3 = (bf16[256,1024]{1,0:T(8,128)(2,1)S(1)}, bf16[256,1024]{1,0:T(8,128)(2,1)}, u32[]{:S(2)}) copy-start(bf16[256,1024]{1,0:T(8,128)(2,1)} %t_ref.3) | copy-start | bytes 1572868
  7.2 73.2 %copy-start.4 = (s32[64]{0:T(128)S(1)}, s32[64]{0:T(128)}, u32[]{:S(2)}) copy-start(s32[64]{0:T(128)} %param.24) | copy-start | bytes 772
  75.8 62.2 %collective-permute-start.2 = (bf16[2,2,3,32,1024]{4,3,2,1,0:T(8,128)(2,1)}, bf16[2,2,3,32,1024]{4,3,2,1,0:T(8,128)(2,1)S(1)}, u32[]{:S(2)}, u32[]{:S(2)}) collective-permute-start(bf16[2,2,3,32,1024]{4,3,2,1,0:T(8,128)(2,1)} %get-tuple-element.69.rest_1_), channel_id=1, source_target_pairs={{0,8},{4,12},{8,0},{12,4},{1,9},{5,13},{9,1},{13,5},{2,10},{6,14},... | collective-permute-start | bytes 2359304 | tf_op jit(solution)/shard_map/ppermute | solution.py:1363
  79.4 58.7 %collective-permute-start.1 = (bf16[2,2,3,32,1024]{4,3,2,1,0:T(8,128)(2,1)}, bf16[2,2,3,32,1024]{4,3,2,1,0:T(8,128)(2,1)S(1)}, u32[]{:S(2)}, u32[]{:S(2)}) collective-permute-start(bf16[2,2,3,32,1024]{4,3,2,1,0:T(8,128)(2,1)} %get-tuple-element.69.rest_1_), channel_id=1, source_target_pairs={{0,4},{4,0},{8,12},{12,8},{1,5},{5,1},{9,13},{13,9},{2,6},{6,2},{1... | collective-permute-start | bytes 2359304 | tf_op jit(solution)/shard_map/ppermute | solution.py:1363
  79.6 58.4 %collective-permute-start = (bf16[256,1024]{1,0:T(8,128)(2,1)S(1)}, bf16[256,1024]{1,0:T(8,128)(2,1)S(1)}, u32[]{:S(2)}, u32[]{:S(2)}) collective-permute-start(bf16[256,1024]{1,0:T(8,128)(2,1)S(1)} %copy-done.3), channel_id=1, source_target_pairs={{0,18},{2,16},{16,2},{18,0},{1,19},{3,17},{17,3},{19,1},{4,22},{6,... | collective-permute-start | bytes 1572872 | tf_op jit(solution)/shard_map/ppermute | solution.py:1359
  138.0 0.8 copy-start.10
  138.0 1.0 copy-start.5
  138.0 1.3 copy-start.6
  199.0 30.4 %copy-start.9 = (bf16[256,1024]{1,0:T(8,128)(2,1)S(1)}, bf16[256,1024]{1,0:T(8,128)(2,1)}, u32[]{:S(2)}) copy-start(bf16[256,1024]{1,0:T(8,128)(2,1)} %get-tuple-element.92) | copy-start | bytes 1572868
  199.0 31.8 %copy-start.8 = (bf16[256,1024]{1,0:T(8,128)(2,1)S(1)}, bf16[256,1024]{1,0:T(8,128)(2,1)}, u32[]{:S(2)}) copy-start(bf16[256,1024]{1,0:T(8,128)(2,1)} %get-tuple-element.93) | copy-start | bytes 1572868
  199.1 33.2 %copy-start.7 = (bf16[256,1024]{1,0:T(8,128)(2,1)S(1)}, bf16[256,1024]{1,0:T(8,128)(2,1)}, u32[]{:S(2)}) copy-start(bf16[256,1024]{1,0:T(8,128)(2,1)} %get-tuple-element.94) | copy-start | bytes 1572868
  229.5 37.8 %collective-permute-start.3 = (bf16[256,1024]{1,0:T(8,128)(2,1)S(1)}, bf16[256,1024]{1,0:T(8,128)(2,1)S(1)}, u32[]{:S(2)}, u32[]{:S(2)}) collective-permute-start(bf16[256,1024]{1,0:T(8,128)(2,1)S(1)} %copy-done.9), channel_id=1, source_target_pairs={{0,2},{2,0},{16,18},{18,16},{1,3},{3,1},{17,19},{19,17},{4,6},{6,4... | collective-permute-start | bytes 1572872 | tf_op jit(solution)/shard_map/ppermute | solution.py:1359
  230.8 36.4 %collective-permute-start.4 = (bf16[256,1024]{1,0:T(8,128)(2,1)S(1)}, bf16[256,1024]{1,0:T(8,128)(2,1)S(1)}, u32[]{:S(2)}, u32[]{:S(2)}) collective-permute-start(bf16[256,1024]{1,0:T(8,128)(2,1)S(1)} %copy-done.8), channel_id=1, source_target_pairs={{0,16},{2,18},{16,0},{18,2},{1,17},{3,19},{17,1},{19,3},{4,20},{6,... | collective-permute-start | bytes 1572872 | tf_op jit(solution)/shard_map/ppermute | solution.py:1359
  232.3 35.0 %collective-permute-start.5 = (bf16[256,1024]{1,0:T(8,128)(2,1)S(1)}, bf16[256,1024]{1,0:T(8,128)(2,1)S(1)}, u32[]{:S(2)}, u32[]{:S(2)}) collective-permute-start(bf16[256,1024]{1,0:T(8,128)(2,1)S(1)} %copy-done.7), channel_id=1, source_target_pairs={{0,18},{2,16},{16,2},{18,0},{1,19},{3,17},{17,3},{19,1},{4,22},{6,... | collective-permute-start | bytes 1572872 | tf_op jit(solution)/shard_map/ppermute | solution.py:1359
  267.3 8.2 %copy-start = (bf16[256,1024]{1,0:T(8,128)(2,1)}, bf16[256,1024]{1,0:T(8,128)(2,1)S(1)}, u32[]{:S(2)}) copy-start(bf16[256,1024]{1,0:T(8,128)(2,1)S(1)} %collective-permute-done.3.yb_ref) | copy-start | bytes 1572868
  267.3 8.2 %copy-start.1 = (bf16[256,1024]{1,0:T(8,128)(2,1)}, bf16[256,1024]{1,0:T(8,128)(2,1)S(1)}, u32[]{:S(2)}) copy-start(bf16[256,1024]{1,0:T(8,128)(2,1)S(1)} %collective-permute-done.4.yc_ref) | copy-start | bytes 1572868
  267.3 8.2 %copy-start.2 = (bf16[256,1024]{1,0:T(8,128)(2,1)}, bf16[256,1024]{1,0:T(8,128)(2,1)S(1)}, u32[]{:S(2)}) copy-start(bf16[256,1024]{1,0:T(8,128)(2,1)S(1)} %collective-permute-done.5.yd_ref) | copy-start | bytes 1572868
Sparse Core Ops, SparseCore 0:
  199.2 76.3 reduce-scatter.1

commit v6 on v5

--- a/solution.py
+++ b/solution.py
@@ -98,11 +98,11 @@
         return (self.x ^ (k // 2 % 2), self.z ^ (k // 4), self.y ^ (k % 2), self.c)
 
 
-def meet(peers):
+def greet(peers):
     barrier = pltpu.get_barrier_semaphore()
     for peer in peers:
         pl.semaphore_signal(barrier, inc=1, device_id=peer, device_id_type=IDS)
-    pl.semaphore_wait(barrier, len(peers))
+    return lambda: pl.semaphore_wait(barrier, len(peers))
 
 
 def trip(source, target, sems, index, device):
@@ -160,15 +160,12 @@
     u_w,
     d_w,
     o_w,
-    t2_ref,
     gain1,
     gain2,
     ng_ref,
     wg_ref,
     fg_ref,
     a_ref,
-    ca_ref,
-    cb_ref,
     og_ref,
     w_ref,
     f_ref,
@@ -190,16 +187,17 @@
     b1,
     s0,
     s1,
-    t0,
-    t1,
     o0,
     o1,
+    p0,
+    p1,
 ):
     me = Place(zc)
     chips = 4 * zc
     per = zc // group
     qw = group * HEAD_DIM
     width = t_ref.shape[1]
+    met = greet([me.any_chip(k) for k in range(1, chips)] + [me.sibling()])
     first_gain, second_gain = column_of(low(gain1[...])), column_of(low(gain2[...]))
     for g in range(4):
         at = slice(g * qw, (g + 1) * qw)
@@ -214,8 +212,8 @@
     wo_ref[...] = o_w[...].astype(BF16)
     x = t_ref[...].astype(F32)
     rows[0] = (x * lax.rsqrt(jnp.mean(x * x, axis=-1, keepdims=True) + EPS)).astype(BF16)
-    meet([me.any_chip(k) for k in range(1, chips)] + [me.sibling()])
-    here = og_ref.at[me.z]
+    met()
+    here = og_ref.at[me.x, me.z, me.y, me.c]
     local = [move(w_ref.at[me.g], weights.at[me.chip, me.c], ls, 0), move(wo_ref, here, ls, 1)]
     pieces = []
     for k in reversed(range(1, chips)):
@@ -250,8 +248,6 @@
         wide.append(
             send(f_ref.at[their_g], fg_ref.at[me.x, me.y, pl.ds(0, 2)], (f0, f1), k, there)
         )
-    for k, ref in ((1, ca_ref), (2, cb_ref)):
-        wide.append(send(t2_ref, ref, (t0, t1), k, me.plane(k)))
     local[0].wait()
     for copy in pieces:
         copy.wait()
@@ -291,6 +287,10 @@
 
     lax.fori_loop(0, 4, project, 0)
     kept.append(move(rows, ng_ref, ls, 8))
+    for copy in outs + local[1:]:
+        copy.wait()
+    column = og_ref.at[me.x, :, me.y, me.c]
+    out_rows = [send(column, column, (p0, p1), k, me.plane(k)) for k in range(1, 4)]
 
     def pass_on(step, carry):
         k, over = step // (zc - 1), step % (zc - 1) + 1
@@ -308,6 +308,10 @@
         return carry
 
     lax.fori_loop(0, 4 * (zc - 1), pass_on, 0)
+    for copy in out_rows:
+        copy.wait()
+    every = og_ref.at[:, :, :, me.c]
+    last = send(every, every, (s0, s1), 1, me.sibling())
 
     def finish(step, carry):
         k, over = step // zc, step % zc
@@ -321,13 +325,13 @@
         pltpu.make_async_copy(
             packed.at[me.z // per, k], a_ref.at[me.z, me.c, me.g], ls.at[4 + k]
         ).wait()
-    for copy in kept + wide + outs + local[1:]:
+    for copy in [last] + kept + wide:
         copy.wait()
     for copy in blocks:
         copy.wait_send()
 
 
-def head_exchange(zc, group, tokens, matrices, cotangent, gains):
+def head_exchange(zc, group, tokens, matrices, gains):
     chips = 4 * zc
     own, width = tokens.shape
     count = matrices[0].shape[0]
@@ -340,12 +344,10 @@
             struct((chips, 2) + piece),
             struct((2, 2, 3, count, width)),
             struct((zc, 2, 4, BLOCK + own, PAIR)),
-            struct((own, width)),
-            struct((own, width)),
-            struct((zc, count, width)),
+            struct((2, zc, 2, 2, count, width)),
         ),
-        [VM] * 8 + [ANY] + [VM] * 2,
-        (ANY,) * 7,
+        [VM] * 10,
+        (ANY,) * 5,
         [
             pltpu.VMEM((4,) + piece, BF16),
             pltpu.VMEM((4, 2, count, width), BF16),
@@ -361,48 +363,22 @@
         + both(4)
         + both(4 * zc)
         + both(4 * zc)
-        + both(1)
-        + both(4)
-        + both(zc),
-        (tokens, *matrices, cotangent, *(g.reshape(1, -1) for g in gains)),
+        + both(2)
+        + both(zc)
+        + both(4),
+        (tokens, *matrices, *(g.reshape(1, -1) for g in gains)),
         2 * 4 * own * width * width,
         16 << 20,
     )
 
 
-def join_kernel(
-    zc,
-    s_ref,
-    x_ref,
-    w_ref,
-    ob_ref,
-    r_ref,
-    n_ref,
-    og_ref,
-    mine,
-    theirs,
-    slabs,
-    all_w,
-    ls,
-    b0,
-    b1,
-    c0,
-    c1,
-    p0,
-    p1,
-):
+def join_kernel(zc, s_ref, x_ref, w_ref, ob_ref, r_ref, n_ref, mine, theirs, slabs, ls, b0, b1, c0, c1):
     me = Place(zc)
     chips = 4 * zc
     heads, per = slabs.shape[:2]
-    meet([me.any_chip(k) for k in range(1, chips)] + [me.sibling()])
+    greet([me.any_chip(k) for k in range(1, chips)] + [me.sibling()])()
     other = send(s_ref.at[:, 1 - me.c], theirs, (b0, b1), 0, me.sibling())
     own = move(s_ref.at[:, me.c], mine, ls, 0)
-    column = all_w.at[me.x, :, me.y, me.c]
-    planes = []
-    for k in range(1, 4):
-        there = me.plane(k)
-        planes.append(send(w_ref, column, (p0, p1), k, there))
-    planes.append(move(w_ref, column, ls, 2))
     own.wait()
     other.wait()
     mine[...] = mine[...] + theirs[...]
@@ -416,10 +392,6 @@
         sends.append(
             send(mine.at[there[1], their_g], slabs.at[head, place], (c0, c1), k, there)
         )
-    for copy in planes:
-        copy.wait()
-    half = all_w.at[:, :, :, me.c]
-    relay = send(half, half, (p0, p1), 0, me.sibling())
     keep.wait()
     for copy in sends:
         copy.wait()
@@ -434,39 +406,32 @@
             ob_ref[block * BLOCK : (block + 1) * BLOCK, lanes(pair)] = pair_up(
                 sides[0], block, sides[1], block
             ).astype(BF16)
-    relay.wait()
-    save = move(all_w, og_ref, ls, 3)
-    square = (x_ref.shape[1], x_ref.shape[1])
-    residual = x_ref[...].astype(F32) + dot(ob_ref[...], all_w[...].reshape(square))
+    residual = x_ref[...].astype(F32) + dot(ob_ref[...], w_ref[...])
     r_ref[...] = residual
     mean = jnp.mean(residual * residual, axis=-1, keepdims=True)
     n_ref[...] = (residual * lax.rsqrt(mean + EPS)).astype(BF16)
-    save.wait()
-
-
-def join_exchange(zc, heads, slabs, tokens, w_column):
+
+
+def join_exchange(zc, heads, slabs, tokens, w_out):
     chips = 4 * zc
     per = 4 * zc // heads
     half = (zc,) + slabs.shape[2:]
     shape = tokens.shape
-    whole = (2, zc, 2, 2) + w_column.shape[1:]
     return exchange(
         functools.partial(join_kernel, zc),
         2,
-        (struct(shape), struct(shape, F32), struct(shape), struct(whole)),
-        [ANY, VM, ANY],
-        (VM,) * 3 + (ANY,),
+        (struct(shape), struct(shape, F32), struct(shape)),
+        [ANY, VM, VM],
+        (VM,) * 3,
         [
             pltpu.VMEM(half, BF16),
             pltpu.VMEM(half, BF16),
             pltpu.VMEM((heads, per) + slabs.shape[3:], BF16),
-            pltpu.VMEM(whole, BF16),
-            DMA((4,)),
+            DMA((2,)),
         ]
         + both(1)
-        + both(chips)
-        + both(4),
-        (slabs, tokens, w_column),
+        + both(chips),
+        (slabs, tokens, w_out),
         0,
         0,
     )
@@ -475,11 +440,12 @@
 def middle_kernel(zc, n_ref, ca_ref, cb_ref, cc_ref, cd_ref, *rest):
     f_refs, rest = rest[: zc // 2 + 1], rest[zc // 2 + 1 :]
     oa_ref, ob_ref, oc_ref, od_ref, cs_ref, sh_ref, rows, cots, gate_w, up_w, down_w, *rest = rest
-    hid, dgate, dup, c_out, c_in, stage, ls, n0, n1, c0, c1, f0, f1, h0, h1 = rest
+    hid, dgate, dup, c_out, c_in, stage, o_out, ls, n0, n1, c0, c1, f0, f1, h0, h1 = rest
     me = Place(zc)
     width = n_ref.shape[1]
-    rows[0] = n_ref[...]
-    meet([me.plane(k) for k in range(1, 4)] + [me.line(1), me.sibling()])
+    met = greet([me.plane(k) for k in range(1, 4)] + [me.line(1), me.sibling()])
+    move(n_ref, rows.at[0], ls, 15).wait()
+    met()
     farthest = send(rows.at[0], rows.at[3], (n0, n1), 3, me.plane(3))
     def places(there):
         return (
@@ -498,7 +464,7 @@
             loads.append(send(ref.at[:, :, i], place, (f0, f1), 3 * k + i, me.sibling()))
             loads.append(move(ref.at[:, :, i], place, ls, 21 + 3 * k + i))
     for k, ref in enumerate((ca_ref, cb_ref, cc_ref, cd_ref)):
-        cots[k] = ref[...]
+        loads.append(move(ref, cots.at[k], ls, 16 + k))
     farthest.wait_send()
     near_rows = [send(rows.at[0], rows.at[k], (n0, n1), k, me.plane(k)) for k in (1, 2)]
     for copy in hops:
@@ -511,9 +477,9 @@
     square = (width, width)
 
     def block(step, carry):
-        k = jnp.where(step == 0, 0, jnp.where(step == 1, 3, step - 1))
-
-        @pl.when(step > 0)
+        k = jnp.where(step == 0, 3, jnp.where(step == 3, 0, step))
+
+        @pl.when(step < 3)
         def _():
             trip(rows.at[0], rows.at[k], (n0, n1), k, me.plane(k)).wait_recv()
 
@@ -528,7 +494,7 @@
         dup[k] = (back * soft).astype(BF16)
         c_out[k] = (nt_dot(dgate[k], gate_mat) + nt_dot(dup[k], up_mat)).astype(BF16)
 
-        @pl.when(step > 0)
+        @pl.when(step < 3)
         def _():
             trip(c_out.at[k], c_in.at[k], (c0, c1), k, me.plane(k)).start()
 
@@ -565,7 +531,8 @@
     )
 
     for k, ref in enumerate((oa_ref, ob_ref, oc_ref, od_ref)):
-        ref[...] = dot(hid[k], down_w[...].reshape(square)).astype(BF16)
+        o_out[k] = dot(hid[k], down_w[...].reshape(square)).astype(BF16).reshape(ref.shape)
+        shares.append(move(o_out.at[k], ref, ls, k))
     total = c_out[0].astype(F32)
     for k in range(1, 4):
         trip(c_out.at[k], c_in.at[k], (c0, c1), k, me.plane(k)).wait()
@@ -586,15 +553,15 @@
         functools.partial(middle_kernel, zc),
         3,
         (
-            *[struct((own, width))] * 4,
+            *[struct((zc, 2, piece, width))] * 4,
             struct((own, width), F32),
             struct((zc, 2, 12, piece, width)),
         ),
-        [VM] * 5 + [ANY] * len(weights),
-        (VM,) * 5 + (ANY,),
+        [ANY] * (5 + len(weights)),
+        (ANY,) * 4 + (VM, ANY),
         [blocks, blocks, wide, wide, pltpu.VMEM((zc, 2, 2, 2, piece, width), BF16)]
         + [blocks] * 5
-        + [pltpu.VMEM((3, width, width), BF16), DMA((21 + 3 * zc,))]
+        + [pltpu.VMEM((3, width, width), BF16), pltpu.VMEM((4, zc, 2, piece, width), BF16), DMA((21 + 3 * zc,))]
         + both(4)
         + both(4)
         + both(3 * zc)
@@ -612,16 +579,27 @@
     r_ref,
     wo_ref,
     ob_ref,
+    yb_ref,
+    yc_ref,
     dr_ref,
     do_ref,
-    dw_ref,
+    va_ref,
+    vb_ref,
+    vc_ref,
+    vd_ref,
+    nb_ref,
+    nc_ref,
     slabs,
     stage,
+    wo_in,
+    ob_in,
     ls,
     d0,
     d1,
     b0,
     b1,
+    y0,
+    y1,
 ):
     me = Place(zc)
     chips = 4 * zc
@@ -629,7 +607,8 @@
     group = heads // 4
     per = zc // group
     width = t_ref.shape[1]
-    meet([me.any_chip(k) for k in range(1, chips)] + [me.sibling()])
+    met = greet([me.any_chip(k) for k in range(1, chips)] + [me.sibling()])
+    loads = [move(wo_ref, wo_in, ls, 5), move(ob_ref, ob_in, ls, 6)]
     total, residual = c_ref[...], r_ref[...]
     scaling = lax.rsqrt(jnp.mean(residual * residual, axis=-1, keepdims=True) + EPS)
     normed = residual * scaling
@@ -637,11 +616,13 @@
     grad = t_ref[...].astype(F32) + scaling * (total - normed * middle)
     dr_ref[...] = grad
     narrow = grad.astype(BF16)
-    back = nt_dot(narrow, wo_ref[...])
+    loads[0].wait()
+    back = nt_dot(narrow, wo_in[...])
     for pair in range(heads // 2):
         two = back[:, lanes(pair)]
         for side in range(2):
             slabs[2 * pair + side] = pair_up(two[:BLOCK], side, two[BLOCK:], side).astype(BF16)
+    met()
     to = do_ref.at[me.z, me.c, me.g]
     own = move(slabs.at[me.g * group + me.z // per], to, ls, 0)
     sends = []
@@ -649,26 +630,29 @@
         there = me.any_chip(k)
         head = (there[0] * 2 + there[2]) * group + there[1] // per
         sends.append(send(slabs.at[head], to, (d0, d1), k, there))
+    sends.append(send(yb_ref, nb_ref, (y0, y1), 1, me.plane(1)))
+    sends.append(send(yc_ref, nc_ref, (y0, y1), 2, me.plane(2)))
     chunk = 256
-    attended = ob_ref[...]
+    loads[1].wait()
+    attended = ob_in[...]
     for first in range(0, width, chunk):
         stage[first : first + chunk] = tn_dot(attended[:, first : first + chunk], narrow).astype(BF16)
     parts = stage.reshape(2, zc, 2, 2, width // (8 * zc), width)
     keeps = []
-    for k in range(4):
+    for k, ref in enumerate((va_ref, vb_ref, vc_ref, vd_ref)):
         there = me.plane(k)
-        keeps.append(move(parts.at[there[0], :, there[2]], dw_ref.at[k], ls, 1 + k))
+        keeps.append(move(parts.at[there[0], :, there[2]], ref, ls, 1 + k))
     own.wait()
-    for copy in sends:
+    for copy in sends[:-2]:
         copy.wait()
     half = do_ref.at[:, me.c]
     relay = send(half, half, (b0, b1), 0, me.sibling())
-    for copy in keeps:
+    for copy in keeps + sends[-2:]:
         copy.wait()
     relay.wait()
 
 
-def turn_exchange(zc, c_sum, cotangent, residual, w_out, attn_rows):
+def turn_exchange(zc, c_sum, cotangent, residual, w_out, attn_rows, near):
     chips = 4 * zc
     own, width = cotangent.shape
     heads = width // HEAD_DIM
@@ -678,18 +662,21 @@
         (
             struct((own, width), F32),
             struct((zc, 2, 4, BLOCK, PAIR)),
-            struct((4, zc, 2, width // (8 * zc), width)),
+            *[struct((zc, 2, width // (8 * zc), width))] * 6,
         ),
-        [VM] * 5,
-        (VM, ANY, ANY),
+        [VM] * 3 + [ANY] * 4,
+        (VM,) + (ANY,) * 7,
         [
             pltpu.VMEM((heads, BLOCK, PAIR), BF16),
             pltpu.VMEM((width, width), BF16),
-            DMA((5,)),
+            pltpu.VMEM((width, width), BF16),
+            pltpu.VMEM((own, width), BF16),
+            DMA((7,)),
         ]
         + both(chips)
-        + both(1),
-        (c_sum, cotangent, residual, w_out, attn_rows),
+        + both(1)
+        + both(3),
+        (c_sum, cotangent, residual, w_out, attn_rows, *near),
         2 * 2 * own * width * width,
         8 << 20,
     )
@@ -698,25 +685,31 @@
 def tail_kernel(
     zc,
     d_ref,
-    n_ref,
-    w_ref,
-    x_ref,
-    g_ref,
-    v_ref,
+    n_any,
+    w_any,
+    x_any,
+    g_any,
     f_ref,
     r_ref,
     ya_ref,
     yb_ref,
     yc_ref,
     yd_ref,
+    va_ref,
+    vb_ref,
+    vc_ref,
+    vd_ref,
     tg_ref,
     gw_ref,
     go_ref,
     gf_ref,
     out_ref,
+    n_ref,
+    w_ref,
+    x_ref,
+    g_ref,
     r_in,
     y_in,
-    o_in,
     o_mine,
     o_theirs,
     o_land,
@@ -741,8 +734,6 @@
     w1,
     q0,
     q1,
-    v0,
-    v1,
     f0,
     f1,
 ):
@@ -750,7 +741,7 @@
     chips = 4 * zc
     group, per = landed.shape[:2]
     qw = group * HEAD_DIM
-    meet([me.any_chip(k) for k in range(1, chips)] + [me.sibling()])
+    greet([me.any_chip(k) for k in range(1, chips)] + [me.sibling()])()
     head, place = me.z // per, me.z % per
 
     def slot(k):
@@ -765,9 +756,8 @@
                 move(d_ref.at[:, me.c, slot(k)], mine.at[k], ls, k),
             )
         )
-    o_parts = [move(v_ref.at[0], o_in.at[0], ls, 9)]
-    for k in (3, 1, 2):
-        o_parts.append(send(v_ref.at[k], o_in.at[k], (v0, v1), k, me.plane(k)))
+    given = ((w_any, w_ref), (n_any, n_ref), (g_any, g_ref), (x_any, x_ref))
+    loads = [move(source, target, ls, 20 + i) for i, (source, target) in enumerate(given)]
     f_parts = [move(f_ref.at[pl.ds(2 * me.g, 2)], gf_ref.at[me.g], ls, 10)]
     for k in (3, 1, 2):
         there = me.plane(k)
@@ -775,7 +765,9 @@
         f_parts.append(send(part, gf_ref.at[me.g], (f0, f1), k, there))
     out_parts = [move(r_ref, r_in, ls, 11)]
     for i, ref in enumerate((ya_ref, yb_ref, yc_ref, yd_ref)):
-        out_parts.append(move(ref, y_in.at[i], ls, 12 + i))
+        out_parts.append(move(ref, y_in.at[i, 0], ls, 12 + i))
+    for i, ref in enumerate((va_ref, vb_ref, vc_ref, vd_ref)):
+        out_parts.append(move(ref, y_in.at[i, 1], ls, 16 + i))
     for k, (far, near) in zip(order, halves):
         near.wait()
         far.wait()
@@ -790,12 +782,16 @@
             )
         move(mine.at[k, me.z], landed.at[head, place, k], ls, 4 + k)
 
-    for copy in out_parts:
+    for copy in out_parts + loads:
         copy.wait()
     final = r_in[...]
+    o_sum = jnp.zeros(o_mine.shape, F32)
     for i in range(4):
-        final = final + y_in[i].astype(F32)
+        final = final + y_in[i, 0].astype(F32).reshape(final.shape)
+        o_sum = o_sum + y_in[i, 1].astype(F32)
     out_ref[...] = final.astype(BF16)
+    o_mine[...] = o_sum.astype(BF16)
+    o_swap = send(o_mine.at[:, 1 - me.c], o_theirs, (s0, s1), 1, me.sibling())
 
     def block(step, carry):
         k = 3 - step
@@ -832,20 +828,12 @@
 
         return carry
 
-    lax.fori_loop(0, 3, block, 0)
-    for copy in o_parts:
-        copy.wait()
-    o_sum = o_in[0].astype(F32)
-    for k in range(1, 4):
-        o_sum = o_sum + o_in[k].astype(F32)
-    o_mine[...] = o_sum.astype(BF16)
-    o_swap = send(o_mine.at[:, 1 - me.c], o_theirs, (s0, s1), 1, me.sibling())
     o_swap.wait()
     o_theirs[...] = o_theirs[...] + o_mine[:, me.c]
     sends = [
         send(o_theirs.at[me.z ^ k], o_land.at[k], (q0, q1), k, me.line(k)) for k in range(1, zc)
     ]
-    lax.fori_loop(3, 4, block, 0)
+    lax.fori_loop(0, 4, block, 0)
     width, cols = w_ref.shape
     all_rows = 4 * n_ref.shape[1]
     normed_all = n_ref[...].reshape(all_rows, width)
@@ -899,7 +887,7 @@
     go_ref[...] = o_sum
 
 
-def tail_exchange(zc, group, slab_grads, n_all, weights, tokens, residual_grad, out_grads, shares, residual, outs):
+def tail_exchange(zc, group, slab_grads, n_all, weights, tokens, residual_grad, shares, residual, packs):
     chips = 4 * zc
     per = zc // group
     own, width = tokens.shape
@@ -917,12 +905,15 @@
             struct((4, 2, piece, width)),
             struct((own, width)),
         ),
-        [ANY] + [VM] * 4 + [ANY] * 7,
+        [ANY] * 15,
         (VM, ANY, VM, ANY, VM),
         [
+            pltpu.VMEM((4, own, width), BF16),
+            pltpu.VMEM((width, cols), BF16),
+            pltpu.VMEM((own, width), BF16),
             pltpu.VMEM((own, width), F32),
-            pltpu.VMEM((4, own, width), BF16),
-            pltpu.VMEM((4, zc, 2, piece, width), BF16),
+            pltpu.VMEM((own, width), F32),
+            pltpu.VMEM((4, 2, zc, 2, piece, width), BF16),
             pltpu.VMEM((zc, 2, piece, width), BF16),
             pltpu.VMEM((zc, piece, width), BF16),
             pltpu.VMEM((zc, piece, width), BF16),
@@ -934,7 +925,7 @@
             blocks,
             pltpu.VMEM((chips, 2, piece, cols), BF16),
             pltpu.VMEM((chips, piece, cols), BF16),
-            DMA((16,)),
+            DMA((24,)),
         ]
         + both(4)
         + both(4 * zc)
@@ -942,9 +933,8 @@
         + both(2 + width // 256)
         + both(chips)
         + both(zc)
-        + both(4)
         + both(4),
-        (slab_grads, n_all, weights, tokens, residual_grad, out_grads, shares, residual, *outs),
+        (slab_grads, n_all, weights, tokens, residual_grad, shares, residual, *packs),
         2 * 4 * own * width * cols * 2,
         24 << 20,
     )
@@ -1393,18 +1383,17 @@
     workers = 2 * per_head
     feature_rows = w_query.shape[0]
 
-    n1_all, qkv_w, ffn_own, by_head, *near, w_column = head_exchange(
+    n1_all, qkv_w, ffn_own, by_head, out_mat = head_exchange(
         zc,
         group,
         tokens,
         (w_query, w_key, w_value, w_gate, w_up, w_down, w_out),
-        cotangent,
         (norm1_gain, norm2_gain),
     )
     qkv_w = qkv_w.reshape(width, 3 * group * HEAD_DIM)
 
-    ffn_own, far = lax.optimization_barrier((ffn_own, cotangent))
-    cots = [cotangent] + near + [around(far, 3)]
+    out_mat, sent = lax.optimization_barrier((out_mat.reshape(width, width), cotangent))
+    cots = [cotangent] + [around(sent, k) for k in range(1, 4)]
     ffn_parts = doubling({0: ffn_own}, zc // 2, 2)
     close = along(ffn_own, 1)
 
@@ -1414,21 +1403,22 @@
     o_slabs, *kept = attention_forward(
         workers, anchors, seq_lengths, who, by_head.reshape((slab_count,) + by_head.shape[3:])
     )
-    attn_rows, residual, normed_two, out_mat = join_exchange(
-        zc, heads, o_slabs.reshape(zc, 2, 4, BLOCK, PAIR), tokens, w_column
-    )
-    out_mat = out_mat.reshape(width, width)
+    attn_rows, residual, normed_two = join_exchange(
+        zc, heads, o_slabs.reshape(zc, 2, 4, BLOCK, PAIR), tokens, out_mat
+    )
     *out_parts, c_sum, shares = middle_exchange(
         zc, normed_two, cots, [close] + [ffn_parts[k] for k in range(0, zc, 2)]
     )
     shares = lax.psum_scatter(
         shares.reshape(zc * 2 * 12, feature_rows, width), ("z", "core"), scatter_dimension=0, tiled=True
     )
-    residual_grad, do_heads, out_grads = turn_exchange(
-        zc, c_sum, cotangent, residual, out_mat, attn_rows
-    )
-    do_heads, *out_parts = lax.optimization_barrier((do_heads, *out_parts))
-    outs = [out_parts[0]] + [around(out_parts[k], k) for k in range(1, 4)]
+    residual_grad, do_heads, *packs = turn_exchange(
+        zc, c_sum, cotangent, residual, out_mat, attn_rows, out_parts[1:3]
+    )
+    w_grads, near = packs[:4], packs[4:]
+    do_heads, far = lax.optimization_barrier((do_heads, out_parts[3]))
+    packs = [out_parts[0], *near, around(far, 3), w_grads[0]]
+    packs += [around(w_grads[k], k) for k in range(1, 4)]
     grad_heads = attention_backward(
         workers, anchors, seq_lengths, who, do_heads.reshape(slab_count, BLOCK, PAIR), kept
     )
@@ -1440,10 +1430,9 @@
         qkv_w,
         tokens,
         residual_grad,
-        out_grads,
         shares,
         residual,
-        outs,
+        packs,
     )
     (
         tokens_grad,

time: 359 us -> 351 us (0.978)
  Pallas kernels: 325 us -> 319 us
  waiting for transfers between devices: 8.23 us -> 3.37 us
  starting transfers between devices: 8.17 us -> 12.7 us
    pallas_call x5, Pallas kernels: 256 us -> 243 us  [exchange(): pl.pallas_call(kernel, out_shape=out_shape, in_specs=in_specs, out_specs=...]
    reduce_scatter x1, waiting for transfers between devices: 8.2 us -> 3.33 us  [body(): lax.psum_scatter(shares.reshape(zc * 2 * 12, feature_rows, width), ('z',...]
    ppermute x4 -> x7, starting transfers between devices: 4.38 us -> 8.96 us  [around(): return lax.ppermute(value, ('head', 'y'), [(i, i ^ k) for i in range(4)])]
    pallas_call x1, Pallas kernels: 34.2 us -> 38.3 us  [attention_backward(): pl.pallas_call(functools.partial(backward_kernel, workers), out_shape=str...]
  transfers between devices with their start and end apart: 7 -> 10, of which waited for: 1 -> 1; matrix products, arithmetic and copies ran while one was open for 0% -> 0% of each run, Pallas kernels for 34% -> 35%
where the time goes in v6:
time: 351 us
  Pallas kernels  319 us (91%)
  between operations  14.3 us (4%)
  starting transfers between devices  12.7 us (4%)
    pallas_call x5, Pallas kernels, exchange(): pl.pallas_call(kernel, out_shape=out_shape, in_specs=in_specs, out_specs=...  243 us
    pallas_call x1, Pallas kernels, attention_backward(): pl.pallas_call(functools.partial(backward_kernel, workers), out_shape=str...  38.3 us
    pallas_call x1, Pallas kernels, attention_forward(): pl.pallas_call(functools.partial(forward_kernel, workers), out_shape=(str...  33.1 us
    ppermute x7, starting transfers between devices, around(): return lax.ppermute(value, ('head', 'y'), [(i, i ^ k) for i in range(4)])  8.96 us
  transfers between devices with their start and end apart: 10, of which 1 were waited for; matrix products, arithmetic and copies ran while one was open for 0% of the time, Pallas kernels for 35%

profile of v6, /device:TPU:0, one launch (start us, length us, event | category | flops | bytes accessed | tf_op | source)
XLA Modules:
  0.0 351.2 jit_solution(5623797555117671055)
XLA Ops:
  7.2 0.0 reduce-scatter.2.cloned.1.call-start
  7.2 0.0 copy-start.4
  7.2 0.0 copy-start.5
  7.2 69.8 %shard_map.212 = (bf16[4,256,1024]{2,1,0:T(8,128)(2,1)}, bf16[16,2,32,768]{3,2,1,0:T(8,128)(2,1)}, bf16[2,2,3,32,1024]{4,3,2,1,0:T(8,128)(2,1)}, bf16[4,2,4,384,...) custom-call(bf16[256,1024]{1,0:T(8,128)(2,1)} %x_any.1, f32[32,1024]{1,0:T(8,128)} %q_any.1, f32[32,1024]{1,0:T(8,128)} %k_any.1, ...), custom_call_target="tpu_custom_call" | custom-call | flops 2147483648 | bytes 16777216 | tf_op jit(solution)/shard_map/pallas_call | solution.py:139
  77.0 3.4 collective-permute-start.4
  80.5 0.3 collective-permute-start.3
  80.7 0.0 copy-done.4
  80.7 0.8 collective-permute-start.2
  81.5 0.9 collective-permute-start.1
  82.4 1.8 collective-permute-start
  84.2 0.0 copy-done.5
  84.2 0.1 reshape.66
  84.4 0.6 reshape.67.anchor_ref
  85.0 33.1 %shard_map.213 = (bf16[32,128,128]{2,1,0:T(8,128)(2,1)}, bf16[8192,128]{1,0:T(8,128)(2,1)}, bf16[128,8192]{1,0:T(8,128)(2,1)}, bf16[8,512,128]{2,1,0:T(8,128)(2,...) custom-call(s32[64]{0:T(128)} %reshape.67.anchor_ref, s32[8]{0:T(128)} %lens_ref.3, ...), custom_call_target="tpu_custom_call" | custom-call | flops 4294967296 | bytes 8388608 | tf_op jit(solution)/shard_map/pallas_call | solution.py:1216
  118.1 22.2 %shard_map.214 = (bf16[256,1024]{1,0:T(8,128)(2,1)}, f32[256,1024]{1,0:T(8,128)}, bf16[256,1024]{1,0:T(8,128)(2,1)}) custom-call(bf16[4,2,4,128,128]{4,3,2,1,0:T(8,128)(2,1)} %bitcast.18, bf16[256,1024]{1,0:T(8,128)(2,1)} %x_any.1, bf16[1024,1024]{1,0:T(8,128)(2,1)} %bitcast.13), custom_call_target="tpu_custom_call" | custom-call | tf_op jit(solution)/shard_map/pallas_call | solution.py:139
  140.2 0.0 collective-permute-done.2.cd_ref
  140.2 0.0 copy-start.9
  140.3 0.0 collective-permute-done.1.cc_ref
  140.3 0.0 copy-start.10
  140.3 0.0 collective-permute-done.cb_ref
  140.3 0.0 collective-permute-done.4.rest_2_
  140.3 0.0 copy-start.6
  140.3 0.0 collective-permute-done.3.rest_0_
  140.3 0.0 copy-start.7
  140.3 0.7 copy-done.9
  141.0 0.2 copy-done.10
  141.2 0.3 copy-done.6
  141.5 0.3 copy-done.7
  141.7 52.4 %shard_map.215 = (bf16[4,2,32,1024]{3,2,1,0:T(8,128)(2,1)}, bf16[4,2,32,1024]{3,2,1,0:T(8,128)(2,1)}, bf16[4,2,32,1024]{3,2,1,0:T(8,128)(2,1)}, bf16[4,2,32,1024...) custom-call(bf16[256,1024]{1,0:T(8,128)(2,1)} %get-tuple-element.64.n_ref, ...), custom_call_target="tpu_custom_call" | custom-call | flops 19327352832 | bytes 67108864 | tf_op jit(solution)/shard_map/pallas_call | solution.py:139
  194.2 0.0 reduce-scatter.2.cloned.1.call-update
  194.2 28.6 %shard_map.216 = (f32[256,1024]{1,0:T(8,128)}, bf16[4,2,4,128,128]{4,3,2,1,0:T(8,128)(2,1)}, bf16[4,2,32,1024]{3,2,1,0:T(8,128)(2,1)}, bf16[4,2,32,1024]{3,2,1,0...) custom-call(f32[256,1024]{1,0:T(8,128)} %get-tuple-element.67.c_ref,, ...), custom_call_target="tpu_custom_call" | custom-call | flops 1073741824 | bytes 8388608 | tf_op jit(solution)/shard_map/pallas_call | solution.py:139
  222.8 0.0 copy-done.8
  222.8 2.0 collective-permute-start.5
  224.8 0.8 collective-permute-start.6
  225.6 0.8 collective-permute-start.7
  226.4 1.9 collective-permute-start.8
  228.3 38.3 %shard_map.217 = bf16[32,384,128]{2,1,0:T(8,128)(2,1)} custom-call(s32[64]{0:T(128)} %reshape.67.anchor_ref, s32[8]{0:T(128)} %lens_ref.3, s32[1]{0:T(128)} %bitcast.1.who_ref, bf16[32,128,128]{2,1,0:T(8,128)(2,1)} %bitcast.24, bf16[8192,128]{1,0:T(8,128)(2,1)} %get-tuple-element.75.kv_ref, bf16[128,8192]{1,0:T(8,128)(2,1)} %get-tuple-element.76.kvt_ref, ...), custom_call_target="tpu_custom_call" | custom-call | flops 10737418240 | bytes 8388608 | tf_op jit(solution)/shard_map/pallas_call | solution.py:1328
  266.6 0.0 collective-permute-done.5.yd_ref
  266.6 0.0 collective-permute-done.6.vb_ref
  266.6 0.0 copy-start.1
  266.6 0.0 collective-permute-done.7.vc_ref
  266.7 0.0 copy-start.2
  266.7 0.0 collective-permute-done.8.vd_ref
  266.7 0.0 copy-start.3
  266.7 3.3 reduce-scatter.2.cloned.1.call-done.f_ref.ds_any
  270.0 0.0 copy-done.2
  270.0 69.6 %shard_map.218 = (bf16[256,1024]{1,0:T(8,128)(2,1)}, bf16[4,4,32,768]{3,2,1,0:T(8,128)(2,1)}, f32[32,1024]{1,0:T(8,128)}, bf16[4,2,32,1024]{3,2,1,0:T(8,128)(2,1)}, bf16[256,1024]{1,0:T(8,128)(2,1)}) custom-call(bf16[4,2,4,384,128]{4,3,2,1,0:T(8,128)(2,1)} %bitcast.16, bf16[4,256,1024]{2,1,0:T(8,128)(2,1)} %get-tuple-element.81.n_any, ...), custom_call_target="tpu_custom_call" | custom-call | flops 3221225472 | bytes 25165824 | tf_op jit(solution)/shard_map/pallas_call | solution.py:139
  339.6 4.8 %shard_map.219 = (bf16[256,1024]{1,0:T(8,128)(2,1)}, bf16[256,1024]{1,0:T(8,128)(2,1)}, f32[32,1024]{1,0:T(8,128)}, f32[1,32]{1,0:T(1,128)}, f32[32,1024]{1,0:T(...) custom-call(bf16[256,1024]{1,0:T(8,128)(2,1)} %get-tuple-element.93., ...), custom_call_target="tpu_custom_call" | custom-call | tf_op jit(solution)/shard_map/pallas_call | solution.py:1026
  (6 shorter events, 0.0 us)
Async XLA Ops:
  7.2 262.8 %reduce-scatter.2.cloned.1.call-start = ((), (), s32[]{:S(2)}) async-start(), calls=%async_computation.1 | async-start | bytes 7077888 | tf_op jit(solution)/shard_map/reduce_scatter | solution.py:1412
  7.2 73.5 %copy-start.4 = (bf16[256,1024]{1,0:T(8,128)(2,1)S(1)}, bf16[256,1024]{1,0:T(8,128)(2,1)}, u32[]{:S(2)}) copy-start(bf16[256,1024]{1,0:T(8,128)(2,1)} %t_ref.3) | copy-start | bytes 1572868
  7.2 77.0 %copy-start.5 = (s32[64]{0:T(128)S(1)}, s32[64]{0:T(128)}, u32[]{:S(2)}) copy-start(s32[64]{0:T(128)} %param.24) | copy-start | bytes 772
  77.0 63.3 %collective-permute-start.4 = (bf16[2,2,3,32,1024]{4,3,2,1,0:T(8,128)(2,1)}, bf16[2,2,3,32,1024]{4,3,2,1,0:T(8,128)(2,1)S(1)}, u32[]{:S(2)}, u32[]{:S(2)}) collective-permute-start(bf16[2,2,3,32,1024]{4,3,2,1,0:T(8,128)(2,1)} %get-tuple-element.66.rest_1_), channel_id=1, source_target_pairs={{0,8},{4,12},{8,0},{12,4},{1,9},{5,13},{9,1},{13,5},{2,10},{6,14},... | collective-permute-start | bytes 2359304 | tf_op jit(solution)/shard_map/ppermute | solution.py:1353
  80.5 59.9 %collective-permute-start.3 = (bf16[2,2,3,32,1024]{4,3,2,1,0:T(8,128)(2,1)}, bf16[2,2,3,32,1024]{4,3,2,1,0:T(8,128)(2,1)S(1)}, u32[]{:S(2)}, u32[]{:S(2)}) collective-permute-start(bf16[2,2,3,32,1024]{4,3,2,1,0:T(8,128)(2,1)} %get-tuple-element.66.rest_1_), channel_id=1, source_target_pairs={{0,4},{4,0},{8,12},{12,8},{1,5},{5,1},{9,13},{13,9},{2,6},{6,2},{1... | collective-permute-start | bytes 2359304 | tf_op jit(solution)/shard_map/ppermute | solution.py:1353
  80.7 59.5 %collective-permute-start.2 = (bf16[256,1024]{1,0:T(8,128)(2,1)S(1)}, bf16[256,1024]{1,0:T(8,128)(2,1)S(1)}, u32[]{:S(2)}, u32[]{:S(2)}) collective-permute-start(bf16[256,1024]{1,0:T(8,128)(2,1)S(1)} %copy-done.4), channel_id=1, source_target_pairs={{0,18},{2,16},{16,2},{18,0},{1,19},{3,17},{17,3},{19,1},{4,22},{6,... | collective-permute-start | bytes 1572872 | tf_op jit(solution)/shard_map/ppermute | solution.py:1349
  81.5 58.7 %collective-permute-start.1 = (bf16[256,1024]{1,0:T(8,128)(2,1)S(1)}, bf16[256,1024]{1,0:T(8,128)(2,1)S(1)}, u32[]{:S(2)}, u32[]{:S(2)}) collective-permute-start(bf16[256,1024]{1,0:T(8,128)(2,1)S(1)} %copy-done.4), channel_id=1, source_target_pairs={{0,16},{2,18},{16,0},{18,2},{1,17},{3,19},{17,1},{19,3},{4,20},{6,... | collective-permute-start | bytes 1572872 | tf_op jit(solution)/shard_map/ppermute | solution.py:1349
  82.4 57.8 %collective-permute-start = (bf16[256,1024]{1,0:T(8,128)(2,1)S(1)}, bf16[256,1024]{1,0:T(8,128)(2,1)}, u32[]{:S(2)}, u32[]{:S(2)}) collective-permute-start(bf16[256,1024]{1,0:T(8,128)(2,1)S(1)} %copy-done.4), channel_id=1, source_target_pairs={{0,2},{2,0},{16,18},{18,16},{1,3},{3,1},{17,19},{19,17},{4,6},{6,4... | collective-permute-start | bytes 1572872 | tf_op jit(solution)/shard_map/ppermute | solution.py:1349
  140.2 0.8 copy-start.9
  140.3 0.9 copy-start.10
  140.3 1.2 copy-start.6
  140.3 1.4 copy-start.7
  194.2 28.6 %copy-start.8 = (bf16[4,2,32,1024]{3,2,1,0:T(8,128)(2,1)S(1)}, bf16[4,2,32,1024]{3,2,1,0:T(8,128)(2,1)}, u32[]{:S(2)}) copy-start(bf16[4,2,32,1024]{3,2,1,0:T(8,128)(2,1)} %get-tuple-element.88) | copy-start | bytes 1572868
  222.8 43.8 %collective-permute-start.5 = (bf16[4,2,32,1024]{3,2,1,0:T(8,128)(2,1)S(1)}, bf16[4,2,32,1024]{3,2,1,0:T(8,128)(2,1)S(1)}, u32[]{:S(2)}, u32[]{:S(2)}) collective-permute-start(bf16[4,2,32,1024]{3,2,1,0:T(8,128)(2,1)S(1)} %copy-done.8), channel_id=1, source_target_pairs={{0,18},{2,16},{16,2},{18,0},{1,19},{3,17},{17,3},{19,1},{4,22},{6,... | collective-permute-start | bytes 1572872 | tf_op jit(solution)/shard_map/ppermute | solution.py:1349
  224.8 41.8 %collective-permute-start.6 = (bf16[4,2,32,1024]{3,2,1,0:T(8,128)(2,1)}, bf16[4,2,32,1024]{3,2,1,0:T(8,128)(2,1)S(1)}, u32[]{:S(2)}, u32[]{:S(2)}) collective-permute-start(bf16[4,2,32,1024]{3,2,1,0:T(8,128)(2,1)} %get-tuple-element.90), channel_id=1, source_target_pairs={{0,2},{2,0},{16,18},{18,16},{1,3},{3,1},{17,19},{19,17},{4,6},{6,4... | collective-permute-start | bytes 1572872 | tf_op jit(solution)/shard_map/ppermute | solution.py:1349
  225.6 41.0 %collective-permute-start.7 = (bf16[4,2,32,1024]{3,2,1,0:T(8,128)(2,1)}, bf16[4,2,32,1024]{3,2,1,0:T(8,128)(2,1)S(1)}, u32[]{:S(2)}, u32[]{:S(2)}) collective-permute-start(bf16[4,2,32,1024]{3,2,1,0:T(8,128)(2,1)} %get-tuple-element.91), channel_id=1, source_target_pairs={{0,16},{2,18},{16,0},{18,2},{1,17},{3,19},{17,1},{19,3},{4,20},{6,... | collective-permute-start | bytes 1572872 | tf_op jit(solution)/shard_map/ppermute | solution.py:1349
  226.4 40.3 %collective-permute-start.8 = (bf16[4,2,32,1024]{3,2,1,0:T(8,128)(2,1)}, bf16[4,2,32,1024]{3,2,1,0:T(8,128)(2,1)S(1)}, u32[]{:S(2)}, u32[]{:S(2)}) collective-permute-start(bf16[4,2,32,1024]{3,2,1,0:T(8,128)(2,1)} %get-tuple-element.92), channel_id=1, source_target_pairs={{0,18},{2,16},{16,2},{18,0},{1,19},{3,17},{17,3},{19,1},{4,22},{6,... | collective-permute-start | bytes 1572872 | tf_op jit(solution)/shard_map/ppermute | solution.py:1349
  266.6 3.4 copy-start
  266.6 3.4 copy-start.1
  266.7 3.4 copy-start.2
  266.7 3.4 copy-start.3
Sparse Core Ops, SparseCore 0:
  194.3 75.6 reduce-scatter.1

commit v7 on v6

--- a/solution.py
+++ b/solution.py
@@ -440,7 +440,7 @@
 def middle_kernel(zc, n_ref, ca_ref, cb_ref, cc_ref, cd_ref, *rest):
     f_refs, rest = rest[: zc // 2 + 1], rest[zc // 2 + 1 :]
     oa_ref, ob_ref, oc_ref, od_ref, cs_ref, sh_ref, rows, cots, gate_w, up_w, down_w, *rest = rest
-    hid, dgate, dup, c_out, c_in, stage, o_out, ls, n0, n1, c0, c1, f0, f1, h0, h1 = rest
+    hid, dgate, dup, c_out, c_in, passed, stage, o_out, ls, n0, n1, c0, c1, f0, f1, h0, h1 = rest
     me = Place(zc)
     width = n_ref.shape[1]
     met = greet([me.plane(k) for k in range(1, 4)] + [me.line(1), me.sibling()])
@@ -475,6 +475,19 @@
     for copy in loads:
         copy.wait()
     square = (width, width)
+    half = n_ref.shape[0] // 2
+    upper, lower = pl.ds(0, half), pl.ds(half, half)
+    c_sems = (c0, c1)
+    far_parts = [
+        trip(c_out.at[3, upper], passed.at[0], c_sems, 0, me.plane(2)),
+        trip(c_out.at[3, lower], passed.at[1], c_sems, 1, me.plane(1)),
+    ]
+    near_parts = [
+        trip(c_out.at[1, lower], c_in.at[0, lower], c_sems, 2, me.plane(1)),
+        trip(c_out.at[2, upper], c_in.at[1, upper], c_sems, 3, me.plane(2)),
+        trip(c_out.at[1, upper], c_in.at[0, upper], c_sems, 4, me.plane(1)),
+        trip(c_out.at[2, lower], c_in.at[1, lower], c_sems, 5, me.plane(2)),
+    ]
 
     def block(step, carry):
         k = jnp.where(step == 0, 3, jnp.where(step == 3, 0, step))
@@ -494,13 +507,28 @@
         dup[k] = (back * soft).astype(BF16)
         c_out[k] = (nt_dot(dgate[k], gate_mat) + nt_dot(dup[k], up_mat)).astype(BF16)
 
-        @pl.when(step < 3)
+        @pl.when(step == 0)
         def _():
-            trip(c_out.at[k], c_in.at[k], (c0, c1), k, me.plane(k)).start()
+            for copy in far_parts:
+                copy.start()
+
+        @pl.when(step == 1)
+        def _():
+            near_parts[0].start()
+
+        @pl.when(step == 2)
+        def _():
+            near_parts[1].start()
 
         return carry
 
     lax.fori_loop(0, 4, block, 0)
+    far_parts[0].wait_recv()
+    c_out[1, upper] = c_out[1, upper] + passed[0]
+    near_parts[2].start()
+    far_parts[1].wait_recv()
+    c_out[2, lower] = c_out[2, lower] + passed[1]
+    near_parts[3].start()
     all_rows = (4 * n_ref.shape[0], width)
 
     def weight_grad(left, right, slot):
@@ -533,11 +561,11 @@
     for k, ref in enumerate((oa_ref, ob_ref, oc_ref, od_ref)):
         o_out[k] = dot(hid[k], down_w[...].reshape(square)).astype(BF16).reshape(ref.shape)
         shares.append(move(o_out.at[k], ref, ls, k))
-    total = c_out[0].astype(F32)
-    for k in range(1, 4):
-        trip(c_out.at[k], c_in.at[k], (c0, c1), k, me.plane(k)).wait()
-        total = total + c_in[k].astype(F32)
-    cs_ref[...] = total
+    for copy in far_parts:
+        copy.wait_send()
+    for copy in near_parts:
+        copy.wait()
+    cs_ref[...] = c_out[0].astype(F32) + c_in[0].astype(F32) + c_in[1].astype(F32)
     for copy in shares:
         copy.wait()
     for copy in near_rows:
@@ -560,10 +588,11 @@
         [ANY] * (5 + len(weights)),
         (ANY,) * 4 + (VM, ANY),
         [blocks, blocks, wide, wide, pltpu.VMEM((zc, 2, 2, 2, piece, width), BF16)]
-        + [blocks] * 5
+        + [blocks] * 4
+        + [pltpu.VMEM((2, own, width), BF16), pltpu.VMEM((2, own // 2, width), BF16)]
         + [pltpu.VMEM((3, width, width), BF16), pltpu.VMEM((4, zc, 2, piece, width), BF16), DMA((21 + 3 * zc,))]
         + both(4)
-        + both(4)
+        + both(6)
         + both(3 * zc)
         + both(3 * zc),
         (normed, *cots, *weights),

time: 351 us -> 345 us (0.983)
  Pallas kernels: 319 us -> 311 us
    pallas_call x5, Pallas kernels: 243 us -> 238 us  [exchange(): pl.pallas_call(kernel, out_shape=out_shape, in_specs=in_specs, out_specs=...]
  transfers between devices with their start and end apart: 10 -> 10, of which waited for: 1 -> 1; matrix products, arithmetic and copies ran while one was open for 0% -> 0% of each run, Pallas kernels for 35% -> 34%
where the time goes in v7:
time: 345 us
  Pallas kernels  311 us (90%)
  between operations  14.3 us (4%)
  starting transfers between devices  12 us (3%)
  waiting for transfers between devices  5.33 us (2%)
    pallas_call x5, Pallas kernels, exchange(): pl.pallas_call(kernel, out_shape=out_shape, in_specs=in_specs, out_specs=...  238 us
    pallas_call x1, Pallas kernels, attention_backward(): pl.pallas_call(functools.partial(backward_kernel, workers), out_shape=str...  36.6 us
    pallas_call x1, Pallas kernels, attention_forward(): pl.pallas_call(functools.partial(forward_kernel, workers), out_shape=(str...  31.7 us
    ppermute x7, starting transfers between devices, around(): return lax.ppermute(value, ('head', 'y'), [(i, i ^ k) for i in range(4)])  8.3 us
  transfers between devices with their start and end apart: 10, of which 1 were waited for; matrix products, arithmetic and copies ran while one was open for 0% of the time, Pallas kernels for 34%

profile of v7, /device:TPU:0, one launch (start us, length us, event | category | flops | bytes accessed | tf_op | source)
XLA Modules:
  0.0 344.8 jit_solution(7367193693200453081)
XLA Ops:
  7.2 0.0 reduce-scatter.2.cloned.1.call-start
  7.2 0.0 copy-start.4
  7.2 0.0 copy-start.5
  7.2 69.8 %shard_map.212 = (bf16[4,256,1024]{2,1,0:T(8,128)(2,1)}, bf16[16,2,32,768]{3,2,1,0:T(8,128)(2,1)}, bf16[2,2,3,32,1024]{4,3,2,1,0:T(8,128)(2,1)}, bf16[4,2,4,384,...) custom-call(bf16[256,1024]{1,0:T(8,128)(2,1)} %x_any.1, f32[32,1024]{1,0:T(8,128)} %q_any.1, f32[32,1024]{1,0:T(8,128)} %k_any.1, ...), custom_call_target="tpu_custom_call" | custom-call | flops 2147483648 | bytes 16777216 | tf_op jit(solution)/shard_map/pallas_call | solution.py:139
  77.0 3.4 collective-permute-start.4
  80.5 0.3 collective-permute-start.3
  80.7 0.0 copy-done.4
  80.7 0.8 collective-permute-start.2
  81.5 0.9 collective-permute-start.1
  82.4 1.8 collective-permute-start
  84.2 0.0 copy-done.5
  84.2 0.1 reshape.66
  84.4 0.6 reshape.67.anchor_ref
  85.0 31.7 %shard_map.213 = (bf16[32,128,128]{2,1,0:T(8,128)(2,1)}, bf16[8192,128]{1,0:T(8,128)(2,1)}, bf16[128,8192]{1,0:T(8,128)(2,1)}, bf16[8,512,128]{2,1,0:T(8,128)(2,...) custom-call(s32[64]{0:T(128)} %reshape.67.anchor_ref, s32[8]{0:T(128)} %lens_ref.3, ...), custom_call_target="tpu_custom_call" | custom-call | flops 4294967296 | bytes 8388608 | tf_op jit(solution)/shard_map/pallas_call | solution.py:1245
  116.7 22.2 %shard_map.214 = (bf16[256,1024]{1,0:T(8,128)(2,1)}, f32[256,1024]{1,0:T(8,128)}, bf16[256,1024]{1,0:T(8,128)(2,1)}) custom-call(bf16[4,2,4,128,128]{4,3,2,1,0:T(8,128)(2,1)} %bitcast.18, bf16[256,1024]{1,0:T(8,128)(2,1)} %x_any.1, bf16[1024,1024]{1,0:T(8,128)(2,1)} %bitcast.13), custom_call_target="tpu_custom_call" | custom-call | tf_op jit(solution)/shard_map/pallas_call | solution.py:139
  138.9 0.0 collective-permute-done.2.cd_ref
  138.9 0.0 copy-start.9
  139.0 0.0 collective-permute-done.1.cc_ref
  139.0 0.0 copy-start.10
  139.0 0.0 collective-permute-done.cb_ref
  139.0 0.0 collective-permute-done.4.rest_2_
  139.0 0.0 copy-start.6
  139.0 0.0 collective-permute-done.3.rest_0_
  139.0 0.7 copy-done.9
  139.7 0.2 copy-done.10
  139.9 0.3 copy-done.6
  140.2 0.3 copy-done.7
  140.4 47.8 %shard_map.215 = (bf16[4,2,32,1024]{3,2,1,0:T(8,128)(2,1)}, bf16[4,2,32,1024]{3,2,1,0:T(8,128)(2,1)}, bf16[4,2,32,1024]{3,2,1,0:T(8,128)(2,1)}, bf16[4,2,32,1024...) custom-call(bf16[256,1024]{1,0:T(8,128)(2,1)} %get-tuple-element.64.n_ref, ...), custom_call_target="tpu_custom_call" | custom-call | flops 19327352832 | bytes 67108864 | tf_op jit(solution)/shard_map/pallas_call | solution.py:139
  188.3 0.0 reduce-scatter.2.cloned.1.call-update
  188.3 0.0 copy-start.8
  188.3 28.2 %shard_map.216 = (f32[256,1024]{1,0:T(8,128)}, bf16[4,2,4,128,128]{4,3,2,1,0:T(8,128)(2,1)}, bf16[4,2,32,1024]{3,2,1,0:T(8,128)(2,1)}, bf16[4,2,32,1024]{3,2,1,0...) custom-call(f32[256,1024]{1,0:T(8,128)} %get-tuple-element.67.c_ref,, ...), custom_call_target="tpu_custom_call" | custom-call | flops 1073741824 | bytes 8388608 | tf_op jit(solution)/shard_map/pallas_call | solution.py:139
  216.5 1.3 collective-permute-start.5
  217.8 0.7 collective-permute-start.6
  218.6 1.5 collective-permute-start.7
  220.1 1.2 collective-permute-start.8
  221.3 36.6 %shard_map.217 = bf16[32,384,128]{2,1,0:T(8,128)(2,1)} custom-call(s32[64]{0:T(128)} %reshape.67.anchor_ref, s32[8]{0:T(128)} %lens_ref.3, s32[1]{0:T(128)} %bitcast.1.who_ref, bf16[32,128,128]{2,1,0:T(8,128)(2,1)} %bitcast.24, bf16[8192,128]{1,0:T(8,128)(2,1)} %get-tuple-element.75.kv_ref, bf16[128,8192]{1,0:T(8,128)(2,1)} %get-tuple-element.76.kvt_ref, ...), custom_call_target="tpu_custom_call" | custom-call | flops 10737418240 | bytes 8388608 | tf_op jit(solution)/shard_map/pallas_call | solution.py:1357
  258.0 0.0 collective-permute-done.5.yd_ref
  258.0 0.0 collective-permute-done.6.vb_ref
  258.0 0.0 copy-start.1
  258.0 0.0 collective-permute-done.7.vc_ref
  258.0 0.0 copy-start.2
  258.0 0.0 collective-permute-done.8.vd_ref
  258.0 0.0 copy-start.3
  258.0 5.3 %reduce-scatter.2.cloned.1.call-done.f_ref.ds_any = bf16[12,32,1024]{2,1,0:T(8,128)(2,1)} async-done(((bf16[96,32,1024]{2,1,0:T(8,128)(2,1)}), bf16[12,32,1024]{2,1,0:T(8,128)(2,1)}) %reduce-scatter.2.cloned.1.call-update) | async-done | bytes 786448 | tf_op jit(solution)/shard_map/reduce_scatter | solution.py:1441
  263.3 0.0 copy-done
  263.3 0.0 copy-done.2
  263.3 69.8 %shard_map.218 = (bf16[256,1024]{1,0:T(8,128)(2,1)}, bf16[4,4,32,768]{3,2,1,0:T(8,128)(2,1)}, f32[32,1024]{1,0:T(8,128)}, bf16[4,2,32,1024]{3,2,1,0:T(8,128)(2,1)}, bf16[256,1024]{1,0:T(8,128)(2,1)}) custom-call(bf16[4,2,4,384,128]{4,3,2,1,0:T(8,128)(2,1)} %bitcast.16, bf16[4,256,1024]{2,1,0:T(8,128)(2,1)} %get-tuple-element.81.n_any, ...), custom_call_target="tpu_custom_call" | custom-call | flops 3221225472 | bytes 25165824 | tf_op jit(solution)/shard_map/pallas_call | solution.py:139
  333.2 4.8 %shard_map.219 = (bf16[256,1024]{1,0:T(8,128)(2,1)}, bf16[256,1024]{1,0:T(8,128)(2,1)}, f32[32,1024]{1,0:T(8,128)}, f32[1,32]{1,0:T(1,128)}, f32[32,1024]{1,0:T(...) custom-call(bf16[256,1024]{1,0:T(8,128)(2,1)} %get-tuple-element.93., ...), custom_call_target="tpu_custom_call" | custom-call | tf_op jit(solution)/shard_map/pallas_call | solution.py:1055
  (6 shorter events, 0.0 us)
Async XLA Ops:
  7.2 256.2 %reduce-scatter.2.cloned.1.call-start = ((), (), s32[]{:S(2)}) async-start(), calls=%async_computation.1 | async-start | bytes 7077888 | tf_op jit(solution)/shard_map/reduce_scatter | solution.py:1441
  7.2 73.5 %copy-start.4 = (bf16[256,1024]{1,0:T(8,128)(2,1)S(1)}, bf16[256,1024]{1,0:T(8,128)(2,1)}, u32[]{:S(2)}) copy-start(bf16[256,1024]{1,0:T(8,128)(2,1)} %t_ref.3) | copy-start | bytes 1572868
  7.2 77.0 %copy-start.5 = (s32[64]{0:T(128)S(1)}, s32[64]{0:T(128)}, u32[]{:S(2)}) copy-start(s32[64]{0:T(128)} %param.24) | copy-start | bytes 772
  77.0 62.0 %collective-permute-start.4 = (bf16[2,2,3,32,1024]{4,3,2,1,0:T(8,128)(2,1)}, bf16[2,2,3,32,1024]{4,3,2,1,0:T(8,128)(2,1)S(1)}, u32[]{:S(2)}, u32[]{:S(2)}) collective-permute-start(bf16[2,2,3,32,1024]{4,3,2,1,0:T(8,128)(2,1)} %get-tuple-element.66.rest_1_), channel_id=1, source_target_pairs={{0,8},{4,12},{8,0},{12,4},{1,9},{5,13},{9,1},{13,5},{2,10},{6,14},... | collective-permute-start | bytes 2359304 | tf_op jit(solution)/shard_map/ppermute | solution.py:1382
  80.5 58.6 %collective-permute-start.3 = (bf16[2,2,3,32,1024]{4,3,2,1,0:T(8,128)(2,1)}, bf16[2,2,3,32,1024]{4,3,2,1,0:T(8,128)(2,1)S(1)}, u32[]{:S(2)}, u32[]{:S(2)}) collective-permute-start(bf16[2,2,3,32,1024]{4,3,2,1,0:T(8,128)(2,1)} %get-tuple-element.66.rest_1_), channel_id=1, source_target_pairs={{0,4},{4,0},{8,12},{12,8},{1,5},{5,1},{9,13},{13,9},{2,6},{6,2},{1... | collective-permute-start | bytes 2359304 | tf_op jit(solution)/shard_map/ppermute | solution.py:1382
  80.7 58.2 %collective-permute-start.2 = (bf16[256,1024]{1,0:T(8,128)(2,1)S(1)}, bf16[256,1024]{1,0:T(8,128)(2,1)S(1)}, u32[]{:S(2)}, u32[]{:S(2)}) collective-permute-start(bf16[256,1024]{1,0:T(8,128)(2,1)S(1)} %copy-done.4), channel_id=1, source_target_pairs={{0,18},{2,16},{16,2},{18,0},{1,19},{3,17},{17,3},{19,1},{4,22},{6,... | collective-permute-start | bytes 1572872 | tf_op jit(solution)/shard_map/ppermute | solution.py:1378
  81.5 57.4 %collective-permute-start.1 = (bf16[256,1024]{1,0:T(8,128)(2,1)S(1)}, bf16[256,1024]{1,0:T(8,128)(2,1)S(1)}, u32[]{:S(2)}, u32[]{:S(2)}) collective-permute-start(bf16[256,1024]{1,0:T(8,128)(2,1)S(1)} %copy-done.4), channel_id=1, source_target_pairs={{0,16},{2,18},{16,0},{18,2},{1,17},{3,19},{17,1},{19,3},{4,20},{6,... | collective-permute-start | bytes 1572872 | tf_op jit(solution)/shard_map/ppermute | solution.py:1378
  82.4 56.5 %collective-permute-start = (bf16[256,1024]{1,0:T(8,128)(2,1)S(1)}, bf16[256,1024]{1,0:T(8,128)(2,1)}, u32[]{:S(2)}, u32[]{:S(2)}) collective-permute-start(bf16[256,1024]{1,0:T(8,128)(2,1)S(1)} %copy-done.4), channel_id=1, source_target_pairs={{0,2},{2,0},{16,18},{18,16},{1,3},{3,1},{17,19},{19,17},{4,6},{6,4... | collective-permute-start | bytes 1572872 | tf_op jit(solution)/shard_map/ppermute | solution.py:1378
  138.9 0.8 copy-start.9
  139.0 0.9 copy-start.10
  139.0 1.2 copy-start.6
  139.0 1.4 copy-start.7
  188.3 28.2 %copy-start.8 = (bf16[4,2,32,1024]{3,2,1,0:T(8,128)(2,1)S(1)}, bf16[4,2,32,1024]{3,2,1,0:T(8,128)(2,1)}, u32[]{:S(2)}) copy-start(bf16[4,2,32,1024]{3,2,1,0:T(8,128)(2,1)} %get-tuple-element.88) | copy-start | bytes 1572868
  216.5 41.5 %collective-permute-start.5 = (bf16[4,2,32,1024]{3,2,1,0:T(8,128)(2,1)S(1)}, bf16[4,2,32,1024]{3,2,1,0:T(8,128)(2,1)S(1)}, u32[]{:S(2)}, u32[]{:S(2)}) collective-permute-start(bf16[4,2,32,1024]{3,2,1,0:T(8,128)(2,1)S(1)} %copy-done.8), channel_id=1, source_target_pairs={{0,18},{2,16},{16,2},{18,0},{1,19},{3,17},{17,3},{19,1},{4,22},{6,... | collective-permute-start | bytes 1572872 | tf_op jit(solution)/shard_map/ppermute | solution.py:1378
  217.8 40.1 %collective-permute-start.6 = (bf16[4,2,32,1024]{3,2,1,0:T(8,128)(2,1)}, bf16[4,2,32,1024]{3,2,1,0:T(8,128)(2,1)S(1)}, u32[]{:S(2)}, u32[]{:S(2)}) collective-permute-start(bf16[4,2,32,1024]{3,2,1,0:T(8,128)(2,1)} %get-tuple-element.90), channel_id=1, source_target_pairs={{0,2},{2,0},{16,18},{18,16},{1,3},{3,1},{17,19},{19,17},{4,6},{6,4... | collective-permute-start | bytes 1572872 | tf_op jit(solution)/shard_map/ppermute | solution.py:1378
  218.6 39.4 %collective-permute-start.7 = (bf16[4,2,32,1024]{3,2,1,0:T(8,128)(2,1)}, bf16[4,2,32,1024]{3,2,1,0:T(8,128)(2,1)S(1)}, u32[]{:S(2)}, u32[]{:S(2)}) collective-permute-start(bf16[4,2,32,1024]{3,2,1,0:T(8,128)(2,1)} %get-tuple-element.91), channel_id=1, source_target_pairs={{0,16},{2,18},{16,0},{18,2},{1,17},{3,19},{17,1},{19,3},{4,20},{6,... | collective-permute-start | bytes 1572872 | tf_op jit(solution)/shard_map/ppermute | solution.py:1378
  220.1 37.9 %collective-permute-start.8 = (bf16[4,2,32,1024]{3,2,1,0:T(8,128)(2,1)}, bf16[4,2,32,1024]{3,2,1,0:T(8,128)(2,1)S(1)}, u32[]{:S(2)}, u32[]{:S(2)}) collective-permute-start(bf16[4,2,32,1024]{3,2,1,0:T(8,128)(2,1)} %get-tuple-element.92), channel_id=1, source_target_pairs={{0,18},{2,16},{16,2},{18,0},{1,19},{3,17},{17,3},{19,1},{4,22},{6,... | collective-permute-start | bytes 1572872 | tf_op jit(solution)/shard_map/ppermute | solution.py:1378
  258.0 5.4 %copy-start = (bf16[4,2,32,1024]{3,2,1,0:T(8,128)(2,1)}, bf16[4,2,32,1024]{3,2,1,0:T(8,128)(2,1)S(1)}, u32[]{:S(2)}) copy-start(bf16[4,2,32,1024]{3,2,1,0:T(8,128)(2,1)S(1)} %collective-permute-done.5.yd_ref) | copy-start | bytes 1572868
  258.0 5.3 %copy-start.1 = (bf16[4,2,32,1024]{3,2,1,0:T(8,128)(2,1)}, bf16[4,2,32,1024]{3,2,1,0:T(8,128)(2,1)S(1)}, u32[]{:S(2)}) copy-start(bf16[4,2,32,1024]{3,2,1,0:T(8,128)(2,1)S(1)} %collective-permute-done.6.vb_ref) | copy-start | bytes 1572868
  258.0 5.3 %copy-start.2 = (bf16[4,2,32,1024]{3,2,1,0:T(8,128)(2,1)}, bf16[4,2,32,1024]{3,2,1,0:T(8,128)(2,1)S(1)}, u32[]{:S(2)}) copy-start(bf16[4,2,32,1024]{3,2,1,0:T(8,128)(2,1)S(1)} %collective-permute-done.7.vc_ref) | copy-start | bytes 1572868
  258.0 5.3 %copy-start.3 = (bf16[4,2,32,1024]{3,2,1,0:T(8,128)(2,1)}, bf16[4,2,32,1024]{3,2,1,0:T(8,128)(2,1)S(1)}, u32[]{:S(2)}) copy-start(bf16[4,2,32,1024]{3,2,1,0:T(8,128)(2,1)S(1)} %collective-permute-done.8.vd_ref) | copy-start | bytes 1572868
Sparse Core Ops, SparseCore 0:
  188.4 74.8 reduce-scatter.1

commit v8 on v7

--- a/solution.py
+++ b/solution.py
@@ -372,10 +372,11 @@
     )
 
 
-def join_kernel(zc, s_ref, x_ref, w_ref, ob_ref, r_ref, n_ref, mine, theirs, slabs, ls, b0, b1, c0, c1):
+def join_kernel(zc, s_ref, x_ref, w_ref, ob_ref, r_ref, n_ref, mine, theirs, slabs, x_in, w_in, ls, b0, b1, c0, c1):
     me = Place(zc)
     chips = 4 * zc
     heads, per = slabs.shape[:2]
+    loads = [move(w_ref, w_in, ls, 2), move(x_ref, x_in, ls, 3)]
     greet([me.any_chip(k) for k in range(1, chips)] + [me.sibling()])()
     other = send(s_ref.at[:, 1 - me.c], theirs, (b0, b1), 0, me.sibling())
     own = move(s_ref.at[:, me.c], mine, ls, 0)
@@ -406,7 +407,9 @@
             ob_ref[block * BLOCK : (block + 1) * BLOCK, lanes(pair)] = pair_up(
                 sides[0], block, sides[1], block
             ).astype(BF16)
-    residual = x_ref[...].astype(F32) + dot(ob_ref[...], w_ref[...])
+    for copy in loads:
+        copy.wait()
+    residual = x_in[...].astype(F32) + dot(ob_ref[...], w_in[...])
     r_ref[...] = residual
     mean = jnp.mean(residual * residual, axis=-1, keepdims=True)
     n_ref[...] = (residual * lax.rsqrt(mean + EPS)).astype(BF16)
@@ -421,13 +424,15 @@
         functools.partial(join_kernel, zc),
         2,
         (struct(shape), struct(shape, F32), struct(shape)),
-        [ANY, VM, VM],
+        [ANY, ANY, ANY],
         (VM,) * 3,
         [
             pltpu.VMEM(half, BF16),
             pltpu.VMEM(half, BF16),
             pltpu.VMEM((heads, per) + slabs.shape[3:], BF16),
-            DMA((2,)),
+            pltpu.VMEM(shape, BF16),
+            pltpu.VMEM(w_out.shape, BF16),
+            DMA((4,)),
         ]
         + both(1)
         + both(chips),
@@ -1163,8 +1168,32 @@
 
 
 def forward_kernel(
-    workers, anchor_ref, lens_ref, who_ref, a_ref, o_ref, kv_ref, kvt_ref, q_ref, qt_ref, ot_ref, l_ref, inv, mine, raw
+    workers,
+    anchor_ref,
+    lens_ref,
+    who_ref,
+    a_any,
+    o_ref,
+    kv_any,
+    kvt_any,
+    q_any,
+    qt_any,
+    ot_any,
+    l_any,
+    inv,
+    mine,
+    raw,
+    a_ref,
+    kv_ref,
+    kvt_ref,
+    q_ref,
+    qt_ref,
+    ot_ref,
+    l_ref,
+    ls,
+    ts,
 ):
+    load = move(a_any, a_ref, ls, 0)
     blocks = anchor_ref.shape[0]
     turns = qt_ref.shape[0]
     per = QTILE // BLOCK
@@ -1173,6 +1202,7 @@
     note_tiles(workers, worker, turns * workers, lens_ref, mine)
     o_ref[...] = jnp.zeros_like(o_ref)
     same = selection(PAIR, PAIR, 0)
+    load.wait()
 
     def order(step, carry):
         for b in range(per):
@@ -1184,6 +1214,7 @@
         return carry
 
     lax.fori_loop(0, blocks // per, order, 0)
+    leaving = [move(kv_ref, kv_any, ls, 1)]
 
     def flip(step, carry):
         at = pl.ds(pl.multiple_of(step * TURNED, TURNED), TURNED)
@@ -1191,6 +1222,12 @@
         return carry
 
     lax.fori_loop(0, blocks * BLOCK // TURNED, flip, 0)
+    leaving.append(move(kvt_ref, kvt_any, ls, 2))
+    kept = ((q_ref, q_any), (qt_ref, qt_any), (ot_ref, ot_any), (l_ref, l_any))
+
+    def leave(turn, i):
+        source, target = kept[i]
+        return pltpu.make_async_copy(source.at[turn], target.at[turn], ts.at[i, turn])
 
     def one_tile(turn, carry):
         tile = mine[turn]
@@ -1228,6 +1265,8 @@
         out = acc / total
         ot_ref[turn] = out
         l_ref[turn] = top + jnp.log(total)
+        for i in range(4):
+            leave(turn, i).start()
         wide = tn_dot(out.astype(BF16), unfold(HEAD_DIM, PAIR, 0)).astype(BF16)
         for b in range(per):
             where = inv[tile * per + b]
@@ -1236,6 +1275,15 @@
         return carry
 
     lax.fori_loop(0, turns, one_tile, 0)
+
+    def left(turn, carry):
+        for i in range(4):
+            leave(turn, i).wait()
+        return carry
+
+    lax.fori_loop(0, turns, left, 0)
+    for copy in leaving:
+        copy.wait()
 
 
 def attention_forward(workers, anchors, lengths, who, packed):
@@ -1253,12 +1301,21 @@
             struct((turns, HEAD_DIM, QTILE), F32),
             struct((turns, 1, QTILE), F32),
         ),
-        in_specs=[SM, SM, SM, VM],
-        out_specs=(VM,) * 7,
+        in_specs=[SM, SM, SM, ANY],
+        out_specs=(VM,) + (ANY,) * 6,
         scratch_shapes=[
             pltpu.SMEM((2 * slabs,), jnp.int32),
             pltpu.SMEM((turns,), jnp.int32),
             pltpu.VMEM((QTILE, PAIR), BF16),
+            pltpu.VMEM(packed.shape, BF16),
+            pltpu.VMEM((rows, PAIR), BF16),
+            pltpu.VMEM((PAIR, rows), BF16),
+            pltpu.VMEM((turns, QTILE, PAIR), BF16),
+            pltpu.VMEM((turns, PAIR, QTILE), BF16),
+            pltpu.VMEM((turns, HEAD_DIM, QTILE), F32),
+            pltpu.VMEM((turns, 1, QTILE), F32),
+            DMA((3,)),
+            DMA((4, turns)),
         ],
         compiler_params=pltpu.CompilerParams(vmem_limit_bytes=60 << 20),
         cost_estimate=pl.CostEstimate(

time: 345 us -> 343 us (level)
  no operation moved by 1% of the time
where the time goes in v8:
time: 343 us
  Pallas kernels  310 us (90%)
  between operations  14.3 us (4%)
  starting transfers between devices  12 us (3%)
  waiting for transfers between devices  3.85 us (1%)
    pallas_call x5, Pallas kernels, exchange(): pl.pallas_call(kernel, out_shape=out_shape, in_specs=in_specs, out_specs=...  236 us
    pallas_call x1, Pallas kernels, attention_backward(): pl.pallas_call(functools.partial(backward_kernel, workers), out_shape=str...  38.3 us
    pallas_call x1, Pallas kernels, attention_forward(): pl.pallas_call(functools.partial(forward_kernel, workers), out_shape=(str...  31 us
    ppermute x7, starting transfers between devices, around(): return lax.ppermute(value, ('head', 'y'), [(i, i ^ k) for i in range(4)])  8.21 us
  transfers between devices with their start and end apart: 10, of which 1 were waited for; matrix products, arithmetic and copies ran while one was open for 0% of the time, Pallas kernels for 34%

profile of v8, /device:TPU:0, one launch (start us, length us, event | category | flops | bytes accessed | tf_op | source)
XLA Modules:
  0.0 342.6 jit_solution(16778053367786899871)
XLA Ops:
  7.2 0.0 reduce-scatter.2.cloned.1.call-start
  7.2 0.0 copy-start.4
  7.2 0.0 copy-start.5
  7.2 69.8 %shard_map.212 = (bf16[4,256,1024]{2,1,0:T(8,128)(2,1)}, bf16[16,2,32,768]{3,2,1,0:T(8,128)(2,1)}, bf16[2,2,3,32,1024]{4,3,2,1,0:T(8,128)(2,1)}, bf16[4,2,4,384,...) custom-call(bf16[256,1024]{1,0:T(8,128)(2,1)} %x_any.1, f32[32,1024]{1,0:T(8,128)} %q_any.1, f32[32,1024]{1,0:T(8,128)} %k_any.1, ...), custom_call_target="tpu_custom_call" | custom-call | flops 2147483648 | bytes 16777216 | tf_op jit(solution)/shard_map/pallas_call | solution.py:139
  77.0 3.4 %collective-permute-start.4 = (bf16[2,2,3,32,1024]{4,3,2,1,0:T(8,128)(2,1)}, bf16[2,2,3,32,1024]{4,3,2,1,0:T(8,128)(2,1)S(1)}, u32[]{:S(2)}, u32[]{:S(2)}) collective-permute-start(bf16[2,2,3,32,1024]{4,3,2,1,0:T(8,128)(2,1)} %get-tuple-element.66.rest_1_), channel_id=1, source_target_pairs={{0,8},{4,12},{8,0},{12,4},{1,9},{5,13},{9,1},{13,5},{2,10},{6,14},... | collective-permute-start | bytes 2359304 | tf_op jit(solution)/shard_map/ppermute | solution.py:1439
  80.5 0.3 collective-permute-start.3
  80.7 0.0 copy-done.4
  80.7 0.8 collective-permute-start.2
  81.5 0.9 collective-permute-start.1
  82.4 1.8 collective-permute-start
  84.2 0.0 copy-done.5
  84.2 0.1 reshape.66
  84.4 0.6 reshape.67.anchor_ref
  85.0 31.0 %shard_map.213 = (bf16[32,128,128]{2,1,0:T(8,128)(2,1)}, bf16[8192,128]{1,0:T(8,128)(2,1)}, bf16[128,8192]{1,0:T(8,128)(2,1)}, bf16[8,512,128]{2,1,0:T(8,128)(2,...) custom-call(s32[64]{0:T(128)} %reshape.67.anchor_ref, s32[8]{0:T(128)} %lens_ref.3, ...), custom_call_target="tpu_custom_call" | custom-call | flops 4294967296 | bytes 8388608 | tf_op jit(solution)/shard_map/pallas_call | solution.py:1293
  116.0 20.8 %shard_map.214 = (bf16[256,1024]{1,0:T(8,128)(2,1)}, f32[256,1024]{1,0:T(8,128)}, bf16[256,1024]{1,0:T(8,128)(2,1)}) custom-call(bf16[4,2,4,128,128]{4,3,2,1,0:T(8,128)(2,1)} %bitcast.18, bf16[256,1024]{1,0:T(8,128)(2,1)} %x_any.1, bf16[1024,1024]{1,0:T(8,128)(2,1)} %bitcast.13), custom_call_target="tpu_custom_call" | custom-call | tf_op jit(solution)/shard_map/pallas_call | solution.py:139
  136.8 0.0 collective-permute-done.2.cd_ref
  136.8 0.0 copy-start.9
  136.8 0.0 collective-permute-done.1.cc_ref
  136.8 0.0 copy-start.10
  136.8 0.0 collective-permute-done.cb_ref
  136.8 0.0 collective-permute-done.4.rest_2_
  136.8 0.0 copy-start.6
  136.8 0.0 collective-permute-done.3.rest_0_
  136.8 0.0 copy-start.7
  136.9 0.7 copy-done.9
  137.6 0.2 copy-done.10
  137.7 0.3 copy-done.6
  138.0 0.3 copy-done.7
  138.3 47.8 %shard_map.215 = (bf16[4,2,32,1024]{3,2,1,0:T(8,128)(2,1)}, bf16[4,2,32,1024]{3,2,1,0:T(8,128)(2,1)}, bf16[4,2,32,1024]{3,2,1,0:T(8,128)(2,1)}, bf16[4,2,32,1024...) custom-call(bf16[256,1024]{1,0:T(8,128)(2,1)} %get-tuple-element.64.n_ref, ...), custom_call_target="tpu_custom_call" | custom-call | flops 19327352832 | bytes 67108864 | tf_op jit(solution)/shard_map/pallas_call | solution.py:139
  186.1 0.0 reduce-scatter.2.cloned.1.call-update
  186.1 28.1 %shard_map.216 = (f32[256,1024]{1,0:T(8,128)}, bf16[4,2,4,128,128]{4,3,2,1,0:T(8,128)(2,1)}, bf16[4,2,32,1024]{3,2,1,0:T(8,128)(2,1)}, bf16[4,2,32,1024]{3,2,1,0...) custom-call(f32[256,1024]{1,0:T(8,128)} %get-tuple-element.67.c_ref,, ...), custom_call_target="tpu_custom_call" | custom-call | flops 1073741824 | bytes 8388608 | tf_op jit(solution)/shard_map/pallas_call | solution.py:139
  214.2 1.2 collective-permute-start.5
  215.5 0.7 collective-permute-start.6
  216.2 1.6 collective-permute-start.7
  217.8 1.2 collective-permute-start.8
  219.0 38.3 %shard_map.217 = bf16[32,384,128]{2,1,0:T(8,128)(2,1)} custom-call(s32[64]{0:T(128)} %reshape.67.anchor_ref, s32[8]{0:T(128)} %lens_ref.3, s32[1]{0:T(128)} %bitcast.1.who_ref, bf16[32,128,128]{2,1,0:T(8,128)(2,1)} %bitcast.24, bf16[8192,128]{1,0:T(8,128)(2,1)} %get-tuple-element.75.kv_ref, bf16[128,8192]{1,0:T(8,128)(2,1)} %get-tuple-element.76.kvt_ref, ...), custom_call_target="tpu_custom_call" | custom-call | flops 10737418240 | bytes 8388608 | tf_op jit(solution)/shard_map/pallas_call | solution.py:1414
  257.3 0.0 collective-permute-done.5.yd_ref
  257.3 0.0 collective-permute-done.6.vb_ref
  257.3 0.0 copy-start.1
  257.3 0.0 collective-permute-done.7.vc_ref
  257.3 0.0 copy-start.2
  257.3 0.0 collective-permute-done.8.vd_ref
  257.3 0.0 copy-start.3
  257.3 3.8 %reduce-scatter.2.cloned.1.call-done.f_ref.ds_any = bf16[12,32,1024]{2,1,0:T(8,128)(2,1)} async-done(((bf16[96,32,1024]{2,1,0:T(8,128)(2,1)}), bf16[12,32,1024]{2,1,0:T(8,128)(2,1)}) %reduce-scatter.2.cloned.1.call-update) | async-done | bytes 786448 | tf_op jit(solution)/shard_map/reduce_scatter | solution.py:1498
  261.2 0.0 copy-done.1
  261.2 0.0 copy-done.3
  261.2 69.8 %shard_map.218 = (bf16[256,1024]{1,0:T(8,128)(2,1)}, bf16[4,4,32,768]{3,2,1,0:T(8,128)(2,1)}, f32[32,1024]{1,0:T(8,128)}, bf16[4,2,32,1024]{3,2,1,0:T(8,128)(2,1)}, bf16[256,1024]{1,0:T(8,128)(2,1)}) custom-call(bf16[4,2,4,384,128]{4,3,2,1,0:T(8,128)(2,1)} %bitcast.16, bf16[4,256,1024]{2,1,0:T(8,128)(2,1)} %get-tuple-element.81.n_any, ...), custom_call_target="tpu_custom_call" | custom-call | flops 3221225472 | bytes 25165824 | tf_op jit(solution)/shard_map/pallas_call | solution.py:139
  331.0 4.8 %shard_map.219 = (bf16[256,1024]{1,0:T(8,128)(2,1)}, bf16[256,1024]{1,0:T(8,128)(2,1)}, f32[32,1024]{1,0:T(8,128)}, f32[1,32]{1,0:T(1,128)}, f32[32,1024]{1,0:T(...) custom-call(bf16[256,1024]{1,0:T(8,128)(2,1)} %get-tuple-element.93., ...), custom_call_target="tpu_custom_call" | custom-call | tf_op jit(solution)/shard_map/pallas_call | solution.py:1060
  (6 shorter events, 0.0 us)
Async XLA Ops:
  7.2 254.0 %reduce-scatter.2.cloned.1.call-start = ((), (), s32[]{:S(2)}) async-start(), calls=%async_computation.1 | async-start | bytes 7077888 | tf_op jit(solution)/shard_map/reduce_scatter | solution.py:1498
  7.2 73.5 %copy-start.4 = (bf16[256,1024]{1,0:T(8,128)(2,1)S(1)}, bf16[256,1024]{1,0:T(8,128)(2,1)}, u32[]{:S(2)}) copy-start(bf16[256,1024]{1,0:T(8,128)(2,1)} %t_ref.3) | copy-start | bytes 1572868
  7.2 77.0 %copy-start.5 = (s32[64]{0:T(128)S(1)}, s32[64]{0:T(128)}, u32[]{:S(2)}) copy-start(s32[64]{0:T(128)} %param.24) | copy-start | bytes 772
  77.0 59.8 %collective-permute-start.4 = (bf16[2,2,3,32,1024]{4,3,2,1,0:T(8,128)(2,1)}, bf16[2,2,3,32,1024]{4,3,2,1,0:T(8,128)(2,1)S(1)}, u32[]{:S(2)}, u32[]{:S(2)}) collective-permute-start(bf16[2,2,3,32,1024]{4,3,2,1,0:T(8,128)(2,1)} %get-tuple-element.66.rest_1_), channel_id=1, source_target_pairs={{0,8},{4,12},{8,0},{12,4},{1,9},{5,13},{9,1},{13,5},{2,10},{6,14},... | collective-permute-start | bytes 2359304 | tf_op jit(solution)/shard_map/ppermute | solution.py:1439
  80.5 56.4 %collective-permute-start.3 = (bf16[2,2,3,32,1024]{4,3,2,1,0:T(8,128)(2,1)}, bf16[2,2,3,32,1024]{4,3,2,1,0:T(8,128)(2,1)S(1)}, u32[]{:S(2)}, u32[]{:S(2)}) collective-permute-start(bf16[2,2,3,32,1024]{4,3,2,1,0:T(8,128)(2,1)} %get-tuple-element.66.rest_1_), channel_id=1, source_target_pairs={{0,4},{4,0},{8,12},{12,8},{1,5},{5,1},{9,13},{13,9},{2,6},{6,2},{1... | collective-permute-start | bytes 2359304 | tf_op jit(solution)/shard_map/ppermute | solution.py:1439
  80.7 56.0 %collective-permute-start.2 = (bf16[256,1024]{1,0:T(8,128)(2,1)S(1)}, bf16[256,1024]{1,0:T(8,128)(2,1)S(1)}, u32[]{:S(2)}, u32[]{:S(2)}) collective-permute-start(bf16[256,1024]{1,0:T(8,128)(2,1)S(1)} %copy-done.4), channel_id=1, source_target_pairs={{0,18},{2,16},{16,2},{18,0},{1,19},{3,17},{17,3},{19,1},{4,22},{6,... | collective-permute-start | bytes 1572872 | tf_op jit(solution)/shard_map/ppermute | solution.py:1435
  81.5 55.3 %collective-permute-start.1 = (bf16[256,1024]{1,0:T(8,128)(2,1)S(1)}, bf16[256,1024]{1,0:T(8,128)(2,1)S(1)}, u32[]{:S(2)}, u32[]{:S(2)}) collective-permute-start(bf16[256,1024]{1,0:T(8,128)(2,1)S(1)} %copy-done.4), channel_id=1, source_target_pairs={{0,16},{2,18},{16,0},{18,2},{1,17},{3,19},{17,1},{19,3},{4,20},{6,... | collective-permute-start | bytes 1572872 | tf_op jit(solution)/shard_map/ppermute | solution.py:1435
  82.4 54.4 %collective-permute-start = (bf16[256,1024]{1,0:T(8,128)(2,1)S(1)}, bf16[256,1024]{1,0:T(8,128)(2,1)}, u32[]{:S(2)}, u32[]{:S(2)}) collective-permute-start(bf16[256,1024]{1,0:T(8,128)(2,1)S(1)} %copy-done.4), channel_id=1, source_target_pairs={{0,2},{2,0},{16,18},{18,16},{1,3},{3,1},{17,19},{19,17},{4,6},{6,4... | collective-permute-start | bytes 1572872 | tf_op jit(solution)/shard_map/ppermute | solution.py:1435
  136.8 0.8 copy-start.9
  136.8 0.9 copy-start.10
  136.8 1.2 copy-start.6
  136.8 1.4 copy-start.7
  186.1 28.1 %copy-start.8 = (bf16[4,2,32,1024]{3,2,1,0:T(8,128)(2,1)S(1)}, bf16[4,2,32,1024]{3,2,1,0:T(8,128)(2,1)}, u32[]{:S(2)}) copy-start(bf16[4,2,32,1024]{3,2,1,0:T(8,128)(2,1)} %get-tuple-element.88) | copy-start | bytes 1572868
  214.2 43.0 %collective-permute-start.5 = (bf16[4,2,32,1024]{3,2,1,0:T(8,128)(2,1)S(1)}, bf16[4,2,32,1024]{3,2,1,0:T(8,128)(2,1)S(1)}, u32[]{:S(2)}, u32[]{:S(2)}) collective-permute-start(bf16[4,2,32,1024]{3,2,1,0:T(8,128)(2,1)S(1)} %copy-done.8), channel_id=1, source_target_pairs={{0,18},{2,16},{16,2},{18,0},{1,19},{3,17},{17,3},{19,1},{4,22},{6,... | collective-permute-start | bytes 1572872 | tf_op jit(solution)/shard_map/ppermute | solution.py:1435
  215.5 41.8 %collective-permute-start.6 = (bf16[4,2,32,1024]{3,2,1,0:T(8,128)(2,1)}, bf16[4,2,32,1024]{3,2,1,0:T(8,128)(2,1)S(1)}, u32[]{:S(2)}, u32[]{:S(2)}) collective-permute-start(bf16[4,2,32,1024]{3,2,1,0:T(8,128)(2,1)} %get-tuple-element.90), channel_id=1, source_target_pairs={{0,2},{2,0},{16,18},{18,16},{1,3},{3,1},{17,19},{19,17},{4,6},{6,4... | collective-permute-start | bytes 1572872 | tf_op jit(solution)/shard_map/ppermute | solution.py:1435
  216.2 41.1 %collective-permute-start.7 = (bf16[4,2,32,1024]{3,2,1,0:T(8,128)(2,1)}, bf16[4,2,32,1024]{3,2,1,0:T(8,128)(2,1)S(1)}, u32[]{:S(2)}, u32[]{:S(2)}) collective-permute-start(bf16[4,2,32,1024]{3,2,1,0:T(8,128)(2,1)} %get-tuple-element.91), channel_id=1, source_target_pairs={{0,16},{2,18},{16,0},{18,2},{1,17},{3,19},{17,1},{19,3},{4,20},{6,... | collective-permute-start | bytes 1572872 | tf_op jit(solution)/shard_map/ppermute | solution.py:1435
  217.8 39.5 %collective-permute-start.8 = (bf16[4,2,32,1024]{3,2,1,0:T(8,128)(2,1)}, bf16[4,2,32,1024]{3,2,1,0:T(8,128)(2,1)S(1)}, u32[]{:S(2)}, u32[]{:S(2)}) collective-permute-start(bf16[4,2,32,1024]{3,2,1,0:T(8,128)(2,1)} %get-tuple-element.92), channel_id=1, source_target_pairs={{0,18},{2,16},{16,2},{18,0},{1,19},{3,17},{17,3},{19,1},{4,22},{6,... | collective-permute-start | bytes 1572872 | tf_op jit(solution)/shard_map/ppermute | solution.py:1435
  257.3 3.9 %copy-start = (bf16[4,2,32,1024]{3,2,1,0:T(8,128)(2,1)}, bf16[4,2,32,1024]{3,2,1,0:T(8,128)(2,1)S(1)}, u32[]{:S(2)}) copy-start(bf16[4,2,32,1024]{3,2,1,0:T(8,128)(2,1)S(1)} %collective-permute-done.5.yd_ref) | copy-start | bytes 1572868
  257.3 3.9 %copy-start.1 = (bf16[4,2,32,1024]{3,2,1,0:T(8,128)(2,1)}, bf16[4,2,32,1024]{3,2,1,0:T(8,128)(2,1)S(1)}, u32[]{:S(2)}) copy-start(bf16[4,2,32,1024]{3,2,1,0:T(8,128)(2,1)S(1)} %collective-permute-done.6.vb_ref) | copy-start | bytes 1572868
  257.3 3.9 %copy-start.2 = (bf16[4,2,32,1024]{3,2,1,0:T(8,128)(2,1)}, bf16[4,2,32,1024]{3,2,1,0:T(8,128)(2,1)S(1)}, u32[]{:S(2)}) copy-start(bf16[4,2,32,1024]{3,2,1,0:T(8,128)(2,1)S(1)} %collective-permute-done.7.vc_ref) | copy-start | bytes 1572868
  257.3 3.8 %copy-start.3 = (bf16[4,2,32,1024]{3,2,1,0:T(8,128)(2,1)}, bf16[4,2,32,1024]{3,2,1,0:T(8,128)(2,1)S(1)}, u32[]{:S(2)}) copy-start(bf16[4,2,32,1024]{3,2,1,0:T(8,128)(2,1)S(1)} %collective-permute-done.8.vd_ref) | copy-start | bytes 1572868
Sparse Core Ops, SparseCore 0:
  186.2 74.8 reduce-scatter.1

commit v9 on v8

--- a/solution.py
+++ b/solution.py
@@ -214,13 +214,13 @@
     rows[0] = (x * lax.rsqrt(jnp.mean(x * x, axis=-1, keepdims=True) + EPS)).astype(BF16)
     met()
     here = og_ref.at[me.x, me.z, me.y, me.c]
-    local = [move(w_ref.at[me.g], weights.at[me.chip, me.c], ls, 0), move(wo_ref, here, ls, 1)]
+    local = [move(w_ref.at[me.g], weights.at[me.x, me.z, me.y, me.c], ls, 0), move(wo_ref, here, ls, 1)]
     pieces = []
     for k in reversed(range(1, chips)):
         there = me.any_chip(k)
         their_g = there[0] * 2 + there[2]
         pieces.append(
-            send(w_ref.at[their_g], weights.at[me.chip, me.c], (w0, w1), k, there)
+            send(w_ref.at[their_g], weights.at[me.x, me.z, me.y, me.c], (w0, w1), k, there)
         )
     outs = [send(wo_ref, here, (o0, o1), k, me.line(k)) for k in range(1, zc)]
     blocks = [send(rows.at[0], rows.at[k], (n0, n1), k, me.plane(k)) for k in range(1, 4)]
@@ -249,12 +249,15 @@
             send(f_ref.at[their_g], fg_ref.at[me.x, me.y, pl.ds(0, 2)], (f0, f1), k, there)
         )
     local[0].wait()
-    for copy in pieces:
+    arrivals = [pieces[chips - 1 - k] for k in range(1, chips)]
+    relays = []
+    for away in range(zc):
+        for k in range(max(1, 4 * away), 4 * away + 4):
+            arrivals[k - 1].wait()
+        got = weights.at[:, me.z ^ away, :, me.c]
+        relays.append(send(got, got, (s0, s1), 1 + away, me.sibling()))
+    for copy in relays:
         copy.wait()
-    relay = send(
-        weights.at[:, me.c], weights.at[:, me.c], (s0, s1), 0, me.sibling()
-    )
-    relay.wait()
     kept = [move(weights, wg_ref, ls, 3)]
 
     def project(k, carry):
@@ -311,7 +314,7 @@
     for copy in out_rows:
         copy.wait()
     every = og_ref.at[:, :, :, me.c]
-    last = send(every, every, (s0, s1), 1, me.sibling())
+    last = send(every, every, (s0, s1), 0, me.sibling())
 
     def finish(step, carry):
         k, over = step // zc, step % zc
@@ -341,7 +344,7 @@
         1,
         (
             struct((4, own, width)),
-            struct((chips, 2) + piece),
+            struct((2, zc, 2, 2) + piece),
             struct((2, 2, 3, count, width)),
             struct((zc, 2, 4, BLOCK + own, PAIR)),
             struct((2, zc, 2, 2, count, width)),
@@ -354,7 +357,7 @@
             pltpu.VMEM((2, 2, count, width), BF16),
             pltpu.VMEM((count, width), BF16),
             pltpu.VMEM((4, own, width), BF16),
-            pltpu.VMEM((chips, 2) + piece, BF16),
+            pltpu.VMEM((2, zc, 2, 2) + piece, BF16),
             pltpu.VMEM((group, 4, BLOCK + own, PAIR), BF16),
             DMA((10,)),
         ]
@@ -363,7 +366,7 @@
         + both(4)
         + both(4 * zc)
         + both(4 * zc)
-        + both(2)
+        + both(1 + zc)
         + both(zc)
         + both(4),
         (tokens, *matrices, *(g.reshape(1, -1) for g in gains)),
@@ -445,7 +448,7 @@
 def middle_kernel(zc, n_ref, ca_ref, cb_ref, cc_ref, cd_ref, *rest):
     f_refs, rest = rest[: zc // 2 + 1], rest[zc // 2 + 1 :]
     oa_ref, ob_ref, oc_ref, od_ref, cs_ref, sh_ref, rows, cots, gate_w, up_w, down_w, *rest = rest
-    hid, dgate, dup, c_out, c_in, passed, stage, o_out, ls, n0, n1, c0, c1, f0, f1, h0, h1 = rest
+    hid, dgate, dup, c_out, c_in, passed, early, stage, o_out, ls, n0, n1, c0, c1, f0, f1, h0, h1 = rest
     me = Place(zc)
     width = n_ref.shape[1]
     met = greet([me.plane(k) for k in range(1, 4)] + [me.line(1), me.sibling()])
@@ -460,25 +463,28 @@
         )
 
     given = dict(zip([1, *range(0, zc, 2)], f_refs))
-    hops, loads = [], []
+    hops, loads = [[], [], []], [[], [], []]
     for k in range(2, zc, 2):
         for i, place in enumerate(places(me.z ^ k)):
-            hops.append(send(given[k].at[:, :, i], place, (h0, h1), 3 * k + i, me.line(1)))
+            hops[i].append(send(given[k].at[:, :, i], place, (h0, h1), 3 * k + i, me.line(1)))
     for k, ref in given.items():
         for i, place in enumerate(places(me.z ^ k)):
-            loads.append(send(ref.at[:, :, i], place, (f0, f1), 3 * k + i, me.sibling()))
-            loads.append(move(ref.at[:, :, i], place, ls, 21 + 3 * k + i))
+            loads[i].append(send(ref.at[:, :, i], place, (f0, f1), 3 * k + i, me.sibling()))
+            loads[i].append(move(ref.at[:, :, i], place, ls, 21 + 3 * k + i))
     for k, ref in enumerate((ca_ref, cb_ref, cc_ref, cd_ref)):
-        loads.append(move(ref, cots.at[k], ls, 16 + k))
+        loads[2].append(move(ref, cots.at[k], ls, 16 + k))
     farthest.wait_send()
     near_rows = [send(rows.at[0], rows.at[k], (n0, n1), k, me.plane(k)) for k in (1, 2)]
-    for copy in hops:
-        copy.wait()
-    for k in range(3, zc, 2):
-        for i, place in enumerate(places(me.z ^ k)):
-            loads.append(send(place, place, (f0, f1), 3 * k + i, me.sibling()))
-    for copy in loads:
-        copy.wait()
+
+    def settle(i):
+        for copy in hops[i]:
+            copy.wait()
+        for k in range(3, zc, 2):
+            place = places(me.z ^ k)[i]
+            loads[i].append(send(place, place, (f0, f1), 3 * k + i, me.sibling()))
+        for copy in loads[i]:
+            copy.wait()
+
     square = (width, width)
     half = n_ref.shape[0] // 2
     upper, lower = pl.ds(0, half), pl.ds(half, half)
@@ -494,28 +500,37 @@
         trip(c_out.at[2, lower], c_in.at[1, lower], c_sems, 5, me.plane(2)),
     ]
 
-    def block(step, carry):
-        k = jnp.where(step == 0, 3, jnp.where(step == 3, 0, step))
-
-        @pl.when(step < 3)
-        def _():
-            trip(rows.at[0], rows.at[k], (n0, n1), k, me.plane(k)).wait_recv()
-
+    def both_products(k):
         gate_mat, up_mat = gate_w[...].reshape(square), up_w[...].reshape(square)
-        gate = dot(rows[k], gate_mat)
-        up = dot(rows[k], up_mat)
+        return dot(rows[k], gate_mat), dot(rows[k], up_mat)
+
+    def finish(k, gate, up):
         back = nt_dot(cots[k], down_w[...].reshape(square))
         sig = jax.nn.sigmoid(gate)
         soft = gate * sig
         hid[k] = (soft * up).astype(BF16)
         dgate[k] = (back * up * sig * (1.0 + gate * (1.0 - sig))).astype(BF16)
         dup[k] = (back * soft).astype(BF16)
+        gate_mat, up_mat = gate_w[...].reshape(square), up_w[...].reshape(square)
         c_out[k] = (nt_dot(dgate[k], gate_mat) + nt_dot(dup[k], up_mat)).astype(BF16)
 
-        @pl.when(step == 0)
+    settle(0)
+    settle(1)
+    trip(rows.at[0], rows.at[3], (n0, n1), 3, me.plane(3)).wait_recv()
+    early[0], early[1] = both_products(3)
+    settle(2)
+    finish(3, early[0], early[1])
+    for copy in far_parts:
+        copy.start()
+
+    def block(step, carry):
+        k = jnp.where(step == 3, 0, step)
+
+        @pl.when(step < 3)
         def _():
-            for copy in far_parts:
-                copy.start()
+            trip(rows.at[0], rows.at[k], (n0, n1), k, me.plane(k)).wait_recv()
+
+        finish(k, *both_products(k))
 
         @pl.when(step == 1)
         def _():
@@ -527,7 +542,7 @@
 
         return carry
 
-    lax.fori_loop(0, 4, block, 0)
+    lax.fori_loop(1, 4, block, 0)
     far_parts[0].wait_recv()
     c_out[1, upper] = c_out[1, upper] + passed[0]
     near_parts[2].start()
@@ -595,6 +610,7 @@
         [blocks, blocks, wide, wide, pltpu.VMEM((zc, 2, 2, 2, piece, width), BF16)]
         + [blocks] * 4
         + [pltpu.VMEM((2, own, width), BF16), pltpu.VMEM((2, own // 2, width), BF16)]
+        + [pltpu.VMEM((2, own, width), F32)]
         + [pltpu.VMEM((3, width, width), BF16), pltpu.VMEM((4, zc, 2, piece, width), BF16), DMA((21 + 3 * zc,))]
         + both(4)
         + both(6)

time: 343 us -> 340 us (level)
  Pallas kernels: 310 us -> 301 us
  waiting for transfers between devices: 3.85 us -> 9.39 us
    reduce_scatter x1, waiting for transfers between devices: 3.81 us -> 9.35 us  [body(): lax.psum_scatter(shares.reshape(zc * 2 * 12, feature_rows, width), ('z',...]
    pallas_call x1, Pallas kernels: 38.3 us -> 34.2 us  [attention_backward(): pl.pallas_call(functools.partial(backward_kernel, workers), out_shape=str...]
  transfers between devices with their start and end apart: 10 -> 10, of which waited for: 1 -> 1; matrix products, arithmetic and copies ran while one was open for 0% -> 0% of each run, Pallas kernels for 34% -> 32%
where the time goes in v9:
time: 340 us; the launch traced here: 339 us
  Pallas kernels  301 us (89%)
  between operations  14.3 us (4%)
  starting transfers between devices  11.3 us (3%)
  waiting for transfers between devices  9.39 us (3%)
    pallas_call x5, Pallas kernels, exchange(): pl.pallas_call(kernel, out_shape=out_shape, in_specs=in_specs, out_specs=...  234 us
    pallas_call x1, Pallas kernels, attention_backward(): pl.pallas_call(functools.partial(backward_kernel, workers), out_shape=str...  34.2 us
    pallas_call x1, Pallas kernels, attention_forward(): pl.pallas_call(functools.partial(forward_kernel, workers), out_shape=(str...  28.7 us
    reduce_scatter x1, waiting for transfers between devices, body(): lax.psum_scatter(shares.reshape(zc * 2 * 12, feature_rows, width), ('z',...  9.35 us
    ppermute x7, starting transfers between devices, around(): return lax.ppermute(value, ('head', 'y'), [(i, i ^ k) for i in range(4)])  7.31 us
  transfers between devices with their start and end apart: 10, of which 1 were waited for; matrix products, arithmetic and copies ran while one was open for 0% of the time, Pallas kernels for 32%

profile of v9, /device:TPU:0, one launch (start us, length us, event | category | flops | bytes accessed | tf_op | source)
XLA Modules:
  0.0 338.6 jit_solution(12879934108203026141)
XLA Ops:
  7.2 0.0 reduce-scatter.2.cloned.1.call-start
  7.2 0.0 copy-start.4
  7.2 0.0 copy-start.5
  7.2 69.3 %shard_map.212 = (bf16[4,256,1024]{2,1,0:T(8,128)(2,1)}, bf16[2,4,2,2,32,768]{5,4,3,2,1,0:T(8,128)(2,1)}, bf16[2,2,3,32,1024]{4,3,2,1,0:T(8,128)(2,1)}, bf16[4,2...) custom-call(bf16[256,1024]{1,0:T(8,128)(2,1)} %x_any.1, f32[32,1024]{1,0:T(8,128)} %q_any.1, ...), custom_call_target="tpu_custom_call" | custom-call | flops 2147483648 | bytes 16777216 | tf_op jit(solution)/shard_map/pallas_call | solution.py:139
  76.6 3.4 collective-permute-start.4
  79.9 0.5 collective-permute-start.3
  80.5 0.0 copy-done.4
  80.5 0.5 collective-permute-start.2
  81.0 1.0 collective-permute-start.1
  82.0 1.9 collective-permute-start
  84.0 0.0 copy-done.5
  84.0 0.1 reshape.66
  84.1 0.6 reshape.67.anchor_ref
  84.7 28.7 %shard_map.213 = (bf16[32,128,128]{2,1,0:T(8,128)(2,1)}, bf16[8192,128]{1,0:T(8,128)(2,1)}, bf16[128,8192]{1,0:T(8,128)(2,1)}, bf16[8,512,128]{2,1,0:T(8,128)(2,...) custom-call(s32[64]{0:T(128)} %reshape.67.anchor_ref, s32[8]{0:T(128)} %lens_ref.3, ...), custom_call_target="tpu_custom_call" | custom-call | flops 4294967296 | bytes 8388608 | tf_op jit(solution)/shard_map/pallas_call | solution.py:1309
  113.4 20.5 %shard_map.214 = (bf16[256,1024]{1,0:T(8,128)(2,1)}, f32[256,1024]{1,0:T(8,128)}, bf16[256,1024]{1,0:T(8,128)(2,1)}) custom-call(bf16[4,2,4,128,128]{4,3,2,1,0:T(8,128)(2,1)} %bitcast.18, bf16[256,1024]{1,0:T(8,128)(2,1)} %x_any.1, bf16[1024,1024]{1,0:T(8,128)(2,1)} %bitcast.13), custom_call_target="tpu_custom_call" | custom-call | tf_op jit(solution)/shard_map/pallas_call | solution.py:139
  133.9 0.0 collective-permute-done.2.cd_ref
  133.9 0.0 copy-start.9
  134.0 0.0 collective-permute-done.1.cc_ref
  134.0 0.0 copy-start.10
  134.0 0.0 collective-permute-done.cb_ref
  134.0 0.0 collective-permute-done.4.rest_2_
  134.0 0.0 copy-start.6
  134.0 0.0 collective-permute-done.3.rest_0_
  134.0 0.7 copy-done.9
  134.7 0.2 copy-done.10
  134.9 0.3 copy-done.6
  135.2 0.3 copy-done.7
  135.4 49.0 %shard_map.215 = (bf16[4,2,32,1024]{3,2,1,0:T(8,128)(2,1)}, bf16[4,2,32,1024]{3,2,1,0:T(8,128)(2,1)}, bf16[4,2,32,1024]{3,2,1,0:T(8,128)(2,1)}, bf16[4,2,32,1024...) custom-call(bf16[256,1024]{1,0:T(8,128)(2,1)} %get-tuple-element.64.n_ref, ...), custom_call_target="tpu_custom_call" | custom-call | flops 19327352832 | bytes 67108864 | tf_op jit(solution)/shard_map/pallas_call | solution.py:139
  184.5 0.0 reduce-scatter.2.cloned.1.call-update
  184.5 0.0 copy-start.8
  184.5 26.5 %shard_map.216 = (f32[256,1024]{1,0:T(8,128)}, bf16[4,2,4,128,128]{4,3,2,1,0:T(8,128)(2,1)}, bf16[4,2,32,1024]{3,2,1,0:T(8,128)(2,1)}, bf16[4,2,32,1024]{3,2,1,0...) custom-call(f32[256,1024]{1,0:T(8,128)} %get-tuple-element.67.c_ref,, ...), custom_call_target="tpu_custom_call" | custom-call | flops 1073741824 | bytes 8388608 | tf_op jit(solution)/shard_map/pallas_call | solution.py:139
  211.0 0.0 copy-done.8
  211.0 0.3 collective-permute-start.5
  211.3 1.7 collective-permute-start.6
  213.0 1.6 collective-permute-start.7
  214.6 0.3 collective-permute-start.8
  214.9 34.2 %shard_map.217 = bf16[32,384,128]{2,1,0:T(8,128)(2,1)} custom-call(s32[64]{0:T(128)} %reshape.67.anchor_ref, s32[8]{0:T(128)} %lens_ref.3, s32[1]{0:T(128)} %bitcast.1.who_ref, bf16[32,128,128]{2,1,0:T(8,128)(2,1)} %bitcast.24, bf16[8192,128]{1,0:T(8,128)(2,1)} %get-tuple-element.75.kv_ref, bf16[128,8192]{1,0:T(8,128)(2,1)} %get-tuple-element.76.kvt_ref, ...), custom_call_target="tpu_custom_call" | custom-call | flops 10737418240 | bytes 8388608 | tf_op jit(solution)/shard_map/pallas_call | solution.py:1430
  249.1 0.0 collective-permute-done.5.yd_ref
  249.1 0.0 collective-permute-done.6.vb_ref
  249.1 0.0 copy-start.1
  249.1 0.0 collective-permute-done.7.vc_ref
  249.1 0.0 copy-start.2
  249.1 0.0 collective-permute-done.8.vd_ref
  249.1 0.0 copy-start.3
  249.1 9.3 %reduce-scatter.2.cloned.1.call-done.f_ref.ds_any = bf16[12,32,1024]{2,1,0:T(8,128)(2,1)} async-done(((bf16[96,32,1024]{2,1,0:T(8,128)(2,1)}), bf16[12,32,1024]{2,1,0:T(8,128)(2,1)}) %reduce-scatter.2.cloned.1.call-update) | async-done | bytes 786448 | tf_op jit(solution)/shard_map/reduce_scatter | solution.py:1514
  258.5 0.0 copy-done.2
  258.5 68.4 %shard_map.218 = (bf16[256,1024]{1,0:T(8,128)(2,1)}, bf16[4,4,32,768]{3,2,1,0:T(8,128)(2,1)}, f32[32,1024]{1,0:T(8,128)}, bf16[4,2,32,1024]{3,2,1,0:T(8,128)(2,1)}, bf16[256,1024]{1,0:T(8,128)(2,1)}) custom-call(bf16[4,2,4,384,128]{4,3,2,1,0:T(8,128)(2,1)} %bitcast.16, bf16[4,256,1024]{2,1,0:T(8,128)(2,1)} %get-tuple-element.81.n_any, ...), custom_call_target="tpu_custom_call" | custom-call | flops 3221225472 | bytes 25165824 | tf_op jit(solution)/shard_map/pallas_call | solution.py:139
  326.9 4.8 %shard_map.219 = (bf16[256,1024]{1,0:T(8,128)(2,1)}, bf16[256,1024]{1,0:T(8,128)(2,1)}, f32[32,1024]{1,0:T(8,128)}, f32[1,32]{1,0:T(1,128)}, f32[32,1024]{1,0:T(...) custom-call(bf16[256,1024]{1,0:T(8,128)(2,1)} %get-tuple-element.93., ...), custom_call_target="tpu_custom_call" | custom-call | tf_op jit(solution)/shard_map/pallas_call | solution.py:1076
  (6 shorter events, 0.0 us)
Async XLA Ops:
  7.2 251.3 %reduce-scatter.2.cloned.1.call-start = ((), (), s32[]{:S(2)}) async-start(), calls=%async_computation.1 | async-start | bytes 7077888 | tf_op jit(solution)/shard_map/reduce_scatter | solution.py:1514
  7.2 73.3 %copy-start.4 = (bf16[256,1024]{1,0:T(8,128)(2,1)S(1)}, bf16[256,1024]{1,0:T(8,128)(2,1)}, u32[]{:S(2)}) copy-start(bf16[256,1024]{1,0:T(8,128)(2,1)} %t_ref.3) | copy-start | bytes 1572868
  7.2 76.7 %copy-start.5 = (s32[64]{0:T(128)S(1)}, s32[64]{0:T(128)}, u32[]{:S(2)}) copy-start(s32[64]{0:T(128)} %param.24) | copy-start | bytes 772
  76.6 57.4 %collective-permute-start.4 = (bf16[2,2,3,32,1024]{4,3,2,1,0:T(8,128)(2,1)}, bf16[2,2,3,32,1024]{4,3,2,1,0:T(8,128)(2,1)S(1)}, u32[]{:S(2)}, u32[]{:S(2)}) collective-permute-start(bf16[2,2,3,32,1024]{4,3,2,1,0:T(8,128)(2,1)} %get-tuple-element.66.rest_1_), channel_id=1, source_target_pairs={{0,8},{4,12},{8,0},{12,4},{1,9},{5,13},{9,1},{13,5},{2,10},{6,14},... | collective-permute-start | bytes 2359304 | tf_op jit(solution)/shard_map/ppermute | solution.py:1455
  79.9 54.1 %collective-permute-start.3 = (bf16[2,2,3,32,1024]{4,3,2,1,0:T(8,128)(2,1)}, bf16[2,2,3,32,1024]{4,3,2,1,0:T(8,128)(2,1)S(1)}, u32[]{:S(2)}, u32[]{:S(2)}) collective-permute-start(bf16[2,2,3,32,1024]{4,3,2,1,0:T(8,128)(2,1)} %get-tuple-element.66.rest_1_), channel_id=1, source_target_pairs={{0,4},{4,0},{8,12},{12,8},{1,5},{5,1},{9,13},{13,9},{2,6},{6,2},{1... | collective-permute-start | bytes 2359304 | tf_op jit(solution)/shard_map/ppermute | solution.py:1455
  80.5 53.5 %collective-permute-start.2 = (bf16[256,1024]{1,0:T(8,128)(2,1)S(1)}, bf16[256,1024]{1,0:T(8,128)(2,1)S(1)}, u32[]{:S(2)}, u32[]{:S(2)}) collective-permute-start(bf16[256,1024]{1,0:T(8,128)(2,1)S(1)} %copy-done.4), channel_id=1, source_target_pairs={{0,18},{2,16},{16,2},{18,0},{1,19},{3,17},{17,3},{19,1},{4,22},{6,... | collective-permute-start | bytes 1572872 | tf_op jit(solution)/shard_map/ppermute | solution.py:1451
  81.0 53.0 %collective-permute-start.1 = (bf16[256,1024]{1,0:T(8,128)(2,1)S(1)}, bf16[256,1024]{1,0:T(8,128)(2,1)S(1)}, u32[]{:S(2)}, u32[]{:S(2)}) collective-permute-start(bf16[256,1024]{1,0:T(8,128)(2,1)S(1)} %copy-done.4), channel_id=1, source_target_pairs={{0,16},{2,18},{16,0},{18,2},{1,17},{3,19},{17,1},{19,3},{4,20},{6,... | collective-permute-start | bytes 1572872 | tf_op jit(solution)/shard_map/ppermute | solution.py:1451
  82.0 51.9 %collective-permute-start = (bf16[256,1024]{1,0:T(8,128)(2,1)S(1)}, bf16[256,1024]{1,0:T(8,128)(2,1)}, u32[]{:S(2)}, u32[]{:S(2)}) collective-permute-start(bf16[256,1024]{1,0:T(8,128)(2,1)S(1)} %copy-done.4), channel_id=1, source_target_pairs={{0,2},{2,0},{16,18},{18,16},{1,3},{3,1},{17,19},{19,17},{4,6},{6,4... | collective-permute-start | bytes 1572872 | tf_op jit(solution)/shard_map/ppermute | solution.py:1451
  133.9 0.8 copy-start.9
  134.0 0.9 copy-start.10
  134.0 1.2 copy-start.6
  134.0 1.4 copy-start.7
  184.5 26.5 %copy-start.8 = (bf16[4,2,32,1024]{3,2,1,0:T(8,128)(2,1)S(1)}, bf16[4,2,32,1024]{3,2,1,0:T(8,128)(2,1)}, u32[]{:S(2)}) copy-start(bf16[4,2,32,1024]{3,2,1,0:T(8,128)(2,1)} %get-tuple-element.88) | copy-start | bytes 1572868
  211.0 38.0 %collective-permute-start.5 = (bf16[4,2,32,1024]{3,2,1,0:T(8,128)(2,1)S(1)}, bf16[4,2,32,1024]{3,2,1,0:T(8,128)(2,1)S(1)}, u32[]{:S(2)}, u32[]{:S(2)}) collective-permute-start(bf16[4,2,32,1024]{3,2,1,0:T(8,128)(2,1)S(1)} %copy-done.8), channel_id=1, source_target_pairs={{0,18},{2,16},{16,2},{18,0},{1,19},{3,17},{17,3},{19,1},{4,22},{6,... | collective-permute-start | bytes 1572872 | tf_op jit(solution)/shard_map/ppermute | solution.py:1451
  211.3 37.7 %collective-permute-start.6 = (bf16[4,2,32,1024]{3,2,1,0:T(8,128)(2,1)}, bf16[4,2,32,1024]{3,2,1,0:T(8,128)(2,1)S(1)}, u32[]{:S(2)}, u32[]{:S(2)}) collective-permute-start(bf16[4,2,32,1024]{3,2,1,0:T(8,128)(2,1)} %get-tuple-element.90), channel_id=1, source_target_pairs={{0,2},{2,0},{16,18},{18,16},{1,3},{3,1},{17,19},{19,17},{4,6},{6,4... | collective-permute-start | bytes 1572872 | tf_op jit(solution)/shard_map/ppermute | solution.py:1451
  213.0 36.1 %collective-permute-start.7 = (bf16[4,2,32,1024]{3,2,1,0:T(8,128)(2,1)}, bf16[4,2,32,1024]{3,2,1,0:T(8,128)(2,1)S(1)}, u32[]{:S(2)}, u32[]{:S(2)}) collective-permute-start(bf16[4,2,32,1024]{3,2,1,0:T(8,128)(2,1)} %get-tuple-element.91), channel_id=1, source_target_pairs={{0,16},{2,18},{16,0},{18,2},{1,17},{3,19},{17,1},{19,3},{4,20},{6,... | collective-permute-start | bytes 1572872 | tf_op jit(solution)/shard_map/ppermute | solution.py:1451
  214.6 34.5 %collective-permute-start.8 = (bf16[4,2,32,1024]{3,2,1,0:T(8,128)(2,1)}, bf16[4,2,32,1024]{3,2,1,0:T(8,128)(2,1)S(1)}, u32[]{:S(2)}, u32[]{:S(2)}) collective-permute-start(bf16[4,2,32,1024]{3,2,1,0:T(8,128)(2,1)} %get-tuple-element.92), channel_id=1, source_target_pairs={{0,18},{2,16},{16,2},{18,0},{1,19},{3,17},{17,3},{19,1},{4,22},{6,... | collective-permute-start | bytes 1572872 | tf_op jit(solution)/shard_map/ppermute | solution.py:1451
  249.1 9.4 %copy-start = (bf16[4,2,32,1024]{3,2,1,0:T(8,128)(2,1)}, bf16[4,2,32,1024]{3,2,1,0:T(8,128)(2,1)S(1)}, u32[]{:S(2)}) copy-start(bf16[4,2,32,1024]{3,2,1,0:T(8,128)(2,1)S(1)} %collective-permute-done.5.yd_ref) | copy-start | bytes 1572868
  249.1 9.4 %copy-start.1 = (bf16[4,2,32,1024]{3,2,1,0:T(8,128)(2,1)}, bf16[4,2,32,1024]{3,2,1,0:T(8,128)(2,1)S(1)}, u32[]{:S(2)}) copy-start(bf16[4,2,32,1024]{3,2,1,0:T(8,128)(2,1)S(1)} %collective-permute-done.6.vb_ref) | copy-start | bytes 1572868
  249.1 9.4 %copy-start.2 = (bf16[4,2,32,1024]{3,2,1,0:T(8,128)(2,1)}, bf16[4,2,32,1024]{3,2,1,0:T(8,128)(2,1)S(1)}, u32[]{:S(2)}) copy-start(bf16[4,2,32,1024]{3,2,1,0:T(8,128)(2,1)S(1)} %collective-permute-done.7.vc_ref) | copy-start | bytes 1572868
  249.1 9.4 %copy-start.3 = (bf16[4,2,32,1024]{3,2,1,0:T(8,128)(2,1)}, bf16[4,2,32,1024]{3,2,1,0:T(8,128)(2,1)S(1)}, u32[]{:S(2)}) copy-start(bf16[4,2,32,1024]{3,2,1,0:T(8,128)(2,1)S(1)} %collective-permute-done.8.vd_ref) | copy-start | bytes 1572868
Sparse Core Ops, SparseCore 0:
  184.6 73.8 reduce-scatter.1

commit v10 on v9

--- a/solution.py
+++ b/solution.py
@@ -156,9 +156,9 @@
     q_w,
     k_w,
     v_w,
-    g_w,
-    u_w,
-    d_w,
+    g_any,
+    u_any,
+    d_any,
     o_w,
     gain1,
     gain2,
@@ -174,6 +174,9 @@
     rows,
     weights,
     packed,
+    g_w,
+    u_w,
+    d_w,
     ls,
     w0,
     w1,
@@ -198,6 +201,7 @@
     qw = group * HEAD_DIM
     width = t_ref.shape[1]
     met = greet([me.any_chip(k) for k in range(1, chips)] + [me.sibling()])
+    loads = [move(f, t, ls, 4 + i) for i, (f, t) in enumerate(((g_any, g_w), (u_any, u_w), (d_any, d_w)))]
     first_gain, second_gain = column_of(low(gain1[...])), column_of(low(gain2[...]))
     for g in range(4):
         at = slice(g * qw, (g + 1) * qw)
@@ -208,7 +212,6 @@
             for half in range(2):
                 start = qw + (2 * pair + half) * PAIR
                 w_ref[g, :, start : start + PAIR] = pair_up(key, half, value, half).astype(BF16)
-    e_ref[...] = d_w[...].astype(BF16).reshape(e_ref.shape)
     wo_ref[...] = o_w[...].astype(BF16)
     x = t_ref[...].astype(F32)
     rows[0] = (x * lax.rsqrt(jnp.mean(x * x, axis=-1, keepdims=True) + EPS)).astype(BF16)
@@ -224,6 +227,9 @@
         )
     outs = [send(wo_ref, here, (o0, o1), k, me.line(k)) for k in range(1, zc)]
     blocks = [send(rows.at[0], rows.at[k], (n0, n1), k, me.plane(k)) for k in range(1, 4)]
+    for copy in loads:
+        copy.wait()
+    e_ref[...] = d_w[...].astype(BF16).reshape(e_ref.shape)
     units = g_w.shape[1] // (4 * zc)
     for which, ref in enumerate((g_w, u_w)):
         for g in range(4):
@@ -349,7 +355,7 @@
             struct((zc, 2, 4, BLOCK + own, PAIR)),
             struct((2, zc, 2, 2, count, width)),
         ),
-        [VM] * 10,
+        [VM] * 4 + [ANY] * 3 + [VM] * 3,
         (ANY,) * 5,
         [
             pltpu.VMEM((4,) + piece, BF16),
@@ -359,6 +365,7 @@
             pltpu.VMEM((4, own, width), BF16),
             pltpu.VMEM((2, zc, 2, 2) + piece, BF16),
             pltpu.VMEM((group, 4, BLOCK + own, PAIR), BF16),
+            *[pltpu.VMEM(w.shape, F32) for w in matrices[3:6]],
             DMA((10,)),
         ]
         + both(chips)

time: 340 us -> 338 us (level)
  transfers between devices with their start and end apart: 10 -> 10, of which waited for: 1 -> 1; matrix products, arithmetic and copies ran while one was open for 0% -> 0% of each run, Pallas kernels for 32% -> 33%
where the time goes in v10:
time: 338 us; the launch traced here: 339 us
  Pallas kernels  303 us (90%)
  between operations  14.3 us (4%)
  starting transfers between devices  11.3 us (3%)
  waiting for transfers between devices  8.18 us (2%)
    pallas_call x5, Pallas kernels, exchange(): pl.pallas_call(kernel, out_shape=out_shape, in_specs=in_specs, out_specs=...  233 us
    pallas_call x1, Pallas kernels, attention_backward(): pl.pallas_call(functools.partial(backward_kernel, workers), out_shape=str...  35.4 us
    pallas_call x1, Pallas kernels, attention_forward(): pl.pallas_call(functools.partial(forward_kernel, workers), out_shape=(str...  29.4 us
    reduce_scatter x1, waiting for transfers between devices, body(): lax.psum_scatter(shares.reshape(zc * 2 * 12, feature_rows, width), ('z',...  8.14 us
    ppermute x7, starting transfers between devices, around(): return lax.ppermute(value, ('head', 'y'), [(i, i ^ k) for i in range(4)])  7.33 us
  transfers between devices with their start and end apart: 10, of which 1 were waited for; matrix products, arithmetic and copies ran while one was open for 0% of the time, Pallas kernels for 33%

profile of v10, /device:TPU:0, one launch (start us, length us, event | category | flops | bytes accessed | tf_op | source)
XLA Modules:
  0.0 338.8 jit_solution(612469428380082058)
XLA Ops:
  7.2 0.0 reduce-scatter.2.cloned.1.call-start
  7.2 0.0 copy-start.4
  7.2 0.0 copy-start.5
  7.2 68.8 %shard_map.212 = (bf16[4,256,1024]{2,1,0:T(8,128)(2,1)}, bf16[2,4,2,2,32,768]{5,4,3,2,1,0:T(8,128)(2,1)}, bf16[2,2,3,32,1024]{4,3,2,1,0:T(8,128)(2,1)}, bf16[4,2...) custom-call(bf16[256,1024]{1,0:T(8,128)(2,1)} %x_any.1, f32[32,1024]{1,0:T(8,128)} %q_any.1, ...), custom_call_target="tpu_custom_call" | custom-call | flops 2147483648 | bytes 16777216 | tf_op jit(solution)/shard_map/pallas_call | solution.py:139
  76.1 3.4 collective-permute-start.4
  79.4 0.5 collective-permute-start.3
  80.0 0.0 copy-done.4
  80.0 0.5 collective-permute-start.2
  80.5 1.0 collective-permute-start.1
  81.6 1.9 collective-permute-start
  83.5 0.0 copy-done.5
  83.5 0.1 reshape.66
  83.6 0.6 reshape.67.anchor_ref
  84.3 29.4 %shard_map.213 = (bf16[32,128,128]{2,1,0:T(8,128)(2,1)}, bf16[8192,128]{1,0:T(8,128)(2,1)}, bf16[128,8192]{1,0:T(8,128)(2,1)}, bf16[8,512,128]{2,1,0:T(8,128)(2,...) custom-call(s32[64]{0:T(128)} %reshape.67.anchor_ref, s32[8]{0:T(128)} %lens_ref.3, ...), custom_call_target="tpu_custom_call" | custom-call | flops 4294967296 | bytes 8388608 | tf_op jit(solution)/shard_map/pallas_call | solution.py:1316
  113.7 20.5 %shard_map.214 = (bf16[256,1024]{1,0:T(8,128)(2,1)}, f32[256,1024]{1,0:T(8,128)}, bf16[256,1024]{1,0:T(8,128)(2,1)}) custom-call(bf16[4,2,4,128,128]{4,3,2,1,0:T(8,128)(2,1)} %bitcast.18, bf16[256,1024]{1,0:T(8,128)(2,1)} %x_any.1, bf16[1024,1024]{1,0:T(8,128)(2,1)} %bitcast.13), custom_call_target="tpu_custom_call" | custom-call | tf_op jit(solution)/shard_map/pallas_call | solution.py:139
  134.2 0.0 collective-permute-done.2.cd_ref
  134.2 0.0 copy-start.9
  134.2 0.0 collective-permute-done.1.cc_ref
  134.2 0.0 copy-start.10
  134.2 0.0 collective-permute-done.cb_ref
  134.2 0.0 collective-permute-done.4.rest_2_
  134.3 0.0 copy-start.6
  134.3 0.0 collective-permute-done.3.rest_0_
  134.3 0.0 copy-start.7
  134.3 0.7 copy-done.9
  135.0 0.2 copy-done.10
  135.2 0.3 copy-done.6
  135.4 0.3 copy-done.7
  135.7 49.1 %shard_map.215 = (bf16[4,2,32,1024]{3,2,1,0:T(8,128)(2,1)}, bf16[4,2,32,1024]{3,2,1,0:T(8,128)(2,1)}, bf16[4,2,32,1024]{3,2,1,0:T(8,128)(2,1)}, bf16[4,2,32,1024...) custom-call(bf16[256,1024]{1,0:T(8,128)(2,1)} %get-tuple-element.64.n_ref, ...), custom_call_target="tpu_custom_call" | custom-call | flops 19327352832 | bytes 67108864 | tf_op jit(solution)/shard_map/pallas_call | solution.py:139
  184.8 0.0 reduce-scatter.2.cloned.1.call-update
  184.8 26.5 %shard_map.216 = (f32[256,1024]{1,0:T(8,128)}, bf16[4,2,4,128,128]{4,3,2,1,0:T(8,128)(2,1)}, bf16[4,2,32,1024]{3,2,1,0:T(8,128)(2,1)}, bf16[4,2,32,1024]{3,2,1,0...) custom-call(f32[256,1024]{1,0:T(8,128)} %get-tuple-element.67.c_ref,, ...), custom_call_target="tpu_custom_call" | custom-call | flops 1073741824 | bytes 8388608 | tf_op jit(solution)/shard_map/pallas_call | solution.py:139
  211.3 0.0 copy-done.8
  211.3 0.3 collective-permute-start.5
  211.6 1.6 collective-permute-start.6
  213.3 1.6 collective-permute-start.7
  214.9 0.3 collective-permute-start.8
  215.1 35.4 %shard_map.217 = bf16[32,384,128]{2,1,0:T(8,128)(2,1)} custom-call(s32[64]{0:T(128)} %reshape.67.anchor_ref, s32[8]{0:T(128)} %lens_ref.3, s32[1]{0:T(128)} %bitcast.1.who_ref, bf16[32,128,128]{2,1,0:T(8,128)(2,1)} %bitcast.24, bf16[8192,128]{1,0:T(8,128)(2,1)} %get-tuple-element.75.kv_ref, bf16[128,8192]{1,0:T(8,128)(2,1)} %get-tuple-element.76.kvt_ref, ...), custom_call_target="tpu_custom_call" | custom-call | flops 10737418240 | bytes 8388608 | tf_op jit(solution)/shard_map/pallas_call | solution.py:1437
  250.5 0.0 collective-permute-done.5.yd_ref
  250.5 0.0 collective-permute-done.6.vb_ref
  250.6 0.0 copy-start.1
  250.6 0.0 collective-permute-done.7.vc_ref
  250.6 0.0 copy-start.2
  250.6 0.0 collective-permute-done.8.vd_ref
  250.6 0.0 copy-start.3
  250.6 8.1 %reduce-scatter.2.cloned.1.call-done.f_ref.ds_any = bf16[12,32,1024]{2,1,0:T(8,128)(2,1)} async-done(((bf16[96,32,1024]{2,1,0:T(8,128)(2,1)}), bf16[12,32,1024]{2,1,0:T(8,128)(2,1)}) %reduce-scatter.2.cloned.1.call-update) | async-done | bytes 786448 | tf_op jit(solution)/shard_map/reduce_scatter | solution.py:1521
  258.8 0.0 copy-done.1
  258.8 68.4 %shard_map.218 = (bf16[256,1024]{1,0:T(8,128)(2,1)}, bf16[4,4,32,768]{3,2,1,0:T(8,128)(2,1)}, f32[32,1024]{1,0:T(8,128)}, bf16[4,2,32,1024]{3,2,1,0:T(8,128)(2,1)}, bf16[256,1024]{1,0:T(8,128)(2,1)}) custom-call(bf16[4,2,4,384,128]{4,3,2,1,0:T(8,128)(2,1)} %bitcast.16, bf16[4,256,1024]{2,1,0:T(8,128)(2,1)} %get-tuple-element.81.n_any, ...), custom_call_target="tpu_custom_call" | custom-call | flops 3221225472 | bytes 25165824 | tf_op jit(solution)/shard_map/pallas_call | solution.py:139
  327.2 4.8 %shard_map.219 = (bf16[256,1024]{1,0:T(8,128)(2,1)}, bf16[256,1024]{1,0:T(8,128)(2,1)}, f32[32,1024]{1,0:T(8,128)}, f32[1,32]{1,0:T(1,128)}, f32[32,1024]{1,0:T(...) custom-call(bf16[256,1024]{1,0:T(8,128)(2,1)} %get-tuple-element.93., ...), custom_call_target="tpu_custom_call" | custom-call | tf_op jit(solution)/shard_map/pallas_call | solution.py:1083
  (6 shorter events, 0.0 us)
Async XLA Ops:
  7.2 251.6 %reduce-scatter.2.cloned.1.call-start = ((), (), s32[]{:S(2)}) async-start(), calls=%async_computation.1 | async-start | bytes 7077888 | tf_op jit(solution)/shard_map/reduce_scatter | solution.py:1521
  7.2 72.8 %copy-start.4 = (bf16[256,1024]{1,0:T(8,128)(2,1)S(1)}, bf16[256,1024]{1,0:T(8,128)(2,1)}, u32[]{:S(2)}) copy-start(bf16[256,1024]{1,0:T(8,128)(2,1)} %t_ref.3) | copy-start | bytes 1572868
  7.2 76.3 %copy-start.5 = (s32[64]{0:T(128)S(1)}, s32[64]{0:T(128)}, u32[]{:S(2)}) copy-start(s32[64]{0:T(128)} %param.24) | copy-start | bytes 772
  76.1 58.2 %collective-permute-start.4 = (bf16[2,2,3,32,1024]{4,3,2,1,0:T(8,128)(2,1)}, bf16[2,2,3,32,1024]{4,3,2,1,0:T(8,128)(2,1)S(1)}, u32[]{:S(2)}, u32[]{:S(2)}) collective-permute-start(bf16[2,2,3,32,1024]{4,3,2,1,0:T(8,128)(2,1)} %get-tuple-element.66.rest_1_), channel_id=1, source_target_pairs={{0,8},{4,12},{8,0},{12,4},{1,9},{5,13},{9,1},{13,5},{2,10},{6,14},... | collective-permute-start | bytes 2359304 | tf_op jit(solution)/shard_map/ppermute | solution.py:1462
  79.4 54.8 %collective-permute-start.3 = (bf16[2,2,3,32,1024]{4,3,2,1,0:T(8,128)(2,1)}, bf16[2,2,3,32,1024]{4,3,2,1,0:T(8,128)(2,1)S(1)}, u32[]{:S(2)}, u32[]{:S(2)}) collective-permute-start(bf16[2,2,3,32,1024]{4,3,2,1,0:T(8,128)(2,1)} %get-tuple-element.66.rest_1_), channel_id=1, source_target_pairs={{0,4},{4,0},{8,12},{12,8},{1,5},{5,1},{9,13},{13,9},{2,6},{6,2},{1... | collective-permute-start | bytes 2359304 | tf_op jit(solution)/shard_map/ppermute | solution.py:1462
  80.0 54.2 %collective-permute-start.2 = (bf16[256,1024]{1,0:T(8,128)(2,1)S(1)}, bf16[256,1024]{1,0:T(8,128)(2,1)S(1)}, u32[]{:S(2)}, u32[]{:S(2)}) collective-permute-start(bf16[256,1024]{1,0:T(8,128)(2,1)S(1)} %copy-done.4), channel_id=1, source_target_pairs={{0,18},{2,16},{16,2},{18,0},{1,19},{3,17},{17,3},{19,1},{4,22},{6,... | collective-permute-start | bytes 1572872 | tf_op jit(solution)/shard_map/ppermute | solution.py:1458
  80.5 53.7 %collective-permute-start.1 = (bf16[256,1024]{1,0:T(8,128)(2,1)S(1)}, bf16[256,1024]{1,0:T(8,128)(2,1)S(1)}, u32[]{:S(2)}, u32[]{:S(2)}) collective-permute-start(bf16[256,1024]{1,0:T(8,128)(2,1)S(1)} %copy-done.4), channel_id=1, source_target_pairs={{0,16},{2,18},{16,0},{18,2},{1,17},{3,19},{17,1},{19,3},{4,20},{6,... | collective-permute-start | bytes 1572872 | tf_op jit(solution)/shard_map/ppermute | solution.py:1458
  81.6 52.7 %collective-permute-start = (bf16[256,1024]{1,0:T(8,128)(2,1)S(1)}, bf16[256,1024]{1,0:T(8,128)(2,1)}, u32[]{:S(2)}, u32[]{:S(2)}) collective-permute-start(bf16[256,1024]{1,0:T(8,128)(2,1)S(1)} %copy-done.4), channel_id=1, source_target_pairs={{0,2},{2,0},{16,18},{18,16},{1,3},{3,1},{17,19},{19,17},{4,6},{6,4... | collective-permute-start | bytes 1572872 | tf_op jit(solution)/shard_map/ppermute | solution.py:1458
  134.2 0.8 copy-start.9
  134.2 0.9 copy-start.10
  134.3 1.2 copy-start.6
  134.3 1.4 copy-start.7
  184.8 26.5 %copy-start.8 = (bf16[4,2,32,1024]{3,2,1,0:T(8,128)(2,1)S(1)}, bf16[4,2,32,1024]{3,2,1,0:T(8,128)(2,1)}, u32[]{:S(2)}) copy-start(bf16[4,2,32,1024]{3,2,1,0:T(8,128)(2,1)} %get-tuple-element.88) | copy-start | bytes 1572868
  211.3 39.2 %collective-permute-start.5 = (bf16[4,2,32,1024]{3,2,1,0:T(8,128)(2,1)S(1)}, bf16[4,2,32,1024]{3,2,1,0:T(8,128)(2,1)S(1)}, u32[]{:S(2)}, u32[]{:S(2)}) collective-permute-start(bf16[4,2,32,1024]{3,2,1,0:T(8,128)(2,1)S(1)} %copy-done.8), channel_id=1, source_target_pairs={{0,18},{2,16},{16,2},{18,0},{1,19},{3,17},{17,3},{19,1},{4,22},{6,... | collective-permute-start | bytes 1572872 | tf_op jit(solution)/shard_map/ppermute | solution.py:1458
  211.6 38.9 %collective-permute-start.6 = (bf16[4,2,32,1024]{3,2,1,0:T(8,128)(2,1)}, bf16[4,2,32,1024]{3,2,1,0:T(8,128)(2,1)S(1)}, u32[]{:S(2)}, u32[]{:S(2)}) collective-permute-start(bf16[4,2,32,1024]{3,2,1,0:T(8,128)(2,1)} %get-tuple-element.90), channel_id=1, source_target_pairs={{0,2},{2,0},{16,18},{18,16},{1,3},{3,1},{17,19},{19,17},{4,6},{6,4... | collective-permute-start | bytes 1572872 | tf_op jit(solution)/shard_map/ppermute | solution.py:1458
  213.3 37.3 %collective-permute-start.7 = (bf16[4,2,32,1024]{3,2,1,0:T(8,128)(2,1)}, bf16[4,2,32,1024]{3,2,1,0:T(8,128)(2,1)S(1)}, u32[]{:S(2)}, u32[]{:S(2)}) collective-permute-start(bf16[4,2,32,1024]{3,2,1,0:T(8,128)(2,1)} %get-tuple-element.91), channel_id=1, source_target_pairs={{0,16},{2,18},{16,0},{18,2},{1,17},{3,19},{17,1},{19,3},{4,20},{6,... | collective-permute-start | bytes 1572872 | tf_op jit(solution)/shard_map/ppermute | solution.py:1458
  214.9 35.7 %collective-permute-start.8 = (bf16[4,2,32,1024]{3,2,1,0:T(8,128)(2,1)}, bf16[4,2,32,1024]{3,2,1,0:T(8,128)(2,1)S(1)}, u32[]{:S(2)}, u32[]{:S(2)}) collective-permute-start(bf16[4,2,32,1024]{3,2,1,0:T(8,128)(2,1)} %get-tuple-element.92), channel_id=1, source_target_pairs={{0,18},{2,16},{16,2},{18,0},{1,19},{3,17},{17,3},{19,1},{4,22},{6,... | collective-permute-start | bytes 1572872 | tf_op jit(solution)/shard_map/ppermute | solution.py:1458
  250.5 8.2 %copy-start = (bf16[4,2,32,1024]{3,2,1,0:T(8,128)(2,1)}, bf16[4,2,32,1024]{3,2,1,0:T(8,128)(2,1)S(1)}, u32[]{:S(2)}) copy-start(bf16[4,2,32,1024]{3,2,1,0:T(8,128)(2,1)S(1)} %collective-permute-done.5.yd_ref) | copy-start | bytes 1572868
  250.6 8.2 %copy-start.1 = (bf16[4,2,32,1024]{3,2,1,0:T(8,128)(2,1)}, bf16[4,2,32,1024]{3,2,1,0:T(8,128)(2,1)S(1)}, u32[]{:S(2)}) copy-start(bf16[4,2,32,1024]{3,2,1,0:T(8,128)(2,1)S(1)} %collective-permute-done.6.vb_ref) | copy-start | bytes 1572868
  250.6 8.2 %copy-start.2 = (bf16[4,2,32,1024]{3,2,1,0:T(8,128)(2,1)}, bf16[4,2,32,1024]{3,2,1,0:T(8,128)(2,1)S(1)}, u32[]{:S(2)}) copy-start(bf16[4,2,32,1024]{3,2,1,0:T(8,128)(2,1)S(1)} %collective-permute-done.7.vc_ref) | copy-start | bytes 1572868
  250.6 8.2 %copy-start.3 = (bf16[4,2,32,1024]{3,2,1,0:T(8,128)(2,1)}, bf16[4,2,32,1024]{3,2,1,0:T(8,128)(2,1)S(1)}, u32[]{:S(2)}) copy-start(bf16[4,2,32,1024]{3,2,1,0:T(8,128)(2,1)S(1)} %collective-permute-done.8.vd_ref) | copy-start | bytes 1572868
Sparse Core Ops, SparseCore 0:
  184.9 73.7 reduce-scatter.1
